TPU v7x, 256 devices: a whole 4x4x8 slice. The times are simulated.
256 devices in a mesh: seq: 64 (over x, z, core), tp: 4 (over y).
Axes of the slice: x: 4, y: 4, z: 8, core: 2. Of those that a mesh axis runs over, the one named last changes fastest.
Arguments:
- hidden_in: bfloat16 [16384, 1536], P('seq', 'tp'), may hold values from -6 to 6
- w_in_gate: float32 [1536, 3072], P('seq', 'tp'), may hold values from -0.15625 to 0.15625
- w_in_value: float32 [1536, 3072], P('seq', 'tp'), may hold values from -0.15625 to 0.15625
- w_in_shared: float32 [1536, 256], P('seq'), may hold values from -0.15625 to 0.15625
- w_in_step: float32 [1536, 48], P('seq', 'tp'), may hold values from -0.15625 to 0.15625
- conv_value: float32 [4, 3072], P(None, 'tp'), may hold values from -3 to 3
- conv_shared: float32 [4, 256], replicated, may hold values from -3 to 3
- dt_bias: float32 [48], P('tp'), may hold values from -4 to -2
- a_log: float32 [48], P('tp'), may hold values from -8 to 0
- skip_gain: float32 [48], P('tp'), may hold values from 0.6 to 4.8
- norm_gain: float32 [3072], P('tp'), may hold values from 0.1 to 1.9
- w_out: float32 [3072, 1536], P('tp', 'seq'), may hold values from -0.109375 to 0.109375
- prompt_lengths: int32 [8], replicated, may hold values from 1 to 8192, 16384 in all
- row_blocks: int32 [64], replicated, may hold values from 0 to 63, each once
Outputs:
- mixed_out: bfloat16 [16384, 1536], P('seq', 'tp')
Inputs may be any that keep to these rules, and one draw needn't show every extreme that they name: `prompt_lengths`: 8 lengths that sum to 16384, the longest exactly 8192. `row_blocks`: a permutation of the row blocks.
All inputs are finite; a program needn't handle non-finite values.
Results may differ from a plain program's by a relative error of at most 0.02.
Values may be sent and summed in bfloat16 or wider, within the bound.
No kernel may reach another device: no remote copies, remote signals or barrier semaphores. Data moves between devices by JAX's collectives and lax.ppermute only.
A program may use at most 128 MiB of HBM per device.

v0:
```python
import jax
import jax.numpy as jnp
from jax import lax
from jax.sharding import PartitionSpec as P

EPSILON = 1e-05
HIGHEST_PREC = lax.Precision.HIGHEST


def passed_along(block, axis, distance):
    devices = range(lax.axis_size(axis))
    route = [(i - distance, i) for i in devices if i - distance in devices]
    return lax.ppermute(block, axis, route)


def prefix_2(x, axis, combine, identity):
    count, here = (lax.axis_size(axis), lax.axis_index(axis))
    everything = jax.tree.map(
        lambda part, kind: lax.all_gather(part.astype(kind), axis), x, (jnp.bfloat16, jnp.bfloat16)
    )
    start = jax.tree.map(
        lambda part, zero: jnp.broadcast_to(jnp.asarray(zero, part.dtype), part.shape), x, identity
    )

    def turn(k, before):
        reached = k < here
        new = combine(
            before, jax.tree.map(lambda part, own: part[k].astype(own.dtype), everything, x)
        )
        return jax.tree.map(lambda a, b: jnp.where(reached, a, b), new, before)

    return lax.fori_loop(0, count, turn, start)


def segment_of(positions, doc_ends):
    return jnp.sum((positions[:, None] >= doc_ends[None, :]).astype(jnp.int32), axis=1)


def span_parts(values, b_half, c_half, steps_dt, decay_rates, segments, prev_seg):
    length = values.shape[0]
    b_rows = b_half.astype(jnp.float32)
    cumulative = jnp.cumsum(-steps_dt * decay_rates[None, :], axis=0)
    places = jnp.arange(length)
    causal = (places[:, None] >= places[None, :]) & (segments[:, None] == segments[None, :])
    gaps_log = jnp.where(causal[:, :, None], cumulative[:, None, :] - cumulative[None, :, :], 0.0)
    decays_in = jnp.where(causal[:, :, None], jnp.exp(gaps_log), 0.0)
    scores = jnp.dot(c_half, b_half.T, preferred_element_type=jnp.float32)
    weights = scores[:, :, None] * decays_in * steps_dt[None, :, :]
    intra_part = jnp.einsum("ijh,jhp->ihp", weights, values, precision=HIGHEST_PREC)
    carry_in = jnp.where((segments == prev_seg)[:, None], jnp.exp(cumulative), 0.0)
    tail_weight = (
        jnp.where(
            (segments == segments[-1])[:, None], jnp.exp(cumulative[-1][None, :] - cumulative), 0.0
        )
        * steps_dt
    )
    fresh_state = jnp.einsum("jh,jhp,jn->hpn", tail_weight, values, b_rows, precision=HIGHEST_PREC)
    keep_factor = jnp.where(segments[-1] == prev_seg, jnp.exp(cumulative[-1]), 0.0)
    return (intra_part, carry_in, fresh_state, keep_factor)


def combine(earlier, later):
    return (earlier[0] * later[0], later[0][:, None, None] * earlier[1] + later[1])


def on_device(
    hidden_in,
    w_in_gate,
    w_in_value,
    w_in_shared,
    w_in_step,
    conv_value,
    conv_shared,
    dt_bias,
    a_log,
    skip_gain,
    norm_gain,
    w_out,
    prompt_lengths,
    row_blocks,
):
    seq_count = lax.axis_size("seq")
    tokens_here = hidden_in.shape[0]
    edge_count = conv_value.shape[0] - 1
    gathered = lax.all_gather(hidden_in, "tp", axis=1, tiled=True)
    row_count = gathered.shape[0]
    model_width = gathered.shape[1]
    permuted = jnp.take(
        gathered.reshape(row_count, seq_count, model_width // seq_count), row_blocks, axis=1
    ).reshape(row_count, model_width)
    stored = (
        w_in_gate.astype(jnp.bfloat16),
        w_in_value.astype(jnp.bfloat16),
        w_in_shared.astype(jnp.bfloat16),
        w_in_step.astype(jnp.bfloat16),
    )
    pieces = (
        lax.all_gather(stored[0], "seq", axis=0, tiled=True),
        lax.all_gather(stored[1], "seq", axis=0, tiled=True),
        lax.all_gather(stored[2], "seq", axis=0, tiled=True),
        lax.all_gather(stored[3], "seq", axis=0, tiled=True),
    )
    projected = tuple(
        (
            jnp.dot(permuted, weight_piece, preferred_element_type=jnp.float32)
            for weight_piece in pieces
        )
    )
    gate_all, value_all, shared_all, raw_all = [result.astype(jnp.bfloat16) for result in projected]
    mixed_in = jnp.concatenate([value_all, shared_all], axis=1)
    edge_mix = passed_along(mixed_in[tokens_here - edge_count :], "seq", 1)
    doc_ends = jnp.cumsum(prompt_lengths)
    first_pos = lax.axis_index("seq") * tokens_here
    positions = first_pos + jnp.arange(tokens_here, dtype=jnp.int32)
    edge_positions = first_pos - edge_count + jnp.arange(edge_count, dtype=jnp.int32)
    segments = segment_of(positions, doc_ends)
    ext_segments = jnp.concatenate([segment_of(edge_positions, doc_ends), segments])
    ext_rows = jnp.concatenate([edge_mix, mixed_in], axis=0)
    kernel = jnp.concatenate([conv_value, conv_shared], axis=1)
    conv_sum = jnp.zeros(mixed_in.shape, jnp.float32)
    for tap_index in range(edge_count + 1):
        same_doc = (ext_segments[tap_index : tap_index + tokens_here] == segments)[:, None]
        conv_sum = conv_sum + jnp.where(
            same_doc,
            kernel[tap_index][None, :]
            * ext_rows[tap_index : tap_index + tokens_here].astype(jnp.float32),
            0.0,
        )
    convolved = jax.nn.silu(conv_sum).astype(jnp.bfloat16)
    local_inner = conv_value.shape[1]
    local_heads = dt_bias.shape[0]
    head_dim = local_inner // local_heads
    state_size = conv_shared.shape[1] // 2
    values = (
        convolved[:, :local_inner].astype(jnp.float32).reshape(tokens_here, local_heads, head_dim)
    )
    b_half = convolved[:, local_inner : local_inner + state_size]
    c_half = convolved[:, local_inner + state_size :]
    c_rows = c_half.astype(jnp.float32)
    steps_dt = jax.nn.softplus(raw_all.astype(jnp.float32) + dt_bias[None, :])
    decay_rates = jnp.exp(a_log)
    prev_first = segment_of(jnp.reshape(first_pos - 1, (1,)), doc_ends)[0]
    device_keep = jnp.ones((local_heads,), jnp.float32)
    device_state = jnp.zeros((local_heads, head_dim, state_size), jnp.float32)
    parts = span_parts(values, b_half, c_half, steps_dt, decay_rates, segments, prev_first)
    device_keep = parts[3] * device_keep
    device_state = parts[3][:, None, None] * device_state + parts[2]
    identity = (jnp.ones_like(device_keep), jnp.zeros_like(device_state))
    prefix = prefix_2((device_keep, device_state), "seq", combine, identity)
    carried = prefix[1]
    intra_part, carry_in, fresh_state, keep_factor = parts
    inter_part = (
        jnp.einsum("in,hpn->ihp", c_rows, carried, precision=HIGHEST_PREC) * carry_in[:, :, None]
    )
    outputs = intra_part + inter_part
    mixed_heads = outputs + skip_gain[None, :, None] * values
    gated = mixed_heads.reshape(tokens_here, local_inner) * jax.nn.silu(
        gate_all.astype(jnp.float32)
    )
    squares = jnp.sum(gated * gated, axis=1)
    square_total = lax.psum(squares, "tp")
    mean_square = square_total / (local_inner * lax.axis_size("tp"))
    normed = (gated * lax.rsqrt(mean_square + EPSILON)[:, None] * norm_gain[None, :]).astype(
        jnp.bfloat16
    )
    out_weight = w_out.astype(jnp.bfloat16)
    partial_terms = jnp.dot(
        normed,
        lax.all_gather(out_weight, "seq", axis=1, tiled=True),
        preferred_element_type=jnp.float32,
    )
    return lax.psum_scatter(
        partial_terms.astype(jnp.bfloat16), "tp", scatter_dimension=1, tiled=True
    )


def solution(mesh):
    return jax.shard_map(
        on_device,
        mesh=mesh,
        in_specs=(
            P("seq", "tp"),
            P("seq", "tp"),
            P("seq", "tp"),
            P("seq", None),
            P("seq", "tp"),
            P(None, "tp"),
            P(),
            P("tp"),
            P("tp"),
            P("tp"),
            P("tp"),
            P("tp", "seq"),
            P(),
            P(),
        ),
        out_specs=P("seq", "tp"),
        check_vma=False,
    )
```

profile of v0, /device:TPU:1, one launch (start us, length us, event | category | flops | bytes accessed | tf_op | source)
XLA Modules:
  0.0 419.9 jit_solution(3729731392679539498)
XLA Ops:
  6.5 1.5 convert_element_type.112
  9.6 1.1 copy.39
  13.0 48.6 %all-gather.1 = bf16[64,24,12]{1,2,0:T(8,128)(2,1)S(1)} all-gather(bf16[1,24,12]{1,2,0:T(8,128)(2,1)S(1)} %convert_bitcast_fusion), channel_id=1, replica_groups=mesh['seq'=64,'tp'=4] {'seq'}, dimensions={0}, use_global_device_ids=true | all-gather | bytes 37440 | tf_op jit(solution)/shard_map/all_gather | solution.py:101
  63.2 12.4 %all_gather.28 = bf16[256,1536]{0,1:T(8,128)(2,1)S(1)} all-gather(bf16[256,384]{0,1:T(8,128)(2,1)S(1)} %copy.39), channel_id=1, replica_groups=mesh['seq'=64,'tp'=4] {'tp'}, dimensions={1}, use_global_device_ids=true | all-gather | bytes 983040 | tf_op jit(solution)/shard_map/all_gather | solution.py:85
  80.0 51.3 %all_gather.30 = bf16[1536,256]{1,0:T(8,128)(2,1)S(1)} all-gather(bf16[24,256]{1,0:T(8,128)(2,1)S(1)} %convert_element_type.114), channel_id=1, replica_groups=mesh['seq'=64,'tp'=4] {'seq'}, dimensions={0}, use_global_device_ids=true | all-gather | bytes 798720 | tf_op jit(solution)/shard_map/all_gather | solution.py:100
  131.4 1.3 broadcast_compare_fusion
  133.2 2.5 convolution_convert_fusion.2
  135.7 1.9 collective-permute-start
  137.6 1.1 collective-permute-done
  139.9 1.2 fusion.20
  143.0 40.6 %all-gather.2 = bf16[64,1,12]{2,1,0:T(2,128)(2,1)S(1)} all-gather(bf16[1,1,12]{2,1,0:T(2,128)(2,1)S(1)} %bitcast.96), channel_id=1, replica_groups=mesh['seq'=64,'tp'=4] {'seq'}, dimensions={0}, use_global_device_ids=true | all-gather | bytes 1560 | tf_op jit(solution)/shard_map/all_gather | solution.py:19
  183.7 3.6 fusion.14
  187.3 44.3 %all-gather.14.cloned.1.call-done = bf16[768,64,128]{2,1,0:T(8,128)(2,1)} async-done(((bf16[12,64,128]{2,1,0:T(8,128)(2,1)}), bf16[768,64,128]{2,1,0:T(8,128)(2,1)}) %all-gather.14.cloned.1.call-update) | async-done | bytes 12582928 | tf_op jit(solution)/shard_map/all_gather | solution.py:19
  231.6 70.1 %while.14 = (s32[]{:T(128)}, f32[12,64,128]{2,1,0:T(8,128)S(1)}, s32[]{:T(128)}, bf16[64,12]{1,0:T(8,128)(2,1)S(1)}, bf16[64,12,64,128]{3,2,1,0:T(8,128)(2,1)}, /*index=5*/s32[]{:T(128)}, s32[]{:T(128)}) while((s32[]{:T(128)}, f32[12,64,128]{2,1,0:T(8,128)S(1)}, s32[]{:T(128)}, bf16[64,12]{1,0:T(8,128)(2,1)S(1)}, ...), condition=%wide.region_7.8_spmd.clone, body=%wide.region_6.7_spmd.clone.sunk | while | flops 491536 | bytes 983265 | solution.py:32
  243.7 1.1 fusion.58
  284.2 1.1 fusion.58
  286.4 1.1 fusion.58
  288.6 1.1 fusion.58
  290.8 1.1 fusion.58
  291.9 1.1 fusion.58
  296.3 1.1 fusion.58
  299.6 1.1 fusion.58
  300.6 1.1 fusion.58
  301.7 1.6 fusion.18
  303.7 5.2 %all-gather.10.cloned.1.call-done = bf16[1536,768]{1,0:T(8,128)(2,1)} async-done(((bf16[24,768]{1,0:T(8,128)(2,1)}), bf16[1536,768]{1,0:T(8,128)(2,1)}) %all-gather.10.cloned.1.call-update) | async-done | bytes 2359312 | tf_op jit(solution)/shard_map/all_gather | solution.py:98
  308.9 2.7 multiply_reduce_fusion
  311.5 8.5 %psum.7 = f32[256]{0:T(256)S(1)} all-reduce(f32[256]{0:T(256)S(1)} %get-tuple-element.160), channel_id=1, replica_groups=mesh['seq'=64,'tp'=4] {'tp'}, use_global_device_ids=true, to_apply=%region_9.10 | all-reduce | flops 256 | bytes 2048 | tf_op jit(solution)/shard_map/psum | solution.py:161
  320.0 66.6 %all-gather.12.cloned.1.call-done = bf16[768,1536]{0,1:T(8,128)(2,1)} async-done(((bf16[768,24]{0,1:T(8,128)(2,1)}), bf16[768,1536]{0,1:T(8,128)(2,1)}) %all-gather.12.cloned.1.call-update) | async-done | bytes 2359312 | tf_op jit(solution)/shard_map/all_gather | solution.py:169
  386.6 2.5 convolution_convert_fusion
  389.1 1.2 copy.50
  390.3 21.3 %reduce-scatter.4.cloned.1.call-done = bf16[384,256]{1,0:T(8,128)(2,1)} async-done(((bf16[1536,256]{1,0:T(8,128)(2,1)}), bf16[384,256]{1,0:T(8,128)(2,1)}) %reduce-scatter.4.cloned.1.call-update) | async-done | bytes 196624
  411.6 1.7 copy.51
  (196 shorter events, 71.1 us)
Async XLA Ops:
  6.5 126.6 %all-gather.8.cloned.1.call-start = ((), (), s32[]{:S(2)}) async-start(), calls=%async_computation.1 | async-start | bytes 2396160 | tf_op jit(solution)/shard_map/all_gather | solution.py:99
  8.1 223.6 %all-gather.14.cloned.1.call-start = ((), (), s32[]{:S(2)}) async-start(), calls=%async_computation.4 | async-start | bytes 12779520 | tf_op jit(solution)/shard_map/all_gather | solution.py:19
  75.6 0.9 copy-start.5
  76.3 3.6 copy-start.2
  76.3 3.6 copy-start.4
  135.7 3.1 collective-permute-start
  138.9 2.3 copy-start
  138.9 3.1 copy-start.1
  141.2 167.7 %all-gather.10.cloned.1.call-start = ((), (), s32[]{:S(2)}) async-start(), calls=%async_computation.2 | async-start | bytes 2396160 | tf_op jit(solution)/shard_map/all_gather | solution.py:98
  141.9 244.7 %all-gather.12.cloned.1.call-start = ((), (), s32[]{:S(2)}) async-start(), calls=%async_computation.3 | async-start | bytes 2396160 | tf_op jit(solution)/shard_map/all_gather | solution.py:169
  142.6 269.0 %reduce-scatter.4.cloned.1.call-start = ((), (), s32[]{:S(2)}) async-start(), calls=%async_computation.5 | async-start | bytes 983040
  231.6 70.1 %copy-start.6 = (f32[12]{0:T(128)S(1)}, f32[12]{0:T(128)}, u32[]{:S(2)}) copy-start(f32[12]{0:T(128)} %param.25) | copy-start | bytes 148
  303.6 83.0 %copy-start.3 = (f32[768]{0:T(1024)S(1)}, f32[768]{0:T(1024)}, u32[]{:S(2)}) copy-start(f32[768]{0:T(1024)} %param.26) | copy-start | bytes 9220
Sparse Core Ops, SparseCore 0:
  10.1 81.6 all-gather.7
  141.3 90.2 all-gather.13
  234.3 74.4 all-gather.9
  311.4 75.1 all-gather.11
  390.4 21.1 reduce-scatter.3
where the time goes:
time: 422 us; the launch traced here: 420 us
  blocking collectives  161 us (38%)
  waiting for transfers between devices  139 us (33%)
  other arithmetic  79 us (19%)
  matrix products  14.9 us (4%)
  between operations  14.6 us (3%)
  local copies, waits for them, and re-layouts  7.21 us (2%)
    select_n x64, other arithmetic, turn(): return jax.tree.map(lambda a, b: jnp.where(reached, a, b), new, before)  67.4 us
    all_gather x1, waiting for transfers between devices, on_device(): lax.all_gather(out_weight, 'seq', axis=1, tiled=True)  66.6 us
    all_gather x1, blocking collectives, on_device(): lax.all_gather(stored[2], 'seq', axis=0, tiled=True)  51.3 us
    all_gather x1, blocking collectives, on_device(): lax.all_gather(stored[3], 'seq', axis=0, tiled=True)  48.6 us
    all_gather x1, waiting for transfers between devices, prefix_2(): lax.all_gather(part.astype(kind), axis)  44.3 us
    all_gather x1, blocking collectives, prefix_2(): lax.all_gather(part.astype(kind), axis)  40.6 us
    unnamed x6, waiting for transfers between devices  21.4 us
    all_gather x1, blocking collectives, on_device(): gathered = lax.all_gather(hidden_in, 'tp', axis=1, tiled=True)  12.4 us
  transfers between devices with their start and end apart: 6, of which 5 were waited for; matrix products, arithmetic and copies ran while one was open for 21% of the time, Pallas kernels for 0%

commit v1 on v0

v1 whole, which is shorter than its diff:
```python
import jax
import jax.numpy as jnp
from jax import lax
from jax.experimental import pallas as pl
from jax.experimental.pallas import tpu as pltpu
from jax.sharding import Mesh, PartitionSpec as P

EPSILON = 1e-05
EDGE = 8
SEQ = ("x", "z", "core")
SIZES = (4, 8, 2)
BF16 = jnp.bfloat16
F32 = jnp.float32


def ahead(block, axis, distance):
    count = lax.axis_size(axis)
    return lax.ppermute(block, axis, [(i, (i + distance) % count) for i in range(count)])


def segment_of(positions, doc_ends):
    return jnp.sum((positions[:, None] >= doc_ends[None, :]).astype(jnp.int32), axis=1)


def scan_body(count, heads, sent_ref, out_ref):
    keeps = sent_ref[:, heads, :].astype(F32) + sent_ref[:, heads + 1, :].astype(F32)
    keeps = keeps.T
    rows = sent_ref.shape[1]
    carried = jnp.zeros((rows, keeps.shape[0]), F32)
    for k in range(count):
        out_ref[k] = carried.astype(BF16)
        keep = keeps[:rows, k : k + 1]
        carried = keep * carried + sent_ref[k].astype(F32)


def scan_states(sent, heads):
    count = sent.shape[0]
    return pl.pallas_call(
        lambda sent_ref, out_ref: scan_body(count, heads, sent_ref, out_ref),
        out_shape=jax.ShapeDtypeStruct(sent.shape, BF16),
        in_specs=[pl.BlockSpec(memory_space=pltpu.VMEM)],
        out_specs=pl.BlockSpec(memory_space=pltpu.VMEM),
        cost_estimate=pl.CostEstimate(
            flops=2 * sent.size, bytes_accessed=4 * sent.size, transcendentals=0
        ),
    )(sent)


def on_device(
    hidden_in,
    w_in_gate,
    w_in_value,
    w_in_shared,
    w_in_step,
    conv_value,
    conv_shared,
    dt_bias,
    a_log,
    skip_gain,
    norm_gain,
    w_out,
    prompt_lengths,
    row_blocks,
):
    x_size, z_size, core_size = SIZES
    seq_count = x_size * z_size * core_size
    tp_count = lax.axis_size("tp")
    tokens, features = hidden_in.shape
    rows_here, inner = w_in_value.shape
    shared = w_in_shared.shape[1]
    heads = dt_bias.shape[0]
    head_dim = inner // heads
    state = shared // 2
    x_at, z_at, core_at = (lax.axis_index(name) for name in SEQ)
    tp_at = lax.axis_index("tp")
    seq_at = (x_at * z_size + z_at) * core_size + core_at

    late = jnp.concatenate([w_in_gate.astype(BF16), w_out.T.astype(BF16)], axis=1)
    late = lax.all_gather(late, SEQ, axis=0, tiled=True)

    before = lax.ppermute(
        hidden_in[tokens - EDGE :], SEQ, [(i, i + 1) for i in range(seq_count - 1)]
    )
    mine = jnp.concatenate([before, hidden_in], axis=0)
    hidden = jnp.concatenate([mine] + [ahead(mine, "tp", d) for d in range(1, tp_count)], axis=1)

    spare = -(inner + shared + heads) % 128
    early = jnp.concatenate(
        [w_in_value, w_in_shared, w_in_step, jnp.zeros((rows_here, spare), F32)], axis=1
    ).astype(BF16)
    along_z = lax.all_gather(early, "z", axis=0, tiled=True)
    own = jnp.concatenate(
        [along_z] + [ahead(along_z, "x", d) for d in range(1, x_size)], axis=0
    )
    other = ahead(own, "core", 1)

    dx = jnp.arange(x_size, dtype=jnp.int32)[:, None]
    dz = jnp.arange(z_size, dtype=jnp.int32)[None, :]
    chips = (((x_at - dx) % x_size) * z_size + dz).reshape(-1) * core_size
    blocks_each = seq_count // tp_count

    def columns_for(stored):
        model = jnp.take(row_blocks, stored)
        piece = (tp_at - model // blocks_each) % tp_count
        place = piece * blocks_each + model % blocks_each
        cut = hidden.reshape(hidden.shape[0], seq_count, rows_here)
        return jnp.take(cut, place, axis=1).reshape(hidden.shape[0], -1)

    h_own = columns_for(chips + core_at)
    h_other = columns_for(chips + (1 - core_at))
    h_all = columns_for(jnp.arange(seq_count, dtype=jnp.int32))

    projected = (
        jnp.dot(h_own, own, preferred_element_type=F32)
        + jnp.dot(h_other, other, preferred_element_type=F32)
    ).astype(BF16)
    mixed = projected[:, : inner + shared]
    raw = projected[EDGE:, inner + shared : inner + shared + heads]

    doc_ends = jnp.cumsum(prompt_lengths)
    first = seq_at * tokens
    ext_segments = segment_of(first - EDGE + jnp.arange(EDGE + tokens, dtype=jnp.int32), doc_ends)
    segments = ext_segments[EDGE:]
    prev_seg = ext_segments[EDGE - 1]
    taps = jnp.concatenate([conv_value, conv_shared], axis=1)
    conv_sum = jnp.zeros((tokens, inner + shared), F32)
    width = taps.shape[0]
    for k in range(width):
        at = EDGE - width + 1 + k
        same = (ext_segments[at : at + tokens] == segments)[:, None]
        conv_sum = conv_sum + jnp.where(
            same, taps[k][None, :] * mixed[at : at + tokens].astype(F32), 0.0
        )
    convolved = jax.nn.silu(conv_sum).astype(BF16)
    values = convolved[:, :inner].reshape(tokens, heads, head_dim)
    b_half = convolved[:, inner : inner + state]
    c_half = convolved[:, inner + state :]
    steps = jax.nn.softplus(raw.astype(F32) + dt_bias[None, :])
    cumulative = jnp.cumsum(-steps * jnp.exp(a_log)[None, :], axis=0)

    tail = (
        jnp.where(
            (segments == segments[-1])[:, None], jnp.exp(cumulative[-1][None, :] - cumulative), 0.0
        )
        * steps
    )
    weighted = (tail[:, :, None] * values.astype(F32)).astype(BF16)
    fresh = lax.dot_general(
        weighted.reshape(tokens, inner), b_half, (((0,), (0,)), ((), ())), preferred_element_type=F32
    )
    keep = jnp.where(segments[-1] == prev_seg, jnp.exp(cumulative[-1]), 0.0)
    keep_hi = keep.astype(BF16)
    keep_lo = (keep - keep_hi.astype(F32)).astype(BF16)
    keep_rows = jnp.pad(jnp.stack([keep_hi, keep_lo]), ((0, 2), (0, state - heads)))
    sent = jnp.concatenate(
        [
            fresh.astype(BF16).reshape(heads, head_dim, state).transpose(1, 0, 2),
            jnp.broadcast_to(keep_rows[None], (head_dim,) + keep_rows.shape),
        ],
        axis=1,
    )
    received = lax.all_to_all(sent, SEQ, 0, 0, tiled=True)
    carried = lax.all_to_all(scan_states(received, heads), SEQ, 0, 0, tiled=True)
    carried = carried[:, :heads].transpose(1, 0, 2).reshape(inner, state)

    places = jnp.arange(tokens)
    causal = (places[:, None] >= places[None, :]) & (segments[:, None] == segments[None, :])
    scores = jnp.dot(c_half, b_half.T, preferred_element_type=F32)
    cum_t = cumulative.T
    gaps = jnp.where(causal[None], cum_t[:, :, None] - cum_t[:, None, :], -jnp.inf)
    weights = (scores[None] * jnp.exp(gaps) * steps.T[:, None, :]).astype(BF16)
    intra = jnp.einsum("hij,jhp->ihp", weights, values, preferred_element_type=F32)
    direct = intra + skip_gain[None, :, None] * values.astype(F32)
    carry_in = jnp.where((segments == prev_seg)[:, None], jnp.exp(cumulative), 0.0)

    gate = jnp.dot(h_all[EDGE:], late[:, :inner], preferred_element_type=F32).astype(BF16)
    inter = lax.dot_general(
        c_half, carried, (((1,), (1,)), ((), ())), preferred_element_type=F32
    ).reshape(tokens, heads, head_dim)
    mixed_heads = (direct + inter * carry_in[:, :, None]).reshape(tokens, inner)
    gated = mixed_heads * jax.nn.silu(gate.astype(F32))

    squares = jnp.sum(gated * gated, axis=1, keepdims=True)
    total = squares + sum(ahead(squares, "tp", d) for d in range(1, tp_count))
    scale = lax.rsqrt(total / (inner * tp_count) + EPSILON)
    terms = lax.dot_general(
        (gated * norm_gain[None, :]).astype(BF16),
        late[:, inner:],
        (((1,), (1,)), ((), ())),
        preferred_element_type=F32,
    ).astype(BF16)

    def share(d):
        return lax.dynamic_slice_in_dim(terms, ((tp_at + d) % tp_count) * features, features, 1)

    summed = share(0).astype(F32)
    for d in range(1, tp_count):
        summed = summed + ahead(share(d), "tp", d).astype(F32)
    return (summed * scale).astype(BF16)


def solution(mesh):
    fine = Mesh(mesh.devices.reshape(SIZES + (-1,)), SEQ + ("tp",))
    return jax.shard_map(
        on_device,
        mesh=fine,
        in_specs=(
            P(SEQ, "tp"),
            P(SEQ, "tp"),
            P(SEQ, "tp"),
            P(SEQ, None),
            P(SEQ, "tp"),
            P(None, "tp"),
            P(),
            P("tp"),
            P("tp"),
            P("tp"),
            P("tp"),
            P("tp", SEQ),
            P(),
            P(),
        ),
        out_specs=P(SEQ, "tp"),
        check_vma=False,
    )
```

time: 422 us -> 164 us (0.39)
  blocking collectives: 161 us -> 23.9 us
  waiting for transfers between devices: 139 us -> 40.5 us
  other arithmetic: 79 us -> 12.4 us
  starting transfers between devices: 2.09 us -> 45.2 us
  local copies, waits for them, and re-layouts: 7.21 us -> 12.1 us
    all_gather x4 -> x1, blocking collectives: 153 us -> 23.9 us  [on_device(): along_z = lax.all_gather(early, 'z', axis=0, tiled=True)]
    all_gather x4 -> x1, waiting for transfers between devices: 116 us -> 0.02 us  [on_device(): late = lax.all_gather(late, SEQ, axis=0, tiled=True)]
    select_n x67 -> x5, other arithmetic: 68.4 us -> 0.51 us  [the longest x4 0.51 us: columns_for(): return jnp.take(cut, place, axis=1).reshape(hidden.shape[0], -1)]
    ppermute x1 -> x14, starting transfers between devices: 1.92 us -> 32 us  [the longest x13 22.1 us: ahead(): lax.ppermute(block, axis, [(i, (i + distance) % count) for i in range(cou...]
    unnamed x6 -> x1, waiting for transfers between devices: 21.4 us -> 0.02 us
    all_to_all x0 -> x2, waiting for transfers between devices: none -> 20.3 us  [the longest x1 10.4 us: on_device(): received = lax.all_to_all(sent, SEQ, 0, 0, tiled=True)]
    ppermute x1 -> x14, waiting for transfers between devices: 1.12 us -> 20.1 us  [the longest x13 20.1 us: ahead(): lax.ppermute(block, axis, [(i, (i + distance) % count) for i in range(cou...]
    all_to_all x0 -> x2, starting transfers between devices: none -> 13.1 us  [the longest x1 7.1 us: on_device(): received = lax.all_to_all(sent, SEQ, 0, 0, tiled=True)]
  transfers between devices with their start and end apart: 6 -> 17, of which waited for: 5 -> 7; matrix products, arithmetic and copies ran while one was open for 21% -> 17% of each run, Pallas kernels for 0% -> 1%
where the time goes in v1:
time: 164 us; the launch traced here: 162 us
  starting transfers between devices  45.2 us (28%)
  waiting for transfers between devices  40.5 us (25%)
  blocking collectives  23.9 us (15%)
  between operations  15.1 us (9%)
  other arithmetic  12.4 us (8%)
  local copies, waits for them, and re-layouts  12.1 us (7%)
  matrix products  10.7 us (7%)
  Pallas kernels  2.04 us (1%)
    all_gather x1, blocking collectives, on_device(): along_z = lax.all_gather(early, 'z', axis=0, tiled=True)  23.9 us
    ppermute x13, starting transfers between devices, ahead(): lax.ppermute(block, axis, [(i, (i + distance) % count) for i in range(cou...  22.1 us
    ppermute x13, waiting for transfers between devices, ahead(): lax.ppermute(block, axis, [(i, (i + distance) % count) for i in range(cou...  20.1 us
    all_to_all x1, waiting for transfers between devices, on_device(): received = lax.all_to_all(sent, SEQ, 0, 0, tiled=True)  10.4 us
    ppermute x1, starting transfers between devices, on_device(): lax.ppermute(hidden_in[tokens - EDGE:], SEQ, [(i, i + 1) for i in range(s...  9.96 us
    all_to_all x1, waiting for transfers between devices, on_device(): lax.all_to_all(scan_states(received, heads), SEQ, 0, 0, tiled=True)  9.92 us
    all_to_all x1, starting transfers between devices, on_device(): received = lax.all_to_all(sent, SEQ, 0, 0, tiled=True)  7.1 us
    all_to_all x1, starting transfers between devices, on_device(): lax.all_to_all(scan_states(received, heads), SEQ, 0, 0, tiled=True)  6.03 us
  transfers between devices with their start and end apart: 17, of which 7 were waited for; matrix products, arithmetic and copies ran while one was open for 17% of the time, Pallas kernels for 1%

profile of v1, /device:TPU:1, one launch (start us, length us, event | category | flops | bytes accessed | tf_op | source)
XLA Modules:
  0.0 161.9 jit_solution(809624649894705320)
XLA Ops:
  6.5 0.9 convert_bitcast_fusion
  7.5 0.9 convert_element_type.109
  9.0 0.9 convert.11
  11.6 23.9 %all_gather.6 = bf16[192,1152]{1,0:T(8,128)(2,1)S(1)} all-gather(bf16[24,1152]{1,0:T(8,128)(2,1)S(1)} %concatenate.25), channel_id=1, replica_groups=mesh['x'=4,'z'=8,'core'=2,'tp'=4] {'z'}, dimensions={0}, use_global_device_ids=true | all-gather | bytes 497664 | tf_op jit(solution)/shard_map/all_gather | solution.py:91
  35.5 1.4 collective-permute-start.4
  36.9 2.4 %collective-permute-start.5 = (bf16[192,1152]{1,0:T(8,128)(2,1)S(1)}, bf16[192,1152]{1,0:T(8,128)(2,1)S(1)}, u32[]{:S(2)}, u32[]{:S(2)}) collective-permute-start(bf16[192,1152]{1,0:T(8,128)(2,1)S(1)} %all_gather.6), channel_id=1, source_target_pairs={{0,128},{64,192},{128,0},{192,64},{1,129},{65,193},{129,1},{193,65... | collective-permute-start | bytes 1327112 | tf_op jit(solution)/shard_map/ppermute | solution.py:18
  39.2 1.2 collective-permute-start.6
  41.3 10.0 %collective-permute-start = (bf16[8,384]{0,1:T(8,128)(2,1)S(1)}, bf16[8,384]{0,1:T(8,128)(2,1)S(1)}, u32[]{:S(2)}, u32[]{:S(2)}) collective-permute-start(bf16[8,384]{0,1:T(8,128)(2,1)S(1)} %copy.80), channel_id=1, source_target_pairs={{0,4},{4,8},{8,12},{12,16},{16,20},{20,24},{24,28},{28,32},{32,36}... | collective-permute-start | bytes 18440 | tf_op jit(solution)/shard_map/ppermute | solution.py:81
  57.3 5.6 %collective-permute-start.7 = (bf16[768,1152]{1,0:T(8,128)(2,1)}, bf16[768,1152]{1,0:T(8,128)(2,1)}, u32[]{:S(2)}, u32[]{:S(2)}) collective-permute-start(bf16[768,1152]{1,0:T(8,128)(2,1)} %constant_dynamic-update-slice_fusion.2), channel_id=1, source_target_pairs={{0,4},{4,0},{1,5},{5,1},{2,6},{6,2},{3,7},{7,3},{8,12},{12,8},{9,1... | collective-permute-start | bytes 5308424 | tf_op jit(solution)/shard_map/ppermute | solution.py:18
  62.8 1.3 broadcast_compare_fusion.1
  66.5 1.3 collective-permute-start.1
  67.8 2.5 %collective-permute-start.2 = (bf16[264,384]{0,1:T(8,128)(2,1)S(1)}, bf16[264,384]{0,1:T(8,128)(2,1)S(1)}, u32[]{:S(2)}, u32[]{:S(2)}) collective-permute-start(bf16[264,384]{0,1:T(8,128)(2,1)S(1)} %pad_maximum_fusion.1), channel_id=1, source_target_pairs={{0,2},{1,3},{2,0},{3,1},{4,6},{5,7},{6,4},{7,5},{8,10},{9,11},{10,... | collective-permute-start | bytes 608264 | tf_op jit(solution)/shard_map/ppermute | solution.py:18
  70.3 1.1 collective-permute-start.3
  71.4 5.0 %collective-permute-done.1 = bf16[264,384]{0,1:T(8,128)(2,1)S(1)} collective-permute-done((bf16[264,384]{0,1:T(8,128)(2,1)S(1)}, bf16[264,384]{0,1:T(8,128)(2,1)S(1)}, u32[]{:S(2)}, u32[]{:S(2)}) %collective-permute-start.1) | collective-permute-done | bytes 202784 | tf_op jit(solution)/shard_map/ppermute | solution.py:18
  76.5 7.3 %collective-permute-done.2 = bf16[264,384]{0,1:T(8,128)(2,1)S(1)} collective-permute-done((bf16[264,384]{0,1:T(8,128)(2,1)S(1)}, bf16[264,384]{0,1:T(8,128)(2,1)S(1)}, u32[]{:S(2)}, u32[]{:S(2)}) %collective-permute-start.2) | collective-permute-done | bytes 202784 | tf_op jit(solution)/shard_map/ppermute | solution.py:18
  85.7 2.6 %fusion.59 = f32[264,1152]{0,1:T(8,128)S(1)} fusion(bf16[264,768]{0,1:T(8,128)(2,1)S(1)} %bitcast.72, bf16[768,1152]{1,0:T(8,128)(2,1)} %collective-permute-done.7), kind=kOutput, calls=%fused_computation.164 | convolution fusion | flops 467140608 | bytes 3391488 | tf_op jit(solution)/shard_map/dot_general | solution.py:115
  88.3 2.7 %fusion = bf16[264,1152]{0,1:T(8,128)(2,1)S(1)} fusion(f32[264,1152]{0,1:T(8,128)S(1)} %fusion.59, bf16[264,768]{0,1:T(8,128)(2,1)S(1)} %bitcast.73, bf16[768,1152]{1,0:T(8,128)(2,1)} %constant_dynamic-update-slice_fusion.2), kind=kOutput, calls=%fused_computation.8 | convolution fusion | flops 467748864 | bytes 3999744 | tf_op jit(solution)/shard_map/dot_general | solution.py:114
  92.4 1.5 multiply_convert_fusion.6
  95.5 7.1 %all-to-all-start = ((bf16[64,16,128]{2,1,0:T(8,128)(2,1)}), bf16[64,16,128]{2,1,0:T(8,128)(2,1)S(1)}, u32[]{:S(2)}, u32[]{:S(2)}) async-start(bf16[64,16,128]{2,1,0:T(8,128)(2,1)} %pad_maximum_fusion.2), calls=%async_computation | async-start | bytes 524288 | tf_op jit(solution)/shard_map/all_to_all | solution.py:162
  104.2 10.4 %all-to-all-done.sent_ref = bf16[64,16,128]{2,1,0:T(8,128)(2,1)S(1)} async-done(((bf16[64,16,128]{2,1,0:T(8,128)(2,1)}), bf16[64,16,128]{2,1,0:T(8,128)(2,1)S(1)}, u32[]{:S(2)}, u32[]{:S(2)}) %all-to-all-start) | async-done | bytes 262176 | tf_op jit(solution)/shard_map/all_to_all | solution.py:162
  115.3 2.0 %shard_map.136 = bf16[64,16,128]{2,1,0:T(8,128)(2,1)} custom-call(bf16[64,16,128]{2,1,0:T(8,128)(2,1)} %copy-done.1), custom_call_target="tpu_custom_call" | custom-call | flops 262144 | bytes 524288 | tf_op jit(solution)/shard_map/pallas_call | solution.py:38
  117.4 6.0 %all-to-all-start.1 = ((bf16[64,16,128]{2,1,0:T(8,128)(2,1)}), bf16[64,16,128]{2,1,0:T(8,128)(2,1)S(1)}, u32[]{:S(2)}, u32[]{:S(2)}) async-start(bf16[64,16,128]{2,1,0:T(8,128)(2,1)} %shard_map.136), calls=%async_computation.1 | async-start | bytes 524288 | tf_op jit(solution)/shard_map/all_to_all | solution.py:163
  124.5 1.0 fusion.12
  125.5 9.9 %all-to-all-done.1 = bf16[64,16,128]{2,1,0:T(8,128)(2,1)S(1)} async-done(((bf16[64,16,128]{2,1,0:T(8,128)(2,1)}), bf16[64,16,128]{2,1,0:T(8,128)(2,1)S(1)}, u32[]{:S(2)}, u32[]{:S(2)}) %all-to-all-start.1) | async-done | bytes 262176 | tf_op jit(solution)/shard_map/all_to_all | solution.py:163
  136.0 2.8 %multiply_reduce_fusion = (f32[256]{0:T(256)S(1)}, f32[256,768]{1,0:T(8,128)S(1)}) fusion(f32[256,768]{1,0:T(8,128)S(1)} %copy.93, bf16[256,1536]{0,1:T(8,128)(2,1)S(1)} %bitcast.70, bf16[1536,1536]{1,0:T(8,128)(2,1)} %all-gather.2.cloned.1.call-done), kind=kOutput, calls=%fused_computation.32 | convolution fusion | flops 605748992 | bytes 4719616 | tf_op jit(solution)/shard_map/dot_general | solution.py:176
  138.8 1.3 collective-permute-start.11
  140.1 2.1 %collective-permute-start.12 = (f32[256,1]{0,1:T(1,128)S(1)}, f32[256,1]{0,1:T(1,128)S(1)}, u32[]{:S(2)}, u32[]{:S(2)}) collective-permute-start(f32[256,1]{0,1:T(1,128)S(1)} %bitcast.85), channel_id=1, source_target_pairs={{0,2},{1,3},{2,0},{3,1},{4,6},{5,7},{6,4},{7,5},{8,10},{9,11},{10,... | collective-permute-start | bytes 3080 | tf_op jit(solution)/shard_map/ppermute | solution.py:18
  142.2 1.1 collective-permute-start.13
  144.3 1.4 collective-permute-start.8
  146.5 3.0 %collective-permute-done.10 = bf16[256,384]{1,0:T(8,128)(2,1)S(1)} collective-permute-done((bf16[256,384]{1,0:T(8,128)(2,1)S(1)}, bf16[256,384]{1,0:T(8,128)(2,1)S(1)}, u32[]{:S(2)}, u32[]{:S(2)}) %collective-permute-start.10) | collective-permute-done | bytes 196640 | tf_op jit(solution)/shard_map/ppermute | solution.py:18
  149.4 1.9 %collective-permute-done.8 = bf16[256,384]{1,0:T(8,128)(2,1)S(1)} collective-permute-done((bf16[256,384]{1,0:T(8,128)(2,1)S(1)}, bf16[256,384]{1,0:T(8,128)(2,1)S(1)}, u32[]{:S(2)}, u32[]{:S(2)}) %collective-permute-start.8) | collective-permute-done | bytes 196640 | tf_op jit(solution)/shard_map/ppermute | solution.py:18
  151.3 2.9 %collective-permute-done.9 = bf16[256,384]{1,0:T(8,128)(2,1)S(1)} collective-permute-done((bf16[256,384]{1,0:T(8,128)(2,1)S(1)}, bf16[256,384]{1,0:T(8,128)(2,1)S(1)}, u32[]{:S(2)}, u32[]{:S(2)}) %collective-permute-start.9) | collective-permute-done | bytes 196640 | tf_op jit(solution)/shard_map/ppermute | solution.py:18
  (121 shorter events, 21.4 us)
Async XLA Ops:
  6.5 45.0 %copy-start = (s32[64]{0:T(128)S(1)}, s32[64]{0:T(128)}, u32[]{:S(2)}) copy-start(s32[64]{0:T(128)} %param.31) | copy-start | bytes 772
  6.5 46.4 %copy-start.9 = (s32[8]{0:T(128)S(1)}, s32[8]{0:T(128)}, u32[]{:S(2)}) copy-start(s32[8]{0:T(128)} %param.30) | copy-start | bytes 100
  6.5 47.4 %copy-start.4 = (f32[4,768]{1,0:T(4,128)S(1)}, f32[4,768]{1,0:T(4,128)}, u32[]{:S(2)}) copy-start(f32[4,768]{1,0:T(4,128)} %param.23) | copy-start | bytes 36868
  6.5 129.4 %all-gather.2.cloned.1.call-start = ((), (), s32[]{:S(2)}) async-start(), calls=%async_computation.2 | async-start | bytes 4792320 | tf_op jit(solution)/shard_map/all_gather | solution.py:79
  35.5 19.3 %collective-permute-start.4 = (bf16[192,1152]{1,0:T(8,128)(2,1)S(1)}, bf16[192,1152]{1,0:T(8,128)(2,1)S(1)}, u32[]{:S(2)}, u32[]{:S(2)}) collective-permute-start(bf16[192,1152]{1,0:T(8,128)(2,1)S(1)} %all_gather.6), channel_id=1, source_target_pairs={{0,64},{64,128},{128,192},{192,0},{1,65},{65,129},{129,193},{193,1... | collective-permute-start | bytes 1327112 | tf_op jit(solution)/shard_map/ppermute | solution.py:18
  36.9 18.7 %collective-permute-start.5 = (bf16[192,1152]{1,0:T(8,128)(2,1)S(1)}, bf16[192,1152]{1,0:T(8,128)(2,1)S(1)}, u32[]{:S(2)}, u32[]{:S(2)}) collective-permute-start(bf16[192,1152]{1,0:T(8,128)(2,1)S(1)} %all_gather.6), channel_id=1, source_target_pairs={{0,128},{64,192},{128,0},{192,64},{1,129},{65,193},{129,1},{193,65... | collective-permute-start | bytes 1327112 | tf_op jit(solution)/shard_map/ppermute | solution.py:18
  39.2 17.2 %collective-permute-start.6 = (bf16[192,1152]{1,0:T(8,128)(2,1)S(1)}, bf16[192,1152]{1,0:T(8,128)(2,1)S(1)}, u32[]{:S(2)}, u32[]{:S(2)}) collective-permute-start(bf16[192,1152]{1,0:T(8,128)(2,1)S(1)} %all_gather.6), channel_id=1, source_target_pairs={{0,192},{64,0},{128,64},{192,128},{1,193},{65,1},{129,65},{193,129... | collective-permute-start | bytes 1327112 | tf_op jit(solution)/shard_map/ppermute | solution.py:18
  41.3 25.1 %collective-permute-start = (bf16[8,384]{0,1:T(8,128)(2,1)S(1)}, bf16[8,384]{0,1:T(8,128)(2,1)S(1)}, u32[]{:S(2)}, u32[]{:S(2)}) collective-permute-start(bf16[8,384]{0,1:T(8,128)(2,1)S(1)} %copy.80), channel_id=1, source_target_pairs={{0,4},{4,8},{8,12},{12,16},{16,20},{20,24},{24,28},{28,32},{32,36}... | collective-permute-start | bytes 18440 | tf_op jit(solution)/shard_map/ppermute | solution.py:81
  53.9 8.9 %copy-start.5 = (f32[4,256]{1,0:T(4,128)S(1)}, f32[4,256]{1,0:T(4,128)}, u32[]{:S(2)}) copy-start(f32[4,256]{1,0:T(4,128)} %param.24) | copy-start | bytes 12292
  54.0 10.2 %copy-start.2 = (bf16[256,384]{1,0:T(8,128)(2,1)S(1)}, bf16[256,384]{1,0:T(8,128)(2,1)}, u32[]{:S(2)}) copy-start(bf16[256,384]{1,0:T(8,128)(2,1)} %param.18) | copy-start | bytes 589828
  54.8 10.8 %copy-start.10 = (f32[12]{0:T(128)S(1)}, f32[12]{0:T(128)}, u32[]{:S(2)}) copy-start(f32[12]{0:T(128)} %param.26) | copy-start | bytes 148
  57.3 28.4 %collective-permute-start.7 = (bf16[768,1152]{1,0:T(8,128)(2,1)}, bf16[768,1152]{1,0:T(8,128)(2,1)}, u32[]{:S(2)}, u32[]{:S(2)}) collective-permute-start(bf16[768,1152]{1,0:T(8,128)(2,1)} %constant_dynamic-update-slice_fusion.2), channel_id=1, source_target_pairs={{0,4},{4,0},{1,5},{5,1},{2,6},{6,2},{3,7},{7,3},{8,12},{12,8},{9,1... | collective-permute-start | bytes 5308424 | tf_op jit(solution)/shard_map/ppermute | solution.py:18
  66.5 9.9 %collective-permute-start.1 = (bf16[264,384]{0,1:T(8,128)(2,1)S(1)}, bf16[264,384]{0,1:T(8,128)(2,1)S(1)}, u32[]{:S(2)}, u32[]{:S(2)}) collective-permute-start(bf16[264,384]{0,1:T(8,128)(2,1)S(1)} %pad_maximum_fusion.1), channel_id=1, source_target_pairs={{0,1},{1,2},{2,3},{3,0},{4,5},{5,6},{6,7},{7,4},{8,9},{9,10},{10,1... | collective-permute-start | bytes 608264 | tf_op jit(solution)/shard_map/ppermute | solution.py:18
  67.8 16.0 %collective-permute-start.2 = (bf16[264,384]{0,1:T(8,128)(2,1)S(1)}, bf16[264,384]{0,1:T(8,128)(2,1)S(1)}, u32[]{:S(2)}, u32[]{:S(2)}) collective-permute-start(bf16[264,384]{0,1:T(8,128)(2,1)S(1)} %pad_maximum_fusion.1), channel_id=1, source_target_pairs={{0,2},{1,3},{2,0},{3,1},{4,6},{5,7},{6,4},{7,5},{8,10},{9,11},{10,... | collective-permute-start | bytes 608264 | tf_op jit(solution)/shard_map/ppermute | solution.py:18
  70.3 13.5 %collective-permute-start.3 = (bf16[264,384]{0,1:T(8,128)(2,1)S(1)}, bf16[264,384]{0,1:T(8,128)(2,1)S(1)}, u32[]{:S(2)}, u32[]{:S(2)}) collective-permute-start(bf16[264,384]{0,1:T(8,128)(2,1)S(1)} %pad_maximum_fusion.1), channel_id=1, source_target_pairs={{0,3},{1,0},{2,1},{3,2},{4,7},{5,4},{6,5},{7,6},{8,11},{9,8},{10,9... | collective-permute-start | bytes 608264 | tf_op jit(solution)/shard_map/ppermute | solution.py:18
  88.3 2.7 %copy-start.6 = (f32[12]{0:T(128)S(1)}, f32[12]{0:T(128)}, u32[]{:S(2)}) copy-start(f32[12]{0:T(128)} %param.25) | copy-start | bytes 148
  95.5 19.1 %all-to-all-start = ((bf16[64,16,128]{2,1,0:T(8,128)(2,1)}), bf16[64,16,128]{2,1,0:T(8,128)(2,1)S(1)}, u32[]{:S(2)}, u32[]{:S(2)}) async-start(bf16[64,16,128]{2,1,0:T(8,128)(2,1)} %pad_maximum_fusion.2), calls=%async_computation | async-start | bytes 524288 | tf_op jit(solution)/shard_map/all_to_all | solution.py:162
  114.6 0.7 copy-start.1
  117.4 18.0 %all-to-all-start.1 = ((bf16[64,16,128]{2,1,0:T(8,128)(2,1)}), bf16[64,16,128]{2,1,0:T(8,128)(2,1)S(1)}, u32[]{:S(2)}, u32[]{:S(2)}) async-start(bf16[64,16,128]{2,1,0:T(8,128)(2,1)} %shard_map.136), calls=%async_computation.1 | async-start | bytes 524288 | tf_op jit(solution)/shard_map/all_to_all | solution.py:163
  123.6 0.8 copy-start.3
  123.6 0.8 copy-start.11
  136.0 7.4 %copy-start.7 = (bf16[1536,1536]{1,0:T(8,128)(2,1)S(1)}, bf16[1536,1536]{1,0:T(8,128)(2,1)}, u32[]{:S(2)}) copy-start(bf16[1536,1536]{1,0:T(8,128)(2,1)} %all-gather.2.cloned.1.call-done) | copy-start | bytes 14155780
  136.0 7.4 %copy-start.8 = (f32[768]{0:T(1024)S(1)}, f32[768]{0:T(1024)}, u32[]{:S(2)}) copy-start(f32[768]{0:T(1024)} %param.28) | copy-start | bytes 9220
  138.8 7.0 %collective-permute-start.11 = (f32[256,1]{0,1:T(1,128)S(1)}, f32[256,1]{0,1:T(1,128)S(1)}, u32[]{:S(2)}, u32[]{:S(2)}) collective-permute-start(f32[256,1]{0,1:T(1,128)S(1)} %bitcast.84), channel_id=1, source_target_pairs={{0,1},{1,2},{2,3},{3,0},{4,5},{5,6},{6,7},{7,4},{8,9},{9,10},{10,1... | collective-permute-start | bytes 3080 | tf_op jit(solution)/shard_map/ppermute | solution.py:18
  140.1 6.4 %collective-permute-start.12 = (f32[256,1]{0,1:T(1,128)S(1)}, f32[256,1]{0,1:T(1,128)S(1)}, u32[]{:S(2)}, u32[]{:S(2)}) collective-permute-start(f32[256,1]{0,1:T(1,128)S(1)} %bitcast.85), channel_id=1, source_target_pairs={{0,2},{1,3},{2,0},{3,1},{4,6},{5,7},{6,4},{7,5},{8,10},{9,11},{10,... | collective-permute-start | bytes 3080 | tf_op jit(solution)/shard_map/ppermute | solution.py:18
  142.2 4.2 %collective-permute-start.13 = (f32[256,1]{0,1:T(1,128)S(1)}, f32[256,1]{0,1:T(1,128)S(1)}, u32[]{:S(2)}, u32[]{:S(2)}) collective-permute-start(f32[256,1]{0,1:T(1,128)S(1)} %bitcast.86), channel_id=1, source_target_pairs={{0,3},{1,0},{2,1},{3,2},{4,7},{5,4},{6,5},{7,6},{8,11},{9,8},{10,9... | collective-permute-start | bytes 3080 | tf_op jit(solution)/shard_map/ppermute | solution.py:18
  144.2 5.2 %collective-permute-start.10 = (bf16[256,384]{1,0:T(8,128)(2,1)S(1)}, bf16[256,384]{1,0:T(8,128)(2,1)S(1)}, u32[]{:S(2)}, u32[]{:S(2)}) collective-permute-start(bf16[256,384]{1,0:T(8,128)(2,1)S(1)} %get-tuple-element.14), channel_id=1, source_target_pairs={{0,3},{1,0},{2,1},{3,2},{4,7},{5,4},{6,5},{7,6},{8,11},{9,8},{10,9... | collective-permute-start | bytes 589832 | tf_op jit(solution)/shard_map/ppermute | solution.py:18
  144.3 7.0 %collective-permute-start.8 = (bf16[256,384]{1,0:T(8,128)(2,1)S(1)}, bf16[256,384]{1,0:T(8,128)(2,1)S(1)}, u32[]{:S(2)}, u32[]{:S(2)}) collective-permute-start(bf16[256,384]{1,0:T(8,128)(2,1)S(1)} %get-tuple-element.13), channel_id=1, source_target_pairs={{0,1},{1,2},{2,3},{3,0},{4,5},{5,6},{6,7},{7,4},{8,9},{9,10},{10,1... | collective-permute-start | bytes 589832 | tf_op jit(solution)/shard_map/ppermute | solution.py:18
  145.8 8.4 %collective-permute-start.9 = (bf16[256,384]{1,0:T(8,128)(2,1)S(1)}, bf16[256,384]{1,0:T(8,128)(2,1)S(1)}, u32[]{:S(2)}, u32[]{:S(2)}) collective-permute-start(bf16[256,384]{1,0:T(8,128)(2,1)S(1)} %get-tuple-element.15), channel_id=1, source_target_pairs={{0,2},{1,3},{2,0},{3,1},{4,6},{5,7},{6,4},{7,5},{8,10},{9,11},{10,... | collective-permute-start | bytes 589832 | tf_op jit(solution)/shard_map/ppermute | solution.py:18
Sparse Core Ops, SparseCore 0:
  10.1 83.6 all-gather.1

commit v2 on v1

--- a/solution.py
+++ b/solution.py
@@ -44,6 +44,26 @@
             flops=2 * sent.size, bytes_accessed=4 * sent.size, transcendentals=0
         ),
     )(sent)
+
+
+def pack_body(value_ref, shared_ref, step_ref, out_ref):
+    inner, shared, heads = value_ref.shape[1], shared_ref.shape[1], step_ref.shape[1]
+    out_ref[:, :inner] = value_ref[...].astype(BF16)
+    out_ref[:, inner : inner + shared] = shared_ref[...].astype(BF16)
+    rest = out_ref.shape[1] - inner - shared
+    step = jnp.pad(step_ref[...], ((0, 0), (0, rest - heads)))
+    out_ref[:, inner + shared :] = step.astype(BF16)
+
+
+def pack_early(value, shared, step):
+    width = value.shape[1] + shared.shape[1] + step.shape[1]
+    width += -width % 128
+    return pl.pallas_call(
+        pack_body,
+        out_shape=jax.ShapeDtypeStruct((value.shape[0], width), BF16),
+        in_specs=[pl.BlockSpec(memory_space=pltpu.VMEM)] * 3,
+        out_specs=pl.BlockSpec(memory_space=pltpu.VMEM),
+    )(value, shared, step)
 
 
 def on_device(
@@ -75,28 +95,30 @@
     tp_at = lax.axis_index("tp")
     seq_at = (x_at * z_size + z_at) * core_size + core_at
 
+    before = lax.ppermute(
+        hidden_in[tokens - EDGE :], SEQ, [(i, i + 1) for i in range(seq_count - 1)]
+    )
+    early = pack_early(w_in_value, w_in_shared, w_in_step)
+
     late = jnp.concatenate([w_in_gate.astype(BF16), w_out.T.astype(BF16)], axis=1)
     late = lax.all_gather(late, SEQ, axis=0, tiled=True)
 
-    before = lax.ppermute(
-        hidden_in[tokens - EDGE :], SEQ, [(i, i + 1) for i in range(seq_count - 1)]
-    )
+    half = z_size // 2
+    pair = jnp.concatenate([early, ahead(early, "z", half)], axis=0)
+    before, pair = lax.optimization_barrier((before, pair))
     mine = jnp.concatenate([before, hidden_in], axis=0)
     hidden = jnp.concatenate([mine] + [ahead(mine, "tp", d) for d in range(1, tp_count)], axis=1)
-
-    spare = -(inner + shared + heads) % 128
-    early = jnp.concatenate(
-        [w_in_value, w_in_shared, w_in_step, jnp.zeros((rows_here, spare), F32)], axis=1
-    ).astype(BF16)
-    along_z = lax.all_gather(early, "z", axis=0, tiled=True)
-    own = jnp.concatenate(
-        [along_z] + [ahead(along_z, "x", d) for d in range(1, x_size)], axis=0
-    )
-    other = ahead(own, "core", 1)
-
-    dx = jnp.arange(x_size, dtype=jnp.int32)[:, None]
-    dz = jnp.arange(z_size, dtype=jnp.int32)[None, :]
-    chips = (((x_at - dx) % x_size) * z_size + dz).reshape(-1) * core_size
+    z_shifts = [0, 1, 2, z_size - 1]
+    along_z = jnp.concatenate([pair] + [ahead(pair, "z", d) for d in z_shifts[1:]], axis=0)
+    z_offsets = [(d + o) % z_size for d in z_shifts for o in (0, half)]
+    own = [along_z] + [ahead(along_z, "x", d) for d in range(1, x_size)]
+    other = [ahead(block, "core", 1) for block in own]
+
+    chips = [
+        jnp.stack([((x_at - d) % x_size * z_size + (z_at - o) % z_size) for o in z_offsets])
+        * core_size
+        for d in range(x_size)
+    ]
     blocks_each = seq_count // tp_count
 
     def columns_for(stored):
@@ -106,13 +128,13 @@
         cut = hidden.reshape(hidden.shape[0], seq_count, rows_here)
         return jnp.take(cut, place, axis=1).reshape(hidden.shape[0], -1)
 
-    h_own = columns_for(chips + core_at)
-    h_other = columns_for(chips + (1 - core_at))
     h_all = columns_for(jnp.arange(seq_count, dtype=jnp.int32))
-
-    projected = (
-        jnp.dot(h_own, own, preferred_element_type=F32)
-        + jnp.dot(h_other, other, preferred_element_type=F32)
+    order = [stored + core_at for stored in chips] + [stored + (1 - core_at) for stored in chips]
+    h_early = columns_for(jnp.concatenate(order))
+    depth = early.shape[0] * z_size
+    projected = sum(
+        jnp.dot(h_early[:, i * depth : (i + 1) * depth], block, preferred_element_type=F32)
+        for i, block in enumerate(own + other)
     ).astype(BF16)
     mixed = projected[:, : inner + shared]
     raw = projected[EDGE:, inner + shared : inner + shared + heads]
@@ -180,9 +202,17 @@
     mixed_heads = (direct + inter * carry_in[:, :, None]).reshape(tokens, inner)
     gated = mixed_heads * jax.nn.silu(gate.astype(F32))
 
-    squares = jnp.sum(gated * gated, axis=1, keepdims=True)
-    total = squares + sum(ahead(squares, "tp", d) for d in range(1, tp_count))
-    scale = lax.rsqrt(total / (inner * tp_count) + EPSILON)
+    squares = lax.dot_general(
+        jnp.ones((1, inner), F32),
+        gated * gated,
+        (((1,), (1,)), ((), ())),
+        precision=lax.Precision.HIGHEST,
+        preferred_element_type=F32,
+    )
+    squares_hi = squares.astype(BF16)
+    squares_lo = (squares - squares_hi.astype(F32)).astype(BF16)
+    riding = jnp.concatenate([squares_hi, squares_lo], axis=0)
+    riding = jnp.pad(riding, ((0, 6), (0, features - tokens)))
     terms = lax.dot_general(
         (gated * norm_gain[None, :]).astype(BF16),
         late[:, inner:],
@@ -191,12 +221,14 @@
     ).astype(BF16)
 
     def share(d):
-        return lax.dynamic_slice_in_dim(terms, ((tp_at + d) % tp_count) * features, features, 1)
-
-    summed = share(0).astype(F32)
-    for d in range(1, tp_count):
-        summed = summed + ahead(share(d), "tp", d).astype(F32)
-    return (summed * scale).astype(BF16)
+        cut = lax.dynamic_slice_in_dim(terms, ((tp_at + d) % tp_count) * features, features, 1)
+        return jnp.concatenate([cut, riding], axis=0)
+
+    parts = [share(0)] + [ahead(share(d), "tp", d) for d in range(1, tp_count)]
+    summed = sum(part.astype(F32) for part in parts)
+    total = summed[tokens, :tokens] + summed[tokens + 1, :tokens]
+    scale = lax.rsqrt(total / (inner * tp_count) + EPSILON)
+    return (summed[:tokens] * scale[:, None]).astype(BF16)
 
 
 def solution(mesh):

time: 164 us -> 152 us (0.927); the launches traced: 162 us -> 152 us
  blocking collectives: 23.9 us -> 0 us
  waiting for transfers between devices: 40.5 us -> 56.3 us
  local copies, waits for them, and re-layouts: 12.1 us -> 9.26 us
  matrix products: 10.7 us -> 13.2 us
  starting transfers between devices: 45.2 us -> 43.2 us
  other arithmetic: 12.4 us -> 10.7 us
    all_gather x1 -> x0, blocking collectives: 23.9 us -> none  [on_device(): along_z = lax.all_gather(early, 'z', axis=0, tiled=True)]
    ppermute x13 -> x17, waiting for transfers between devices: 20.1 us -> 34.6 us  [ahead(): lax.ppermute(block, axis, [(i, (i + distance) % count) for i in range(cou...]
    ppermute x1, starting transfers between devices: 9.96 us -> 3.49 us  [on_device(): lax.ppermute(hidden_in[tokens - EDGE:], SEQ, [(i, i + 1) for i in range(s...]
    ppermute x13 -> x17, starting transfers between devices: 22.1 us -> 27.3 us  [ahead(): lax.ppermute(block, axis, [(i, (i + distance) % count) for i in range(cou...]
    dot_general x2 -> x9, matrix products: 5.29 us -> 7.95 us  [the longest x8 7.24 us: on_device(): jnp.dot(h_early[:, i * depth:(i + 1) * depth], block, preferred_element_t...]
    another operation x7 -> x4, other arithmetic: 3.21 us -> 1.53 us
    unnamed x31 -> x32, local copies, waits for them, and re-layouts: 3.58 us -> 2.65 us
  transfers between devices with their start and end apart: 17 -> 21, of which waited for: 7 -> 10; matrix products, arithmetic and copies ran while one was open for 17% -> 17% of each run, Pallas kernels for 1% -> 1%
where the time goes in v2:
time: 152 us
  waiting for transfers between devices  56.3 us (37%)
  starting transfers between devices  43.2 us (28%)
  between operations  15.5 us (10%)
  matrix products  13.2 us (9%)
  other arithmetic  10.7 us (7%)
  local copies, waits for them, and re-layouts  9.26 us (6%)
  Pallas kernels  3.57 us (2%)
    ppermute x17, waiting for transfers between devices, ahead(): lax.ppermute(block, axis, [(i, (i + distance) % count) for i in range(cou...  34.6 us
    ppermute x17, starting transfers between devices, ahead(): lax.ppermute(block, axis, [(i, (i + distance) % count) for i in range(cou...  27.3 us
    all_to_all x1, waiting for transfers between devices, on_device(): received = lax.all_to_all(sent, SEQ, 0, 0, tiled=True)  11.7 us
    all_to_all x1, waiting for transfers between devices, on_device(): lax.all_to_all(scan_states(received, heads), SEQ, 0, 0, tiled=True)  9.91 us
    dot_general x8, matrix products, on_device(): jnp.dot(h_early[:, i * depth:(i + 1) * depth], block, preferred_element_t...  7.24 us
    all_to_all x1, starting transfers between devices, on_device(): lax.all_to_all(scan_states(received, heads), SEQ, 0, 0, tiled=True)  6.3 us
    all_to_all x1, starting transfers between devices, on_device(): received = lax.all_to_all(sent, SEQ, 0, 0, tiled=True)  6.11 us
    ppermute x1, starting transfers between devices, on_device(): lax.ppermute(hidden_in[tokens - EDGE:], SEQ, [(i, i + 1) for i in range(s...  3.49 us
  transfers between devices with their start and end apart: 21, of which 10 were waited for; matrix products, arithmetic and copies ran while one was open for 17% of the time, Pallas kernels for 1%

profile of v2, /device:TPU:1, one launch (start us, length us, event | category | flops | bytes accessed | tf_op | source)
XLA Modules:
  0.0 151.8 jit_solution(2092531895874329381)
XLA Ops:
  6.6 1.5 copy.93.step_ref
  8.0 1.5 %shard_map.136 = bf16[24,1152]{1,0:T(8,128)(2,1)} custom-call(f32[24,768]{1,0:T(8,128)} %value_ref.1, f32[24,256]{1,0:T(8,128)} %shared_ref.1, f32[24,12]{1,0:T(8,128)} %copy.93.step_ref), custom_call_target="tpu_custom_call" | custom-call | tf_op jit(solution)/shard_map/pallas_call | solution.py:61
  9.6 7.7 %collective-permute-start.1 = (bf16[24,1152]{1,0:T(8,128)(2,1)}, bf16[24,1152]{1,0:T(8,128)(2,1)S(1)}, u32[]{:S(2)}, u32[]{:S(2)}) collective-permute-start(bf16[24,1152]{1,0:T(8,128)(2,1)} %shard_map.136), channel_id=1, source_target_pairs={{0,32},{8,40},{16,48},{24,56},{32,0},{40,8},{48,16},{56,24},{1,33}... | collective-permute-start | bytes 165896 | tf_op jit(solution)/shard_map/ppermute | solution.py:18
  18.2 3.5 %collective-permute-start = (bf16[8,384]{0,1:T(8,128)(2,1)S(1)}, bf16[8,384]{0,1:T(8,128)(2,1)S(1)}, u32[]{:S(2)}, u32[]{:S(2)}) collective-permute-start(bf16[8,384]{0,1:T(8,128)(2,1)S(1)} %copy.92), channel_id=1, source_target_pairs={{0,4},{4,8},{8,12},{12,16},{16,20},{20,24},{24,28},{28,32},{32,36}... | collective-permute-start | bytes 18440 | tf_op jit(solution)/shard_map/ppermute | solution.py:98
  21.7 0.9 convert_bitcast_fusion
  27.2 1.3 broadcast_compare_fusion.1
  31.1 1.4 collective-permute-start.2
  32.4 2.6 %collective-permute-start.3 = (bf16[264,384]{0,1:T(8,128)(2,1)S(1)}, bf16[264,384]{0,1:T(8,128)(2,1)S(1)}, u32[]{:S(2)}, u32[]{:S(2)}) collective-permute-start(bf16[264,384]{0,1:T(8,128)(2,1)S(1)} %pad_maximum_fusion.5), channel_id=1, source_target_pairs={{0,2},{1,3},{2,0},{3,1},{4,6},{5,7},{6,4},{7,5},{8,10},{9,11},{10,... | collective-permute-start | bytes 608264 | tf_op jit(solution)/shard_map/ppermute | solution.py:18
  35.0 1.1 collective-permute-start.4
  37.4 5.3 %collective-permute-done.5 = bf16[48,1152]{1,0:T(8,128)(2,1)S(1)} collective-permute-done((bf16[48,1152]{1,0:T(8,128)(2,1)S(1)}, bf16[48,1152]{1,0:T(8,128)(2,1)S(1)}, u32[]{:S(2)}, u32[]{:S(2)}) %collective-permute-start.5) | collective-permute-done | bytes 110624 | tf_op jit(solution)/shard_map/ppermute | solution.py:18
  43.4 4.3 %collective-permute-done.6 = bf16[48,1152]{1,0:T(8,128)(2,1)S(1)} collective-permute-done((bf16[48,1152]{1,0:T(8,128)(2,1)S(1)}, bf16[48,1152]{1,0:T(8,128)(2,1)S(1)}, u32[]{:S(2)}, u32[]{:S(2)}) %collective-permute-start.6) | collective-permute-done | bytes 110624 | tf_op jit(solution)/shard_map/ppermute | solution.py:18
  48.4 5.1 %collective-permute-start.10 = (bf16[192,1152]{1,0:T(8,128)(2,1)S(1)}, bf16[192,1152]{1,0:T(8,128)(2,1)S(1)}, u32[]{:S(2)}, u32[]{:S(2)}) collective-permute-start(bf16[192,1152]{1,0:T(8,128)(2,1)S(1)} %constant_dynamic-update-slice_fusion.2), channel_id=1, source_target_pairs={{0,192},{64,0},{128,64},{192,128},{1,193},{65,1},{129,65},{193,129... | collective-permute-start | bytes 1327112 | tf_op jit(solution)/shard_map/ppermute | solution.py:18
  55.4 11.2 %collective-permute-done.9 = bf16[192,1152]{1,0:T(8,128)(2,1)} collective-permute-done((bf16[192,1152]{1,0:T(8,128)(2,1)S(1)}, bf16[192,1152]{1,0:T(8,128)(2,1)}, u32[]{:S(2)}, u32[]{:S(2)}) %collective-permute-start.9) | collective-permute-done | bytes 442400 | tf_op jit(solution)/shard_map/ppermute | solution.py:18
  66.6 2.0 %collective-permute-start.13 = (bf16[192,1152]{1,0:T(8,128)(2,1)}, bf16[192,1152]{1,0:T(8,128)(2,1)S(1)}, u32[]{:S(2)}, u32[]{:S(2)}) collective-permute-start(bf16[192,1152]{1,0:T(8,128)(2,1)} %collective-permute-done.9), channel_id=1, source_target_pairs={{0,4},{4,0},{1,5},{5,1},{2,6},{6,2},{3,7},{7,3},{8,12},{12,8},{9,1... | collective-permute-start | bytes 1327112 | tf_op jit(solution)/shard_map/ppermute | solution.py:18
  68.6 4.0 %collective-permute-done.10 = bf16[192,1152]{1,0:T(8,128)(2,1)S(1)} collective-permute-done((bf16[192,1152]{1,0:T(8,128)(2,1)S(1)}, bf16[192,1152]{1,0:T(8,128)(2,1)S(1)}, u32[]{:S(2)}, u32[]{:S(2)}) %collective-permute-start.10) | collective-permute-done | bytes 442400 | tf_op jit(solution)/shard_map/ppermute | solution.py:18
  73.9 1.5 %fusion.43 = f32[264,1152]{0,1:T(8,128)S(1)} fusion(bf16[192,1152]{1,0:T(8,128)(2,1)} %collective-permute-done.9, bf16[264,1536]{0,1:T(8,128)(2,1)S(1)} %bitcast.95), kind=kOutput, calls=%fused_computation.65 | convolution fusion | flops 116785152 | bytes 1806336 | tf_op jit(solution)/shard_map/dot_general | solution.py:136
  75.5 1.5 %fusion.39 = f32[264,1152]{0,1:T(8,128)S(1)} fusion(bf16[192,1152]{1,0:T(8,128)(2,1)} %collective-permute-done.11, bf16[264,1536]{0,1:T(8,128)(2,1)S(1)} %bitcast.96), kind=kOutput, calls=%fused_computation.61 | convolution fusion | flops 116785152 | bytes 1806336 | tf_op jit(solution)/shard_map/dot_general | solution.py:136
  77.0 1.5 %fusion.45 = f32[264,1152]{0,1:T(8,128)S(1)} fusion(bf16[192,1152]{1,0:T(8,128)(2,1)} %collective-permute-done.8, bf16[264,1536]{0,1:T(8,128)(2,1)S(1)} %bitcast.97), kind=kOutput, calls=%fused_computation.67 | convolution fusion | flops 116785152 | bytes 1806336 | tf_op jit(solution)/shard_map/dot_general | solution.py:136
  80.3 0.9 collective-permute-done.12
  83.1 1.5 multiply_convert_fusion.6
  86.3 6.1 %all-to-all-start = ((bf16[64,16,128]{2,1,0:T(8,128)(2,1)}), bf16[64,16,128]{2,1,0:T(8,128)(2,1)S(1)}, u32[]{:S(2)}, u32[]{:S(2)}) async-start(bf16[64,16,128]{2,1,0:T(8,128)(2,1)} %pad_maximum_fusion.6), calls=%async_computation | async-start | bytes 524288 | tf_op jit(solution)/shard_map/all_to_all | solution.py:184
  94.0 11.7 %all-to-all-done.sent_ref = bf16[64,16,128]{2,1,0:T(8,128)(2,1)S(1)} async-done(((bf16[64,16,128]{2,1,0:T(8,128)(2,1)}), bf16[64,16,128]{2,1,0:T(8,128)(2,1)S(1)}, u32[]{:S(2)}, u32[]{:S(2)}) %all-to-all-start) | async-done | bytes 262176 | tf_op jit(solution)/shard_map/all_to_all | solution.py:184
  106.4 2.0 %shard_map.137 = bf16[64,16,128]{2,1,0:T(8,128)(2,1)} custom-call(bf16[64,16,128]{2,1,0:T(8,128)(2,1)} %copy-done.1), custom_call_target="tpu_custom_call" | custom-call | flops 262144 | bytes 524288 | tf_op jit(solution)/shard_map/pallas_call | solution.py:38
  108.5 6.3 %all-to-all-start.1 = ((bf16[64,16,128]{2,1,0:T(8,128)(2,1)}), bf16[64,16,128]{2,1,0:T(8,128)(2,1)S(1)}, u32[]{:S(2)}, u32[]{:S(2)}) async-start(bf16[64,16,128]{2,1,0:T(8,128)(2,1)} %shard_map.137), calls=%async_computation.1 | async-start | bytes 524288 | tf_op jit(solution)/shard_map/all_to_all | solution.py:185
  115.8 1.0 fusion.17
  116.9 9.9 %all-to-all-done.1 = bf16[64,16,128]{2,1,0:T(8,128)(2,1)S(1)} async-done(((bf16[64,16,128]{2,1,0:T(8,128)(2,1)}), bf16[64,16,128]{2,1,0:T(8,128)(2,1)S(1)}, u32[]{:S(2)}, u32[]{:S(2)}) %all-to-all-start.1) | async-done | bytes 262176 | tf_op jit(solution)/shard_map/all_to_all | solution.py:185
  127.4 2.7 %multiply_multiply_fusion = f32[256,768]{1,0:T(8,128)S(1)} fusion(f32[256,768]{1,0:T(8,128)S(1)} %copy.111, bf16[256,1536]{0,1:T(8,128)(2,1)S(1)} %bitcast.104, bf16[1536,1536]{1,0:T(8,128)(2,1)} %all-gather.2.cloned.1.call-done), kind=kOutput, calls=%fused_computation.40 | convolution fusion | flops 605356032 | bytes 4718592 | tf_op jit(solution)/shard_map/dot_general | solution.py:198
  132.6 1.0 collective-permute-start.16
  133.7 1.4 collective-permute-start.17
  135.1 5.1 %collective-permute-done.15 = bf16[264,384]{1,0:T(8,128)(2,1)S(1)} collective-permute-done((bf16[264,384]{1,0:T(8,128)(2,1)S(1)}, bf16[264,384]{1,0:T(8,128)(2,1)S(1)}, u32[]{:S(2)}, u32[]{:S(2)}) %collective-permute-start.15) | collective-permute-done | bytes 202784 | tf_op jit(solution)/shard_map/ppermute | solution.py:18
  140.2 2.5 %collective-permute-done.16 = bf16[264,384]{1,0:T(8,128)(2,1)S(1)} collective-permute-done((bf16[264,384]{1,0:T(8,128)(2,1)S(1)}, bf16[264,384]{1,0:T(8,128)(2,1)S(1)}, u32[]{:S(2)}, u32[]{:S(2)}) %collective-permute-start.16) | collective-permute-done | bytes 202784 | tf_op jit(solution)/shard_map/ppermute | solution.py:18
  142.7 1.3 collective-permute-done.17
  (134 shorter events, 24.7 us)
Async XLA Ops:
  6.5 19.1 %copy-start = (s32[64]{0:T(128)S(1)}, s32[64]{0:T(128)}, u32[]{:S(2)}) copy-start(s32[64]{0:T(128)} %param.31) | copy-start | bytes 772
  6.5 22.0 %copy-start.3 = (bf16[256,384]{1,0:T(8,128)(2,1)S(1)}, bf16[256,384]{1,0:T(8,128)(2,1)}, u32[]{:S(2)}) copy-start(bf16[256,384]{1,0:T(8,128)(2,1)} %param.18) | copy-start | bytes 589828
  6.5 19.9 %copy-start.5 = (f32[4,768]{1,0:T(4,128)S(1)}, f32[4,768]{1,0:T(4,128)}, u32[]{:S(2)}) copy-start(f32[4,768]{1,0:T(4,128)} %param.23) | copy-start | bytes 36868
  6.5 20.0 %copy-start.6 = (f32[4,256]{1,0:T(4,128)S(1)}, f32[4,256]{1,0:T(4,128)}, u32[]{:S(2)}) copy-start(f32[4,256]{1,0:T(4,128)} %param.24) | copy-start | bytes 12292
  6.5 23.5 %copy-start.10 = (f32[12]{0:T(128)S(1)}, f32[12]{0:T(128)}, u32[]{:S(2)}) copy-start(f32[12]{0:T(128)} %param.26) | copy-start | bytes 148
  6.5 120.8 %all-gather.2.cloned.1.call-start = ((), (), s32[]{:S(2)}) async-start(), calls=%async_computation.2 | async-start | bytes 4792320 | tf_op jit(solution)/shard_map/all_gather | solution.py:104
  9.6 21.3 %copy-start.2 = (bf16[24,1152]{1,0:T(8,128)(2,1)S(1)}, bf16[24,1152]{1,0:T(8,128)(2,1)}, u32[]{:S(2)}) copy-start(bf16[24,1152]{1,0:T(8,128)(2,1)} %shard_map.136) | copy-start | bytes 165892
  9.6 21.3 %collective-permute-start.1 = (bf16[24,1152]{1,0:T(8,128)(2,1)}, bf16[24,1152]{1,0:T(8,128)(2,1)S(1)}, u32[]{:S(2)}, u32[]{:S(2)}) collective-permute-start(bf16[24,1152]{1,0:T(8,128)(2,1)} %shard_map.136), channel_id=1, source_target_pairs={{0,32},{8,40},{16,48},{24,56},{32,0},{40,8},{48,16},{56,24},{1,33}... | collective-permute-start | bytes 165896 | tf_op jit(solution)/shard_map/ppermute | solution.py:18
  18.2 12.7 %collective-permute-start = (bf16[8,384]{0,1:T(8,128)(2,1)S(1)}, bf16[8,384]{0,1:T(8,128)(2,1)S(1)}, u32[]{:S(2)}, u32[]{:S(2)}) collective-permute-start(bf16[8,384]{0,1:T(8,128)(2,1)S(1)} %copy.92), channel_id=1, source_target_pairs={{0,4},{4,8},{8,12},{12,16},{16,20},{20,24},{24,28},{28,32},{32,36}... | collective-permute-start | bytes 18440 | tf_op jit(solution)/shard_map/ppermute | solution.py:98
  31.1 22.5 %collective-permute-start.2 = (bf16[264,384]{0,1:T(8,128)(2,1)S(1)}, bf16[264,384]{0,1:T(8,128)(2,1)S(1)}, u32[]{:S(2)}, u32[]{:S(2)}) collective-permute-start(bf16[264,384]{0,1:T(8,128)(2,1)S(1)} %pad_maximum_fusion.5), channel_id=1, source_target_pairs={{0,1},{1,2},{2,3},{3,0},{4,5},{5,6},{6,7},{7,4},{8,9},{9,10},{10,1... | collective-permute-start | bytes 608264 | tf_op jit(solution)/shard_map/ppermute | solution.py:18
  32.4 21.1 %collective-permute-start.3 = (bf16[264,384]{0,1:T(8,128)(2,1)S(1)}, bf16[264,384]{0,1:T(8,128)(2,1)S(1)}, u32[]{:S(2)}, u32[]{:S(2)}) collective-permute-start(bf16[264,384]{0,1:T(8,128)(2,1)S(1)} %pad_maximum_fusion.5), channel_id=1, source_target_pairs={{0,2},{1,3},{2,0},{3,1},{4,6},{5,7},{6,4},{7,5},{8,10},{9,11},{10,... | collective-permute-start | bytes 608264 | tf_op jit(solution)/shard_map/ppermute | solution.py:18
  35.0 19.1 %collective-permute-start.4 = (bf16[264,384]{0,1:T(8,128)(2,1)S(1)}, bf16[264,384]{0,1:T(8,128)(2,1)S(1)}, u32[]{:S(2)}, u32[]{:S(2)}) collective-permute-start(bf16[264,384]{0,1:T(8,128)(2,1)S(1)} %pad_maximum_fusion.5), channel_id=1, source_target_pairs={{0,3},{1,0},{2,1},{3,2},{4,7},{5,4},{6,5},{7,6},{8,11},{9,8},{10,9... | collective-permute-start | bytes 608264 | tf_op jit(solution)/shard_map/ppermute | solution.py:18
  36.1 6.5 %collective-permute-start.5 = (bf16[48,1152]{1,0:T(8,128)(2,1)S(1)}, bf16[48,1152]{1,0:T(8,128)(2,1)S(1)}, u32[]{:S(2)}, u32[]{:S(2)}) collective-permute-start(bf16[48,1152]{1,0:T(8,128)(2,1)S(1)} %pad_maximum_fusion.7), channel_id=1, source_target_pairs={{0,8},{8,16},{16,24},{24,32},{32,40},{40,48},{48,56},{56,0},{1,9},... | collective-permute-start | bytes 331784 | tf_op jit(solution)/shard_map/ppermute | solution.py:18
  36.9 10.9 %collective-permute-start.6 = (bf16[48,1152]{1,0:T(8,128)(2,1)S(1)}, bf16[48,1152]{1,0:T(8,128)(2,1)S(1)}, u32[]{:S(2)}, u32[]{:S(2)}) collective-permute-start(bf16[48,1152]{1,0:T(8,128)(2,1)S(1)} %pad_maximum_fusion.7), channel_id=1, source_target_pairs={{0,16},{8,24},{16,32},{24,40},{32,48},{40,56},{48,0},{56,8},{1,17}... | collective-permute-start | bytes 331784 | tf_op jit(solution)/shard_map/ppermute | solution.py:18
  42.7 5.1 %collective-permute-start.7 = (bf16[48,1152]{1,0:T(8,128)(2,1)S(1)}, bf16[48,1152]{1,0:T(8,128)(2,1)S(1)}, u32[]{:S(2)}, u32[]{:S(2)}) collective-permute-start(bf16[48,1152]{1,0:T(8,128)(2,1)S(1)} %pad_maximum_fusion.7), channel_id=1, source_target_pairs={{0,56},{8,0},{16,8},{24,16},{32,24},{40,32},{48,40},{56,48},{1,57}... | collective-permute-start | bytes 331784 | tf_op jit(solution)/shard_map/ppermute | solution.py:18
  47.8 27.7 %collective-permute-start.11 = (bf16[192,1152]{1,0:T(8,128)(2,1)S(1)}, bf16[192,1152]{1,0:T(8,128)(2,1)}, u32[]{:S(2)}, u32[]{:S(2)}) collective-permute-start(bf16[192,1152]{1,0:T(8,128)(2,1)S(1)} %constant_dynamic-update-slice_fusion.2), channel_id=1, source_target_pairs={{0,4},{4,0},{1,5},{5,1},{2,6},{6,2},{3,7},{7,3},{8,12},{12,8},{9,1... | collective-permute-start | bytes 1327112 | tf_op jit(solution)/shard_map/ppermute | solution.py:18
  48.4 24.1 %collective-permute-start.10 = (bf16[192,1152]{1,0:T(8,128)(2,1)S(1)}, bf16[192,1152]{1,0:T(8,128)(2,1)S(1)}, u32[]{:S(2)}, u32[]{:S(2)}) collective-permute-start(bf16[192,1152]{1,0:T(8,128)(2,1)S(1)} %constant_dynamic-update-slice_fusion.2), channel_id=1, source_target_pairs={{0,192},{64,0},{128,64},{192,128},{1,193},{65,1},{129,65},{193,129... | collective-permute-start | bytes 1327112 | tf_op jit(solution)/shard_map/ppermute | solution.py:18
  53.6 13.1 %collective-permute-start.9 = (bf16[192,1152]{1,0:T(8,128)(2,1)S(1)}, bf16[192,1152]{1,0:T(8,128)(2,1)}, u32[]{:S(2)}, u32[]{:S(2)}) collective-permute-start(bf16[192,1152]{1,0:T(8,128)(2,1)S(1)} %constant_dynamic-update-slice_fusion.2), channel_id=1, source_target_pairs={{0,128},{64,192},{128,0},{192,64},{1,129},{65,193},{129,1},{193,65... | collective-permute-start | bytes 1327112 | tf_op jit(solution)/shard_map/ppermute | solution.py:18
  53.6 23.5 %collective-permute-start.8 = (bf16[192,1152]{1,0:T(8,128)(2,1)S(1)}, bf16[192,1152]{1,0:T(8,128)(2,1)}, u32[]{:S(2)}, u32[]{:S(2)}) collective-permute-start(bf16[192,1152]{1,0:T(8,128)(2,1)S(1)} %constant_dynamic-update-slice_fusion.2), channel_id=1, source_target_pairs={{0,64},{64,128},{128,192},{192,0},{1,65},{65,129},{129,193},{193,1... | collective-permute-start | bytes 1327112 | tf_op jit(solution)/shard_map/ppermute | solution.py:18
  66.6 12.6 %collective-permute-start.13 = (bf16[192,1152]{1,0:T(8,128)(2,1)}, bf16[192,1152]{1,0:T(8,128)(2,1)S(1)}, u32[]{:S(2)}, u32[]{:S(2)}) collective-permute-start(bf16[192,1152]{1,0:T(8,128)(2,1)} %collective-permute-done.9), channel_id=1, source_target_pairs={{0,4},{4,0},{1,5},{5,1},{2,6},{6,2},{3,7},{7,3},{8,12},{12,8},{9,1... | collective-permute-start | bytes 1327112 | tf_op jit(solution)/shard_map/ppermute | solution.py:18
  72.6 7.2 %collective-permute-start.14 = (bf16[192,1152]{1,0:T(8,128)(2,1)S(1)}, bf16[192,1152]{1,0:T(8,128)(2,1)S(1)}, u32[]{:S(2)}, u32[]{:S(2)}) collective-permute-start(bf16[192,1152]{1,0:T(8,128)(2,1)S(1)} %collective-permute-done.10), channel_id=1, source_target_pairs={{0,4},{4,0},{1,5},{5,1},{2,6},{6,2},{3,7},{7,3},{8,12},{12,8},{9,1... | collective-permute-start | bytes 1327112 | tf_op jit(solution)/shard_map/ppermute | solution.py:18
  79.1 2.1 %collective-permute-start.12 = (bf16[192,1152]{1,0:T(8,128)(2,1)}, bf16[192,1152]{1,0:T(8,128)(2,1)S(1)}, u32[]{:S(2)}, u32[]{:S(2)}) collective-permute-start(bf16[192,1152]{1,0:T(8,128)(2,1)} %collective-permute-done.8), channel_id=1, source_target_pairs={{0,4},{4,0},{1,5},{5,1},{2,6},{6,2},{3,7},{7,3},{8,12},{12,8},{9,1... | collective-permute-start | bytes 1327112 | tf_op jit(solution)/shard_map/ppermute | solution.py:18
  80.3 1.5 copy-start.7
  86.3 19.4 %all-to-all-start = ((bf16[64,16,128]{2,1,0:T(8,128)(2,1)}), bf16[64,16,128]{2,1,0:T(8,128)(2,1)S(1)}, u32[]{:S(2)}, u32[]{:S(2)}) async-start(bf16[64,16,128]{2,1,0:T(8,128)(2,1)} %pad_maximum_fusion.6), calls=%async_computation | async-start | bytes 524288 | tf_op jit(solution)/shard_map/all_to_all | solution.py:184
  108.5 18.3 %all-to-all-start.1 = ((bf16[64,16,128]{2,1,0:T(8,128)(2,1)}), bf16[64,16,128]{2,1,0:T(8,128)(2,1)S(1)}, u32[]{:S(2)}, u32[]{:S(2)}) async-start(bf16[64,16,128]{2,1,0:T(8,128)(2,1)} %shard_map.137), calls=%async_computation.1 | async-start | bytes 524288 | tf_op jit(solution)/shard_map/all_to_all | solution.py:185
  115.0 0.8 copy-start.4
  115.0 0.8 copy-start.11
  127.4 3.5 %copy-start.8 = (bf16[1536,1536]{1,0:T(8,128)(2,1)S(1)}, bf16[1536,1536]{1,0:T(8,128)(2,1)}, u32[]{:S(2)}) copy-start(bf16[1536,1536]{1,0:T(8,128)(2,1)} %all-gather.2.cloned.1.call-done) | copy-start | bytes 14155780
  127.4 3.5 %copy-start.9 = (f32[768]{0:T(1024)S(1)}, f32[768]{0:T(1024)}, u32[]{:S(2)}) copy-start(f32[768]{0:T(1024)} %param.28) | copy-start | bytes 9220
  131.9 8.3 %collective-permute-start.15 = (bf16[264,384]{1,0:T(8,128)(2,1)S(1)}, bf16[264,384]{1,0:T(8,128)(2,1)S(1)}, u32[]{:S(2)}, u32[]{:S(2)}) collective-permute-start(bf16[264,384]{1,0:T(8,128)(2,1)S(1)} %get-tuple-element.30), channel_id=1, source_target_pairs={{0,1},{1,2},{2,3},{3,0},{4,5},{5,6},{6,7},{7,4},{8,9},{9,10},{10,1... | collective-permute-start | bytes 608264 | tf_op jit(solution)/shard_map/ppermute | solution.py:18
  132.6 10.1 %collective-permute-start.16 = (bf16[264,384]{1,0:T(8,128)(2,1)S(1)}, bf16[264,384]{1,0:T(8,128)(2,1)S(1)}, u32[]{:S(2)}, u32[]{:S(2)}) collective-permute-start(bf16[264,384]{1,0:T(8,128)(2,1)S(1)} %get-tuple-element.31), channel_id=1, source_target_pairs={{0,2},{1,3},{2,0},{3,1},{4,6},{5,7},{6,4},{7,5},{8,10},{9,11},{10,... | collective-permute-start | bytes 608264 | tf_op jit(solution)/shard_map/ppermute | solution.py:18
  133.7 10.4 %collective-permute-start.17 = (bf16[264,384]{1,0:T(8,128)(2,1)S(1)}, bf16[264,384]{1,0:T(8,128)(2,1)S(1)}, u32[]{:S(2)}, u32[]{:S(2)}) collective-permute-start(bf16[264,384]{1,0:T(8,128)(2,1)S(1)} %get-tuple-element.32), channel_id=1, source_target_pairs={{0,3},{1,0},{2,1},{3,2},{4,7},{5,4},{6,5},{7,6},{8,11},{9,8},{10,9... | collective-permute-start | bytes 608264 | tf_op jit(solution)/shard_map/ppermute | solution.py:18
  (1 other events, 0.7 us)
Sparse Core Ops, SparseCore 0:
  24.2 83.2 all-gather.1

commit v3 on v2

--- a/solution.py
+++ b/solution.py
@@ -47,23 +47,24 @@
 
 
 def pack_body(value_ref, shared_ref, step_ref, out_ref):
-    inner, shared, heads = value_ref.shape[1], shared_ref.shape[1], step_ref.shape[1]
-    out_ref[:, :inner] = value_ref[...].astype(BF16)
-    out_ref[:, inner : inner + shared] = shared_ref[...].astype(BF16)
-    rest = out_ref.shape[1] - inner - shared
-    step = jnp.pad(step_ref[...], ((0, 0), (0, rest - heads)))
-    out_ref[:, inner + shared :] = step.astype(BF16)
-
-
-def pack_early(value, shared, step):
-    width = value.shape[1] + shared.shape[1] + step.shape[1]
+    inner, half, heads = value_ref.shape[1], shared_ref.shape[1] // 2, step_ref.shape[0]
+    rest = out_ref.shape[2] - inner - half
+    step = jnp.pad(step_ref[...].T, ((0, 0), (0, rest - heads)))
+    packed = jnp.concatenate([value_ref[...], shared_ref[:, :half], step], axis=1).astype(BF16)
+    for k in range(out_ref.shape[0]):
+        out_ref[k] = packed
+
+
+def pack_early(value, shared, step, copies):
+    rows, inner = value.shape
+    width = inner + shared.shape[1] // 2 + step.shape[1]
     width += -width % 128
     return pl.pallas_call(
         pack_body,
-        out_shape=jax.ShapeDtypeStruct((value.shape[0], width), BF16),
+        out_shape=jax.ShapeDtypeStruct((copies, rows, width), BF16),
         in_specs=[pl.BlockSpec(memory_space=pltpu.VMEM)] * 3,
         out_specs=pl.BlockSpec(memory_space=pltpu.VMEM),
-    )(value, shared, step)
+    )(value, shared, step.T)
 
 
 def on_device(
@@ -95,30 +96,21 @@
     tp_at = lax.axis_index("tp")
     seq_at = (x_at * z_size + z_at) * core_size + core_at
 
+    early = pack_early(w_in_value, w_in_shared, w_in_step, x_size * z_size)
+    own = lax.all_to_all(early, SEQ[:2], 0, 0, tiled=True).reshape(-1, early.shape[2])
+
+    late = jnp.concatenate(
+        [w_in_gate.astype(BF16), w_out.T.astype(BF16), w_in_shared[:, state:].astype(BF16)], axis=1
+    )
+    late = lax.all_gather(late, SEQ, axis=0, tiled=True)
+
     before = lax.ppermute(
         hidden_in[tokens - EDGE :], SEQ, [(i, i + 1) for i in range(seq_count - 1)]
     )
-    early = pack_early(w_in_value, w_in_shared, w_in_step)
-
-    late = jnp.concatenate([w_in_gate.astype(BF16), w_out.T.astype(BF16)], axis=1)
-    late = lax.all_gather(late, SEQ, axis=0, tiled=True)
-
-    half = z_size // 2
-    pair = jnp.concatenate([early, ahead(early, "z", half)], axis=0)
-    before, pair = lax.optimization_barrier((before, pair))
     mine = jnp.concatenate([before, hidden_in], axis=0)
     hidden = jnp.concatenate([mine] + [ahead(mine, "tp", d) for d in range(1, tp_count)], axis=1)
-    z_shifts = [0, 1, 2, z_size - 1]
-    along_z = jnp.concatenate([pair] + [ahead(pair, "z", d) for d in z_shifts[1:]], axis=0)
-    z_offsets = [(d + o) % z_size for d in z_shifts for o in (0, half)]
-    own = [along_z] + [ahead(along_z, "x", d) for d in range(1, x_size)]
-    other = [ahead(block, "core", 1) for block in own]
-
-    chips = [
-        jnp.stack([((x_at - d) % x_size * z_size + (z_at - o) % z_size) for o in z_offsets])
-        * core_size
-        for d in range(x_size)
-    ]
+
+    chips = jnp.arange(x_size * z_size, dtype=jnp.int32) * core_size
     blocks_each = seq_count // tp_count
 
     def columns_for(stored):
@@ -129,34 +121,37 @@
         return jnp.take(cut, place, axis=1).reshape(hidden.shape[0], -1)
 
     h_all = columns_for(jnp.arange(seq_count, dtype=jnp.int32))
-    order = [stored + core_at for stored in chips] + [stored + (1 - core_at) for stored in chips]
-    h_early = columns_for(jnp.concatenate(order))
-    depth = early.shape[0] * z_size
-    projected = sum(
-        jnp.dot(h_early[:, i * depth : (i + 1) * depth], block, preferred_element_type=F32)
-        for i, block in enumerate(own + other)
+    h_own = columns_for(chips + core_at)
+    h_other = columns_for(chips + (1 - core_at))
+    own, h_own, h_other = lax.optimization_barrier((own, h_own, h_other))
+    other = ahead(own, "core", 1)
+    projected = (
+        jnp.dot(h_own, own, preferred_element_type=F32)
+        + jnp.dot(h_other, other, preferred_element_type=F32)
     ).astype(BF16)
-    mixed = projected[:, : inner + shared]
-    raw = projected[EDGE:, inner + shared : inner + shared + heads]
+    mixed = projected[:, : inner + state]
+    raw = projected[EDGE:, inner + state : inner + state + heads]
 
     doc_ends = jnp.cumsum(prompt_lengths)
     first = seq_at * tokens
     ext_segments = segment_of(first - EDGE + jnp.arange(EDGE + tokens, dtype=jnp.int32), doc_ends)
     segments = ext_segments[EDGE:]
     prev_seg = ext_segments[EDGE - 1]
-    taps = jnp.concatenate([conv_value, conv_shared], axis=1)
-    conv_sum = jnp.zeros((tokens, inner + shared), F32)
-    width = taps.shape[0]
-    for k in range(width):
-        at = EDGE - width + 1 + k
-        same = (ext_segments[at : at + tokens] == segments)[:, None]
-        conv_sum = conv_sum + jnp.where(
-            same, taps[k][None, :] * mixed[at : at + tokens].astype(F32), 0.0
-        )
-    convolved = jax.nn.silu(conv_sum).astype(BF16)
+
+    def convolve(rows, taps):
+        conv_sum = jnp.zeros((tokens, rows.shape[1]), F32)
+        width = taps.shape[0]
+        for k in range(width):
+            at = EDGE - width + 1 + k
+            same = (ext_segments[at : at + tokens] == segments)[:, None]
+            conv_sum = conv_sum + jnp.where(
+                same, taps[k][None, :] * rows[at : at + tokens].astype(F32), 0.0
+            )
+        return jax.nn.silu(conv_sum).astype(BF16)
+
+    convolved = convolve(mixed, jnp.concatenate([conv_value, conv_shared[:, :state]], axis=1))
     values = convolved[:, :inner].reshape(tokens, heads, head_dim)
-    b_half = convolved[:, inner : inner + state]
-    c_half = convolved[:, inner + state :]
+    b_half = convolved[:, inner:]
     steps = jax.nn.softplus(raw.astype(F32) + dt_bias[None, :])
     cumulative = jnp.cumsum(-steps * jnp.exp(a_log)[None, :], axis=0)
 
@@ -185,6 +180,8 @@
     carried = lax.all_to_all(scan_states(received, heads), SEQ, 0, 0, tiled=True)
     carried = carried[:, :heads].transpose(1, 0, 2).reshape(inner, state)
 
+    c_rows = jnp.dot(h_all, late[:, 2 * inner :], preferred_element_type=F32).astype(BF16)
+    c_half = convolve(c_rows, conv_shared[:, state:])
     places = jnp.arange(tokens)
     causal = (places[:, None] >= places[None, :]) & (segments[:, None] == segments[None, :])
     scores = jnp.dot(c_half, b_half.T, preferred_element_type=F32)
@@ -215,7 +212,7 @@
     riding = jnp.pad(riding, ((0, 6), (0, features - tokens)))
     terms = lax.dot_general(
         (gated * norm_gain[None, :]).astype(BF16),
-        late[:, inner:],
+        late[:, inner : 2 * inner],
         (((1,), (1,)), ((), ())),
         preferred_element_type=F32,
     ).astype(BF16)

time: 152 us -> 170 us (1.12)
  waiting for transfers between devices: 56.3 us -> 65.3 us
  starting transfers between devices: 43.2 us -> 50.3 us
    ppermute x1, waiting for transfers between devices: 0.01 us -> 30.1 us  [on_device(): lax.ppermute(hidden_in[tokens - EDGE:], SEQ, [(i, i + 1) for i in range(s...]
    ppermute x17 -> x7, waiting for transfers between devices: 34.6 us -> 14.1 us  [ahead(): lax.ppermute(block, axis, [(i, (i + distance) % count) for i in range(cou...]
    ppermute x17 -> x7, starting transfers between devices: 27.3 us -> 9.47 us  [ahead(): lax.ppermute(block, axis, [(i, (i + distance) % count) for i in range(cou...]
    all_to_all x1, starting transfers between devices: 6.11 us -> 18.5 us  [on_device(): received = lax.all_to_all(sent, SEQ, 0, 0, tiled=True)]
    all_to_all x0 -> x1, starting transfers between devices: none -> 12.1 us  [on_device(): lax.all_to_all(early, SEQ[:2], 0, 0, tiled=True).reshape(-1, early.shape[2])]
    all_to_all x1, waiting for transfers between devices: 11.7 us -> 9.52 us  [on_device(): received = lax.all_to_all(sent, SEQ, 0, 0, tiled=True)]
    dot_general x8 -> x3, matrix products: 7.24 us -> 6.54 us  [the longest x1 2.57 us: on_device(): jnp.dot(h_other, other, preferred_element_type=F32)]
  transfers between devices with their start and end apart: 21 -> 12, of which waited for: 10 -> 7; matrix products, arithmetic and copies ran while one was open for 17% -> 11% of each run, Pallas kernels for 1% -> 3%
where the time goes in v3:
time: 170 us; the launch traced here: 169 us
  waiting for transfers between devices  65.3 us (38%)
  starting transfers between devices  50.3 us (30%)
  between operations  15.3 us (9%)
  matrix products  14 us (8%)
  other arithmetic  11.1 us (7%)
  local copies, waits for them, and re-layouts  8.85 us (5%)
  Pallas kernels  4.26 us (3%)
    ppermute x1, waiting for transfers between devices, on_device(): lax.ppermute(hidden_in[tokens - EDGE:], SEQ, [(i, i + 1) for i in range(s...  30.1 us
    all_to_all x1, starting transfers between devices, on_device(): received = lax.all_to_all(sent, SEQ, 0, 0, tiled=True)  18.5 us
    ppermute x7, waiting for transfers between devices, ahead(): lax.ppermute(block, axis, [(i, (i + distance) % count) for i in range(cou...  14.1 us
    all_to_all x1, starting transfers between devices, on_device(): lax.all_to_all(early, SEQ[:2], 0, 0, tiled=True).reshape(-1, early.shape[2])  12.1 us
    all_to_all x1, waiting for transfers between devices, on_device(): lax.all_to_all(scan_states(received, heads), SEQ, 0, 0, tiled=True)  11.6 us
    all_to_all x1, waiting for transfers between devices, on_device(): received = lax.all_to_all(sent, SEQ, 0, 0, tiled=True)  9.52 us
    ppermute x7, starting transfers between devices, ahead(): lax.ppermute(block, axis, [(i, (i + distance) % count) for i in range(cou...  9.47 us
    all_to_all x1, starting transfers between devices, on_device(): lax.all_to_all(scan_states(received, heads), SEQ, 0, 0, tiled=True)  6.03 us
  transfers between devices with their start and end apart: 12, of which 7 were waited for; matrix products, arithmetic and copies ran while one was open for 11% of the time, Pallas kernels for 3%

profile of v3, /device:TPU:1, one launch (start us, length us, event | category | flops | bytes accessed | tf_op | source)
XLA Modules:
  0.0 169.1 jit_solution(6739603450872475118)
XLA Ops:
  6.5 0.9 convert_bitcast_fusion
  7.4 0.9 convert_element_type.136
  9.7 2.2 %shard_map.136 = bf16[32,24,1024]{2,1,0:T(8,128)(2,1)} custom-call(f32[24,768]{1,0:T(8,128)} %value_ref.1, f32[24,256]{1,0:T(8,128)} %shared_ref.1, f32[12,24]{1,0:T(8,128)} %bitcast.90), custom_call_target="tpu_custom_call" | custom-call | tf_op jit(solution)/shard_map/pallas_call | solution.py:62
  11.9 12.1 %all-to-all-start = ((bf16[32,24,1024]{2,1,0:T(8,128)(2,1)}), bf16[32,24,1024]{2,1,0:T(8,128)(2,1)}, u32[]{:S(2)}, u32[]{:S(2)}) async-start(bf16[32,24,1024]{2,1,0:T(8,128)(2,1)} %shard_map.136), calls=%async_computation | async-start | bytes 3145728 | tf_op jit(solution)/shard_map/all_to_all | solution.py:100
  24.2 4.2 %collective-permute-start = (bf16[8,384]{0,1:T(8,128)(2,1)S(1)}, bf16[8,384]{0,1:T(8,128)(2,1)S(1)}, u32[]{:S(2)}, u32[]{:S(2)}) collective-permute-start(bf16[8,384]{0,1:T(8,128)(2,1)S(1)} %copy.73), channel_id=1, source_target_pairs={{0,4},{4,8},{8,12},{12,16},{16,20},{20,24},{24,28},{28,32},{32,36}... | collective-permute-start | bytes 18440 | tf_op jit(solution)/shard_map/ppermute | solution.py:107
  30.1 30.1 %collective-permute-done = bf16[8,384]{0,1:T(8,128)(2,1)S(1)} collective-permute-done((bf16[8,384]{0,1:T(8,128)(2,1)S(1)}, bf16[8,384]{0,1:T(8,128)(2,1)S(1)}, u32[]{:S(2)}, u32[]{:S(2)}) %collective-permute-start) | collective-permute-done | bytes 6176 | tf_op jit(solution)/shard_map/ppermute | solution.py:107
  60.3 1.2 collective-permute-start.1
  61.5 2.8 %collective-permute-start.2 = (bf16[264,384]{0,1:T(8,128)(2,1)S(1)}, bf16[264,384]{0,1:T(8,128)(2,1)S(1)}, u32[]{:S(2)}, u32[]{:S(2)}) collective-permute-start(bf16[264,384]{0,1:T(8,128)(2,1)S(1)} %pad_maximum_fusion.5), channel_id=1, source_target_pairs={{0,2},{1,3},{2,0},{3,1},{4,6},{5,7},{6,4},{7,5},{8,10},{9,11},{10,... | collective-permute-start | bytes 608264 | tf_op jit(solution)/shard_map/ppermute | solution.py:18
  64.4 0.9 collective-permute-start.3
  65.2 2.4 %collective-permute-done.1 = bf16[264,384]{0,1:T(8,128)(2,1)S(1)} collective-permute-done((bf16[264,384]{0,1:T(8,128)(2,1)S(1)}, bf16[264,384]{0,1:T(8,128)(2,1)S(1)}, u32[]{:S(2)}, u32[]{:S(2)}) %collective-permute-start.1) | collective-permute-done | bytes 202784 | tf_op jit(solution)/shard_map/ppermute | solution.py:18
  67.7 3.9 %collective-permute-done.2 = bf16[264,384]{0,1:T(8,128)(2,1)S(1)} collective-permute-done((bf16[264,384]{0,1:T(8,128)(2,1)S(1)}, bf16[264,384]{0,1:T(8,128)(2,1)S(1)}, u32[]{:S(2)}, u32[]{:S(2)}) %collective-permute-start.2) | collective-permute-done | bytes 202784 | tf_op jit(solution)/shard_map/ppermute | solution.py:18
  77.1 1.4 broadcast_compare_fusion.1
  78.4 2.4 %fusion.71 = f32[264,1024]{0,1:T(8,128)S(1)} fusion(bf16[264,768]{0,1:T(8,128)(2,1)S(1)} %bitcast.84, bf16[768,1024]{1,0:T(8,128)(2,1)} %bitcast.3), kind=kOutput, calls=%fused_computation.191 | convolution fusion | flops 415236096 | bytes 3059712 | tf_op jit(solution)/shard_map/dot_general | solution.py:129
  80.9 2.6 %add_convert_fusion = bf16[264,1024]{0,1:T(8,128)(2,1)S(1)} fusion(f32[264,1024]{0,1:T(8,128)S(1)} %fusion.71, bf16[264,768]{0,1:T(8,128)(2,1)S(1)} %bitcast.83, bf16[768,1024]{1,0:T(8,128)(2,1)} %collective-permute-done.4), kind=kOutput, calls=%fused_computation.17 | convolution fusion | flops 415776768 | bytes 3600384 | tf_op jit(solution)/shard_map/dot_general | solution.py:130
  84.8 1.3 multiply_convert_fusion.6
  87.0 0.8 pad_maximum_fusion.6
  87.8 18.5 %all-to-all-start.1 = ((bf16[64,16,128]{2,1,0:T(8,128)(2,1)}), bf16[64,16,128]{2,1,0:T(8,128)(2,1)S(1)}, u32[]{:S(2)}, u32[]{:S(2)}) async-start(bf16[64,16,128]{2,1,0:T(8,128)(2,1)} %pad_maximum_fusion.6), calls=%async_computation.1 | async-start | bytes 524288 | tf_op jit(solution)/shard_map/all_to_all | solution.py:179
  106.7 0.8 gather_fusion.1
  107.5 1.3 slice_select_fusion
  108.7 9.5 %all-to-all-done.1.sent_ref = bf16[64,16,128]{2,1,0:T(8,128)(2,1)S(1)} async-done(((bf16[64,16,128]{2,1,0:T(8,128)(2,1)}), bf16[64,16,128]{2,1,0:T(8,128)(2,1)S(1)}, u32[]{:S(2)}, u32[]{:S(2)}) %all-to-all-start.1) | async-done | bytes 262176 | tf_op jit(solution)/shard_map/all_to_all | solution.py:179
  118.9 2.0 %shard_map.137 = bf16[64,16,128]{2,1,0:T(8,128)(2,1)} custom-call(bf16[64,16,128]{2,1,0:T(8,128)(2,1)} %copy-done.1), custom_call_target="tpu_custom_call" | custom-call | flops 262144 | bytes 524288 | tf_op jit(solution)/shard_map/pallas_call | solution.py:38
  121.0 6.0 %all-to-all-start.2 = ((bf16[64,16,128]{2,1,0:T(8,128)(2,1)}), bf16[64,16,128]{2,1,0:T(8,128)(2,1)S(1)}, u32[]{:S(2)}, u32[]{:S(2)}) async-start(bf16[64,16,128]{2,1,0:T(8,128)(2,1)} %shard_map.137), calls=%async_computation.2 | async-start | bytes 524288 | tf_op jit(solution)/shard_map/all_to_all | solution.py:180
  127.4 11.6 %all-to-all-done.2 = bf16[64,16,128]{2,1,0:T(8,128)(2,1)S(1)} async-done(((bf16[64,16,128]{2,1,0:T(8,128)(2,1)}), bf16[64,16,128]{2,1,0:T(8,128)(2,1)S(1)}, u32[]{:S(2)}, u32[]{:S(2)}) %all-to-all-start.2) | async-done | bytes 262176 | tf_op jit(solution)/shard_map/all_to_all | solution.py:180
  139.1 1.5 convolution_convert_fusion.2
  141.0 1.0 fusion.11
  143.1 2.6 %multiply_multiply_fusion = f32[256,768]{1,0:T(8,128)S(1)} fusion(f32[256,768]{1,0:T(8,128)S(1)} %copy.84, bf16[256,1536]{0,1:T(8,128)(2,1)S(1)} %bitcast.81, bf16[1536,1664]{1,0:T(8,128)(2,1)} %all-gather.2.cloned.1.call-done), kind=kOutput, calls=%fused_computation.36 | convolution fusion | flops 605356032 | bytes 4718592 | tf_op jit(solution)/shard_map/dot_general | solution.py:195
  146.5 2.5 %convolution_convert_fusion = bf16[256,1536]{1,0:T(8,128)(2,1)S(1)} fusion(bf16[1536,1664]{1,0:T(8,128)(2,1)} %all-gather.2.cloned.1.call-done, f32[256,768]{1,0:T(8,128)S(1)} %multiply_multiply_fusion, f32[768]{0:T(1024)S(1)} %copy-done.7), kind=kOutput, calls=%fused_computation.7 | convolution fusion | flops 604766208 | bytes 3935232 | tf_op jit(solution)/shard_map/dot_general | solution.py:213
  149.2 1.1 collective-permute-start.5
  150.2 2.1 %collective-permute-start.6 = (bf16[264,384]{1,0:T(8,128)(2,1)S(1)}, bf16[264,384]{1,0:T(8,128)(2,1)S(1)}, u32[]{:S(2)}, u32[]{:S(2)}) collective-permute-start(bf16[264,384]{1,0:T(8,128)(2,1)S(1)} %get-tuple-element.33), channel_id=1, source_target_pairs={{0,2},{1,3},{2,0},{3,1},{4,6},{5,7},{6,4},{7,5},{8,10},{9,11},{10,... | collective-permute-start | bytes 608264 | tf_op jit(solution)/shard_map/ppermute | solution.py:18
  152.3 1.3 collective-permute-start.7
  153.6 3.0 %collective-permute-done.5 = bf16[264,384]{1,0:T(8,128)(2,1)S(1)} collective-permute-done((bf16[264,384]{1,0:T(8,128)(2,1)S(1)}, bf16[264,384]{1,0:T(8,128)(2,1)S(1)}, u32[]{:S(2)}, u32[]{:S(2)}) %collective-permute-start.5) | collective-permute-done | bytes 202784 | tf_op jit(solution)/shard_map/ppermute | solution.py:18
  156.6 4.7 %collective-permute-done.6 = bf16[264,384]{1,0:T(8,128)(2,1)S(1)} collective-permute-done((bf16[264,384]{1,0:T(8,128)(2,1)S(1)}, bf16[264,384]{1,0:T(8,128)(2,1)S(1)}, u32[]{:S(2)}, u32[]{:S(2)}) %collective-permute-start.6) | collective-permute-done | bytes 202784 | tf_op jit(solution)/shard_map/ppermute | solution.py:18
  (109 shorter events, 14.2 us)
Async XLA Ops:
  6.5 21.9 %copy-start = (s32[64]{0:T(128)S(1)}, s32[64]{0:T(128)}, u32[]{:S(2)}) copy-start(s32[64]{0:T(128)} %param.31) | copy-start | bytes 772
  6.5 132.5 %all-gather.2.cloned.1.call-start = ((), (), s32[]{:S(2)}) async-start(), calls=%async_computation.3 | async-start | bytes 5191680 | tf_op jit(solution)/shard_map/all_gather | solution.py:105
  11.9 12.1 %slice-start = ((bf16[256,384]{1,0:T(8,128)(2,1)}), bf16[8,384]{1,0:T(8,128)(2,1)S(1)}, s32[]{:S(2)}) async-start(bf16[256,384]{1,0:T(8,128)(2,1)} %param.18), calls=%async_computation.4 | async-start | bytes 12288 | tf_op jit(solution)/shard_map/slice | solution.py:108
  11.9 18.0 %copy-start.3 = (bf16[256,384]{1,0:T(8,128)(2,1)S(1)}, bf16[256,384]{1,0:T(8,128)(2,1)}, u32[]{:S(2)}) copy-start(bf16[256,384]{1,0:T(8,128)(2,1)} %param.18) | copy-start | bytes 589828
  11.9 61.6 %all-to-all-start = ((bf16[32,24,1024]{2,1,0:T(8,128)(2,1)}), bf16[32,24,1024]{2,1,0:T(8,128)(2,1)}, u32[]{:S(2)}, u32[]{:S(2)}) async-start(bf16[32,24,1024]{2,1,0:T(8,128)(2,1)} %shard_map.136), calls=%async_computation | async-start | bytes 3145728 | tf_op jit(solution)/shard_map/all_to_all | solution.py:100
  24.2 35.9 %collective-permute-start = (bf16[8,384]{0,1:T(8,128)(2,1)S(1)}, bf16[8,384]{0,1:T(8,128)(2,1)S(1)}, u32[]{:S(2)}, u32[]{:S(2)}) collective-permute-start(bf16[8,384]{0,1:T(8,128)(2,1)S(1)} %copy.73), channel_id=1, source_target_pairs={{0,4},{4,8},{8,12},{12,16},{16,20},{20,24},{24,28},{28,32},{32,36}... | collective-permute-start | bytes 18440 | tf_op jit(solution)/shard_map/ppermute | solution.py:107
  60.3 7.4 %collective-permute-start.1 = (bf16[264,384]{0,1:T(8,128)(2,1)S(1)}, bf16[264,384]{0,1:T(8,128)(2,1)S(1)}, u32[]{:S(2)}, u32[]{:S(2)}) collective-permute-start(bf16[264,384]{0,1:T(8,128)(2,1)S(1)} %pad_maximum_fusion.5), channel_id=1, source_target_pairs={{0,1},{1,2},{2,3},{3,0},{4,5},{5,6},{6,7},{7,4},{8,9},{9,10},{10,1... | collective-permute-start | bytes 608264 | tf_op jit(solution)/shard_map/ppermute | solution.py:18
  61.5 10.1 %collective-permute-start.2 = (bf16[264,384]{0,1:T(8,128)(2,1)S(1)}, bf16[264,384]{0,1:T(8,128)(2,1)S(1)}, u32[]{:S(2)}, u32[]{:S(2)}) collective-permute-start(bf16[264,384]{0,1:T(8,128)(2,1)S(1)} %pad_maximum_fusion.5), channel_id=1, source_target_pairs={{0,2},{1,3},{2,0},{3,1},{4,6},{5,7},{6,4},{7,5},{8,10},{9,11},{10,... | collective-permute-start | bytes 608264 | tf_op jit(solution)/shard_map/ppermute | solution.py:18
  64.4 7.3 %collective-permute-start.3 = (bf16[264,384]{0,1:T(8,128)(2,1)S(1)}, bf16[264,384]{0,1:T(8,128)(2,1)S(1)}, u32[]{:S(2)}, u32[]{:S(2)}) collective-permute-start(bf16[264,384]{0,1:T(8,128)(2,1)S(1)} %pad_maximum_fusion.5), channel_id=1, source_target_pairs={{0,3},{1,0},{2,1},{3,2},{4,7},{5,4},{6,5},{7,6},{8,11},{9,8},{10,9... | collective-permute-start | bytes 608264 | tf_op jit(solution)/shard_map/ppermute | solution.py:18
  73.2 0.7 copy-start.8
  73.2 1.4 copy-start.9
  73.2 3.7 %copy-start.4 = (f32[4,768]{1,0:T(4,128)S(1)}, f32[4,768]{1,0:T(4,128)}, u32[]{:S(2)}) copy-start(f32[4,768]{1,0:T(4,128)} %param.23) | copy-start | bytes 36868
  73.3 3.7 %slice-start.1 = ((f32[4,256]{1,0:T(4,128)}), f32[4,128]{1,0:T(4,128)S(1)}, s32[]{:S(2)}) async-start(f32[4,256]{1,0:T(4,128)} %param.24), calls=%async_computation.5 | async-start | bytes 4096 | tf_op jit(solution)/shard_map/slice | solution.py:152
  73.3 3.8 %copy-start.5 = (f32[4,256]{1,0:T(4,128)S(1)}, f32[4,256]{1,0:T(4,128)}, u32[]{:S(2)}) copy-start(f32[4,256]{1,0:T(4,128)} %param.24) | copy-start | bytes 12292
  73.6 7.3 %collective-permute-start.4 = (bf16[768,1024]{1,0:T(8,128)(2,1)}, bf16[768,1024]{1,0:T(8,128)(2,1)}, u32[]{:S(2)}, u32[]{:S(2)}) collective-permute-start(bf16[768,1024]{1,0:T(8,128)(2,1)} %bitcast.3), channel_id=1, source_target_pairs={{0,4},{4,0},{1,5},{5,1},{2,6},{6,2},{3,7},{7,3},{8,12},{12,8},{9,1... | collective-permute-start | bytes 4718600 | tf_op jit(solution)/shard_map/ppermute | solution.py:18
  80.9 2.6 %copy-start.6 = (f32[12]{0:T(128)S(1)}, f32[12]{0:T(128)}, u32[]{:S(2)}) copy-start(f32[12]{0:T(128)} %param.25) | copy-start | bytes 148
  87.8 30.5 %all-to-all-start.1 = ((bf16[64,16,128]{2,1,0:T(8,128)(2,1)}), bf16[64,16,128]{2,1,0:T(8,128)(2,1)S(1)}, u32[]{:S(2)}, u32[]{:S(2)}) async-start(bf16[64,16,128]{2,1,0:T(8,128)(2,1)} %pad_maximum_fusion.6), calls=%async_computation.1 | async-start | bytes 524288 | tf_op jit(solution)/shard_map/all_to_all | solution.py:179
  118.3 0.7 copy-start.1
  121.0 18.0 %all-to-all-start.2 = ((bf16[64,16,128]{2,1,0:T(8,128)(2,1)}), bf16[64,16,128]{2,1,0:T(8,128)(2,1)S(1)}, u32[]{:S(2)}, u32[]{:S(2)}) async-start(bf16[64,16,128]{2,1,0:T(8,128)(2,1)} %shard_map.137), calls=%async_computation.2 | async-start | bytes 524288 | tf_op jit(solution)/shard_map/all_to_all | solution.py:180
  127.4 13.6 %copy-start.10 = (f32[12]{0:T(128)S(1)}, f32[12]{0:T(128)}, u32[]{:S(2)}) copy-start(f32[12]{0:T(128)} %param.27) | copy-start | bytes 148
  142.0 1.1 copy-start.2
  143.1 3.4 %copy-start.7 = (f32[768]{0:T(1024)S(1)}, f32[768]{0:T(1024)}, u32[]{:S(2)}) copy-start(f32[768]{0:T(1024)} %param.28) | copy-start | bytes 9220
  149.2 7.5 %collective-permute-start.5 = (bf16[264,384]{1,0:T(8,128)(2,1)S(1)}, bf16[264,384]{1,0:T(8,128)(2,1)S(1)}, u32[]{:S(2)}, u32[]{:S(2)}) collective-permute-start(bf16[264,384]{1,0:T(8,128)(2,1)S(1)} %get-tuple-element.32), channel_id=1, source_target_pairs={{0,1},{1,2},{2,3},{3,0},{4,5},{5,6},{6,7},{7,4},{8,9},{9,10},{10,1... | collective-permute-start | bytes 608264 | tf_op jit(solution)/shard_map/ppermute | solution.py:18
  150.2 11.1 %collective-permute-start.6 = (bf16[264,384]{1,0:T(8,128)(2,1)S(1)}, bf16[264,384]{1,0:T(8,128)(2,1)S(1)}, u32[]{:S(2)}, u32[]{:S(2)}) collective-permute-start(bf16[264,384]{1,0:T(8,128)(2,1)S(1)} %get-tuple-element.33), channel_id=1, source_target_pairs={{0,2},{1,3},{2,0},{3,1},{4,6},{5,7},{6,4},{7,5},{8,10},{9,11},{10,... | collective-permute-start | bytes 608264 | tf_op jit(solution)/shard_map/ppermute | solution.py:18
  152.3 9.0 %collective-permute-start.7 = (bf16[264,384]{1,0:T(8,128)(2,1)S(1)}, bf16[264,384]{1,0:T(8,128)(2,1)S(1)}, u32[]{:S(2)}, u32[]{:S(2)}) collective-permute-start(bf16[264,384]{1,0:T(8,128)(2,1)S(1)} %get-tuple-element.34), channel_id=1, source_target_pairs={{0,3},{1,0},{2,1},{3,2},{4,7},{5,4},{6,5},{7,6},{8,11},{9,8},{10,9... | collective-permute-start | bytes 608264 | tf_op jit(solution)/shard_map/ppermute | solution.py:18
Sparse Core Ops, SparseCore 0:
  10.1 89.6 all-gather.1

commit v4 on v3

--- a/solution.py
+++ b/solution.py
@@ -48,23 +48,52 @@
 
 def pack_body(value_ref, shared_ref, step_ref, out_ref):
     inner, half, heads = value_ref.shape[1], shared_ref.shape[1] // 2, step_ref.shape[0]
-    rest = out_ref.shape[2] - inner - half
+    rest = out_ref.shape[1] - inner - half
     step = jnp.pad(step_ref[...].T, ((0, 0), (0, rest - heads)))
-    packed = jnp.concatenate([value_ref[...], shared_ref[:, :half], step], axis=1).astype(BF16)
-    for k in range(out_ref.shape[0]):
-        out_ref[k] = packed
-
-
-def pack_early(value, shared, step, copies):
+    out_ref[:, :inner] = value_ref[...].astype(BF16)
+    out_ref[:, inner : inner + half] = shared_ref[:, :half].astype(BF16)
+    out_ref[:, inner + half :] = step.astype(BF16)
+
+
+def pack_early(value, shared, step):
     rows, inner = value.shape
     width = inner + shared.shape[1] // 2 + step.shape[1]
     width += -width % 128
     return pl.pallas_call(
         pack_body,
-        out_shape=jax.ShapeDtypeStruct((copies, rows, width), BF16),
+        out_shape=jax.ShapeDtypeStruct((rows, width), BF16),
         in_specs=[pl.BlockSpec(memory_space=pltpu.VMEM)] * 3,
         out_specs=pl.BlockSpec(memory_space=pltpu.VMEM),
     )(value, shared, step.T)
+
+
+def project_body(h_ref, *refs):
+    *blocks, out_ref, held = refs
+    depth = blocks[0].shape[0]
+    for i, block in enumerate(blocks):
+        held[i * depth : (i + 1) * depth] = block[...]
+    width = 256
+    for at in range(0, out_ref.shape[1], width):
+        end = min(at + width, out_ref.shape[1])
+        out_ref[:, at:end] = jnp.dot(
+            h_ref[...], held[:, at:end], preferred_element_type=F32
+        ).astype(BF16)
+
+
+def project(h, blocks):
+    depth, width = blocks[0].shape
+    rows, features = h.shape
+    return pl.pallas_call(
+        project_body,
+        out_shape=jax.ShapeDtypeStruct((rows, width), BF16),
+        in_specs=[pl.BlockSpec(memory_space=pltpu.VMEM)] * (1 + len(blocks)),
+        out_specs=pl.BlockSpec(memory_space=pltpu.VMEM),
+        scratch_shapes=[pltpu.VMEM((features, width), BF16)],
+        compiler_params=pltpu.CompilerParams(vmem_limit_bytes=32 << 20),
+        cost_estimate=pl.CostEstimate(
+            flops=2 * rows * features * width, bytes_accessed=2 * features * width, transcendentals=0
+        ),
+    )(h, *blocks)
 
 
 def on_device(
@@ -96,39 +125,55 @@
     tp_at = lax.axis_index("tp")
     seq_at = (x_at * z_size + z_at) * core_size + core_at
 
-    early = pack_early(w_in_value, w_in_shared, w_in_step, x_size * z_size)
-    own = lax.all_to_all(early, SEQ[:2], 0, 0, tiled=True).reshape(-1, early.shape[2])
-
-    late = jnp.concatenate(
-        [w_in_gate.astype(BF16), w_out.T.astype(BF16), w_in_shared[:, state:].astype(BF16)], axis=1
-    )
-    late = lax.all_gather(late, SEQ, axis=0, tiled=True)
-
+    half = z_size // 2
+    z_shifts = [1, 2, z_size - 1]
+    z_offsets = [(d + o) % z_size for d in [0] + z_shifts for o in (0, half)]
+    x_shifts = list(range(1, x_size))
+
+    def z_pair(block):
+        return jnp.concatenate([block, ahead(block, "z", half)], axis=0)
+
+    def z_all(pair):
+        return jnp.concatenate([pair] + [ahead(pair, "z", d) for d in z_shifts], axis=0)
+
+    def x_all(block):
+        return [block] + [ahead(block, "x", d) for d in x_shifts]
+
+    tie = lax.optimization_barrier
+
+    early = pack_early(w_in_value, w_in_shared, w_in_step)
     before = lax.ppermute(
         hidden_in[tokens - EDGE :], SEQ, [(i, i + 1) for i in range(seq_count - 1)]
     )
+    along_z = z_all(z_pair(early))
+    late = jnp.concatenate(
+        [w_in_gate.astype(BF16), w_in_shared[:, state:].astype(BF16), w_out.T.astype(BF16)], axis=1
+    )
+    late_pair = z_pair(late)
     mine = jnp.concatenate([before, hidden_in], axis=0)
-    hidden = jnp.concatenate([mine] + [ahead(mine, "tp", d) for d in range(1, tp_count)], axis=1)
-
-    chips = jnp.arange(x_size * z_size, dtype=jnp.int32) * core_size
+    next_to = [ahead(mine, "tp", d) for d in (1, tp_count - 1)]
+    along_z, next_to, late_pair = tie((along_z, next_to, late_pair))
+    own = x_all(along_z)
+    across = [ahead(mine, "tp", d) for d in range(2, tp_count - 1)]
+    hidden = jnp.concatenate([mine, next_to[0]] + across + [next_to[1]], axis=1)
+
+    chips = jnp.concatenate(
+        [
+            jnp.stack([((x_at - d) % x_size * z_size + (z_at - o) % z_size) for o in z_offsets])
+            for d in range(x_size)
+        ]
+    )
+    stored = jnp.concatenate([chips * core_size + core_at, chips * core_size + 1 - core_at])
     blocks_each = seq_count // tp_count
-
-    def columns_for(stored):
-        model = jnp.take(row_blocks, stored)
-        piece = (tp_at - model // blocks_each) % tp_count
-        place = piece * blocks_each + model % blocks_each
-        cut = hidden.reshape(hidden.shape[0], seq_count, rows_here)
-        return jnp.take(cut, place, axis=1).reshape(hidden.shape[0], -1)
-
-    h_all = columns_for(jnp.arange(seq_count, dtype=jnp.int32))
-    h_own = columns_for(chips + core_at)
-    h_other = columns_for(chips + (1 - core_at))
-    own, h_own, h_other = lax.optimization_barrier((own, h_own, h_other))
-    other = ahead(own, "core", 1)
-    projected = (
-        jnp.dot(h_own, own, preferred_element_type=F32)
-        + jnp.dot(h_other, other, preferred_element_type=F32)
-    ).astype(BF16)
+    model = jnp.take(row_blocks, stored)
+    place = (tp_at - model // blocks_each) % tp_count * blocks_each + model % blocks_each
+    h = jnp.take(hidden.reshape(hidden.shape[0], seq_count, rows_here), place, axis=1)
+    h = h.reshape(hidden.shape[0], -1)
+    own[-1], h = tie((own[-1], h))
+    other = [ahead(block, "core", 1) for block in own]
+    late_pair, own[-1] = tie((late_pair, own[-1]))
+    late_z = z_all(late_pair)
+    projected = project(h, own + other)
     mixed = projected[:, : inner + state]
     raw = projected[EDGE:, inner + state : inner + state + heads]
 
@@ -176,12 +221,19 @@
         ],
         axis=1,
     )
+    sent, late_z = tie((sent, late_z))
     received = lax.all_to_all(sent, SEQ, 0, 0, tiled=True)
+    gate_own = x_all(late_z[:, : inner + state])
+    received, gate_own = tie((received, gate_own))
     carried = lax.all_to_all(scan_states(received, heads), SEQ, 0, 0, tiled=True)
+    gate_other = [ahead(block, "core", 1) for block in gate_own]
+    gate_all = project(h, gate_own + gate_other)
+    out_own = x_all(late_z[:, inner + state :])
+    carried, out_own = tie((carried, out_own))
+    out_other = [ahead(block, "core", 1) for block in out_own]
     carried = carried[:, :heads].transpose(1, 0, 2).reshape(inner, state)
 
-    c_rows = jnp.dot(h_all, late[:, 2 * inner :], preferred_element_type=F32).astype(BF16)
-    c_half = convolve(c_rows, conv_shared[:, state:])
+    c_half = convolve(gate_all[:, inner:], conv_shared[:, state:])
     places = jnp.arange(tokens)
     causal = (places[:, None] >= places[None, :]) & (segments[:, None] == segments[None, :])
     scores = jnp.dot(c_half, b_half.T, preferred_element_type=F32)
@@ -192,7 +244,7 @@
     direct = intra + skip_gain[None, :, None] * values.astype(F32)
     carry_in = jnp.where((segments == prev_seg)[:, None], jnp.exp(cumulative), 0.0)
 
-    gate = jnp.dot(h_all[EDGE:], late[:, :inner], preferred_element_type=F32).astype(BF16)
+    gate = gate_all[EDGE:, :inner]
     inter = lax.dot_general(
         c_half, carried, (((1,), (1,)), ((), ())), preferred_element_type=F32
     ).reshape(tokens, heads, head_dim)
@@ -210,22 +262,36 @@
     squares_lo = (squares - squares_hi.astype(F32)).astype(BF16)
     riding = jnp.concatenate([squares_hi, squares_lo], axis=0)
     riding = jnp.pad(riding, ((0, 6), (0, features - tokens)))
-    terms = lax.dot_general(
-        (gated * norm_gain[None, :]).astype(BF16),
-        late[:, inner : 2 * inner],
-        (((1,), (1,)), ((), ())),
-        preferred_element_type=F32,
-    ).astype(BF16)
+    normed = (gated * norm_gain[None, :]).astype(BF16)
+    terms = jnp.stack(
+        [
+            lax.dot_general(
+                normed,
+                jnp.concatenate(pair, axis=0),
+                (((1,), (1,)), ((), ())),
+                preferred_element_type=F32,
+            ).astype(BF16)
+            for pair in zip(out_own, out_other)
+        ]
+    )
 
     def share(d):
-        cut = lax.dynamic_slice_in_dim(terms, ((tp_at + d) % tp_count) * features, features, 1)
+        cut = lax.dynamic_index_in_dim(terms, (x_at - tp_at - d) % x_size, 0, keepdims=False)
         return jnp.concatenate([cut, riding], axis=0)
 
     parts = [share(0)] + [ahead(share(d), "tp", d) for d in range(1, tp_count)]
     summed = sum(part.astype(F32) for part in parts)
     total = summed[tokens, :tokens] + summed[tokens + 1, :tokens]
     scale = lax.rsqrt(total / (inner * tp_count) + EPSILON)
-    return (summed[:tokens] * scale[:, None]).astype(BF16)
+    result = (summed[:tokens] * scale[:, None]).astype(BF16)
+
+    lane = jnp.arange(features, dtype=jnp.int32)
+    part, rest = lane // (z_size * rows_here), lane % (z_size * rows_here)
+    offset = jnp.take(jnp.array(z_offsets, jnp.int32), rest // rows_here)
+    core_of = jnp.where(part == 0, core_at, 1 - core_at)
+    target = ((z_at - offset) % z_size * core_size + core_of) * rows_here + rest % rows_here
+    moves = (target[:, None] == lane[None, :]).astype(BF16)
+    return jnp.dot(result, moves, preferred_element_type=F32).astype(BF16)
 
 
 def solution(mesh):

time: 170 us -> 177 us (1.041)
  starting transfers between devices: 50.3 us -> 82.6 us
  waiting for transfers between devices: 65.3 us -> 41.7 us
  between operations: 15.3 us -> 1.91 us
  local copies, waits for them, and re-layouts: 8.85 us -> 20.2 us
  matrix products: 14 us -> 10 us
  Pallas kernels: 4.26 us -> 6.83 us
    ppermute x7 -> x35, starting transfers between devices: 9.47 us -> 59.7 us  [ahead(): lax.ppermute(block, axis, [(i, (i + distance) % count) for i in range(cou...]
    ppermute x1, waiting for transfers between devices: 30.1 us -> 0.01 us  [on_device(): lax.ppermute(hidden_in[tokens - EDGE:], SEQ, [(i, i + 1) for i in range(s...]
    ppermute x7 -> x35, waiting for transfers between devices: 14.1 us -> 41.7 us  [ahead(): lax.ppermute(block, axis, [(i, (i + distance) % count) for i in range(cou...]
    all_to_all x1 -> x0, starting transfers between devices: 12.1 us -> none  [on_device(): lax.all_to_all(early, SEQ[:2], 0, 0, tiled=True).reshape(-1, early.shape[2])]
    all_to_all x1, waiting for transfers between devices: 11.6 us -> 0.01 us  [on_device(): lax.all_to_all(scan_states(received, heads), SEQ, 0, 0, tiled=True)]
    all_to_all x1, waiting for transfers between devices: 9.52 us -> 0.01 us  [on_device(): received = lax.all_to_all(sent, SEQ, 0, 0, tiled=True)]
    all_to_all x1, starting transfers between devices: 18.5 us -> 10.3 us  [on_device(): received = lax.all_to_all(sent, SEQ, 0, 0, tiled=True)]
    dot_general x5, matrix products: 11.6 us -> 5.52 us  [the longest x4 4.44 us: on_device(): lax.dot_general(normed, jnp.concatenate(pair, axis=0), (((1,), (1,)), (()...]
  transfers between devices with their start and end apart: 12 -> 38, of which waited for: 7 -> 10; matrix products, arithmetic and copies ran while one was open for 11% -> 17% of each run, Pallas kernels for 3% -> 2%
where the time goes in v4:
time: 177 us; the launch traced here: 176 us
  starting transfers between devices  82.6 us (47%)
  waiting for transfers between devices  41.7 us (24%)
  local copies, waits for them, and re-layouts  20.2 us (11%)
  other arithmetic  12.3 us (7%)
  matrix products  10 us (6%)
  Pallas kernels  6.83 us (4%)
  between operations  1.91 us (1%)
    ppermute x35, starting transfers between devices, ahead(): lax.ppermute(block, axis, [(i, (i + distance) % count) for i in range(cou...  59.7 us
    ppermute x35, waiting for transfers between devices, ahead(): lax.ppermute(block, axis, [(i, (i + distance) % count) for i in range(cou...  41.7 us
    all_to_all x1, starting transfers between devices, on_device(): received = lax.all_to_all(sent, SEQ, 0, 0, tiled=True)  10.3 us
    all_to_all x1, starting transfers between devices, on_device(): lax.all_to_all(scan_states(received, heads), SEQ, 0, 0, tiled=True)  9.13 us
    dot_general x4, matrix products, on_device(): lax.dot_general(normed, jnp.concatenate(pair, axis=0), (((1,), (1,)), (()...  4.44 us
    gather x2, local copies, waits for them, and re-layouts, on_device(): jnp.take(hidden.reshape(hidden.shape[0], seq_count, rows_here), place, ax...  4.01 us
    slice x2, local copies, waits for them, and re-layouts, on_device(): values = convolved[:, :inner].reshape(tokens, heads, head_dim)  3.73 us
  transfers between devices with their start and end apart: 38, of which 10 were waited for; matrix products, arithmetic and copies ran while one was open for 17% of the time, Pallas kernels for 2%

profile of v4, /device:TPU:1, one launch (start us, length us, event | category | flops | bytes accessed | tf_op | source)
XLA Modules:
  0.0 175.5 jit_solution(275159199627877285)
XLA Ops:
  0.0 1.6 shard_map.145
  1.7 7.7 %collective-permute-start = (bf16[24,1024]{1,0:T(8,128)(2,1)}, bf16[24,1024]{1,0:T(8,128)(2,1)S(1)}, u32[]{:S(2)}, u32[]{:S(2)}) collective-permute-start(bf16[24,1024]{1,0:T(8,128)(2,1)} %shard_map.145), channel_id=1, source_target_pairs={{0,32},{8,40},{16,48},{24,56},{32,0},{40,8},{48,16},{56,24},{1,33}... | collective-permute-start | bytes 147464 | tf_op jit(solution)/shard_map/ppermute | solution.py:18
  10.2 3.5 %collective-permute-start.4 = (bf16[8,384]{0,1:T(8,128)(2,1)S(1)}, bf16[8,384]{0,1:T(8,128)(2,1)S(1)}, u32[]{:S(2)}, u32[]{:S(2)}) collective-permute-start(bf16[8,384]{0,1:T(8,128)(2,1)S(1)} %copy.56), channel_id=1, source_target_pairs={{0,4},{4,8},{8,12},{12,16},{16,20},{20,24},{24,28},{28,32},{32,36}... | collective-permute-start | bytes 18440 | tf_op jit(solution)/shard_map/ppermute | solution.py:145
  20.5 1.5 collective-permute-start.6
  22.0 1.6 collective-permute-start.9
  24.6 5.2 %collective-permute-start.2 = (bf16[48,1024]{1,0:T(8,128)(2,1)S(1)}, bf16[48,1024]{1,0:T(8,128)(2,1)S(1)}, u32[]{:S(2)}, u32[]{:S(2)}) collective-permute-start(bf16[48,1024]{1,0:T(8,128)(2,1)S(1)} %pad_maximum_fusion.10), channel_id=1, source_target_pairs={{0,16},{8,24},{16,32},{24,40},{32,48},{40,56},{48,0},{56,8},{1,17}... | collective-permute-start | bytes 294920 | tf_op jit(solution)/shard_map/ppermute | solution.py:18
  30.7 2.1 %collective-permute-done.2 = bf16[48,1024]{1,0:T(8,128)(2,1)S(1)} collective-permute-done((bf16[48,1024]{1,0:T(8,128)(2,1)S(1)}, bf16[48,1024]{1,0:T(8,128)(2,1)S(1)}, u32[]{:S(2)}, u32[]{:S(2)}) %collective-permute-start.2) | collective-permute-done | bytes 98336 | tf_op jit(solution)/shard_map/ppermute | solution.py:18
  35.3 2.5 %collective-permute-start.11 = (bf16[192,1024]{1,0:T(8,128)(2,1)S(1)}, bf16[192,1024]{1,0:T(8,128)(2,1)S(1)}, u32[]{:S(2)}, u32[]{:S(2)}) collective-permute-start(bf16[192,1024]{1,0:T(8,128)(2,1)S(1)} %constant_dynamic-update-slice_fusion.refs_0_), channel_id=1, source_target_pairs={{0,128},{64,192},{128,0},{192,64},{1,129},{65,193},{129,1},{193,65... | collective-permute-start | bytes 1179656 | tf_op jit(solution)/shard_map/ppermute | solution.py:18
  37.9 1.8 %gather_fusion.1 = bf16[64,264,24]{1,2,0:T(8,128)(2,1)} fusion(bf16[264,64,24]{0,2,1:T(8,128)(2,1)S(1)} %bitcast.113, s32[1024]{0:T(1024)S(1)} %pad_clamp_fusion), kind=kCustom, calls=%fused_computation.1 | custom fusion | bytes 1622272 | tf_op jit(solution)/shard_map/jit(_take)/gather | solution.py:170
  39.7 2.2 %copy.58 = bf16[264,1536]{1,0:T(8,128)(2,1)} copy(bf16[264,1536]{0,1:T(8,128)(2,1)} %bitcast.114) | data formatting | bytes 1622016 | tf_op jit(solution)/shard_map/jit(_take)/gather | solution.py:170
  43.2 2.9 %collective-permute-start.18 = (bf16[48,1664]{1,0:T(8,128)(2,1)S(1)}, bf16[48,1664]{1,0:T(8,128)(2,1)S(1)}, u32[]{:S(2)}, u32[]{:S(2)}) collective-permute-start(bf16[48,1664]{1,0:T(8,128)(2,1)S(1)} %pad_maximum_fusion.9), channel_id=1, source_target_pairs={{0,56},{8,0},{16,8},{24,16},{32,24},{40,32},{48,40},{56,48},{1,57}... | collective-permute-start | bytes 479240 | tf_op jit(solution)/shard_map/ppermute | solution.py:18
  49.3 10.7 %collective-permute-start.12 = (bf16[192,1024]{1,0:T(8,128)(2,1)S(1)}, bf16[192,1024]{1,0:T(8,128)(2,1)S(1)}, u32[]{:S(2)}, u32[]{:S(2)}) collective-permute-start(bf16[192,1024]{1,0:T(8,128)(2,1)S(1)} %constant_dynamic-update-slice_fusion.refs_0_), channel_id=1, source_target_pairs={{0,4},{4,0},{1,5},{5,1},{2,6},{6,2},{3,7},{7,3},{8,12},{12,8},{9,1... | collective-permute-start | bytes 1179656 | tf_op jit(solution)/shard_map/ppermute | solution.py:18
  61.9 2.5 %collective-permute-start.14 = (bf16[192,1024]{1,0:T(8,128)(2,1)S(1)}, bf16[192,1024]{1,0:T(8,128)(2,1)S(1)}, u32[]{:S(2)}, u32[]{:S(2)}) collective-permute-start(bf16[192,1024]{1,0:T(8,128)(2,1)S(1)} %collective-permute-done.11.refs_2_), channel_id=1, source_target_pairs={{0,4},{4,0},{1,5},{5,1},{2,6},{6,2},{3,7},{7,3},{8,12},{12,8},{9,1... | collective-permute-start | bytes 1179656 | tf_op jit(solution)/shard_map/ppermute | solution.py:18
  71.4 1.5 multiply_convert_fusion.6
  75.3 10.3 %all-to-all-start = ((bf16[64,16,128]{2,1,0:T(8,128)(2,1)}), bf16[64,16,128]{2,1,0:T(8,128)(2,1)S(1)}, u32[]{:S(2)}, u32[]{:S(2)}) async-start(bf16[64,16,128]{2,1,0:T(8,128)(2,1)} %pad_maximum_fusion.8), calls=%async_computation | async-start | bytes 524288 | tf_op jit(solution)/shard_map/all_to_all | solution.py:225
  85.7 1.5 collective-permute-start.19
  87.2 2.6 %collective-permute-start.20 = (bf16[192,896]{1,0:T(8,128)(2,1)S(1)}, bf16[192,896]{1,0:T(8,128)(2,1)S(1)}, u32[]{:S(2)}, u32[]{:S(2)}) collective-permute-start(bf16[192,896]{1,0:T(8,128)(2,1)S(1)} %slice.162.refs_0_), channel_id=1, source_target_pairs={{0,128},{64,192},{128,0},{192,64},{1,129},{65,193},{129,1},{193,65... | collective-permute-start | bytes 1032200 | tf_op jit(solution)/shard_map/ppermute | solution.py:18
  91.5 7.9 %collective-permute-done.19.refs_1_ = bf16[192,896]{1,0:T(8,128)(2,1)S(1)} collective-permute-done((bf16[192,896]{1,0:T(8,128)(2,1)S(1)}, bf16[192,896]{1,0:T(8,128)(2,1)S(1)}, u32[]{:S(2)}, u32[]{:S(2)}) %collective-permute-start.19) | collective-permute-done | bytes 344096 | tf_op jit(solution)/shard_map/ppermute | solution.py:18
  99.4 8.1 %collective-permute-done.20.refs_2_ = bf16[192,896]{1,0:T(8,128)(2,1)S(1)} collective-permute-done((bf16[192,896]{1,0:T(8,128)(2,1)S(1)}, bf16[192,896]{1,0:T(8,128)(2,1)S(1)}, u32[]{:S(2)}, u32[]{:S(2)}) %collective-permute-start.20) | collective-permute-done | bytes 344096 | tf_op jit(solution)/shard_map/ppermute | solution.py:18
  110.6 1.8 %slice.200 = bf16[256,768]{1,0:T(8,128)(2,1)} slice(bf16[256,896]{1,0:T(8,128)(2,1)} %multiply_convert_fusion.6), slice={[0:256], [0:768]} | slice | bytes 786432 | tf_op jit(solution)/shard_map/slice | solution.py:198
  112.4 1.7 slice.170
  114.1 1.9 %copy.59 = bf16[256,768]{0,1:T(8,128)(2,1)} copy(bf16[256,768]{1,0:T(8,128)(2,1)} %slice.200) | data formatting | bytes 786432 | tf_op jit(solution)/shard_map/slice | solution.py:198
  116.0 1.6 copy.67
  119.0 2.1 %shard_map.148 = bf16[64,16,128]{2,1,0:T(8,128)(2,1)} custom-call(bf16[64,16,128]{2,1,0:T(8,128)(2,1)} %copy-done.4), custom_call_target="tpu_custom_call" | custom-call | flops 262144 | bytes 524288 | tf_op jit(solution)/shard_map/pallas_call | solution.py:38
  121.2 9.1 %all-to-all-start.1 = ((bf16[64,16,128]{2,1,0:T(8,128)(2,1)}), bf16[64,16,128]{2,1,0:T(8,128)(2,1)}, u32[]{:S(2)}, u32[]{:S(2)}) async-start(bf16[64,16,128]{2,1,0:T(8,128)(2,1)} %shard_map.148), calls=%async_computation.1 | async-start | bytes 524288 | tf_op jit(solution)/shard_map/all_to_all | solution.py:228
  130.3 3.1 %collective-permute-start.27 = (bf16[192,768]{1,0:T(8,128)(2,1)}, bf16[192,768]{1,0:T(8,128)(2,1)}, u32[]{:S(2)}, u32[]{:S(2)}) collective-permute-start(bf16[192,768]{1,0:T(8,128)(2,1)} %slice.170), channel_id=1, source_target_pairs={{0,128},{64,192},{128,0},{192,64},{1,129},{65,193},{129,1},{193,65... | collective-permute-start | bytes 884744 | tf_op jit(solution)/shard_map/ppermute | solution.py:18
  135.9 2.1 %shard_map.147 = bf16[264,896]{1,0:T(8,128)(2,1)S(1)} custom-call(bf16[264,1536]{1,0:T(8,128)(2,1)S(1)} %broadcast_select_fusion.h_ref, bf16[192,896]{1,0:T(8,128)(2,1)S(1)} %slice.162.refs_0_, bf16[192,896]{1,0:T(8,128)(2,1)S(1)} %collective-permute-done.19.refs_1_, bf16[192,896]{1,0:T(8,128)(2,1)S(1)} %collective-permute-done.20.refs_2_, ...), custom_call_target="tpu_custom_call" | custom-call | flops 726663168 | bytes 2752512 | tf_op jit(solution)/shard_map/pallas_call | solution.py:86
  140.4 2.7 %collective-permute-done.27 = bf16[192,768]{1,0:T(8,128)(2,1)} collective-permute-done((bf16[192,768]{1,0:T(8,128)(2,1)}, bf16[192,768]{1,0:T(8,128)(2,1)}, u32[]{:S(2)}, u32[]{:S(2)}) %collective-permute-start.27) | collective-permute-done | bytes 294944 | tf_op jit(solution)/shard_map/ppermute | solution.py:18
  143.0 6.6 %collective-permute-done.28 = bf16[192,768]{1,0:T(8,128)(2,1)} collective-permute-done((bf16[192,768]{1,0:T(8,128)(2,1)}, bf16[192,768]{1,0:T(8,128)(2,1)}, u32[]{:S(2)}, u32[]{:S(2)}) %collective-permute-start.28) | collective-permute-done | bytes 294944 | tf_op jit(solution)/shard_map/ppermute | solution.py:18
  159.5 2.6 %collective-permute-start.35 = (bf16[264,384]{1,0:T(8,128)(2,1)S(1)}, bf16[264,384]{1,0:T(8,128)(2,1)S(1)}, u32[]{:S(2)}, u32[]{:S(2)}) collective-permute-start(bf16[264,384]{1,0:T(8,128)(2,1)S(1)} %get-tuple-element.63), channel_id=1, source_target_pairs={{0,3},{1,0},{2,1},{3,2},{4,7},{5,4},{6,5},{7,6},{8,11},{9,8},{10,9... | collective-permute-start | bytes 608264 | tf_op jit(solution)/shard_map/ppermute | solution.py:18
  162.9 7.5 %collective-permute-done.35 = bf16[264,384]{1,0:T(8,128)(2,1)S(1)} collective-permute-done((bf16[264,384]{1,0:T(8,128)(2,1)S(1)}, bf16[264,384]{1,0:T(8,128)(2,1)S(1)}, u32[]{:S(2)}, u32[]{:S(2)}) %collective-permute-start.35) | collective-permute-done | bytes 202784 | tf_op jit(solution)/shard_map/ppermute | solution.py:18
  170.4 4.0 %collective-permute-done.33 = bf16[264,384]{1,0:T(8,128)(2,1)S(1)} collective-permute-done((bf16[264,384]{1,0:T(8,128)(2,1)S(1)}, bf16[264,384]{1,0:T(8,128)(2,1)S(1)}, u32[]{:S(2)}, u32[]{:S(2)}) %collective-permute-start.33) | collective-permute-done | bytes 202784 | tf_op jit(solution)/shard_map/ppermute | solution.py:18
  (195 shorter events, 49.2 us)
Async XLA Ops:
  1.7 21.9 %collective-permute-start = (bf16[24,1024]{1,0:T(8,128)(2,1)}, bf16[24,1024]{1,0:T(8,128)(2,1)S(1)}, u32[]{:S(2)}, u32[]{:S(2)}) collective-permute-start(bf16[24,1024]{1,0:T(8,128)(2,1)} %shard_map.145), channel_id=1, source_target_pairs={{0,32},{8,40},{16,48},{24,56},{32,0},{40,8},{48,16},{56,24},{1,33}... | collective-permute-start | bytes 147464 | tf_op jit(solution)/shard_map/ppermute | solution.py:18
  10.2 8.7 %collective-permute-start.4 = (bf16[8,384]{0,1:T(8,128)(2,1)S(1)}, bf16[8,384]{0,1:T(8,128)(2,1)S(1)}, u32[]{:S(2)}, u32[]{:S(2)}) collective-permute-start(bf16[8,384]{0,1:T(8,128)(2,1)S(1)} %copy.56), channel_id=1, source_target_pairs={{0,4},{4,8},{8,12},{12,16},{16,20},{20,24},{24,28},{28,32},{32,36}... | collective-permute-start | bytes 18440 | tf_op jit(solution)/shard_map/ppermute | solution.py:145
  16.2 8.4 %collective-permute-start.7 = (bf16[24,1664]{1,0:T(8,128)(2,1)S(1)}, bf16[24,1664]{1,0:T(8,128)(2,1)S(1)}, u32[]{:S(2)}, u32[]{:S(2)}) collective-permute-start(bf16[24,1664]{1,0:T(8,128)(2,1)S(1)} %pad_maximum_fusion.11), channel_id=1, source_target_pairs={{0,32},{8,40},{16,48},{24,56},{32,0},{40,8},{48,16},{56,24},{1,33}... | collective-permute-start | bytes 239624 | tf_op jit(solution)/shard_map/ppermute | solution.py:18
  19.1 14.6 %collective-permute-start.5 = (bf16[264,384]{0,1:T(8,128)(2,1)S(1)}, bf16[264,384]{0,1:T(8,128)(2,1)S(1)}, u32[]{:S(2)}, u32[]{:S(2)}) collective-permute-start(bf16[264,384]{0,1:T(8,128)(2,1)S(1)} %pad_maximum_fusion.7), channel_id=1, source_target_pairs={{0,1},{1,2},{2,3},{3,0},{4,5},{5,6},{6,7},{7,4},{8,9},{9,10},{10,1... | collective-permute-start | bytes 608264 | tf_op jit(solution)/shard_map/ppermute | solution.py:18
  20.5 13.3 %collective-permute-start.6 = (bf16[264,384]{0,1:T(8,128)(2,1)S(1)}, bf16[264,384]{0,1:T(8,128)(2,1)S(1)}, u32[]{:S(2)}, u32[]{:S(2)}) collective-permute-start(bf16[264,384]{0,1:T(8,128)(2,1)S(1)} %pad_maximum_fusion.7), channel_id=1, source_target_pairs={{0,3},{1,0},{2,1},{3,2},{4,7},{5,4},{6,5},{7,6},{8,11},{9,8},{10,9... | collective-permute-start | bytes 608264 | tf_op jit(solution)/shard_map/ppermute | solution.py:18
  22.0 15.7 %collective-permute-start.9 = (bf16[264,384]{0,1:T(8,128)(2,1)S(1)}, bf16[264,384]{0,1:T(8,128)(2,1)S(1)}, u32[]{:S(2)}, u32[]{:S(2)}) collective-permute-start(bf16[264,384]{0,1:T(8,128)(2,1)S(1)} %pad_maximum_fusion.7), channel_id=1, source_target_pairs={{0,2},{1,3},{2,0},{3,1},{4,6},{5,7},{6,4},{7,5},{8,10},{9,11},{10,... | collective-permute-start | bytes 608264 | tf_op jit(solution)/shard_map/ppermute | solution.py:18
  23.6 6.3 %collective-permute-start.1 = (bf16[48,1024]{1,0:T(8,128)(2,1)S(1)}, bf16[48,1024]{1,0:T(8,128)(2,1)S(1)}, u32[]{:S(2)}, u32[]{:S(2)}) collective-permute-start(bf16[48,1024]{1,0:T(8,128)(2,1)S(1)} %pad_maximum_fusion.10), channel_id=1, source_target_pairs={{0,8},{8,16},{16,24},{24,32},{32,40},{40,48},{48,56},{56,0},{1,9},... | collective-permute-start | bytes 294920 | tf_op jit(solution)/shard_map/ppermute | solution.py:18
  24.6 8.1 %collective-permute-start.2 = (bf16[48,1024]{1,0:T(8,128)(2,1)S(1)}, bf16[48,1024]{1,0:T(8,128)(2,1)S(1)}, u32[]{:S(2)}, u32[]{:S(2)}) collective-permute-start(bf16[48,1024]{1,0:T(8,128)(2,1)S(1)} %pad_maximum_fusion.10), channel_id=1, source_target_pairs={{0,16},{8,24},{16,32},{24,40},{32,48},{40,56},{48,0},{56,8},{1,17}... | collective-permute-start | bytes 294920 | tf_op jit(solution)/shard_map/ppermute | solution.py:18
  33.7 9.5 %collective-permute-start.8 = (bf16[192,1024]{1,0:T(8,128)(2,1)S(1)}, bf16[192,1024]{1,0:T(8,128)(2,1)S(1)}, u32[]{:S(2)}, u32[]{:S(2)}) collective-permute-start(bf16[192,1024]{1,0:T(8,128)(2,1)S(1)} %constant_dynamic-update-slice_fusion.refs_0_), channel_id=1, source_target_pairs={{0,192},{64,0},{128,64},{192,128},{1,193},{65,1},{129,65},{193,129... | collective-permute-start | bytes 1179656 | tf_op jit(solution)/shard_map/ppermute | solution.py:18
  35.0 25.0 %collective-permute-start.10 = (bf16[192,1024]{1,0:T(8,128)(2,1)S(1)}, bf16[192,1024]{1,0:T(8,128)(2,1)S(1)}, u32[]{:S(2)}, u32[]{:S(2)}) collective-permute-start(bf16[192,1024]{1,0:T(8,128)(2,1)S(1)} %constant_dynamic-update-slice_fusion.refs_0_), channel_id=1, source_target_pairs={{0,64},{64,128},{128,192},{192,0},{1,65},{65,129},{129,193},{193,1... | collective-permute-start | bytes 1179656 | tf_op jit(solution)/shard_map/ppermute | solution.py:18
  35.3 25.0 %collective-permute-start.11 = (bf16[192,1024]{1,0:T(8,128)(2,1)S(1)}, bf16[192,1024]{1,0:T(8,128)(2,1)S(1)}, u32[]{:S(2)}, u32[]{:S(2)}) collective-permute-start(bf16[192,1024]{1,0:T(8,128)(2,1)S(1)} %constant_dynamic-update-slice_fusion.refs_0_), channel_id=1, source_target_pairs={{0,128},{64,192},{128,0},{192,64},{1,129},{65,193},{129,1},{193,65... | collective-permute-start | bytes 1179656 | tf_op jit(solution)/shard_map/ppermute | solution.py:18
  43.2 18.2 %collective-permute-start.18 = (bf16[48,1664]{1,0:T(8,128)(2,1)S(1)}, bf16[48,1664]{1,0:T(8,128)(2,1)S(1)}, u32[]{:S(2)}, u32[]{:S(2)}) collective-permute-start(bf16[48,1664]{1,0:T(8,128)(2,1)S(1)} %pad_maximum_fusion.9), channel_id=1, source_target_pairs={{0,56},{8,0},{16,8},{24,16},{32,24},{40,32},{48,40},{56,48},{1,57}... | collective-permute-start | bytes 479240 | tf_op jit(solution)/shard_map/ppermute | solution.py:18
  46.1 15.8 %collective-permute-start.17 = (bf16[48,1664]{1,0:T(8,128)(2,1)S(1)}, bf16[48,1664]{1,0:T(8,128)(2,1)S(1)}, u32[]{:S(2)}, u32[]{:S(2)}) collective-permute-start(bf16[48,1664]{1,0:T(8,128)(2,1)S(1)} %pad_maximum_fusion.9), channel_id=1, source_target_pairs={{0,16},{8,24},{16,32},{24,40},{32,48},{40,56},{48,0},{56,8},{1,17}... | collective-permute-start | bytes 479240 | tf_op jit(solution)/shard_map/ppermute | solution.py:18
  49.3 18.6 %collective-permute-start.12 = (bf16[192,1024]{1,0:T(8,128)(2,1)S(1)}, bf16[192,1024]{1,0:T(8,128)(2,1)S(1)}, u32[]{:S(2)}, u32[]{:S(2)}) collective-permute-start(bf16[192,1024]{1,0:T(8,128)(2,1)S(1)} %constant_dynamic-update-slice_fusion.refs_0_), channel_id=1, source_target_pairs={{0,4},{4,0},{1,5},{5,1},{2,6},{6,2},{3,7},{7,3},{8,12},{12,8},{9,1... | collective-permute-start | bytes 1179656 | tf_op jit(solution)/shard_map/ppermute | solution.py:18
  60.0 7.9 %collective-permute-start.15 = (bf16[192,1024]{1,0:T(8,128)(2,1)S(1)}, bf16[192,1024]{1,0:T(8,128)(2,1)S(1)}, u32[]{:S(2)}, u32[]{:S(2)}) collective-permute-start(bf16[192,1024]{1,0:T(8,128)(2,1)S(1)} %collective-permute-done.8.refs_3_), channel_id=1, source_target_pairs={{0,4},{4,0},{1,5},{5,1},{2,6},{6,2},{3,7},{7,3},{8,12},{12,8},{9,1... | collective-permute-start | bytes 1179656 | tf_op jit(solution)/shard_map/ppermute | solution.py:18
  60.3 6.7 %collective-permute-start.16 = (bf16[48,1664]{1,0:T(8,128)(2,1)S(1)}, bf16[48,1664]{1,0:T(8,128)(2,1)S(1)}, u32[]{:S(2)}, u32[]{:S(2)}) collective-permute-start(bf16[48,1664]{1,0:T(8,128)(2,1)S(1)} %pad_maximum_fusion.9), channel_id=1, source_target_pairs={{0,8},{8,16},{16,24},{24,32},{32,40},{40,48},{48,56},{56,0},{1,9},... | collective-permute-start | bytes 479240 | tf_op jit(solution)/shard_map/ppermute | solution.py:18
  61.4 6.5 %collective-permute-start.13 = (bf16[192,1024]{1,0:T(8,128)(2,1)S(1)}, bf16[192,1024]{1,0:T(8,128)(2,1)S(1)}, u32[]{:S(2)}, u32[]{:S(2)}) collective-permute-start(bf16[192,1024]{1,0:T(8,128)(2,1)S(1)} %collective-permute-done.10.refs_1_), channel_id=1, source_target_pairs={{0,4},{4,0},{1,5},{5,1},{2,6},{6,2},{3,7},{7,3},{8,12},{12,8},{9,1... | collective-permute-start | bytes 1179656 | tf_op jit(solution)/shard_map/ppermute | solution.py:18
  75.3 32.1 %all-to-all-start = ((bf16[64,16,128]{2,1,0:T(8,128)(2,1)}), bf16[64,16,128]{2,1,0:T(8,128)(2,1)S(1)}, u32[]{:S(2)}, u32[]{:S(2)}) async-start(bf16[64,16,128]{2,1,0:T(8,128)(2,1)} %pad_maximum_fusion.8), calls=%async_computation | async-start | bytes 524288 | tf_op jit(solution)/shard_map/all_to_all | solution.py:225
  85.7 13.7 %collective-permute-start.19 = (bf16[192,896]{1,0:T(8,128)(2,1)S(1)}, bf16[192,896]{1,0:T(8,128)(2,1)S(1)}, u32[]{:S(2)}, u32[]{:S(2)}) collective-permute-start(bf16[192,896]{1,0:T(8,128)(2,1)S(1)} %slice.162.refs_0_), channel_id=1, source_target_pairs={{0,64},{64,128},{128,192},{192,0},{1,65},{65,129},{129,193},{193,1... | collective-permute-start | bytes 1032200 | tf_op jit(solution)/shard_map/ppermute | solution.py:18
  87.2 20.3 %collective-permute-start.20 = (bf16[192,896]{1,0:T(8,128)(2,1)S(1)}, bf16[192,896]{1,0:T(8,128)(2,1)S(1)}, u32[]{:S(2)}, u32[]{:S(2)}) collective-permute-start(bf16[192,896]{1,0:T(8,128)(2,1)S(1)} %slice.162.refs_0_), channel_id=1, source_target_pairs={{0,128},{64,192},{128,0},{192,64},{1,129},{65,193},{129,1},{193,65... | collective-permute-start | bytes 1032200 | tf_op jit(solution)/shard_map/ppermute | solution.py:18
  89.8 17.7 %collective-permute-start.21 = (bf16[192,896]{1,0:T(8,128)(2,1)S(1)}, bf16[192,896]{1,0:T(8,128)(2,1)S(1)}, u32[]{:S(2)}, u32[]{:S(2)}) collective-permute-start(bf16[192,896]{1,0:T(8,128)(2,1)S(1)} %slice.162.refs_0_), channel_id=1, source_target_pairs={{0,192},{64,0},{128,64},{192,128},{1,193},{65,1},{129,65},{193,129... | collective-permute-start | bytes 1032200 | tf_op jit(solution)/shard_map/ppermute | solution.py:18
  107.5 22.8 %collective-permute-start.22 = (bf16[192,896]{1,0:T(8,128)(2,1)S(1)}, bf16[192,896]{1,0:T(8,128)(2,1)S(1)}, u32[]{:S(2)}, u32[]{:S(2)}) collective-permute-start(bf16[192,896]{1,0:T(8,128)(2,1)S(1)} %slice.162.refs_0_), channel_id=1, source_target_pairs={{0,4},{4,0},{1,5},{5,1},{2,6},{6,2},{3,7},{7,3},{8,12},{12,8},{9,1... | collective-permute-start | bytes 1032200 | tf_op jit(solution)/shard_map/ppermute | solution.py:18
  108.7 24.7 %collective-permute-start.23 = (bf16[192,896]{1,0:T(8,128)(2,1)S(1)}, bf16[192,896]{1,0:T(8,128)(2,1)S(1)}, u32[]{:S(2)}, u32[]{:S(2)}) collective-permute-start(bf16[192,896]{1,0:T(8,128)(2,1)S(1)} %collective-permute-done.19.refs_1_), channel_id=1, source_target_pairs={{0,4},{4,0},{1,5},{5,1},{2,6},{6,2},{3,7},{7,3},{8,12},{12,8},{9,1... | collective-permute-start | bytes 1032200 | tf_op jit(solution)/shard_map/ppermute | solution.py:18
  109.3 24.9 %collective-permute-start.24 = (bf16[192,896]{1,0:T(8,128)(2,1)S(1)}, bf16[192,896]{1,0:T(8,128)(2,1)S(1)}, u32[]{:S(2)}, u32[]{:S(2)}) collective-permute-start(bf16[192,896]{1,0:T(8,128)(2,1)S(1)} %collective-permute-done.20.refs_2_), channel_id=1, source_target_pairs={{0,4},{4,0},{1,5},{5,1},{2,6},{6,2},{3,7},{7,3},{8,12},{12,8},{9,1... | collective-permute-start | bytes 1032200 | tf_op jit(solution)/shard_map/ppermute | solution.py:18
  109.3 25.6 %collective-permute-start.25 = (bf16[192,896]{1,0:T(8,128)(2,1)S(1)}, bf16[192,896]{1,0:T(8,128)(2,1)}, u32[]{:S(2)}, u32[]{:S(2)}) collective-permute-start(bf16[192,896]{1,0:T(8,128)(2,1)S(1)} %collective-permute-done.21.refs_3_), channel_id=1, source_target_pairs={{0,4},{4,0},{1,5},{5,1},{2,6},{6,2},{3,7},{7,3},{8,12},{12,8},{9,1... | collective-permute-start | bytes 1032200 | tf_op jit(solution)/shard_map/ppermute | solution.py:18
  118.4 22.0 %collective-permute-start.26 = (bf16[192,768]{1,0:T(8,128)(2,1)}, bf16[192,768]{1,0:T(8,128)(2,1)}, u32[]{:S(2)}, u32[]{:S(2)}) collective-permute-start(bf16[192,768]{1,0:T(8,128)(2,1)} %slice.170), channel_id=1, source_target_pairs={{0,64},{64,128},{128,192},{192,0},{1,65},{65,129},{129,193},{193,1... | collective-permute-start | bytes 884744 | tf_op jit(solution)/shard_map/ppermute | solution.py:18
  121.2 28.4 %all-to-all-start.1 = ((bf16[64,16,128]{2,1,0:T(8,128)(2,1)}), bf16[64,16,128]{2,1,0:T(8,128)(2,1)}, u32[]{:S(2)}, u32[]{:S(2)}) async-start(bf16[64,16,128]{2,1,0:T(8,128)(2,1)} %shard_map.148), calls=%async_computation.1 | async-start | bytes 524288 | tf_op jit(solution)/shard_map/all_to_all | solution.py:228
  130.3 12.7 %collective-permute-start.27 = (bf16[192,768]{1,0:T(8,128)(2,1)}, bf16[192,768]{1,0:T(8,128)(2,1)}, u32[]{:S(2)}, u32[]{:S(2)}) collective-permute-start(bf16[192,768]{1,0:T(8,128)(2,1)} %slice.170), channel_id=1, source_target_pairs={{0,128},{64,192},{128,0},{192,64},{1,129},{65,193},{129,1},{193,65... | collective-permute-start | bytes 884744 | tf_op jit(solution)/shard_map/ppermute | solution.py:18
  133.4 16.2 %collective-permute-start.28 = (bf16[192,768]{1,0:T(8,128)(2,1)}, bf16[192,768]{1,0:T(8,128)(2,1)}, u32[]{:S(2)}, u32[]{:S(2)}) collective-permute-start(bf16[192,768]{1,0:T(8,128)(2,1)} %slice.170), channel_id=1, source_target_pairs={{0,192},{64,0},{128,64},{192,128},{1,193},{65,1},{129,65},{193,129... | collective-permute-start | bytes 884744 | tf_op jit(solution)/shard_map/ppermute | solution.py:18
  159.5 10.9 %collective-permute-start.35 = (bf16[264,384]{1,0:T(8,128)(2,1)S(1)}, bf16[264,384]{1,0:T(8,128)(2,1)S(1)}, u32[]{:S(2)}, u32[]{:S(2)}) collective-permute-start(bf16[264,384]{1,0:T(8,128)(2,1)S(1)} %get-tuple-element.63), channel_id=1, source_target_pairs={{0,3},{1,0},{2,1},{3,2},{4,7},{5,4},{6,5},{7,6},{8,11},{9,8},{10,9... | collective-permute-start | bytes 608264 | tf_op jit(solution)/shard_map/ppermute | solution.py:18
  162.1 8.2 %collective-permute-start.34 = (bf16[264,384]{1,0:T(8,128)(2,1)S(1)}, bf16[264,384]{1,0:T(8,128)(2,1)S(1)}, u32[]{:S(2)}, u32[]{:S(2)}) collective-permute-start(bf16[264,384]{1,0:T(8,128)(2,1)S(1)} %get-tuple-element.62), channel_id=1, source_target_pairs={{0,2},{1,3},{2,0},{3,1},{4,6},{5,7},{6,4},{7,5},{8,10},{9,11},{10,... | collective-permute-start | bytes 608264 | tf_op jit(solution)/shard_map/ppermute | solution.py:18
  162.2 12.2 %collective-permute-start.33 = (bf16[264,384]{1,0:T(8,128)(2,1)S(1)}, bf16[264,384]{1,0:T(8,128)(2,1)S(1)}, u32[]{:S(2)}, u32[]{:S(2)}) collective-permute-start(bf16[264,384]{1,0:T(8,128)(2,1)S(1)} %get-tuple-element.61), channel_id=1, source_target_pairs={{0,1},{1,2},{2,3},{3,0},{4,5},{5,6},{6,7},{7,4},{8,9},{9,10},{10,1... | collective-permute-start | bytes 608264 | tf_op jit(solution)/shard_map/ppermute | solution.py:18
  (34 other events, 315.3 us)

commit v5 on v4

--- a/solution.py
+++ b/solution.py
@@ -46,32 +46,40 @@
     )(sent)
 
 
-def pack_body(value_ref, shared_ref, step_ref, out_ref):
+def pack_body(value_ref, shared_ref, step_ref, gate_ref, out_t_ref, out_ref):
     inner, half, heads = value_ref.shape[1], shared_ref.shape[1] // 2, step_ref.shape[0]
-    rest = out_ref.shape[1] - inner - half
-    step = jnp.pad(step_ref[...].T, ((0, 0), (0, rest - heads)))
-    out_ref[:, :inner] = value_ref[...].astype(BF16)
-    out_ref[:, inner : inner + half] = shared_ref[:, :half].astype(BF16)
-    out_ref[:, inner + half :] = step.astype(BF16)
-
-
-def pack_early(value, shared, step):
+    rest = -heads % 128
+    step = jnp.pad(step_ref[...].T, ((0, 0), (0, rest)))
+    at = 0
+    for piece in (
+        value_ref[...],
+        shared_ref[:, :half],
+        step,
+        gate_ref[...],
+        shared_ref[:, half:],
+        out_t_ref[...],
+    ):
+        out_ref[:, at : at + piece.shape[1]] = piece.astype(BF16)
+        at += piece.shape[1]
+
+
+def pack(value, shared, step, gate, out_t):
     rows, inner = value.shape
-    width = inner + shared.shape[1] // 2 + step.shape[1]
-    width += -width % 128
+    heads = step.shape[1]
+    width = 3 * inner + shared.shape[1] + heads + -heads % 128
     return pl.pallas_call(
         pack_body,
         out_shape=jax.ShapeDtypeStruct((rows, width), BF16),
-        in_specs=[pl.BlockSpec(memory_space=pltpu.VMEM)] * 3,
+        in_specs=[pl.BlockSpec(memory_space=pltpu.VMEM)] * 5,
         out_specs=pl.BlockSpec(memory_space=pltpu.VMEM),
-    )(value, shared, step.T)
+    )(value, shared, step.T, gate, out_t)
 
 
 def project_body(h_ref, *refs):
     *blocks, out_ref, held = refs
     depth = blocks[0].shape[0]
     for i, block in enumerate(blocks):
-        held[i * depth : (i + 1) * depth] = block[...]
+        held[i * depth : (i + 1) * depth] = block[:, : held.shape[1]]
     width = 256
     for at in range(0, out_ref.shape[1], width):
         end = min(at + width, out_ref.shape[1])
@@ -80,8 +88,7 @@
         ).astype(BF16)
 
 
-def project(h, blocks):
-    depth, width = blocks[0].shape
+def project(h, blocks, width):
     rows, features = h.shape
     return pl.pallas_call(
         project_body,
@@ -125,41 +132,28 @@
     tp_at = lax.axis_index("tp")
     seq_at = (x_at * z_size + z_at) * core_size + core_at
 
-    half = z_size // 2
-    z_shifts = [1, 2, z_size - 1]
-    z_offsets = [(d + o) % z_size for d in [0] + z_shifts for o in (0, half)]
     x_shifts = list(range(1, x_size))
-
-    def z_pair(block):
-        return jnp.concatenate([block, ahead(block, "z", half)], axis=0)
-
-    def z_all(pair):
-        return jnp.concatenate([pair] + [ahead(pair, "z", d) for d in z_shifts], axis=0)
 
     def x_all(block):
         return [block] + [ahead(block, "x", d) for d in x_shifts]
 
     tie = lax.optimization_barrier
 
-    early = pack_early(w_in_value, w_in_shared, w_in_step)
     before = lax.ppermute(
         hidden_in[tokens - EDGE :], SEQ, [(i, i + 1) for i in range(seq_count - 1)]
     )
-    along_z = z_all(z_pair(early))
-    late = jnp.concatenate(
-        [w_in_gate.astype(BF16), w_in_shared[:, state:].astype(BF16), w_out.T.astype(BF16)], axis=1
-    )
-    late_pair = z_pair(late)
+    packed = pack(w_in_value, w_in_shared, w_in_step, w_in_gate, w_out.T)
+    packed, before = tie((packed, before))
+    along_z = lax.all_gather(packed, "z", axis=0, tiled=True)
+    early_width = packed.shape[1] - 2 * inner - state
+    own = x_all(along_z[:, :early_width])
+    late = along_z[:, early_width:]
     mine = jnp.concatenate([before, hidden_in], axis=0)
-    next_to = [ahead(mine, "tp", d) for d in (1, tp_count - 1)]
-    along_z, next_to, late_pair = tie((along_z, next_to, late_pair))
-    own = x_all(along_z)
-    across = [ahead(mine, "tp", d) for d in range(2, tp_count - 1)]
-    hidden = jnp.concatenate([mine, next_to[0]] + across + [next_to[1]], axis=1)
+    hidden = jnp.concatenate([mine] + [ahead(mine, "tp", d) for d in range(1, tp_count)], axis=1)
 
     chips = jnp.concatenate(
         [
-            jnp.stack([((x_at - d) % x_size * z_size + (z_at - o) % z_size) for o in z_offsets])
+            (x_at - d) % x_size * z_size + jnp.arange(z_size, dtype=jnp.int32)
             for d in range(x_size)
         ]
     )
@@ -169,11 +163,10 @@
     place = (tp_at - model // blocks_each) % tp_count * blocks_each + model % blocks_each
     h = jnp.take(hidden.reshape(hidden.shape[0], seq_count, rows_here), place, axis=1)
     h = h.reshape(hidden.shape[0], -1)
-    own[-1], h = tie((own[-1], h))
+    own[-1], h, late = tie((own[-1], h, late))
     other = [ahead(block, "core", 1) for block in own]
-    late_pair, own[-1] = tie((late_pair, own[-1]))
-    late_z = z_all(late_pair)
-    projected = project(h, own + other)
+    late_own = x_all(late)
+    projected = project(h, own + other, early_width)
     mixed = projected[:, : inner + state]
     raw = projected[EDGE:, inner + state : inner + state + heads]
 
@@ -221,16 +214,13 @@
         ],
         axis=1,
     )
-    sent, late_z = tie((sent, late_z))
     received = lax.all_to_all(sent, SEQ, 0, 0, tiled=True)
-    gate_own = x_all(late_z[:, : inner + state])
-    received, gate_own = tie((received, gate_own))
+    received, late_own = tie((received, late_own))
     carried = lax.all_to_all(scan_states(received, heads), SEQ, 0, 0, tiled=True)
-    gate_other = [ahead(block, "core", 1) for block in gate_own]
-    gate_all = project(h, gate_own + gate_other)
-    out_own = x_all(late_z[:, inner + state :])
-    carried, out_own = tie((carried, out_own))
-    out_other = [ahead(block, "core", 1) for block in out_own]
+    late_other = [ahead(block, "core", 1) for block in late_own]
+    gate_all = project(h, late_own + late_other, inner + state)
+    out_own = [block[:, inner + state :] for block in late_own]
+    out_other = [block[:, inner + state :] for block in late_other]
     carried = carried[:, :heads].transpose(1, 0, 2).reshape(inner, state)
 
     c_half = convolve(gate_all[:, inner:], conv_shared[:, state:])
@@ -287,9 +277,8 @@
 
     lane = jnp.arange(features, dtype=jnp.int32)
     part, rest = lane // (z_size * rows_here), lane % (z_size * rows_here)
-    offset = jnp.take(jnp.array(z_offsets, jnp.int32), rest // rows_here)
     core_of = jnp.where(part == 0, core_at, 1 - core_at)
-    target = ((z_at - offset) % z_size * core_size + core_of) * rows_here + rest % rows_here
+    target = (rest // rows_here * core_size + core_of) * rows_here + rest % rows_here
     moves = (target[:, None] == lane[None, :]).astype(BF16)
     return jnp.dot(result, moves, preferred_element_type=F32).astype(BF16)
 

time: 177 us -> 155 us (0.88)
  starting transfers between devices: 82.6 us -> 50.5 us
  blocking collectives: 0 us -> 25 us
  waiting for transfers between devices: 41.7 us -> 23.1 us
  local copies, waits for them, and re-layouts: 20.2 us -> 26.1 us
  matrix products: 10 us -> 6.11 us
  Pallas kernels: 6.83 us -> 9.49 us
    ppermute x35 -> x20, starting transfers between devices: 59.7 us -> 30.3 us  [ahead(): lax.ppermute(block, axis, [(i, (i + distance) % count) for i in range(cou...]
    all_gather x0 -> x1, blocking collectives: none -> 25 us  [on_device(): along_z = lax.all_gather(packed, 'z', axis=0, tiled=True)]
    ppermute x35 -> x20, waiting for transfers between devices: 41.7 us -> 17.6 us  [ahead(): lax.ppermute(block, axis, [(i, (i + distance) % count) for i in range(cou...]
    slice x4 -> x11, local copies, waits for them, and re-layouts: 2.62 us -> 8.36 us  [the longest x4 4.18 us: on_device(): out_own = [block[:, inner + state:] for block in late_own]]
    all_to_all x1, waiting for transfers between devices: 0.01 us -> 3.53 us  [on_device(): received = lax.all_to_all(sent, SEQ, 0, 0, tiled=True)]
    dot_general x4, matrix products: 4.44 us -> 1.54 us  [on_device(): lax.dot_general(normed, jnp.concatenate(pair, axis=0), (((1,), (1,)), (()...]
    slice x2, local copies, waits for them, and re-layouts: 3.73 us -> 0.96 us  [on_device(): values = convolved[:, :inner].reshape(tokens, heads, head_dim)]
    pallas_call x2, Pallas kernels: 3.13 us -> 5.74 us  [project(): pl.pallas_call(project_body, out_shape=jax.ShapeDtypeStruct((rows, width)...]
  transfers between devices with their start and end apart: 38 -> 23, of which waited for: 10 -> 6; matrix products, arithmetic and copies ran while one was open for 17% -> 19% of each run, Pallas kernels for 2% -> 3%
where the time goes in v5:
time: 155 us; the launch traced here: 154 us
  starting transfers between devices  50.5 us (33%)
  local copies, waits for them, and re-layouts  26.1 us (17%)
  blocking collectives  25 us (16%)
  waiting for transfers between devices  23.1 us (15%)
  other arithmetic  11.6 us (7%)
  Pallas kernels  9.49 us (6%)
  matrix products  6.11 us (4%)
  between operations  2.08 us (1%)
    ppermute x20, starting transfers between devices, ahead(): lax.ppermute(block, axis, [(i, (i + distance) % count) for i in range(cou...  30.3 us
    all_gather x1, blocking collectives, on_device(): along_z = lax.all_gather(packed, 'z', axis=0, tiled=True)  25 us
    ppermute x20, waiting for transfers between devices, ahead(): lax.ppermute(block, axis, [(i, (i + distance) % count) for i in range(cou...  17.6 us
    all_to_all x1, starting transfers between devices, on_device(): received = lax.all_to_all(sent, SEQ, 0, 0, tiled=True)  8.71 us
    all_to_all x1, starting transfers between devices, on_device(): lax.all_to_all(scan_states(received, heads), SEQ, 0, 0, tiled=True)  6.53 us
    pallas_call x2, Pallas kernels, project(): pl.pallas_call(project_body, out_shape=jax.ShapeDtypeStruct((rows, width)...  5.74 us
    ppermute x1, starting transfers between devices, on_device(): lax.ppermute(hidden_in[tokens - EDGE:], SEQ, [(i, i + 1) for i in range(s...  4.93 us
    slice x4, local copies, waits for them, and re-layouts, on_device(): out_own = [block[:, inner + state:] for block in late_own]  4.18 us
  transfers between devices with their start and end apart: 23, of which 6 were waited for; matrix products, arithmetic and copies ran while one was open for 19% of the time, Pallas kernels for 3%

profile of v5, /device:TPU:1, one launch (start us, length us, event | category | flops | bytes accessed | tf_op | source)
XLA Modules:
  0.0 153.9 jit_solution(17347007413573182437)
XLA Ops:
  0.9 4.9 %collective-permute-start = (bf16[8,384]{0,1:T(8,128)(2,1)S(1)}, bf16[8,384]{0,1:T(8,128)(2,1)S(1)}, u32[]{:S(2)}, u32[]{:S(2)}) collective-permute-start(bf16[8,384]{0,1:T(8,128)(2,1)S(1)} %copy.55), channel_id=1, source_target_pairs={{0,4},{4,8},{8,12},{12,16},{16,20},{20,24},{24,28},{28,32},{32,36}... | collective-permute-start | bytes 18440 | tf_op jit(solution)/shard_map/ppermute | solution.py:142
  8.6 1.7 %shard_map.136 = bf16[24,2688]{1,0:T(8,128)(2,1)} custom-call(f32[24,768]{1,0:T(8,128)} %value_ref.1, f32[24,256]{1,0:T(8,128)} %shared_ref.1, f32[12,24]{1,0:T(8,128)} %bitcast.92, f32[24,768]{1,0:T(8,128)} %gate_ref.1, f32[24,768]{1,0:T(8,128)} %bitcast.91), custom_call_target="tpu_custom_call" | custom-call | tf_op jit(solution)/shard_map/pallas_call | solution.py:70
  10.4 1.4 collective-permute-start.2
  11.8 2.6 %collective-permute-start.3 = (bf16[264,384]{0,1:T(8,128)(2,1)S(1)}, bf16[264,384]{0,1:T(8,128)(2,1)S(1)}, u32[]{:S(2)}, u32[]{:S(2)}) collective-permute-start(bf16[264,384]{0,1:T(8,128)(2,1)S(1)} %pad_maximum_fusion.6), channel_id=1, source_target_pairs={{0,2},{1,3},{2,0},{3,1},{4,6},{5,7},{6,4},{7,5},{8,10},{9,11},{10,... | collective-permute-start | bytes 608264 | tf_op jit(solution)/shard_map/ppermute | solution.py:18
  15.5 25.0 %all_gather.3 = bf16[192,2688]{1,0:T(8,128)(2,1)S(1)} all-gather(bf16[24,2688]{1,0:T(8,128)(2,1)} %shard_map.136), channel_id=1, replica_groups=mesh['x'=4,'z'=8,'core'=2,'tp'=4] {'z'}, dimensions={0}, use_global_device_ids=true | all-gather | bytes 1161216 | tf_op jit(solution)/shard_map/all_gather | solution.py:147
  40.6 2.5 %collective-permute-start.1 = (bf16[192,1024]{1,0:T(8,128)(2,1)S(1)}, bf16[192,1024]{1,0:T(8,128)(2,1)S(1)}, u32[]{:S(2)}, u32[]{:S(2)}) collective-permute-start(bf16[192,1024]{1,0:T(8,128)(2,1)S(1)} %slice.209.refs_0_), channel_id=1, source_target_pairs={{0,192},{64,0},{128,64},{192,128},{1,193},{65,1},{129,65},{193,129... | collective-permute-start | bytes 1179656 | tf_op jit(solution)/shard_map/ppermute | solution.py:18
  43.1 1.7 %collective-permute-start.6 = (bf16[192,1024]{1,0:T(8,128)(2,1)S(1)}, bf16[192,1024]{1,0:T(8,128)(2,1)}, u32[]{:S(2)}, u32[]{:S(2)}) collective-permute-start(bf16[192,1024]{1,0:T(8,128)(2,1)S(1)} %slice.209.refs_0_), channel_id=1, source_target_pairs={{0,128},{64,192},{128,0},{192,64},{1,129},{65,193},{129,1},{193,65... | collective-permute-start | bytes 1179656 | tf_op jit(solution)/shard_map/ppermute | solution.py:18
  44.9 5.7 %collective-permute-start.7 = (bf16[192,1024]{1,0:T(8,128)(2,1)S(1)}, bf16[192,1024]{1,0:T(8,128)(2,1)}, u32[]{:S(2)}, u32[]{:S(2)}) collective-permute-start(bf16[192,1024]{1,0:T(8,128)(2,1)S(1)} %slice.209.refs_0_), channel_id=1, source_target_pairs={{0,4},{4,0},{1,5},{5,1},{2,6},{6,2},{3,7},{7,3},{8,12},{12,8},{9,1... | collective-permute-start | bytes 1179656 | tf_op jit(solution)/shard_map/ppermute | solution.py:18
  50.8 1.8 %gather_fusion.1 = bf16[64,264,24]{1,2,0:T(8,128)(2,1)} fusion(bf16[264,64,24]{0,2,1:T(8,128)(2,1)S(1)} %bitcast.81, s32[1024]{0:T(1024)S(1)} %pad_clamp_fusion), kind=kCustom, calls=%fused_computation.1 | custom fusion | bytes 1622272 | tf_op jit(solution)/shard_map/jit(_take)/gather | solution.py:164
  52.6 2.3 %copy.57 = bf16[264,1536]{1,0:T(8,128)(2,1)} copy(bf16[264,1536]{0,1:T(8,128)(2,1)} %bitcast.82) | data formatting | bytes 1622016 | tf_op jit(solution)/shard_map/jit(_take)/gather | solution.py:164
  54.8 1.3 broadcast_select_fusion.h_ref
  56.1 4.8 %collective-permute-start.10 = (bf16[192,1024]{1,0:T(8,128)(2,1)S(1)}, bf16[192,1024]{1,0:T(8,128)(2,1)}, u32[]{:S(2)}, u32[]{:S(2)}) collective-permute-start(bf16[192,1024]{1,0:T(8,128)(2,1)S(1)} %collective-permute-done.1.refs_3_), channel_id=1, source_target_pairs={{0,4},{4,0},{1,5},{5,1},{2,6},{6,2},{3,7},{7,3},{8,12},{12,8},{9,1... | collective-permute-start | bytes 1179656 | tf_op jit(solution)/shard_map/ppermute | solution.py:18
  60.9 3.4 %collective-permute-start.8 = (bf16[192,1024]{1,0:T(8,128)(2,1)S(1)}, bf16[192,1024]{1,0:T(8,128)(2,1)}, u32[]{:S(2)}, u32[]{:S(2)}) collective-permute-start(bf16[192,1024]{1,0:T(8,128)(2,1)S(1)} %collective-permute-done.5.refs_1_), channel_id=1, source_target_pairs={{0,4},{4,0},{1,5},{5,1},{2,6},{6,2},{3,7},{7,3},{8,12},{12,8},{9,1... | collective-permute-start | bytes 1179656 | tf_op jit(solution)/shard_map/ppermute | solution.py:18
  67.6 1.9 %broadcast_compare_fusion = (pred[256]{0:T(512)(128)(4,1)}, pred[256]{0:T(512)(128)(4,1)}, pred[256]{0:T(512)(128)(4,1)}, pred[256]{0:T(512)(128)(4,1)}, pred[256]{0:T(512)(128)(4,1)}) fusion(s32[]{:T(128)} %bitcast.23, s32[264]{0:T(512)S(1)} %convert_reduce_fusion, s32[]{:T(128)} %bitcast.14), kind=kLoop, calls=%fused_computation.175 | loop fusion | flops 1280 | bytes 5384 | tf_op jit(solution)/shard_map/eq | solution.py:235
  69.5 1.7 %collective-permute-start.12 = (bf16[192,1664]{1,0:T(8,128)(2,1)S(1)}, bf16[192,1664]{1,0:T(8,128)(2,1)}, u32[]{:S(2)}, u32[]{:S(2)}) collective-permute-start(bf16[192,1664]{1,0:T(8,128)(2,1)S(1)} %slice.210.refs_0_), channel_id=1, source_target_pairs={{0,128},{64,192},{128,0},{192,64},{1,129},{65,193},{129,1},{193,65... | collective-permute-start | bytes 1916936 | tf_op jit(solution)/shard_map/ppermute | solution.py:18
  71.2 1.2 collective-permute-start.13
  73.5 2.5 %shard_map.137 = bf16[264,1024]{1,0:T(8,128)(2,1)S(1)} custom-call(bf16[264,1536]{1,0:T(8,128)(2,1)S(1)} %broadcast_select_fusion.h_ref, bf16[192,1024]{1,0:T(8,128)(2,1)S(1)} %slice.209.refs_0_, bf16[192,1024]{1,0:T(8,128)(2,1)S(1)} %copy-done.2, bf16[192,1024]{1,0:T(8,128)(2,1)} %collective-permute-done.6.refs_2_, ...), custom_call_target="tpu_custom_call" | custom-call | flops 830472192 | bytes 3145728 | tf_op jit(solution)/shard_map/pallas_call | solution.py:93
  77.8 1.5 select_multiply_fusion
  80.8 1.2 copy.62
  82.0 1.5 multiply_convert_fusion.6
  85.2 8.7 %all-to-all-start = ((bf16[64,16,128]{2,1,0:T(8,128)(2,1)}), bf16[64,16,128]{2,1,0:T(8,128)(2,1)S(1)}, u32[]{:S(2)}, u32[]{:S(2)}) async-start(bf16[64,16,128]{2,1,0:T(8,128)(2,1)} %pad_maximum_fusion.7), calls=%async_computation | async-start | bytes 524288 | tf_op jit(solution)/shard_map/all_to_all | solution.py:217
  93.9 5.7 %collective-permute-done.12.refs_2_ = bf16[192,1664]{1,0:T(8,128)(2,1)} collective-permute-done((bf16[192,1664]{1,0:T(8,128)(2,1)S(1)}, bf16[192,1664]{1,0:T(8,128)(2,1)}, u32[]{:S(2)}, u32[]{:S(2)}) %collective-permute-start.12) | collective-permute-done | bytes 639008 | tf_op jit(solution)/shard_map/ppermute | solution.py:18
  99.6 2.8 %collective-permute-done.13.refs_3_ = bf16[192,1664]{1,0:T(8,128)(2,1)} collective-permute-done((bf16[192,1664]{1,0:T(8,128)(2,1)S(1)}, bf16[192,1664]{1,0:T(8,128)(2,1)}, u32[]{:S(2)}, u32[]{:S(2)}) %collective-permute-start.13) | collective-permute-done | bytes 639008 | tf_op jit(solution)/shard_map/ppermute | solution.py:18
  102.4 3.5 %all-to-all-done.sent_ref = bf16[64,16,128]{2,1,0:T(8,128)(2,1)S(1)} async-done(((bf16[64,16,128]{2,1,0:T(8,128)(2,1)}), bf16[64,16,128]{2,1,0:T(8,128)(2,1)S(1)}, u32[]{:S(2)}, u32[]{:S(2)}) %all-to-all-start) | async-done | bytes 262176 | tf_op jit(solution)/shard_map/all_to_all | solution.py:217
  106.6 2.0 %shard_map.139 = bf16[64,16,128]{2,1,0:T(8,128)(2,1)} custom-call(bf16[64,16,128]{2,1,0:T(8,128)(2,1)} %copy-done.5), custom_call_target="tpu_custom_call" | custom-call | flops 262144 | bytes 524288 | tf_op jit(solution)/shard_map/pallas_call | solution.py:38
  108.7 6.5 %all-to-all-start.1 = ((bf16[64,16,128]{2,1,0:T(8,128)(2,1)}), bf16[64,16,128]{2,1,0:T(8,128)(2,1)S(1)}, u32[]{:S(2)}, u32[]{:S(2)}) async-start(bf16[64,16,128]{2,1,0:T(8,128)(2,1)} %shard_map.139), calls=%async_computation.1 | async-start | bytes 524288 | tf_op jit(solution)/shard_map/all_to_all | solution.py:219
  117.8 1.6 %copy.66 = f32[12,256]{1,0:T(8,128)} copy(f32[12,256]{0,1:T(8,128)} %get-tuple-element.38) | data formatting | bytes 24576 | tf_op jit(solution)/shard_map/transpose | solution.py:232
  122.6 1.7 %slice.196 = bf16[192,768]{1,0:T(8,128)(2,1)} slice(bf16[192,1664]{1,0:T(8,128)(2,1)} %collective-permute-done.12.refs_2_), slice={[0:192], [896:1664]} | slice | bytes 589824 | tf_op jit(solution)/shard_map/slice | solution.py:222
  125.3 1.9 %all-to-all-done.1 = bf16[64,16,128]{2,1,0:T(8,128)(2,1)S(1)} async-done(((bf16[64,16,128]{2,1,0:T(8,128)(2,1)}), bf16[64,16,128]{2,1,0:T(8,128)(2,1)S(1)}, u32[]{:S(2)}, u32[]{:S(2)}) %all-to-all-start.1) | async-done | bytes 262176 | tf_op jit(solution)/shard_map/all_to_all | solution.py:219
  127.4 3.2 %shard_map.138 = bf16[264,896]{1,0:T(8,128)(2,1)S(1)} custom-call(bf16[264,1536]{1,0:T(8,128)(2,1)S(1)} %broadcast_select_fusion.h_ref, bf16[192,1664]{1,0:T(8,128)(2,1)S(1)} %slice.210.refs_0_, bf16[192,1664]{1,0:T(8,128)(2,1)S(1)} %collective-permute-done.11.refs_1_, bf16[192,1664]{1,0:T(8,128)(2,1)} %collective-permute-done.12.refs_2_, ...), custom_call_target="tpu_custom_call" | custom-call | flops 726663168 | bytes 2752512 | tf_op jit(solution)/shard_map/pallas_call | solution.py:93
  141.9 1.6 %collective-permute-start.20 = (bf16[264,384]{1,0:T(8,128)(2,1)S(1)}, bf16[264,384]{1,0:T(8,128)(2,1)S(1)}, u32[]{:S(2)}, u32[]{:S(2)}) collective-permute-start(bf16[264,384]{1,0:T(8,128)(2,1)S(1)} %get-tuple-element.45), channel_id=1, source_target_pairs={{0,3},{1,0},{2,1},{3,2},{4,7},{5,4},{6,5},{7,6},{8,11},{9,8},{10,9... | collective-permute-start | bytes 608264 | tf_op jit(solution)/shard_map/ppermute | solution.py:18
  143.6 8.8 %collective-permute-done.18 = bf16[264,384]{1,0:T(8,128)(2,1)S(1)} collective-permute-done((bf16[264,384]{1,0:T(8,128)(2,1)S(1)}, bf16[264,384]{1,0:T(8,128)(2,1)S(1)}, u32[]{:S(2)}, u32[]{:S(2)}) %collective-permute-start.18) | collective-permute-done | bytes 202784 | tf_op jit(solution)/shard_map/ppermute | solution.py:18
  (167 shorter events, 33.1 us)
Async XLA Ops:
  0.0 6.1 %copy-start = (s32[64]{0:T(128)S(1)}, s32[64]{0:T(128)}, u32[]{:S(2)}) copy-start(s32[64]{0:T(128)} %param.27) | copy-start | bytes 772
  0.0 8.4 %copy-start.26 = (s32[8]{0:T(128)S(1)}, s32[8]{0:T(128)}, u32[]{:S(2)}) copy-start(s32[8]{0:T(128)} %param.26) | copy-start | bytes 100
  0.9 9.4 %collective-permute-start = (bf16[8,384]{0,1:T(8,128)(2,1)S(1)}, bf16[8,384]{0,1:T(8,128)(2,1)S(1)}, u32[]{:S(2)}, u32[]{:S(2)}) collective-permute-start(bf16[8,384]{0,1:T(8,128)(2,1)S(1)} %copy.55), channel_id=1, source_target_pairs={{0,4},{4,8},{8,12},{12,16},{16,20},{20,24},{24,28},{28,32},{32,36}... | collective-permute-start | bytes 18440 | tf_op jit(solution)/shard_map/ppermute | solution.py:142
  10.4 32.7 %collective-permute-start.2 = (bf16[264,384]{0,1:T(8,128)(2,1)S(1)}, bf16[264,384]{0,1:T(8,128)(2,1)S(1)}, u32[]{:S(2)}, u32[]{:S(2)}) collective-permute-start(bf16[264,384]{0,1:T(8,128)(2,1)S(1)} %pad_maximum_fusion.6), channel_id=1, source_target_pairs={{0,1},{1,2},{2,3},{3,0},{4,5},{5,6},{6,7},{7,4},{8,9},{9,10},{10,1... | collective-permute-start | bytes 608264 | tf_op jit(solution)/shard_map/ppermute | solution.py:18
  11.8 33.0 %collective-permute-start.3 = (bf16[264,384]{0,1:T(8,128)(2,1)S(1)}, bf16[264,384]{0,1:T(8,128)(2,1)S(1)}, u32[]{:S(2)}, u32[]{:S(2)}) collective-permute-start(bf16[264,384]{0,1:T(8,128)(2,1)S(1)} %pad_maximum_fusion.6), channel_id=1, source_target_pairs={{0,2},{1,3},{2,0},{3,1},{4,6},{5,7},{6,4},{7,5},{8,10},{9,11},{10,... | collective-permute-start | bytes 608264 | tf_op jit(solution)/shard_map/ppermute | solution.py:18
  14.4 36.2 %collective-permute-start.4 = (bf16[264,384]{0,1:T(8,128)(2,1)S(1)}, bf16[264,384]{0,1:T(8,128)(2,1)S(1)}, u32[]{:S(2)}, u32[]{:S(2)}) collective-permute-start(bf16[264,384]{0,1:T(8,128)(2,1)S(1)} %pad_maximum_fusion.6), channel_id=1, source_target_pairs={{0,3},{1,0},{2,1},{3,2},{4,7},{5,4},{6,5},{7,6},{8,11},{9,8},{10,9... | collective-permute-start | bytes 608264 | tf_op jit(solution)/shard_map/ppermute | solution.py:18
  40.6 15.6 %collective-permute-start.1 = (bf16[192,1024]{1,0:T(8,128)(2,1)S(1)}, bf16[192,1024]{1,0:T(8,128)(2,1)S(1)}, u32[]{:S(2)}, u32[]{:S(2)}) collective-permute-start(bf16[192,1024]{1,0:T(8,128)(2,1)S(1)} %slice.209.refs_0_), channel_id=1, source_target_pairs={{0,192},{64,0},{128,64},{192,128},{1,193},{65,1},{129,65},{193,129... | collective-permute-start | bytes 1179656 | tf_op jit(solution)/shard_map/ppermute | solution.py:18
  43.1 17.8 %collective-permute-start.5 = (bf16[192,1024]{1,0:T(8,128)(2,1)S(1)}, bf16[192,1024]{1,0:T(8,128)(2,1)S(1)}, u32[]{:S(2)}, u32[]{:S(2)}) collective-permute-start(bf16[192,1024]{1,0:T(8,128)(2,1)S(1)} %slice.209.refs_0_), channel_id=1, source_target_pairs={{0,64},{64,128},{128,192},{192,0},{1,65},{65,129},{129,193},{193,1... | collective-permute-start | bytes 1179656 | tf_op jit(solution)/shard_map/ppermute | solution.py:18
  43.1 21.9 %collective-permute-start.6 = (bf16[192,1024]{1,0:T(8,128)(2,1)S(1)}, bf16[192,1024]{1,0:T(8,128)(2,1)}, u32[]{:S(2)}, u32[]{:S(2)}) collective-permute-start(bf16[192,1024]{1,0:T(8,128)(2,1)S(1)} %slice.209.refs_0_), channel_id=1, source_target_pairs={{0,128},{64,192},{128,0},{192,64},{1,129},{65,193},{129,1},{193,65... | collective-permute-start | bytes 1179656 | tf_op jit(solution)/shard_map/ppermute | solution.py:18
  44.9 24.7 %collective-permute-start.7 = (bf16[192,1024]{1,0:T(8,128)(2,1)S(1)}, bf16[192,1024]{1,0:T(8,128)(2,1)}, u32[]{:S(2)}, u32[]{:S(2)}) collective-permute-start(bf16[192,1024]{1,0:T(8,128)(2,1)S(1)} %slice.209.refs_0_), channel_id=1, source_target_pairs={{0,4},{4,0},{1,5},{5,1},{2,6},{6,2},{3,7},{7,3},{8,12},{12,8},{9,1... | collective-permute-start | bytes 1179656 | tf_op jit(solution)/shard_map/ppermute | solution.py:18
  54.8 10.3 %copy-start.27 = (f32[12]{0:T(128)S(1)}, f32[12]{0:T(128)}, u32[]{:S(2)}) copy-start(f32[12]{0:T(128)} %param.22) | copy-start | bytes 148
  54.8 12.1 %copy-start.14 = (f32[4,768]{1,0:T(4,128)S(1)}, f32[4,768]{1,0:T(4,128)}, u32[]{:S(2)}) copy-start(f32[4,768]{1,0:T(4,128)} %param.19) | copy-start | bytes 36868
  54.8 12.1 %slice-start = ((f32[4,256]{1,0:T(4,128)}), f32[4,128]{1,0:T(4,128)S(1)}, s32[]{:S(2)}) async-start(f32[4,256]{1,0:T(4,128)} %param.20), calls=%async_computation.2 | async-start | bytes 4096 | tf_op jit(solution)/shard_map/slice | solution.py:190
  56.1 15.1 %collective-permute-start.10 = (bf16[192,1024]{1,0:T(8,128)(2,1)S(1)}, bf16[192,1024]{1,0:T(8,128)(2,1)}, u32[]{:S(2)}, u32[]{:S(2)}) collective-permute-start(bf16[192,1024]{1,0:T(8,128)(2,1)S(1)} %collective-permute-done.1.refs_3_), channel_id=1, source_target_pairs={{0,4},{4,0},{1,5},{5,1},{2,6},{6,2},{3,7},{7,3},{8,12},{12,8},{9,1... | collective-permute-start | bytes 1179656 | tf_op jit(solution)/shard_map/ppermute | solution.py:18
  60.9 11.6 %collective-permute-start.8 = (bf16[192,1024]{1,0:T(8,128)(2,1)S(1)}, bf16[192,1024]{1,0:T(8,128)(2,1)}, u32[]{:S(2)}, u32[]{:S(2)}) collective-permute-start(bf16[192,1024]{1,0:T(8,128)(2,1)S(1)} %collective-permute-done.5.refs_1_), channel_id=1, source_target_pairs={{0,4},{4,0},{1,5},{5,1},{2,6},{6,2},{3,7},{7,3},{8,12},{12,8},{9,1... | collective-permute-start | bytes 1179656 | tf_op jit(solution)/shard_map/ppermute | solution.py:18
  65.0 7.5 %collective-permute-start.9 = (bf16[192,1024]{1,0:T(8,128)(2,1)}, bf16[192,1024]{1,0:T(8,128)(2,1)}, u32[]{:S(2)}, u32[]{:S(2)}) collective-permute-start(bf16[192,1024]{1,0:T(8,128)(2,1)} %collective-permute-done.6.refs_2_), channel_id=1, source_target_pairs={{0,4},{4,0},{1,5},{5,1},{2,6},{6,2},{3,7},{7,3},{8,12},{12,8},{9,1... | collective-permute-start | bytes 1179656 | tf_op jit(solution)/shard_map/ppermute | solution.py:18
  67.6 8.4 %copy-start.20 = (f32[12]{0:T(128)S(1)}, f32[12]{0:T(128)}, u32[]{:S(2)}) copy-start(f32[12]{0:T(128)} %param.21) | copy-start | bytes 148
  69.5 24.4 %collective-permute-start.11 = (bf16[192,1664]{1,0:T(8,128)(2,1)S(1)}, bf16[192,1664]{1,0:T(8,128)(2,1)S(1)}, u32[]{:S(2)}, u32[]{:S(2)}) collective-permute-start(bf16[192,1664]{1,0:T(8,128)(2,1)S(1)} %slice.210.refs_0_), channel_id=1, source_target_pairs={{0,64},{64,128},{128,192},{192,0},{1,65},{65,129},{129,193},{193,1... | collective-permute-start | bytes 1916936 | tf_op jit(solution)/shard_map/ppermute | solution.py:18
  69.5 30.1 %collective-permute-start.12 = (bf16[192,1664]{1,0:T(8,128)(2,1)S(1)}, bf16[192,1664]{1,0:T(8,128)(2,1)}, u32[]{:S(2)}, u32[]{:S(2)}) collective-permute-start(bf16[192,1664]{1,0:T(8,128)(2,1)S(1)} %slice.210.refs_0_), channel_id=1, source_target_pairs={{0,128},{64,192},{128,0},{192,64},{1,129},{65,193},{129,1},{193,65... | collective-permute-start | bytes 1916936 | tf_op jit(solution)/shard_map/ppermute | solution.py:18
  71.2 31.2 %collective-permute-start.13 = (bf16[192,1664]{1,0:T(8,128)(2,1)S(1)}, bf16[192,1664]{1,0:T(8,128)(2,1)}, u32[]{:S(2)}, u32[]{:S(2)}) collective-permute-start(bf16[192,1664]{1,0:T(8,128)(2,1)S(1)} %slice.210.refs_0_), channel_id=1, source_target_pairs={{0,192},{64,0},{128,64},{192,128},{1,193},{65,1},{129,65},{193,129... | collective-permute-start | bytes 1916936 | tf_op jit(solution)/shard_map/ppermute | solution.py:18
  83.5 34.3 %copy-start.3 = (bf16[256,896]{1,0:T(8,128)(2,1)}, bf16[256,896]{1,0:T(8,128)(2,1)S(1)}, u32[]{:S(2)}) copy-start(bf16[256,896]{1,0:T(8,128)(2,1)S(1)} %multiply_convert_fusion.6) | copy-start | bytes 1376260
  84.4 32.1 %copy-start.15 = (f32[4,256]{1,0:T(4,128)S(1)}, f32[4,256]{1,0:T(4,128)}, u32[]{:S(2)}) copy-start(f32[4,256]{1,0:T(4,128)} %param.20) | copy-start | bytes 12292
  85.2 20.7 %all-to-all-start = ((bf16[64,16,128]{2,1,0:T(8,128)(2,1)}), bf16[64,16,128]{2,1,0:T(8,128)(2,1)S(1)}, u32[]{:S(2)}, u32[]{:S(2)}) async-start(bf16[64,16,128]{2,1,0:T(8,128)(2,1)} %pad_maximum_fusion.7), calls=%async_computation | async-start | bytes 524288 | tf_op jit(solution)/shard_map/all_to_all | solution.py:217
  108.7 12.3 %copy-start.6 = (f32[256,12]{1,0:T(8,128)S(1)}, f32[256,12]{1,0:T(8,128)}, u32[]{:S(2)}) copy-start(f32[256,12]{1,0:T(8,128)} %get-tuple-element.39) | copy-start | bytes 36868
  108.7 18.5 %all-to-all-start.1 = ((bf16[64,16,128]{2,1,0:T(8,128)(2,1)}), bf16[64,16,128]{2,1,0:T(8,128)(2,1)S(1)}, u32[]{:S(2)}, u32[]{:S(2)}) async-start(bf16[64,16,128]{2,1,0:T(8,128)(2,1)} %shard_map.139), calls=%async_computation.1 | async-start | bytes 524288 | tf_op jit(solution)/shard_map/all_to_all | solution.py:219
  115.3 12.0 %collective-permute-start.14 = (bf16[192,1664]{1,0:T(8,128)(2,1)S(1)}, bf16[192,1664]{1,0:T(8,128)(2,1)}, u32[]{:S(2)}, u32[]{:S(2)}) collective-permute-start(bf16[192,1664]{1,0:T(8,128)(2,1)S(1)} %slice.210.refs_0_), channel_id=1, source_target_pairs={{0,4},{4,0},{1,5},{5,1},{2,6},{6,2},{3,7},{7,3},{8,12},{12,8},{9,1... | collective-permute-start | bytes 1916936 | tf_op jit(solution)/shard_map/ppermute | solution.py:18
  115.8 11.5 %collective-permute-start.15 = (bf16[192,1664]{1,0:T(8,128)(2,1)S(1)}, bf16[192,1664]{1,0:T(8,128)(2,1)}, u32[]{:S(2)}, u32[]{:S(2)}) collective-permute-start(bf16[192,1664]{1,0:T(8,128)(2,1)S(1)} %collective-permute-done.11.refs_1_), channel_id=1, source_target_pairs={{0,4},{4,0},{1,5},{5,1},{2,6},{6,2},{3,7},{7,3},{8,12},{12,8},{9,1... | collective-permute-start | bytes 1916936 | tf_op jit(solution)/shard_map/ppermute | solution.py:18
  115.9 11.4 %collective-permute-start.16 = (bf16[192,1664]{1,0:T(8,128)(2,1)}, bf16[192,1664]{1,0:T(8,128)(2,1)}, u32[]{:S(2)}, u32[]{:S(2)}) collective-permute-start(bf16[192,1664]{1,0:T(8,128)(2,1)} %collective-permute-done.12.refs_2_), channel_id=1, source_target_pairs={{0,4},{4,0},{1,5},{5,1},{2,6},{6,2},{3,7},{7,3},{8,12},{12,8},{9,1... | collective-permute-start | bytes 1916936 | tf_op jit(solution)/shard_map/ppermute | solution.py:18
  116.3 11.0 %collective-permute-start.17 = (bf16[192,1664]{1,0:T(8,128)(2,1)}, bf16[192,1664]{1,0:T(8,128)(2,1)}, u32[]{:S(2)}, u32[]{:S(2)}) collective-permute-start(bf16[192,1664]{1,0:T(8,128)(2,1)} %collective-permute-done.13.refs_3_), channel_id=1, source_target_pairs={{0,4},{4,0},{1,5},{5,1},{2,6},{6,2},{3,7},{7,3},{8,12},{12,8},{9,1... | collective-permute-start | bytes 1916936 | tf_op jit(solution)/shard_map/ppermute | solution.py:18
  140.6 11.8 %collective-permute-start.18 = (bf16[264,384]{1,0:T(8,128)(2,1)S(1)}, bf16[264,384]{1,0:T(8,128)(2,1)S(1)}, u32[]{:S(2)}, u32[]{:S(2)}) collective-permute-start(bf16[264,384]{1,0:T(8,128)(2,1)S(1)} %get-tuple-element.43), channel_id=1, source_target_pairs={{0,1},{1,2},{2,3},{3,0},{4,5},{5,6},{6,7},{7,4},{8,9},{9,10},{10,1... | collective-permute-start | bytes 608264 | tf_op jit(solution)/shard_map/ppermute | solution.py:18
  141.1 11.3 %collective-permute-start.19 = (bf16[264,384]{1,0:T(8,128)(2,1)S(1)}, bf16[264,384]{1,0:T(8,128)(2,1)S(1)}, u32[]{:S(2)}, u32[]{:S(2)}) collective-permute-start(bf16[264,384]{1,0:T(8,128)(2,1)S(1)} %get-tuple-element.44), channel_id=1, source_target_pairs={{0,2},{1,3},{2,0},{3,1},{4,6},{5,7},{6,4},{7,5},{8,10},{9,11},{10,... | collective-permute-start | bytes 608264 | tf_op jit(solution)/shard_map/ppermute | solution.py:18
  141.9 10.8 %collective-permute-start.20 = (bf16[264,384]{1,0:T(8,128)(2,1)S(1)}, bf16[264,384]{1,0:T(8,128)(2,1)S(1)}, u32[]{:S(2)}, u32[]{:S(2)}) collective-permute-start(bf16[264,384]{1,0:T(8,128)(2,1)S(1)} %get-tuple-element.45), channel_id=1, source_target_pairs={{0,3},{1,0},{2,1},{3,2},{4,7},{5,4},{6,5},{7,6},{8,11},{9,8},{10,9... | collective-permute-start | bytes 608264 | tf_op jit(solution)/shard_map/ppermute | solution.py:18
  (21 other events, 53.6 us)

commit v6 on v5

v6 whole, which is shorter than its diff:
```python
import functools

import jax
import jax.numpy as jnp
from jax import lax
from jax.experimental import pallas as pl
from jax.experimental.pallas import tpu as pltpu
from jax.sharding import Mesh, PartitionSpec as P

EPSILON = 1e-05
EDGE = 8
LINES = 16
SEQ = ("x", "z", "core")
SIZES = (4, 8, 2)
BF16 = jnp.bfloat16
F32 = jnp.float32


def ahead(block, axis, distance):
    count = lax.axis_size(axis)
    return lax.ppermute(block, axis, [(i, (i + distance) % count) for i in range(count)])


def pack_body(value_ref, shared_ref, step_ref, gate_ref, out_t_ref, out_ref):
    inner, half, heads = value_ref.shape[1], shared_ref.shape[1] // 2, step_ref.shape[0]
    rest = -heads % 128
    step = jnp.pad(step_ref[...].T, ((0, 0), (0, rest)))
    at = 0
    for piece in (
        value_ref[...],
        shared_ref[:, :half],
        step,
        gate_ref[...],
        shared_ref[:, half:],
        out_t_ref[...],
    ):
        out_ref[:, at : at + piece.shape[1]] = piece.astype(BF16)
        at += piece.shape[1]


def pack(value, shared, step, gate, out_t):
    rows, inner = value.shape
    heads = step.shape[1]
    width = 3 * inner + shared.shape[1] + heads + -heads % 128
    return pl.pallas_call(
        pack_body,
        out_shape=jax.ShapeDtypeStruct((rows, width), BF16),
        in_specs=[pl.BlockSpec(memory_space=pltpu.VMEM)] * 5,
        out_specs=pl.BlockSpec(memory_space=pltpu.VMEM),
    )(value, shared, step.T, gate, out_t)


def call(body, shapes, args, scalars=0, scratch=(), flops=0):
    smem, vmem = pl.BlockSpec(memory_space=pltpu.SMEM), pl.BlockSpec(memory_space=pltpu.VMEM)
    moved = sum(x.size * x.dtype.itemsize for x in args)
    return pl.pallas_call(
        body,
        out_shape=[jax.ShapeDtypeStruct(shape, kind) for shape, kind in shapes],
        in_specs=[smem] * scalars + [vmem] * (len(args) - scalars),
        out_specs=[vmem] * len(shapes),
        scratch_shapes=[pltpu.VMEM(shape, kind) for shape, kind in scratch],
        compiler_params=pltpu.CompilerParams(vmem_limit_bytes=44 << 20),
        cost_estimate=pl.CostEstimate(flops=flops, bytes_accessed=moved, transcendentals=0),
    )(*args)


def dot(a, b, **kw):
    return jnp.dot(a, b, preferred_element_type=F32, **kw)


def iota(shape, dim):
    return lax.broadcasted_iota(jnp.int32, shape, dim)


def one_hot(rows, columns, width, wrap):
    return ((iota((rows, columns), 0) & (wrap - 1)) == iota((rows, columns), 1) // width).astype(BF16)


def spread(x, head_of):
    hi = x.astype(BF16)
    return dot(hi, head_of) + dot((x - hi.astype(F32)).astype(BF16), head_of)


def prompt_start(ends_ref, positions):
    start = jnp.zeros_like(positions)
    for i in range(ends_ref.shape[0]):
        start = jnp.maximum(start, jnp.where(positions >= ends_ref[i], ends_ref[i], 0))
    return start


def silu(x):
    return x / (1.0 + jnp.exp(-x))


def convolve(rows_ref, at, taps, positions, start):
    tokens, width = positions.shape[0], taps.shape[0]
    total = jnp.zeros(positions.shape, F32)
    for k in range(width):
        back = width - 1 - k
        rows = rows_ref[EDGE - back : EDGE - back + tokens, at : at + positions.shape[1]]
        total = total + jnp.where(positions - back >= start, taps[k : k + 1] * rows, 0.0)
    return silu(total).astype(BF16)


def gather_blocks(blocks, held):
    depth = blocks[0].shape[0]
    for i, block in enumerate(blocks):
        held[i * depth : (i + 1) * depth] = block[:, : held.shape[1]]


def early_body(head_dim, first_ref, ends_ref, h_ref, *refs):
    *blocks, conv_value, conv_shared, bias, a_log = refs[:-8]
    x_ref, b_ref, dt_ref, cum_ref, sent_ref, held, rows, lines = refs[-8:]
    tokens, inner = x_ref.shape
    gather_blocks(blocks, held)
    for at in range(0, held.shape[1], 256):
        rows[:, at : at + 256] = dot(h_ref[...], held[:, at : at + 256]).astype(BF16).astype(F32)
    first = first_ref[0]
    positions = first + iota((tokens, 128), 0)
    start = prompt_start(ends_ref, positions)
    last_start = prompt_start(ends_ref, first + tokens - 1)
    for at in range(0, inner, 128):
        x_ref[:, at : at + 128] = convolve(
            rows, at, conv_value[:, at : at + 128], positions, start
        )
    b_half = convolve(rows, inner, conv_shared[:, :128], positions, start)
    b_ref[...] = b_half
    raw = rows[EDGE:, inner + 128 :] + bias[...]
    dt = jnp.maximum(raw, 0.0) + jnp.log1p(jnp.exp(-jnp.abs(raw)))
    below = (iota((tokens, tokens), 0) >= iota((tokens, tokens), 1)).astype(F32)
    cum = dot(below, -dt * jnp.exp(a_log[...]), precision=lax.Precision.HIGHEST)
    dt_ref[...] = dt
    cum_ref[...] = cum
    last = cum[tokens - 1 :]
    tail = jnp.where(positions >= last_start, jnp.exp(last - cum), 0.0) * dt
    head_of = one_hot(128, inner, head_dim, 128)
    weighted = (spread(tail, head_of) * x_ref[...].astype(F32)).astype(BF16)
    fresh = dot(b_half.astype(F32).T.astype(BF16), weighted)
    lines[...] = jnp.zeros_like(lines)
    count = lines.shape[0] // LINES
    line = 0
    for row in range(0, fresh.shape[0], count):
        for at in range(0, inner, 128):
            lines[pl.ds(line, count, stride=LINES), :] = fresh[row : row + count, at : at + 128]
            line += 1
    keep = jnp.where(last_start < first, jnp.exp(last), 0.0)
    keep = jnp.broadcast_to(keep, (8, 128))
    keep_hi = keep.astype(BF16).astype(F32)
    keep_lo = pltpu.roll(keep - keep_hi, 64, axis=1)
    both = jnp.where(iota((8, 128), 1) < 64, keep_hi, keep_lo)
    lines[pl.ds(line, count, stride=LINES), :] = jnp.concatenate([both] * (count // 8), axis=0)
    sent_ref[...] = lines[...].astype(BF16)


def scan_body(head_dim, inner, copies, sent_ref, out_ref, lines):
    lines[...] = sent_ref[...].astype(F32)
    count = lines.shape[0] // LINES
    tiles = inner // 128

    def line(r):
        return lines[pl.ds(r, count, stride=LINES), :]

    keeps = line(copies * tiles).astype(BF16)
    row = iota((count, 128), 0)

    def down(x, d):
        return jnp.where(row >= d, pltpu.roll(x, d, axis=0), 0.0)

    head_of = one_hot(128, inner, head_dim, 64)
    for t in range(tiles):
        keep = dot(keeps, head_of[:, t * 128 : (t + 1) * 128])
        states = [line(i * tiles + t) for i in range(copies)]
        d = 1
        while d < count:
            states = [x + keep * down(x, d) for x in states]
            keep = keep * down(keep, d)
            d *= 2
        for i, x in enumerate(states):
            lines[pl.ds(i * tiles + t, count, stride=LINES), :] = down(x, 1)
    out_ref[...] = lines[...].astype(BF16)


def middle_body(head_dim, first_ref, ends_ref, h_ref, *refs):
    *blocks, conv_shared, x_ref, b_ref, dt_ref, cum_ref, skip = refs[:-7]
    direct_ref, carry_ref, c_ref, out_w_ref, held, c_rows, gate = refs[-7:]
    tokens, inner = x_ref.shape
    gather_blocks(blocks, held)
    wide = held.shape[1]
    half = len(blocks) // 2
    depth = blocks[0].shape[0]
    for i in range(half):
        for j, block in enumerate((blocks[i], blocks[half + i])):
            at = (2 * i + j) * depth
            out_w_ref[at : at + depth] = block[:, wide:]
    for at in range(0, inner, 256):
        g = dot(h_ref[EDGE:], held[:, at : at + 256])
        gate[:, at : at + 256] = silu(g.astype(BF16).astype(F32))
    c_rows[...] = dot(h_ref[...], held[:, inner:]).astype(BF16).astype(F32)
    first = first_ref[0]
    positions = first + iota((tokens, 128), 0)
    start = prompt_start(ends_ref, positions)
    c_half = convolve(c_rows, 0, conv_shared[:, 128:], positions, start)
    c_ref[...] = c_half
    scores = lax.dot_general(
        c_half, b_ref[...], (((1,), (1,)), ((), ())), preferred_element_type=F32
    )
    i, j = iota((tokens, tokens), 0), iota((tokens, tokens), 1)
    start_wide = jnp.concatenate([start] * (tokens // 128), axis=1)
    scores = jnp.where((j <= i) & (first + j >= start_wide), scores, 0.0)
    dt, cum = dt_ref[...], cum_ref[...]
    head_of = one_hot(128, inner, head_dim, 128)
    stepped = (spread(dt, head_of) * x_ref[...].astype(F32)).astype(BF16)
    cum_t = cum.T
    carry = jnp.where(start < first, jnp.exp(cum), 0.0)
    carry_ref[...] = spread(carry, head_of) * gate[...]
    each = 128 // head_dim
    for at in range(0, inner, 128):
        sums = []
        for h in range(at // head_dim, at // head_dim + each):
            gaps = jnp.minimum(cum[:, h : h + 1] - cum_t[h : h + 1, :], 0.0)
            weights = (jnp.exp(gaps) * scores).astype(BF16)
            sums.append(dot(weights, stepped[:, h * head_dim : (h + 1) * head_dim]))
        cut = slice(at, at + 128)
        direct = jnp.concatenate(sums, axis=1) + skip[:, cut] * x_ref[:, cut].astype(F32)
        direct_ref[:, cut] = direct * gate[:, cut]


def last_body(turn_ref, direct_ref, carry_ref, c_ref, carried_ref, out_w_ref, gain, *refs):
    *outs, held, lines, shares = refs
    tokens, inner = direct_ref.shape
    lines[...] = carried_ref[...].astype(F32)
    count = lines.shape[0] // LINES
    line = 0
    for row in range(0, held.shape[0], count):
        for at in range(0, inner, 128):
            cut = lines[pl.ds(line, count, stride=LINES), :]
            held[row : row + count, at : at + 128] = cut.astype(BF16)
            line += 1
    gated = direct_ref[...] + carry_ref[...] * dot(c_ref[...], held[...])
    scaled = (gated * gain[...]).astype(BF16)
    nt = (((1,), (1,)), ((), ()))
    features = shares.shape[2]
    for i in range(shares.shape[0]):
        rows = out_w_ref[i * features : (i + 1) * features]
        shares[i] = lax.dot_general(scaled, rows, nt, preferred_element_type=F32).astype(BF16)
    squares = lax.dot_general(
        jnp.ones((8, inner), F32),
        gated * gated,
        nt,
        precision=lax.Precision.HIGHEST,
        preferred_element_type=F32,
    )
    hi = squares.astype(BF16).astype(F32)
    row = iota(squares.shape, 0)
    riding = jnp.where(row == 0, hi, jnp.where(row == 1, squares - hi, 0.0)).astype(BF16)
    for d, out in enumerate(outs):
        out[:tokens] = shares[(turn_ref[0] + len(outs) - d) % len(outs)]
        out[tokens:, :tokens] = riding
        out[tokens:, tokens:] = jnp.zeros((8, features - tokens), BF16)


def on_device(
    hidden_in,
    w_in_gate,
    w_in_value,
    w_in_shared,
    w_in_step,
    conv_value,
    conv_shared,
    dt_bias,
    a_log,
    skip_gain,
    norm_gain,
    w_out,
    prompt_lengths,
    row_blocks,
):
    x_size, z_size, core_size = SIZES
    seq_count = x_size * z_size * core_size
    tp_count = lax.axis_size("tp")
    tokens, features = hidden_in.shape
    rows_here, inner = w_in_value.shape
    shared = w_in_shared.shape[1]
    heads = dt_bias.shape[0]
    head_dim = inner // heads
    state = shared // 2
    x_at, z_at, core_at = (lax.axis_index(name) for name in SEQ)
    tp_at = lax.axis_index("tp")
    seq_at = (x_at * z_size + z_at) * core_size + core_at

    x_shifts = list(range(1, x_size))

    def x_all(block):
        return [block] + [ahead(block, "x", d) for d in x_shifts]

    tie = lax.optimization_barrier

    before = lax.ppermute(
        hidden_in[tokens - EDGE :], SEQ, [(i, i + 1) for i in range(seq_count - 1)]
    )
    packed = pack(w_in_value, w_in_shared, w_in_step, w_in_gate, w_out.T)
    packed, before = tie((packed, before))
    along_z = lax.all_gather(packed, "z", axis=0, tiled=True)
    early_width = packed.shape[1] - 2 * inner - state
    own = x_all(along_z[:, :early_width])
    late = along_z[:, early_width:]
    mine = jnp.concatenate([before, hidden_in], axis=0)
    hidden = jnp.concatenate([mine] + [ahead(mine, "tp", d) for d in range(1, tp_count)], axis=1)

    chips = jnp.concatenate(
        [
            (x_at - d) % x_size * z_size + jnp.arange(z_size, dtype=jnp.int32)
            for d in range(x_size)
        ]
    )
    stored = jnp.concatenate([chips * core_size + core_at, chips * core_size + 1 - core_at])
    blocks_each = seq_count // tp_count
    model = jnp.take(row_blocks, stored)
    place = (tp_at - model // blocks_each) % tp_count * blocks_each + model % blocks_each
    h = jnp.take(hidden.reshape(hidden.shape[0], seq_count, rows_here), place, axis=1)
    h = h.reshape(hidden.shape[0], -1)
    own[-1], h, late = tie((own[-1], h, late))
    other = [ahead(block, "core", 1) for block in own]
    late_own = x_all(late)
    def lanes(row):
        return jnp.pad(row, (0, -row.shape[0] % 128))[None]

    first = jnp.reshape(seq_at * tokens, (1,))
    doc_ends = jnp.cumsum(prompt_lengths)
    rows, model_width = h.shape
    copies = state // seq_count
    x_rows, b_half, steps, cumulative, sent = call(
        functools.partial(early_body, head_dim),
        [
            ((tokens, inner), BF16),
            ((tokens, state), BF16),
            ((tokens, 128), F32),
            ((tokens, 128), F32),
            ((seq_count * LINES, 128), BF16),
        ],
        [first, doc_ends, h] + own + other + [conv_value, conv_shared, lanes(dt_bias), lanes(a_log)],
        scalars=2,
        scratch=[
            ((model_width, early_width), BF16),
            ((rows, early_width), F32),
            ((seq_count * LINES, 128), F32),
        ],
        flops=2 * rows * model_width * early_width,
    )
    received = lax.all_to_all(sent.reshape(seq_count, LINES, 128), SEQ, 0, 0, tiled=True)
    received, late_own = tie((received, late_own))
    (scanned,) = call(
        functools.partial(scan_body, head_dim, inner, copies),
        [((seq_count * LINES, 128), BF16)],
        [received.reshape(seq_count * LINES, 128)],
        scratch=[((seq_count * LINES, 128), F32)],
    )
    carried = lax.all_to_all(scanned.reshape(seq_count, LINES, 128), SEQ, 0, 0, tiled=True)
    carried = carried.reshape(seq_count * LINES, 128)
    late_other = [ahead(block, "core", 1) for block in late_own]
    direct, carry, c_half, out_w = call(
        functools.partial(middle_body, head_dim),
        [
            ((tokens, inner), F32),
            ((tokens, inner), F32),
            ((tokens, state), BF16),
            ((model_width, inner), BF16),
        ],
        [first, doc_ends, h]
        + late_own
        + late_other
        + [conv_shared, x_rows, b_half, steps, cumulative, jnp.repeat(skip_gain, head_dim)[None]],
        scalars=2,
        scratch=[
            ((model_width, inner + state), BF16),
            ((rows, state), F32),
            ((tokens, inner), F32),
        ],
        flops=2 * rows * model_width * (inner + state),
    )
    shares = call(
        last_body,
        [((tokens + 8, features), BF16)] * tp_count,
        [
            jnp.reshape(x_at - tp_at + tp_count, (1,)),
            direct,
            carry,
            c_half,
            carried,
            out_w,
            norm_gain[None],
        ],
        scalars=1,
        scratch=[
            ((state, inner), BF16),
            ((seq_count * LINES, 128), F32),
            ((tp_count, tokens, features), BF16),
        ],
        flops=2 * tokens * inner * model_width,
    )
    parts = [shares[0]] + [ahead(shares[d], "tp", d) for d in range(1, tp_count)]
    summed = sum(part.astype(F32) for part in parts)
    total = summed[tokens, :tokens] + summed[tokens + 1, :tokens]
    scale = lax.rsqrt(total / (inner * tp_count) + EPSILON)
    result = (summed[:tokens] * scale[:, None]).astype(BF16)

    lane = jnp.arange(features, dtype=jnp.int32)
    part, rest = lane // (z_size * rows_here), lane % (z_size * rows_here)
    core_of = jnp.where(part == 0, core_at, 1 - core_at)
    target = (rest // rows_here * core_size + core_of) * rows_here + rest % rows_here
    moves = (target[:, None] == lane[None, :]).astype(BF16)
    return jnp.dot(result, moves, preferred_element_type=F32).astype(BF16)


def solution(mesh):
    fine = Mesh(mesh.devices.reshape(SIZES + (-1,)), SEQ + ("tp",))
    return jax.shard_map(
        on_device,
        mesh=fine,
        in_specs=(
            P(SEQ, "tp"),
            P(SEQ, "tp"),
            P(SEQ, "tp"),
            P(SEQ, None),
            P(SEQ, "tp"),
            P(None, "tp"),
            P(),
            P("tp"),
            P("tp"),
            P("tp"),
            P("tp"),
            P("tp", SEQ),
            P(),
            P(),
        ),
        out_specs=P(SEQ, "tp"),
        check_vma=False,
    )
```

time: 155 us -> 141 us (0.910)
  other arithmetic: 11.6 us -> 3.32 us
  Pallas kernels: 9.49 us -> 15.4 us
  matrix products: 6.11 us -> 1.07 us
  local copies, waits for them, and re-layouts: 26.1 us -> 23.7 us
  waiting for transfers between devices: 23.1 us -> 21.3 us
  between operations: 2.08 us -> 0.36 us
    unnamed x59 -> x53, local copies, waits for them, and re-layouts: 3.99 us -> 16.2 us
    slice x15 -> x0, local copies, waits for them, and re-layouts: 9.9 us -> none  [the longest x4 4.18 us: on_device(): out_own = [block[:, inner + state:] for block in late_own]]
    pallas_call x3 -> x4, Pallas kernels: 7.78 us -> 13.7 us  [call(): pl.pallas_call(body, out_shape=[jax.ShapeDtypeStruct(shape, kind) for sha...]
    dot_general x9 -> x0, matrix products: 5.03 us -> none  [the longest x4 1.54 us: on_device(): lax.dot_general(normed, jnp.concatenate(pair, axis=0), (((1,), (1,)), (()...]
    all_to_all x2, waiting for transfers between devices: 5.47 us -> 1.5 us  [the longest x1 1.5 us: on_device(): lax.all_to_all(sent.reshape(seq_count, LINES, 128), SEQ, 0, 0, tiled=True)]
    mul x4 -> x0, local copies, waits for them, and re-layouts: 3.19 us -> none  [the longest x2 1.93 us: on_device(): weighted = (tail[:, :, None] * values.astype(F32)).astype(BF16)]
    ppermute x20, starting transfers between devices: 30.3 us -> 27.6 us  [ahead(): lax.ppermute(block, axis, [(i, (i + distance) % count) for i in range(cou...]
    all_to_all x2, starting transfers between devices: 15.2 us -> 17.4 us  [the longest x1 9.13 us: on_device(): lax.all_to_all(sent.reshape(seq_count, LINES, 128), SEQ, 0, 0, tiled=True)]
  transfers between devices with their start and end apart: 23 -> 23, of which waited for: 6 -> 5; matrix products, arithmetic and copies ran while one was open for 19% -> 8% of each run, Pallas kernels for 3% -> 10%
where the time goes in v6:
time: 141 us; the launch traced here: 140 us
  starting transfers between devices  50 us (35%)
  blocking collectives  25 us (18%)
  local copies, waits for them, and re-layouts  23.7 us (17%)
  waiting for transfers between devices  21.3 us (15%)
  Pallas kernels  15.4 us (11%)
  other arithmetic  3.32 us (2%)
    ppermute x20, starting transfers between devices, ahead(): lax.ppermute(block, axis, [(i, (i + distance) % count) for i in range(cou...  27.6 us
    all_gather x1, blocking collectives, on_device(): along_z = lax.all_gather(packed, 'z', axis=0, tiled=True)  25 us
    ppermute x20, waiting for transfers between devices, ahead(): lax.ppermute(block, axis, [(i, (i + distance) % count) for i in range(cou...  19.8 us
    unnamed x53, local copies, waits for them, and re-layouts  16.2 us
    pallas_call x4, Pallas kernels, call(): pl.pallas_call(body, out_shape=[jax.ShapeDtypeStruct(shape, kind) for sha...  13.7 us
    all_to_all x1, starting transfers between devices, on_device(): lax.all_to_all(sent.reshape(seq_count, LINES, 128), SEQ, 0, 0, tiled=True)  9.13 us
    all_to_all x1, starting transfers between devices, on_device(): lax.all_to_all(scanned.reshape(seq_count, LINES, 128), SEQ, 0, 0, tiled=T...  8.28 us
    gather x2, local copies, waits for them, and re-layouts, on_device(): jnp.take(hidden.reshape(hidden.shape[0], seq_count, rows_here), place, ax...  5.37 us
  transfers between devices with their start and end apart: 23, of which 5 were waited for; matrix products, arithmetic and copies ran while one was open for 8% of the time, Pallas kernels for 10%

profile of v6, /device:TPU:1, one launch (start us, length us, event | category | flops | bytes accessed | tf_op | source)
XLA Modules:
  0.0 140.0 jit_solution(14344851847062888584)
XLA Ops:
  0.9 4.9 %collective-permute-start = (bf16[8,384]{0,1:T(8,128)(2,1)S(1)}, bf16[8,384]{0,1:T(8,128)(2,1)S(1)}, u32[]{:S(2)}, u32[]{:S(2)}) collective-permute-start(bf16[8,384]{0,1:T(8,128)(2,1)S(1)} %copy.15), channel_id=1, source_target_pairs={{0,4},{4,8},{8,12},{12,16},{16,20},{20,24},{24,28},{28,32},{32,36}... | collective-permute-start | bytes 18440 | tf_op jit(solution)/shard_map/ppermute | solution.py:298
  8.3 1.7 %shard_map.136 = bf16[24,2688]{1,0:T(8,128)(2,1)} custom-call(f32[24,768]{1,0:T(8,128)} %value_ref.1, f32[24,256]{1,0:T(8,128)} %shared_ref.1, f32[12,24]{1,0:T(8,128)} %bitcast.38, f32[24,768]{1,0:T(8,128)} %gate_ref.1, f32[24,768]{1,0:T(8,128)} %bitcast.37), custom_call_target="tpu_custom_call" | custom-call | tf_op jit(solution)/shard_map/pallas_call | solution.py:45
  10.2 1.4 collective-permute-start.2
  11.6 2.6 %collective-permute-start.3 = (bf16[264,384]{0,1:T(8,128)(2,1)S(1)}, bf16[264,384]{0,1:T(8,128)(2,1)S(1)}, u32[]{:S(2)}, u32[]{:S(2)}) collective-permute-start(bf16[264,384]{0,1:T(8,128)(2,1)S(1)} %pad_maximum_fusion.1), channel_id=1, source_target_pairs={{0,2},{1,3},{2,0},{3,1},{4,6},{5,7},{6,4},{7,5},{8,10},{9,11},{10,... | collective-permute-start | bytes 608264 | tf_op jit(solution)/shard_map/ppermute | solution.py:21
  14.2 1.1 collective-permute-start.4
  15.3 25.0 %all_gather.3 = bf16[192,2688]{1,0:T(8,128)(2,1)S(1)} all-gather(bf16[24,2688]{1,0:T(8,128)(2,1)} %shard_map.136), channel_id=1, replica_groups=mesh['x'=4,'z'=8,'core'=2,'tp'=4] {'z'}, dimensions={0}, use_global_device_ids=true | all-gather | bytes 1161216 | tf_op jit(solution)/shard_map/all_gather | solution.py:303
  40.3 2.5 %collective-permute-start.1 = (bf16[192,1024]{1,0:T(8,128)(2,1)S(1)}, bf16[192,1024]{1,0:T(8,128)(2,1)S(1)}, u32[]{:S(2)}, u32[]{:S(2)}) collective-permute-start(bf16[192,1024]{1,0:T(8,128)(2,1)S(1)} %slice.28.refs_0_), channel_id=1, source_target_pairs={{0,192},{64,0},{128,64},{192,128},{1,193},{65,1},{129,65},{193,129... | collective-permute-start | bytes 1179656 | tf_op jit(solution)/shard_map/ppermute | solution.py:21
  42.9 1.7 %collective-permute-start.6 = (bf16[192,1024]{1,0:T(8,128)(2,1)S(1)}, bf16[192,1024]{1,0:T(8,128)(2,1)}, u32[]{:S(2)}, u32[]{:S(2)}) collective-permute-start(bf16[192,1024]{1,0:T(8,128)(2,1)S(1)} %slice.28.refs_0_), channel_id=1, source_target_pairs={{0,128},{64,192},{128,0},{192,64},{1,129},{65,193},{129,1},{193,65... | collective-permute-start | bytes 1179656 | tf_op jit(solution)/shard_map/ppermute | solution.py:21
  44.6 5.8 %collective-permute-start.7 = (bf16[192,1024]{1,0:T(8,128)(2,1)S(1)}, bf16[192,1024]{1,0:T(8,128)(2,1)S(1)}, u32[]{:S(2)}, u32[]{:S(2)}) collective-permute-start(bf16[192,1024]{1,0:T(8,128)(2,1)S(1)} %slice.28.refs_0_), channel_id=1, source_target_pairs={{0,4},{4,0},{1,5},{5,1},{2,6},{6,2},{3,7},{7,3},{8,12},{12,8},{9,1... | collective-permute-start | bytes 1179656 | tf_op jit(solution)/shard_map/ppermute | solution.py:21
  50.4 1.2 pad_maximum_fusion
  51.6 3.1 %gather_fusion.1 = bf16[64,264,24]{1,2,0:T(8,128)(2,1)} fusion(bf16[264,64,24]{0,2,1:T(8,128)(2,1)} %bitcast.35, s32[1024]{0:T(1024)S(1)} %pad_clamp_fusion), kind=kCustom, calls=%fused_computation.1 | custom fusion | bytes 1622272 | tf_op jit(solution)/shard_map/jit(_take)/gather | solution.py:320
  54.7 2.3 %copy.17 = bf16[264,1536]{1,0:T(8,128)(2,1)} copy(bf16[264,1536]{0,1:T(8,128)(2,1)} %bitcast.36) | data formatting | bytes 1622016 | tf_op jit(solution)/shard_map/jit(_take)/gather | solution.py:320
  57.0 1.2 broadcast_select_fusion.h_ref
  58.2 2.4 %collective-permute-start.10 = (bf16[192,1024]{1,0:T(8,128)(2,1)S(1)}, bf16[192,1024]{1,0:T(8,128)(2,1)S(1)}, u32[]{:S(2)}, u32[]{:S(2)}) collective-permute-start(bf16[192,1024]{1,0:T(8,128)(2,1)S(1)} %collective-permute-done.1.refs_3_), channel_id=1, source_target_pairs={{0,4},{4,0},{1,5},{5,1},{2,6},{6,2},{3,7},{7,3},{8,12},{12,8},{9,1... | collective-permute-start | bytes 1179656 | tf_op jit(solution)/shard_map/ppermute | solution.py:21
  60.7 3.5 %collective-permute-start.8 = (bf16[192,1024]{1,0:T(8,128)(2,1)}, bf16[192,1024]{1,0:T(8,128)(2,1)}, u32[]{:S(2)}, u32[]{:S(2)}) collective-permute-start(bf16[192,1024]{1,0:T(8,128)(2,1)} %collective-permute-done.5.refs_1_), channel_id=1, source_target_pairs={{0,4},{4,0},{1,5},{5,1},{2,6},{6,2},{3,7},{7,3},{8,12},{12,8},{9,1... | collective-permute-start | bytes 1179656 | tf_op jit(solution)/shard_map/ppermute | solution.py:21
  64.9 1.6 %collective-permute-start.12 = (bf16[192,1664]{1,0:T(8,128)(2,1)S(1)}, bf16[192,1664]{1,0:T(8,128)(2,1)S(1)}, u32[]{:S(2)}, u32[]{:S(2)}) collective-permute-start(bf16[192,1664]{1,0:T(8,128)(2,1)S(1)} %slice.29.refs_0_), channel_id=1, source_target_pairs={{0,128},{64,192},{128,0},{192,64},{1,129},{65,193},{129,1},{193,65... | collective-permute-start | bytes 1916936 | tf_op jit(solution)/shard_map/ppermute | solution.py:21
  67.3 1.1 collective-permute-start.13
  70.6 4.4 %shard_map.137 = (bf16[256,768]{1,0:T(8,128)(2,1)S(1)}, bf16[256,128]{1,0:T(8,128)(2,1)S(1)}, f32[256,128]{1,0:T(8,128)S(1)}, f32[256,128]{1,0:T(8,128)S(1)}, bf16[1024,128]{1,0:T(8,128)(2,1)S(1)}) custom-call(s32[1]{0:T(128)} %bitcast.1.first_ref, s32[8]{0:T(128)S(1)} %bitcast.33, bf16[264,1536]{1,0:T(8,128)(2,1)S(1)} %broadcast_select_fusion.h_ref, ...), custom_call_target="tpu_custom_call" | custom-call | flops 830472192 | bytes 3974180 | tf_op jit(solution)/shard_map/pallas_call | solution.py:56
  78.4 9.1 %all-to-all-start = ((bf16[64,16,128]{2,1,0:T(8,128)(2,1)}), bf16[64,16,128]{2,1,0:T(8,128)(2,1)S(1)}, u32[]{:S(2)}, u32[]{:S(2)}) async-start(bf16[64,16,128]{2,1,0:T(8,128)(2,1)} %bitcast.32), calls=%async_computation | async-start | bytes 524288 | tf_op jit(solution)/shard_map/all_to_all | solution.py:350
  87.5 6.8 %collective-permute-done.11.refs_1_ = bf16[192,1664]{1,0:T(8,128)(2,1)S(1)} collective-permute-done((bf16[192,1664]{1,0:T(8,128)(2,1)S(1)}, bf16[192,1664]{1,0:T(8,128)(2,1)S(1)}, u32[]{:S(2)}, u32[]{:S(2)}) %collective-permute-start.11) | collective-permute-done | bytes 639008 | tf_op jit(solution)/shard_map/ppermute | solution.py:21
  94.3 3.8 %collective-permute-done.13.refs_3_ = bf16[192,1664]{1,0:T(8,128)(2,1)} collective-permute-done((bf16[192,1664]{1,0:T(8,128)(2,1)S(1)}, bf16[192,1664]{1,0:T(8,128)(2,1)}, u32[]{:S(2)}, u32[]{:S(2)}) %collective-permute-start.13) | collective-permute-done | bytes 639008 | tf_op jit(solution)/shard_map/ppermute | solution.py:21
  98.1 1.5 %all-to-all-done = bf16[64,16,128]{2,1,0:T(8,128)(2,1)S(1)} async-done(((bf16[64,16,128]{2,1,0:T(8,128)(2,1)}), bf16[64,16,128]{2,1,0:T(8,128)(2,1)S(1)}, u32[]{:S(2)}, u32[]{:S(2)}) %all-to-all-start) | async-done | bytes 262176 | tf_op jit(solution)/shard_map/all_to_all | solution.py:350
  101.4 1.4 %shard_map.139 = bf16[1024,128]{1,0:T(8,128)(2,1)} custom-call(bf16[1024,128]{1,0:T(8,128)(2,1)S(1)} %bitcast.31), custom_call_target="tpu_custom_call" | custom-call | bytes 262144 | tf_op jit(solution)/shard_map/pallas_call | solution.py:56
  102.9 8.3 %all-to-all-start.1 = ((bf16[64,16,128]{2,1,0:T(8,128)(2,1)}), bf16[64,16,128]{2,1,0:T(8,128)(2,1)S(1)}, u32[]{:S(2)}, u32[]{:S(2)}) async-start(bf16[64,16,128]{2,1,0:T(8,128)(2,1)} %bitcast.18), calls=%async_computation.1 | async-start | bytes 524288 | tf_op jit(solution)/shard_map/all_to_all | solution.py:358
  111.4 1.1 copy-done.3
  112.5 1.1 copy-done.5
  117.2 6.0 %shard_map.138 = (f32[256,768]{1,0:T(8,128)S(1)}, f32[256,768]{1,0:T(8,128)S(1)}, bf16[256,128]{1,0:T(8,128)(2,1)S(1)}, bf16[1536,768]{1,0:T(8,128)(2,1)}) custom-call(s32[1]{0:T(128)} %bitcast.1.first_ref, s32[8]{0:T(128)S(1)} %bitcast.34, bf16[264,1536]{1,0:T(8,128)(2,1)S(1)} %broadcast_select_fusion.h_ref, bf16[192,1664]{1,0:T(8,128)(2,1)S(1)} %slice.29.refs_0_, ...), custom_call_target="tpu_custom_call" | custom-call | flops 726663168 | bytes 6650916 | tf_op jit(solution)/shard_map/pallas_call | solution.py:56
  123.2 1.7 %copy-done.1 = bf16[1536,768]{1,0:T(8,128)(2,1)S(1)} copy-done((bf16[1536,768]{1,0:T(8,128)(2,1)S(1)}, bf16[1536,768]{1,0:T(8,128)(2,1)}, u32[]{:S(2)}) %copy-start.1) | copy-done | bytes 2359320
  124.9 1.9 %shard_map.140 = (bf16[264,384]{1,0:T(8,128)(2,1)S(1)}, bf16[264,384]{1,0:T(8,128)(2,1)S(1)}, bf16[264,384]{1,0:T(8,128)(2,1)S(1)}, bf16[264,384]{1,0:T(8,128)(2,1)S(1)}) custom-call(s32[1]{0:T(128)} %bitcast.turn_ref, f32[256,768]{1,0:T(8,128)S(1)} %get-tuple-element.42.direct_ref, f32[256,768]{1,0:T(8,128)S(1)} %get-tuple-element.43.carry_ref, ...), custom_call_target="tpu_custom_call" | custom-call | flops 603979776 | bytes 4262916 | tf_op jit(solution)/shard_map/pallas_call | solution.py:56
  128.0 1.7 %collective-permute-start.20 = (bf16[264,384]{1,0:T(8,128)(2,1)S(1)}, bf16[264,384]{1,0:T(8,128)(2,1)S(1)}, u32[]{:S(2)}, u32[]{:S(2)}) collective-permute-start(bf16[264,384]{1,0:T(8,128)(2,1)S(1)} %get-tuple-element.50), channel_id=1, source_target_pairs={{0,3},{1,0},{2,1},{3,2},{4,7},{5,4},{6,5},{7,6},{8,11},{9,8},{10,9... | collective-permute-start | bytes 608264 | tf_op jit(solution)/shard_map/ppermute | solution.py:21
  129.7 8.8 %collective-permute-done.18 = bf16[264,384]{1,0:T(8,128)(2,1)S(1)} collective-permute-done((bf16[264,384]{1,0:T(8,128)(2,1)S(1)}, bf16[264,384]{1,0:T(8,128)(2,1)S(1)}, u32[]{:S(2)}, u32[]{:S(2)}) %collective-permute-start.18) | collective-permute-done | bytes 202784 | tf_op jit(solution)/shard_map/ppermute | solution.py:21
  139.0 1.1 convolution_convert_fusion
  (104 shorter events, 18.0 us)
Async XLA Ops:
  0.0 6.1 %copy-start = (s32[64]{0:T(128)S(1)}, s32[64]{0:T(128)}, u32[]{:S(2)}) copy-start(s32[64]{0:T(128)} %param.27) | copy-start | bytes 772
  0.9 9.2 %collective-permute-start = (bf16[8,384]{0,1:T(8,128)(2,1)S(1)}, bf16[8,384]{0,1:T(8,128)(2,1)S(1)}, u32[]{:S(2)}, u32[]{:S(2)}) collective-permute-start(bf16[8,384]{0,1:T(8,128)(2,1)S(1)} %copy.15), channel_id=1, source_target_pairs={{0,4},{4,8},{8,12},{12,16},{16,20},{20,24},{24,28},{28,32},{32,36}... | collective-permute-start | bytes 18440 | tf_op jit(solution)/shard_map/ppermute | solution.py:298
  10.2 32.7 %collective-permute-start.2 = (bf16[264,384]{0,1:T(8,128)(2,1)S(1)}, bf16[264,384]{0,1:T(8,128)(2,1)S(1)}, u32[]{:S(2)}, u32[]{:S(2)}) collective-permute-start(bf16[264,384]{0,1:T(8,128)(2,1)S(1)} %pad_maximum_fusion.1), channel_id=1, source_target_pairs={{0,1},{1,2},{2,3},{3,0},{4,5},{5,6},{6,7},{7,4},{8,9},{9,10},{10,1... | collective-permute-start | bytes 608264 | tf_op jit(solution)/shard_map/ppermute | solution.py:21
  11.6 33.0 %collective-permute-start.3 = (bf16[264,384]{0,1:T(8,128)(2,1)S(1)}, bf16[264,384]{0,1:T(8,128)(2,1)S(1)}, u32[]{:S(2)}, u32[]{:S(2)}) collective-permute-start(bf16[264,384]{0,1:T(8,128)(2,1)S(1)} %pad_maximum_fusion.1), channel_id=1, source_target_pairs={{0,2},{1,3},{2,0},{3,1},{4,6},{5,7},{6,4},{7,5},{8,10},{9,11},{10,... | collective-permute-start | bytes 608264 | tf_op jit(solution)/shard_map/ppermute | solution.py:21
  14.2 36.2 %collective-permute-start.4 = (bf16[264,384]{0,1:T(8,128)(2,1)S(1)}, bf16[264,384]{0,1:T(8,128)(2,1)S(1)}, u32[]{:S(2)}, u32[]{:S(2)}) collective-permute-start(bf16[264,384]{0,1:T(8,128)(2,1)S(1)} %pad_maximum_fusion.1), channel_id=1, source_target_pairs={{0,3},{1,0},{2,1},{3,2},{4,7},{5,4},{6,5},{7,6},{8,11},{9,8},{10,9... | collective-permute-start | bytes 608264 | tf_op jit(solution)/shard_map/ppermute | solution.py:21
  40.3 17.9 %collective-permute-start.1 = (bf16[192,1024]{1,0:T(8,128)(2,1)S(1)}, bf16[192,1024]{1,0:T(8,128)(2,1)S(1)}, u32[]{:S(2)}, u32[]{:S(2)}) collective-permute-start(bf16[192,1024]{1,0:T(8,128)(2,1)S(1)} %slice.28.refs_0_), channel_id=1, source_target_pairs={{0,192},{64,0},{128,64},{192,128},{1,193},{65,1},{129,65},{193,129... | collective-permute-start | bytes 1179656 | tf_op jit(solution)/shard_map/ppermute | solution.py:21
  42.9 17.8 %collective-permute-start.5 = (bf16[192,1024]{1,0:T(8,128)(2,1)S(1)}, bf16[192,1024]{1,0:T(8,128)(2,1)}, u32[]{:S(2)}, u32[]{:S(2)}) collective-permute-start(bf16[192,1024]{1,0:T(8,128)(2,1)S(1)} %slice.28.refs_0_), channel_id=1, source_target_pairs={{0,64},{64,128},{128,192},{192,0},{1,65},{65,129},{129,193},{193,1... | collective-permute-start | bytes 1179656 | tf_op jit(solution)/shard_map/ppermute | solution.py:21
  42.9 21.3 %collective-permute-start.6 = (bf16[192,1024]{1,0:T(8,128)(2,1)S(1)}, bf16[192,1024]{1,0:T(8,128)(2,1)}, u32[]{:S(2)}, u32[]{:S(2)}) collective-permute-start(bf16[192,1024]{1,0:T(8,128)(2,1)S(1)} %slice.28.refs_0_), channel_id=1, source_target_pairs={{0,128},{64,192},{128,0},{192,64},{1,129},{65,193},{129,1},{193,65... | collective-permute-start | bytes 1179656 | tf_op jit(solution)/shard_map/ppermute | solution.py:21
  44.6 19.6 %collective-permute-start.7 = (bf16[192,1024]{1,0:T(8,128)(2,1)S(1)}, bf16[192,1024]{1,0:T(8,128)(2,1)S(1)}, u32[]{:S(2)}, u32[]{:S(2)}) collective-permute-start(bf16[192,1024]{1,0:T(8,128)(2,1)S(1)} %slice.28.refs_0_), channel_id=1, source_target_pairs={{0,4},{4,0},{1,5},{5,1},{2,6},{6,2},{3,7},{7,3},{8,12},{12,8},{9,1... | collective-permute-start | bytes 1179656 | tf_op jit(solution)/shard_map/ppermute | solution.py:21
  54.7 13.7 %copy-start.23 = (f32[12]{0:T(128)S(1)}, f32[12]{0:T(128)}, u32[]{:S(2)}) copy-start(f32[12]{0:T(128)} %param.22) | copy-start | bytes 148
  54.7 13.7 %copy-start.24 = (f32[12]{0:T(128)S(1)}, f32[12]{0:T(128)}, u32[]{:S(2)}) copy-start(f32[12]{0:T(128)} %param.21) | copy-start | bytes 148
  54.7 13.7 %copy-start.25 = (s32[8]{0:T(128)S(1)}, s32[8]{0:T(128)}, u32[]{:S(2)}) copy-start(s32[8]{0:T(128)} %param.26) | copy-start | bytes 100
  54.7 13.9 %copy-start.19 = (f32[4,256]{1,0:T(4,128)S(1)}, f32[4,256]{1,0:T(4,128)}, u32[]{:S(2)}) copy-start(f32[4,256]{1,0:T(4,128)} %refs_8_.3) | copy-start | bytes 12292
  54.7 13.9 %copy-start.20 = (f32[4,768]{1,0:T(4,128)S(1)}, f32[4,768]{1,0:T(4,128)}, u32[]{:S(2)}) copy-start(f32[4,768]{1,0:T(4,128)} %refs_8_.2) | copy-start | bytes 36868
  58.2 8.3 %collective-permute-start.10 = (bf16[192,1024]{1,0:T(8,128)(2,1)S(1)}, bf16[192,1024]{1,0:T(8,128)(2,1)S(1)}, u32[]{:S(2)}, u32[]{:S(2)}) collective-permute-start(bf16[192,1024]{1,0:T(8,128)(2,1)S(1)} %collective-permute-done.1.refs_3_), channel_id=1, source_target_pairs={{0,4},{4,0},{1,5},{5,1},{2,6},{6,2},{3,7},{7,3},{8,12},{12,8},{9,1... | collective-permute-start | bytes 1179656 | tf_op jit(solution)/shard_map/ppermute | solution.py:21
  60.7 7.9 %collective-permute-start.8 = (bf16[192,1024]{1,0:T(8,128)(2,1)}, bf16[192,1024]{1,0:T(8,128)(2,1)}, u32[]{:S(2)}, u32[]{:S(2)}) collective-permute-start(bf16[192,1024]{1,0:T(8,128)(2,1)} %collective-permute-done.5.refs_1_), channel_id=1, source_target_pairs={{0,4},{4,0},{1,5},{5,1},{2,6},{6,2},{3,7},{7,3},{8,12},{12,8},{9,1... | collective-permute-start | bytes 1179656 | tf_op jit(solution)/shard_map/ppermute | solution.py:21
  64.2 4.4 %collective-permute-start.9 = (bf16[192,1024]{1,0:T(8,128)(2,1)}, bf16[192,1024]{1,0:T(8,128)(2,1)}, u32[]{:S(2)}, u32[]{:S(2)}) collective-permute-start(bf16[192,1024]{1,0:T(8,128)(2,1)} %collective-permute-done.6.refs_2_), channel_id=1, source_target_pairs={{0,4},{4,0},{1,5},{5,1},{2,6},{6,2},{3,7},{7,3},{8,12},{12,8},{9,1... | collective-permute-start | bytes 1179656 | tf_op jit(solution)/shard_map/ppermute | solution.py:21
  64.2 30.2 %collective-permute-start.11 = (bf16[192,1664]{1,0:T(8,128)(2,1)S(1)}, bf16[192,1664]{1,0:T(8,128)(2,1)S(1)}, u32[]{:S(2)}, u32[]{:S(2)}) collective-permute-start(bf16[192,1664]{1,0:T(8,128)(2,1)S(1)} %slice.29.refs_0_), channel_id=1, source_target_pairs={{0,64},{64,128},{128,192},{192,0},{1,65},{65,129},{129,193},{193,1... | collective-permute-start | bytes 1916936 | tf_op jit(solution)/shard_map/ppermute | solution.py:21
  64.9 29.4 %collective-permute-start.12 = (bf16[192,1664]{1,0:T(8,128)(2,1)S(1)}, bf16[192,1664]{1,0:T(8,128)(2,1)S(1)}, u32[]{:S(2)}, u32[]{:S(2)}) collective-permute-start(bf16[192,1664]{1,0:T(8,128)(2,1)S(1)} %slice.29.refs_0_), channel_id=1, source_target_pairs={{0,128},{64,192},{128,0},{192,64},{1,129},{65,193},{129,1},{193,65... | collective-permute-start | bytes 1916936 | tf_op jit(solution)/shard_map/ppermute | solution.py:21
  67.3 30.8 %collective-permute-start.13 = (bf16[192,1664]{1,0:T(8,128)(2,1)S(1)}, bf16[192,1664]{1,0:T(8,128)(2,1)}, u32[]{:S(2)}, u32[]{:S(2)}) collective-permute-start(bf16[192,1664]{1,0:T(8,128)(2,1)S(1)} %slice.29.refs_0_), channel_id=1, source_target_pairs={{0,192},{64,0},{128,64},{192,128},{1,193},{65,1},{129,65},{193,129... | collective-permute-start | bytes 1916936 | tf_op jit(solution)/shard_map/ppermute | solution.py:21
  70.6 40.6 %copy-start.22 = (f32[12]{0:T(128)S(1)}, f32[12]{0:T(128)}, u32[]{:S(2)}) copy-start(f32[12]{0:T(128)} %param.23) | copy-start | bytes 148
  70.6 40.7 %copy-start.21 = (f32[768]{0:T(1024)S(1)}, f32[768]{0:T(1024)}, u32[]{:S(2)}) copy-start(f32[768]{0:T(1024)} %param.24) | copy-start | bytes 9220
  78.4 21.2 %all-to-all-start = ((bf16[64,16,128]{2,1,0:T(8,128)(2,1)}), bf16[64,16,128]{2,1,0:T(8,128)(2,1)S(1)}, u32[]{:S(2)}, u32[]{:S(2)}) async-start(bf16[64,16,128]{2,1,0:T(8,128)(2,1)} %bitcast.32), calls=%async_computation | async-start | bytes 524288 | tf_op jit(solution)/shard_map/all_to_all | solution.py:350
  94.3 17.1 %copy-start.2 = (bf16[192,1664]{1,0:T(8,128)(2,1)}, bf16[192,1664]{1,0:T(8,128)(2,1)S(1)}, u32[]{:S(2)}) copy-start(bf16[192,1664]{1,0:T(8,128)(2,1)S(1)} %collective-permute-done.11.refs_1_) | copy-start | bytes 1916932
  99.6 11.7 %collective-permute-start.14 = (bf16[192,1664]{1,0:T(8,128)(2,1)S(1)}, bf16[192,1664]{1,0:T(8,128)(2,1)}, u32[]{:S(2)}, u32[]{:S(2)}) collective-permute-start(bf16[192,1664]{1,0:T(8,128)(2,1)S(1)} %slice.29.refs_0_), channel_id=1, source_target_pairs={{0,4},{4,0},{1,5},{5,1},{2,6},{6,2},{3,7},{7,3},{8,12},{12,8},{9,1... | collective-permute-start | bytes 1916936 | tf_op jit(solution)/shard_map/ppermute | solution.py:21
  100.0 11.4 %collective-permute-start.15 = (bf16[192,1664]{1,0:T(8,128)(2,1)S(1)}, bf16[192,1664]{1,0:T(8,128)(2,1)}, u32[]{:S(2)}, u32[]{:S(2)}) collective-permute-start(bf16[192,1664]{1,0:T(8,128)(2,1)S(1)} %collective-permute-done.11.refs_1_), channel_id=1, source_target_pairs={{0,4},{4,0},{1,5},{5,1},{2,6},{6,2},{3,7},{7,3},{8,12},{12,8},{9,1... | collective-permute-start | bytes 1916936 | tf_op jit(solution)/shard_map/ppermute | solution.py:21
  100.1 11.3 %collective-permute-start.16 = (bf16[192,1664]{1,0:T(8,128)(2,1)S(1)}, bf16[192,1664]{1,0:T(8,128)(2,1)}, u32[]{:S(2)}, u32[]{:S(2)}) collective-permute-start(bf16[192,1664]{1,0:T(8,128)(2,1)S(1)} %collective-permute-done.12.refs_2_), channel_id=1, source_target_pairs={{0,4},{4,0},{1,5},{5,1},{2,6},{6,2},{3,7},{7,3},{8,12},{12,8},{9,1... | collective-permute-start | bytes 1916936 | tf_op jit(solution)/shard_map/ppermute | solution.py:21
  101.3 10.0 %collective-permute-start.17 = (bf16[192,1664]{1,0:T(8,128)(2,1)}, bf16[192,1664]{1,0:T(8,128)(2,1)}, u32[]{:S(2)}, u32[]{:S(2)}) collective-permute-start(bf16[192,1664]{1,0:T(8,128)(2,1)} %collective-permute-done.13.refs_3_), channel_id=1, source_target_pairs={{0,4},{4,0},{1,5},{5,1},{2,6},{6,2},{3,7},{7,3},{8,12},{12,8},{9,1... | collective-permute-start | bytes 1916936 | tf_op jit(solution)/shard_map/ppermute | solution.py:21
  102.9 20.3 %all-to-all-start.1 = ((bf16[64,16,128]{2,1,0:T(8,128)(2,1)}), bf16[64,16,128]{2,1,0:T(8,128)(2,1)S(1)}, u32[]{:S(2)}, u32[]{:S(2)}) async-start(bf16[64,16,128]{2,1,0:T(8,128)(2,1)} %bitcast.18), calls=%async_computation.1 | async-start | bytes 524288 | tf_op jit(solution)/shard_map/all_to_all | solution.py:358
  126.8 11.7 %collective-permute-start.18 = (bf16[264,384]{1,0:T(8,128)(2,1)S(1)}, bf16[264,384]{1,0:T(8,128)(2,1)S(1)}, u32[]{:S(2)}, u32[]{:S(2)}) collective-permute-start(bf16[264,384]{1,0:T(8,128)(2,1)S(1)} %get-tuple-element.48), channel_id=1, source_target_pairs={{0,1},{1,2},{2,3},{3,0},{4,5},{5,6},{6,7},{7,4},{8,9},{9,10},{10,1... | collective-permute-start | bytes 608264 | tf_op jit(solution)/shard_map/ppermute | solution.py:21
  127.2 11.3 %collective-permute-start.19 = (bf16[264,384]{1,0:T(8,128)(2,1)S(1)}, bf16[264,384]{1,0:T(8,128)(2,1)S(1)}, u32[]{:S(2)}, u32[]{:S(2)}) collective-permute-start(bf16[264,384]{1,0:T(8,128)(2,1)S(1)} %get-tuple-element.49), channel_id=1, source_target_pairs={{0,2},{1,3},{2,0},{3,1},{4,6},{5,7},{6,4},{7,5},{8,10},{9,11},{10,... | collective-permute-start | bytes 608264 | tf_op jit(solution)/shard_map/ppermute | solution.py:21
  128.0 10.9 %collective-permute-start.20 = (bf16[264,384]{1,0:T(8,128)(2,1)S(1)}, bf16[264,384]{1,0:T(8,128)(2,1)S(1)}, u32[]{:S(2)}, u32[]{:S(2)}) collective-permute-start(bf16[264,384]{1,0:T(8,128)(2,1)S(1)} %get-tuple-element.50), channel_id=1, source_target_pairs={{0,3},{1,0},{2,1},{3,2},{4,7},{5,4},{6,5},{7,6},{8,11},{9,8},{10,9... | collective-permute-start | bytes 608264 | tf_op jit(solution)/shard_map/ppermute | solution.py:21
  (17 other events, 15.2 us)

commit v7 on v6

--- a/solution.py
+++ b/solution.py
@@ -50,16 +50,56 @@
     )(value, shared, step.T, gate, out_t)
 
 
-def call(body, shapes, args, scalars=0, scratch=(), flops=0):
-    smem, vmem = pl.BlockSpec(memory_space=pltpu.SMEM), pl.BlockSpec(memory_space=pltpu.VMEM)
+def call(
+    body, shapes, args, scalars=0, blocks=0, near_in=0, near_out=0, scratch=(), flops=0, grant=60
+):
+    hbm, vmem = pl.BlockSpec(memory_space=pltpu.HBM), pl.BlockSpec(memory_space=pltpu.VMEM)
+    fixed = scalars + blocks + near_in
+    far_in, far_out = args[fixed:], shapes[near_out:]
     moved = sum(x.size * x.dtype.itemsize for x in args)
+
+    def wrapped(*refs):
+        ins, rest = refs[: len(args)], refs[len(args) :]
+        outs, rest = rest[: len(shapes)], rest[len(shapes) :]
+        held_in, rest = rest[: len(far_in)], rest[len(far_in) :]
+        held_out, rest = rest[: len(far_out)], rest[len(far_out) :]
+        *room, sems = rest
+        copies = [
+            pltpu.make_async_copy(src, dst, sems.at[i])
+            for i, (src, dst) in enumerate(zip(ins[fixed:], held_in))
+        ]
+        for copy in copies:
+            copy.start()
+        free = sems.at[pl.ds(len(far_in) + len(far_out), blocks)] if blocks else None
+
+        def ready():
+            for copy in copies:
+                copy.wait()
+
+        body(ready, free, *ins[:fixed], *held_in, *outs[:near_out], *held_out, *room)
+        copies_out = [
+            pltpu.make_async_copy(src, dst, sems.at[len(far_in) + i])
+            for i, (src, dst) in enumerate(zip(held_out, outs[near_out:]))
+        ]
+        for copy in copies_out:
+            copy.start()
+        for copy in copies_out:
+            copy.wait()
+
+    room = [pltpu.VMEM(x.shape, x.dtype) for x in far_in]
+    room += [pltpu.VMEM(shape, kind) for shape, kind in far_out]
+    room += [pltpu.VMEM(shape, kind) for shape, kind in scratch]
+    room.append(pltpu.SemaphoreType.DMA((len(far_in) + len(far_out) + blocks,)))
     return pl.pallas_call(
-        body,
+        wrapped,
         out_shape=[jax.ShapeDtypeStruct(shape, kind) for shape, kind in shapes],
-        in_specs=[smem] * scalars + [vmem] * (len(args) - scalars),
-        out_specs=[vmem] * len(shapes),
-        scratch_shapes=[pltpu.VMEM(shape, kind) for shape, kind in scratch],
-        compiler_params=pltpu.CompilerParams(vmem_limit_bytes=44 << 20),
+        in_specs=[pl.BlockSpec(memory_space=pltpu.SMEM)] * scalars
+        + [hbm] * blocks
+        + [vmem] * near_in
+        + [hbm] * len(far_in),
+        out_specs=[vmem] * near_out + [hbm] * len(far_out),
+        scratch_shapes=room,
+        compiler_params=pltpu.CompilerParams(vmem_limit_bytes=grant << 20),
         cost_estimate=pl.CostEstimate(flops=flops, bytes_accessed=moved, transcendentals=0),
     )(*args)
 
@@ -102,19 +142,62 @@
     return silu(total).astype(BF16)
 
 
-def gather_blocks(blocks, held):
+def fetch(blocks, held, sems, columns, order=None):
     depth = blocks[0].shape[0]
-    for i, block in enumerate(blocks):
-        held[i * depth : (i + 1) * depth] = block[:, : held.shape[1]]
-
-
-def early_body(head_dim, first_ref, ends_ref, h_ref, *refs):
-    *blocks, conv_value, conv_shared, bias, a_log = refs[:-8]
+    copies = []
+    for i, k in enumerate(order or range(len(blocks))):
+        copy = pltpu.make_async_copy(
+            blocks[k].at[:, columns], held.at[i * depth : (i + 1) * depth], sems.at[i]
+        )
+        copy.start()
+        copies.append(copy)
+    return copies
+
+
+def arrange_body(block_rows, ready, sems, at_ref, order_ref, *refs):
+    *pieces, edge_ref, h_ref, held = refs
+    ready()
+    x_at, core_at, tp_at = at_ref[0], at_ref[1], at_ref[2]
+    tokens, features = pieces[0].shape
+    x_size, z_size, core_size = SIZES
+    for d, piece in enumerate(pieces):
+        held[:tokens, d * features : (d + 1) * features] = piece[...]
+    held[tokens:] = edge_ref[...]
+    wide = h_ref.shape[1]
+    each = features // block_rows
+    lane = iota((8, wide), 1)
+    block = lane // block_rows
+    source = lane - block * block_rows
+    count = 0
+    for turn in range(core_size):
+        for d in range(x_size):
+            chip = ((x_at + x_size - d) & (x_size - 1)) * z_size
+            for z in range(z_size):
+                model = order_ref[(chip + z) * core_size + (core_at ^ turn)]
+                piece = (tp_at + len(pieces) - model // each) & (len(pieces) - 1)
+                base = (piece * each + (model & (each - 1))) * block_rows
+                source = source + jnp.where(block == count, base, 0)
+                count += 1
+    for at in range(0, wide, 256):
+        total = jnp.zeros((h_ref.shape[0], 256), F32)
+        for k in range(0, wide, features):
+            match = iota((features, 256), 0) + k == source[:1, at : at + 256]
+            total = total + dot(held[:, k : k + features], match.astype(F32).astype(BF16))
+        h_ref[:, at : at + 256] = total.astype(BF16)
+
+
+def early_body(head_dim, ready, sems, first_ref, ends_ref, *refs):
+    *blocks, h_ref, conv_value, conv_shared, bias, a_log = refs[:-8]
     x_ref, b_ref, dt_ref, cum_ref, sent_ref, held, rows, lines = refs[-8:]
     tokens, inner = x_ref.shape
-    gather_blocks(blocks, held)
+    copies = fetch(blocks, held, sems, slice(0, held.shape[1]))
+    ready()
+    for copy in copies:
+        copy.wait()
     for at in range(0, held.shape[1], 256):
-        rows[:, at : at + 256] = dot(h_ref[...], held[:, at : at + 256]).astype(BF16).astype(F32)
+        part = dot(h_ref[...], held[:, at : at + 256]).astype(BF16).astype(F32)
+        rows[EDGE:, at : at + 256] = part[:tokens]
+        rows[:EDGE, at : at + 256] = part[tokens:]
     first = first_ref[0]
     positions = first + iota((tokens, 128), 0)
     start = prompt_start(ends_ref, positions)
@@ -152,7 +235,8 @@
     sent_ref[...] = lines[...].astype(BF16)
 
 
-def scan_body(head_dim, inner, copies, sent_ref, out_ref, lines):
+def scan_body(head_dim, inner, copies, ready, sems, sent_ref, out_ref, lines):
+    ready()
     lines[...] = sent_ref[...].astype(F32)
     count = lines.shape[0] // LINES
     tiles = inner // 128
@@ -180,22 +264,21 @@
     out_ref[...] = lines[...].astype(BF16)
 
 
-def middle_body(head_dim, first_ref, ends_ref, h_ref, *refs):
-    *blocks, conv_shared, x_ref, b_ref, dt_ref, cum_ref, skip = refs[:-7]
-    direct_ref, carry_ref, c_ref, out_w_ref, held, c_rows, gate = refs[-7:]
+def middle_body(head_dim, ready, sems, first_ref, ends_ref, *refs):
+    *blocks, h_ref, conv_shared, x_ref, b_ref, dt_ref, cum_ref, skip = refs[:-6]
+    direct_ref, carry_ref, c_ref, held, c_rows, gate = refs[-6:]
     tokens, inner = x_ref.shape
-    gather_blocks(blocks, held)
     wide = held.shape[1]
-    half = len(blocks) // 2
-    depth = blocks[0].shape[0]
-    for i in range(half):
-        for j, block in enumerate((blocks[i], blocks[half + i])):
-            at = (2 * i + j) * depth
-            out_w_ref[at : at + depth] = block[:, wide:]
+    copies = fetch(blocks, held, sems, slice(0, wide))
+    ready()
+    for copy in copies:
+        copy.wait()
     for at in range(0, inner, 256):
-        g = dot(h_ref[EDGE:], held[:, at : at + 256])
+        g = dot(h_ref[:tokens], held[:, at : at + 256])
         gate[:, at : at + 256] = silu(g.astype(BF16).astype(F32))
-    c_rows[...] = dot(h_ref[...], held[:, inner:]).astype(BF16).astype(F32)
+    part = dot(h_ref[...], held[:, inner:]).astype(BF16).astype(F32)
+    c_rows[EDGE:] = part[:tokens]
+    c_rows[:EDGE] = part[tokens:]
     first = first_ref[0]
     positions = first + iota((tokens, 128), 0)
     start = prompt_start(ends_ref, positions)
@@ -225,8 +308,13 @@
         direct_ref[:, cut] = direct * gate[:, cut]
 
 
-def last_body(turn_ref, direct_ref, carry_ref, c_ref, carried_ref, out_w_ref, gain, *refs):
-    *outs, held, lines, shares = refs
+def last_body(ready, sems, turn_ref, *refs):
+    *blocks, carried_ref, direct_ref, carry_ref, c_ref, gain = refs[:-8]
+    *outs, held, lines, shares, out_w = refs[-8:]
+    half, wide = len(blocks) // 2, blocks[0].shape[1]
+    order = [i + half * j for i in range(half) for j in (0, 1)]
+    copies = fetch(blocks, out_w, sems, slice(wide - out_w.shape[1], wide), order=order)
+    ready()
     tokens, inner = direct_ref.shape
     lines[...] = carried_ref[...].astype(F32)
     count = lines.shape[0] // LINES
@@ -240,8 +328,10 @@
     scaled = (gated * gain[...]).astype(BF16)
     nt = (((1,), (1,)), ((), ()))
     features = shares.shape[2]
+    for copy in copies:
+        copy.wait()
     for i in range(shares.shape[0]):
-        rows = out_w_ref[i * features : (i + 1) * features]
+        rows = out_w[i * features : (i + 1) * features]
         shares[i] = lax.dot_general(scaled, rows, nt, preferred_element_type=F32).astype(BF16)
     squares = lax.dot_general(
         jnp.ones((8, inner), F32),
@@ -295,39 +385,32 @@
 
     tie = lax.optimization_barrier
 
-    before = lax.ppermute(
-        hidden_in[tokens - EDGE :], SEQ, [(i, i + 1) for i in range(seq_count - 1)]
-    )
+    pieces = [hidden_in] + [ahead(hidden_in, "tp", d) for d in range(1, tp_count)]
     packed = pack(w_in_value, w_in_shared, w_in_step, w_in_gate, w_out.T)
-    packed, before = tie((packed, before))
     along_z = lax.all_gather(packed, "z", axis=0, tiled=True)
     early_width = packed.shape[1] - 2 * inner - state
     own = x_all(along_z[:, :early_width])
     late = along_z[:, early_width:]
-    mine = jnp.concatenate([before, hidden_in], axis=0)
-    hidden = jnp.concatenate([mine] + [ahead(mine, "tp", d) for d in range(1, tp_count)], axis=1)
-
-    chips = jnp.concatenate(
-        [
-            (x_at - d) % x_size * z_size + jnp.arange(z_size, dtype=jnp.int32)
-            for d in range(x_size)
-        ]
-    )
-    stored = jnp.concatenate([chips * core_size + core_at, chips * core_size + 1 - core_at])
-    blocks_each = seq_count // tp_count
-    model = jnp.take(row_blocks, stored)
-    place = (tp_at - model // blocks_each) % tp_count * blocks_each + model % blocks_each
-    h = jnp.take(hidden.reshape(hidden.shape[0], seq_count, rows_here), place, axis=1)
-    h = h.reshape(hidden.shape[0], -1)
+    edge = jnp.concatenate([piece[tokens - EDGE :] for piece in pieces], axis=1)
+    edge = lax.ppermute(edge, SEQ, [(i, i + 1) for i in range(seq_count - 1)])
+    rows, model_width = tokens + EDGE, features * tp_count
+    (h,) = call(
+        functools.partial(arrange_body, rows_here),
+        [((rows, model_width), BF16)],
+        [jnp.stack([x_at, core_at, tp_at]), row_blocks] + pieces + [edge],
+        scalars=2,
+        scratch=[((rows, model_width), BF16)],
+        flops=2 * rows * model_width * model_width,
+    )
     own[-1], h, late = tie((own[-1], h, late))
     other = [ahead(block, "core", 1) for block in own]
     late_own = x_all(late)
+
     def lanes(row):
         return jnp.pad(row, (0, -row.shape[0] % 128))[None]
 
     first = jnp.reshape(seq_at * tokens, (1,))
     doc_ends = jnp.cumsum(prompt_lengths)
-    rows, model_width = h.shape
     copies = state // seq_count
     x_rows, b_half, steps, cumulative, sent = call(
         functools.partial(early_body, head_dim),
@@ -338,8 +421,9 @@
             ((tokens, 128), F32),
             ((seq_count * LINES, 128), BF16),
         ],
-        [first, doc_ends, h] + own + other + [conv_value, conv_shared, lanes(dt_bias), lanes(a_log)],
+        [first, doc_ends] + own + other + [h, conv_value, conv_shared, lanes(dt_bias), lanes(a_log)],
         scalars=2,
+        blocks=len(own + other),
         scratch=[
             ((model_width, early_width), BF16),
             ((rows, early_width), F32),
@@ -348,29 +432,31 @@
         flops=2 * rows * model_width * early_width,
     )
     received = lax.all_to_all(sent.reshape(seq_count, LINES, 128), SEQ, 0, 0, tiled=True)
-    received, late_own = tie((received, late_own))
     (scanned,) = call(
         functools.partial(scan_body, head_dim, inner, copies),
         [((seq_count * LINES, 128), BF16)],
         [received.reshape(seq_count * LINES, 128)],
+        near_in=1,
+        grant=40,
         scratch=[((seq_count * LINES, 128), F32)],
     )
     carried = lax.all_to_all(scanned.reshape(seq_count, LINES, 128), SEQ, 0, 0, tiled=True)
     carried = carried.reshape(seq_count * LINES, 128)
     late_other = [ahead(block, "core", 1) for block in late_own]
-    direct, carry, c_half, out_w = call(
+    direct, carry, c_half = call(
         functools.partial(middle_body, head_dim),
         [
             ((tokens, inner), F32),
             ((tokens, inner), F32),
             ((tokens, state), BF16),
-            ((model_width, inner), BF16),
         ],
-        [first, doc_ends, h]
+        [first, doc_ends]
         + late_own
         + late_other
-        + [conv_shared, x_rows, b_half, steps, cumulative, jnp.repeat(skip_gain, head_dim)[None]],
+        + [h, conv_shared, x_rows, b_half, steps, cumulative, jnp.repeat(skip_gain, head_dim)[None]],
         scalars=2,
+        blocks=len(late_own + late_other),
+        near_out=3,
         scratch=[
             ((model_width, inner + state), BF16),
             ((rows, state), F32),
@@ -383,18 +469,22 @@
         [((tokens + 8, features), BF16)] * tp_count,
         [
             jnp.reshape(x_at - tp_at + tp_count, (1,)),
+            *late_own,
+            *late_other,
+            carried,
             direct,
             carry,
             c_half,
-            carried,
-            out_w,
             norm_gain[None],
         ],
         scalars=1,
+        blocks=len(late_own + late_other),
+        near_in=4,
         scratch=[
             ((state, inner), BF16),
             ((seq_count * LINES, 128), F32),
             ((tp_count, tokens, features), BF16),
+            ((model_width, inner), BF16),
         ],
         flops=2 * tokens * inner * model_width,
     )

time: 141 us -> 136 us (0.965)
  local copies, waits for them, and re-layouts: 23.7 us -> 6.09 us
  Pallas kernels: 15.4 us -> 27.2 us
  waiting for transfers between devices: 21.3 us -> 23.7 us
    unnamed x53 -> x38, local copies, waits for them, and re-layouts: 16.2 us -> 3.45 us
    pallas_call x4 -> x5, Pallas kernels: 13.7 us -> 25.5 us  [call(): pl.pallas_call(wrapped, out_shape=[jax.ShapeDtypeStruct(shape, kind) for...]
    gather x3 -> x0, local copies, waits for them, and re-layouts: 6.15 us -> none  [the longest x2 5.37 us: on_device(): jnp.take(hidden.reshape(hidden.shape[0], seq_count, rows_here), place, ax...]
    ppermute x20, starting transfers between devices: 27.6 us -> 32 us  [ahead(): lax.ppermute(block, axis, [(i, (i + distance) % count) for i in range(cou...]
    ppermute x1, starting transfers between devices: 4.94 us -> 2.18 us  [on_device(): edge = lax.ppermute(edge, SEQ, [(i, i + 1) for i in range(seq_count - 1)])]
    all_to_all x1, waiting for transfers between devices: 0.01 us -> 2.72 us  [on_device(): lax.all_to_all(scanned.reshape(seq_count, LINES, 128), SEQ, 0, 0, tiled=T...]
    all_to_all x1, starting transfers between devices: 9.13 us -> 7.35 us  [on_device(): lax.all_to_all(sent.reshape(seq_count, LINES, 128), SEQ, 0, 0, tiled=True)]
    all_to_all x1, waiting for transfers between devices: 1.5 us -> 0.01 us  [on_device(): lax.all_to_all(sent.reshape(seq_count, LINES, 128), SEQ, 0, 0, tiled=True)]
  transfers between devices with their start and end apart: 23 -> 23, of which waited for: 5 -> 5; matrix products, arithmetic and copies ran while one was open for 8% -> 3% of each run, Pallas kernels for 10% -> 16%
where the time goes in v7:
time: 136 us; the launch traced here: 135 us
  starting transfers between devices  49.2 us (36%)
  Pallas kernels  27.2 us (20%)
  blocking collectives  25.3 us (19%)
  waiting for transfers between devices  23.7 us (17%)
  local copies, waits for them, and re-layouts  6.09 us (4%)
  other arithmetic  2.3 us (2%)
    ppermute x20, starting transfers between devices, ahead(): lax.ppermute(block, axis, [(i, (i + distance) % count) for i in range(cou...  32 us
    pallas_call x5, Pallas kernels, call(): pl.pallas_call(wrapped, out_shape=[jax.ShapeDtypeStruct(shape, kind) for...  25.5 us
    all_gather x1, blocking collectives, on_device(): along_z = lax.all_gather(packed, 'z', axis=0, tiled=True)  25.3 us
    ppermute x20, waiting for transfers between devices, ahead(): lax.ppermute(block, axis, [(i, (i + distance) % count) for i in range(cou...  20.7 us
    all_to_all x1, starting transfers between devices, on_device(): lax.all_to_all(scanned.reshape(seq_count, LINES, 128), SEQ, 0, 0, tiled=T...  7.69 us
    all_to_all x1, starting transfers between devices, on_device(): lax.all_to_all(sent.reshape(seq_count, LINES, 128), SEQ, 0, 0, tiled=True)  7.35 us
    unnamed x38, local copies, waits for them, and re-layouts  3.45 us
    all_to_all x1, waiting for transfers between devices, on_device(): lax.all_to_all(scanned.reshape(seq_count, LINES, 128), SEQ, 0, 0, tiled=T...  2.72 us
  transfers between devices with their start and end apart: 23, of which 5 were waited for; matrix products, arithmetic and copies ran while one was open for 3% of the time, Pallas kernels for 16%

profile of v7, /device:TPU:1, one launch (start us, length us, event | category | flops | bytes accessed | tf_op | source)
XLA Modules:
  0.0 135.2 jit_solution(6902802402026732396)
XLA Ops:
  0.0 2.1 %collective-permute-start.1 = (bf16[256,384]{1,0:T(8,128)(2,1)}, bf16[256,384]{1,0:T(8,128)(2,1)S(1)}, u32[]{:S(2)}, u32[]{:S(2)}) collective-permute-start(bf16[256,384]{1,0:T(8,128)(2,1)} %refs_2_.1), channel_id=1, source_target_pairs={{0,1},{1,2},{2,3},{3,0},{4,5},{5,6},{6,7},{7,4},{8,9},{9,10},{10,1... | collective-permute-start | bytes 589832 | tf_op jit(solution)/shard_map/ppermute | solution.py:21
  2.1 2.6 %collective-permute-start.2 = (bf16[256,384]{1,0:T(8,128)(2,1)}, bf16[256,384]{1,0:T(8,128)(2,1)S(1)}, u32[]{:S(2)}, u32[]{:S(2)}) collective-permute-start(bf16[256,384]{1,0:T(8,128)(2,1)} %refs_2_.1), channel_id=1, source_target_pairs={{0,2},{1,3},{2,0},{3,1},{4,6},{5,7},{6,4},{7,5},{8,10},{9,11},{10,... | collective-permute-start | bytes 589832 | tf_op jit(solution)/shard_map/ppermute | solution.py:21
  4.7 1.1 collective-permute-start.3
  5.8 1.7 %shard_map.136 = bf16[24,2688]{1,0:T(8,128)(2,1)} custom-call(f32[24,768]{1,0:T(8,128)} %value_ref.1, f32[24,256]{1,0:T(8,128)} %shared_ref.1, f32[12,24]{1,0:T(8,128)} %bitcast.22, f32[24,768]{1,0:T(8,128)} %gate_ref.1, f32[24,768]{1,0:T(8,128)} %bitcast.21), custom_call_target="tpu_custom_call" | custom-call | tf_op jit(solution)/shard_map/pallas_call | solution.py:45
  7.5 25.3 %all_gather.3 = bf16[192,2688]{1,0:T(8,128)(2,1)S(1)} all-gather(bf16[24,2688]{1,0:T(8,128)(2,1)} %shard_map.136), channel_id=1, replica_groups=mesh['x'=4,'z'=8,'core'=2,'tp'=4] {'z'}, dimensions={0}, use_global_device_ids=true | all-gather | bytes 1161216 | tf_op jit(solution)/shard_map/all_gather | solution.py:390
  32.9 2.6 %collective-permute-start = (bf16[192,1024]{1,0:T(8,128)(2,1)S(1)}, bf16[192,1024]{1,0:T(8,128)(2,1)S(1)}, u32[]{:S(2)}, u32[]{:S(2)}) collective-permute-start(bf16[192,1024]{1,0:T(8,128)(2,1)S(1)} %slice.36.refs_2_), channel_id=1, source_target_pairs={{0,192},{64,0},{128,64},{192,128},{1,193},{65,1},{129,65},{193,129... | collective-permute-start | bytes 1179656 | tf_op jit(solution)/shard_map/ppermute | solution.py:21
  35.5 0.7 slice.28
  36.2 1.7 %collective-permute-start.13 = (bf16[192,1024]{1,0:T(8,128)(2,1)S(1)}, bf16[192,1024]{1,0:T(8,128)(2,1)}, u32[]{:S(2)}, u32[]{:S(2)}) collective-permute-start(bf16[192,1024]{1,0:T(8,128)(2,1)S(1)} %slice.36.refs_2_), channel_id=1, source_target_pairs={{0,128},{64,192},{128,0},{192,64},{1,129},{65,193},{129,1},{193,65... | collective-permute-start | bytes 1179656 | tf_op jit(solution)/shard_map/ppermute | solution.py:21
  37.9 7.9 %collective-permute-start.14 = (bf16[192,1024]{1,0:T(8,128)(2,1)S(1)}, bf16[192,1024]{1,0:T(8,128)(2,1)S(1)}, u32[]{:S(2)}, u32[]{:S(2)}) collective-permute-start(bf16[192,1024]{1,0:T(8,128)(2,1)S(1)} %slice.36.refs_2_), channel_id=1, source_target_pairs={{0,4},{4,0},{1,5},{5,1},{2,6},{6,2},{3,7},{7,3},{8,12},{12,8},{9,1... | collective-permute-start | bytes 1179656 | tf_op jit(solution)/shard_map/ppermute | solution.py:21
  45.8 2.2 %collective-permute-start.4 = (bf16[8,1536]{1,0:T(8,128)(2,1)S(1)}, bf16[8,1536]{1,0:T(8,128)(2,1)S(1)}, u32[]{:S(2)}, u32[]{:S(2)}) collective-permute-start(bf16[8,1536]{1,0:T(8,128)(2,1)S(1)} %pad_maximum_fusion), channel_id=1, source_target_pairs={{0,4},{4,8},{8,12},{12,16},{16,20},{20,24},{24,28},{28,32},{32,36}... | collective-permute-start | bytes 73736 | tf_op jit(solution)/shard_map/ppermute | solution.py:395
  49.5 5.2 %shard_map.137.refs_10_ = bf16[264,1536]{1,0:T(8,128)(2,1)} custom-call(s32[3]{0:T(128)} %pad_add_fusion.refs_0_, s32[64]{0:T(128)} %refs_1_.1, bf16[256,384]{1,0:T(8,128)(2,1)} %refs_2_.1, bf16[256,384]{1,0:T(8,128)(2,1)} %copy-done.14, bf16[256,384]{1,0:T(8,128)(2,1)} %copy-done.15, bf16[256,384]{1,0:T(8,128)(2,1)} %copy-done.16, bf16[8,1536]{1,0:T(8,128)(2,1)} %copy-done.17), custom_call_target="tpu_custom_call" | custom-call | flops 1245708288 | bytes 811276 | tf_op jit(solution)/shard_map/pallas_call | solution.py:93
  55.1 1.6 %collective-permute-start.15 = (bf16[192,1024]{1,0:T(8,128)(2,1)S(1)}, bf16[192,1024]{1,0:T(8,128)(2,1)}, u32[]{:S(2)}, u32[]{:S(2)}) collective-permute-start(bf16[192,1024]{1,0:T(8,128)(2,1)S(1)} %collective-permute-done.12.refs_3_), channel_id=1, source_target_pairs={{0,4},{4,0},{1,5},{5,1},{2,6},{6,2},{3,7},{7,3},{8,12},{12,8},{9,1... | collective-permute-start | bytes 1179656 | tf_op jit(solution)/shard_map/ppermute | solution.py:21
  56.7 4.2 %collective-permute-start.6 = (bf16[192,1664]{1,0:T(8,128)(2,1)S(1)}, bf16[192,1664]{1,0:T(8,128)(2,1)S(1)}, u32[]{:S(2)}, u32[]{:S(2)}) collective-permute-start(bf16[192,1664]{1,0:T(8,128)(2,1)S(1)} %slice.40.refs_2_.refs_1_), channel_id=1, source_target_pairs={{0,128},{64,192},{128,0},{192,64},{1,129},{65,193},{129,1},{193,65... | collective-permute-start | bytes 1916936 | tf_op jit(solution)/shard_map/ppermute | solution.py:21
  60.9 2.7 %collective-permute-start.7 = (bf16[192,1664]{1,0:T(8,128)(2,1)S(1)}, bf16[192,1664]{1,0:T(8,128)(2,1)S(1)}, u32[]{:S(2)}, u32[]{:S(2)}) collective-permute-start(bf16[192,1664]{1,0:T(8,128)(2,1)S(1)} %slice.40.refs_2_.refs_1_), channel_id=1, source_target_pairs={{0,192},{64,0},{128,64},{192,128},{1,193},{65,1},{129,65},{193,129... | collective-permute-start | bytes 1916936 | tf_op jit(solution)/shard_map/ppermute | solution.py:21
  64.3 0.7 reduce-window.9
  65.5 6.7 %shard_map.138 = (bf16[256,768]{1,0:T(8,128)(2,1)}, bf16[256,128]{1,0:T(8,128)(2,1)}, f32[256,128]{1,0:T(8,128)}, f32[256,128]{1,0:T(8,128)}, bf16[1024,128]{1,0:T(8,128)(2,1)}) custom-call(s32[1]{0:T(128)} %bitcast.6.refs_0_, s32[8]{0:T(128)} %bitcast.23, bf16[192,1024]{1,0:T(8,128)(2,1)} %copy-done.5, bf16[192,1024]{1,0:T(8,128)(2,1)} %copy-done.8, ...), custom_call_target="tpu_custom_call" | custom-call | flops 830472192 | bytes 3974180 | tf_op jit(solution)/shard_map/pallas_call | solution.py:93
  72.2 7.4 %all-to-all-start = ((bf16[64,16,128]{2,1,0:T(8,128)(2,1)}), bf16[64,16,128]{2,1,0:T(8,128)(2,1)S(1)}, u32[]{:S(2)}, u32[]{:S(2)}) async-start(bf16[64,16,128]{2,1,0:T(8,128)(2,1)} %bitcast.20), calls=%async_computation | async-start | bytes 524288 | tf_op jit(solution)/shard_map/all_to_all | solution.py:434
  80.2 11.6 %collective-permute-done.7.refs_5_.refs_4_ = bf16[192,1664]{1,0:T(8,128)(2,1)S(1)} collective-permute-done((bf16[192,1664]{1,0:T(8,128)(2,1)S(1)}, bf16[192,1664]{1,0:T(8,128)(2,1)S(1)}, u32[]{:S(2)}, u32[]{:S(2)}) %collective-permute-start.7) | collective-permute-done | bytes 639008 | tf_op jit(solution)/shard_map/ppermute | solution.py:21
  91.8 1.1 collective-permute-start.11
  93.0 1.4 %shard_map.139 = bf16[1024,128]{1,0:T(8,128)(2,1)} custom-call(bf16[1024,128]{1,0:T(8,128)(2,1)S(1)} %bitcast.18), custom_call_target="tpu_custom_call" | custom-call | bytes 262144 | tf_op jit(solution)/shard_map/pallas_call | solution.py:93
  94.4 7.7 %all-to-all-start.1 = ((bf16[64,16,128]{2,1,0:T(8,128)(2,1)}), bf16[64,16,128]{2,1,0:T(8,128)(2,1)S(1)}, u32[]{:S(2)}, u32[]{:S(2)}) async-start(bf16[64,16,128]{2,1,0:T(8,128)(2,1)} %bitcast.13), calls=%async_computation.1 | async-start | bytes 524288 | tf_op jit(solution)/shard_map/all_to_all | solution.py:443
  102.9 0.7 broadcast_in_dim_reshape.3.refs_16_
  104.2 0.8 copy-done.4
  105.0 6.4 %shard_map.140 = (f32[256,768]{1,0:T(8,128)}, f32[256,768]{1,0:T(8,128)}, bf16[256,128]{1,0:T(8,128)(2,1)}) custom-call(s32[1]{0:T(128)} %bitcast.6.refs_0_, s32[8]{0:T(128)} %bitcast.24, bf16[192,1664]{1,0:T(8,128)(2,1)} %copy-done, bf16[192,1664]{1,0:T(8,128)(2,1)} %copy-done.3, bf16[192,1664]{1,0:T(8,128)(2,1)} %copy-done.1, bf16[192,1664]{1,0:T(8,128)(2,1)} %copy-done.2, ...), custom_call_target="tpu_custom_call" | custom-call | flops 726663168 | bytes 6650916 | tf_op jit(solution)/shard_map/pallas_call | solution.py:93
  111.4 2.7 %all-to-all-done.1 = bf16[64,16,128]{2,1,0:T(8,128)(2,1)S(1)} async-done(((bf16[64,16,128]{2,1,0:T(8,128)(2,1)}), bf16[64,16,128]{2,1,0:T(8,128)(2,1)S(1)}, u32[]{:S(2)}, u32[]{:S(2)}) %all-to-all-start.1) | async-done | bytes 262176 | tf_op jit(solution)/shard_map/all_to_all | solution.py:443
  114.1 0.7 copy-done.6
  114.8 5.7 %shard_map.141 = (bf16[264,384]{1,0:T(8,128)(2,1)}, bf16[264,384]{1,0:T(8,128)(2,1)}, bf16[264,384]{1,0:T(8,128)(2,1)}, bf16[264,384]{1,0:T(8,128)(2,1)}) custom-call(s32[1]{0:T(128)} %bitcast.refs_0_, bf16[192,1664]{1,0:T(8,128)(2,1)} %copy-done, bf16[192,1664]{1,0:T(8,128)(2,1)} %copy-done.3, bf16[192,1664]{1,0:T(8,128)(2,1)} %copy-done.1, ...), custom_call_target="tpu_custom_call" | custom-call | flops 603979776 | bytes 7015428 | tf_op jit(solution)/shard_map/pallas_call | solution.py:93
  120.6 0.9 collective-permute-start.18
  121.8 2.1 %collective-permute-start.20 = (bf16[264,384]{1,0:T(8,128)(2,1)}, bf16[264,384]{1,0:T(8,128)(2,1)S(1)}, u32[]{:S(2)}, u32[]{:S(2)}) collective-permute-start(bf16[264,384]{1,0:T(8,128)(2,1)} %get-tuple-element.34), channel_id=1, source_target_pairs={{0,3},{1,0},{2,1},{3,2},{4,7},{5,4},{6,5},{7,6},{8,11},{9,8},{10,9... | collective-permute-start | bytes 608264 | tf_op jit(solution)/shard_map/ppermute | solution.py:21
  124.0 8.6 %collective-permute-done.18 = bf16[264,384]{1,0:T(8,128)(2,1)S(1)} collective-permute-done((bf16[264,384]{1,0:T(8,128)(2,1)}, bf16[264,384]{1,0:T(8,128)(2,1)S(1)}, u32[]{:S(2)}, u32[]{:S(2)}) %collective-permute-start.18) | collective-permute-done | bytes 202784 | tf_op jit(solution)/shard_map/ppermute | solution.py:21
  133.1 1.0 convert_add_fusion
  134.1 1.1 convolution_convert_fusion
  (76 shorter events, 6.1 us)
Async XLA Ops:
  0.0 36.2 %collective-permute-start.1 = (bf16[256,384]{1,0:T(8,128)(2,1)}, bf16[256,384]{1,0:T(8,128)(2,1)S(1)}, u32[]{:S(2)}, u32[]{:S(2)}) collective-permute-start(bf16[256,384]{1,0:T(8,128)(2,1)} %refs_2_.1), channel_id=1, source_target_pairs={{0,1},{1,2},{2,3},{3,0},{4,5},{5,6},{6,7},{7,4},{8,9},{9,10},{10,1... | collective-permute-start | bytes 589832 | tf_op jit(solution)/shard_map/ppermute | solution.py:21
  2.1 35.8 %collective-permute-start.2 = (bf16[256,384]{1,0:T(8,128)(2,1)}, bf16[256,384]{1,0:T(8,128)(2,1)S(1)}, u32[]{:S(2)}, u32[]{:S(2)}) collective-permute-start(bf16[256,384]{1,0:T(8,128)(2,1)} %refs_2_.1), channel_id=1, source_target_pairs={{0,2},{1,3},{2,0},{3,1},{4,6},{5,7},{6,4},{7,5},{8,10},{9,11},{10,... | collective-permute-start | bytes 589832 | tf_op jit(solution)/shard_map/ppermute | solution.py:21
  4.7 41.0 %collective-permute-start.3 = (bf16[256,384]{1,0:T(8,128)(2,1)}, bf16[256,384]{1,0:T(8,128)(2,1)S(1)}, u32[]{:S(2)}, u32[]{:S(2)}) collective-permute-start(bf16[256,384]{1,0:T(8,128)(2,1)} %refs_2_.1), channel_id=1, source_target_pairs={{0,3},{1,0},{2,1},{3,2},{4,7},{5,4},{6,5},{7,6},{8,11},{9,8},{10,9... | collective-permute-start | bytes 589832 | tf_op jit(solution)/shard_map/ppermute | solution.py:21
  32.9 15.7 %copy-start.5 = (bf16[192,1024]{1,0:T(8,128)(2,1)}, bf16[192,1024]{1,0:T(8,128)(2,1)S(1)}, u32[]{:S(2)}) copy-start(bf16[192,1024]{1,0:T(8,128)(2,1)S(1)} %slice.36.refs_2_) | copy-start | bytes 1179652
  32.9 21.9 %collective-permute-start = (bf16[192,1024]{1,0:T(8,128)(2,1)S(1)}, bf16[192,1024]{1,0:T(8,128)(2,1)S(1)}, u32[]{:S(2)}, u32[]{:S(2)}) collective-permute-start(bf16[192,1024]{1,0:T(8,128)(2,1)S(1)} %slice.36.refs_2_), channel_id=1, source_target_pairs={{0,192},{64,0},{128,64},{192,128},{1,193},{65,1},{129,65},{193,129... | collective-permute-start | bytes 1179656 | tf_op jit(solution)/shard_map/ppermute | solution.py:21
  35.5 19.6 %collective-permute-start.12 = (bf16[192,1024]{1,0:T(8,128)(2,1)S(1)}, bf16[192,1024]{1,0:T(8,128)(2,1)S(1)}, u32[]{:S(2)}, u32[]{:S(2)}) collective-permute-start(bf16[192,1024]{1,0:T(8,128)(2,1)S(1)} %slice.36.refs_2_), channel_id=1, source_target_pairs={{0,64},{64,128},{128,192},{192,0},{1,65},{65,129},{129,193},{193,1... | collective-permute-start | bytes 1179656 | tf_op jit(solution)/shard_map/ppermute | solution.py:21
  36.2 12.5 %copy-start.14 = (bf16[256,384]{1,0:T(8,128)(2,1)}, bf16[256,384]{1,0:T(8,128)(2,1)S(1)}, u32[]{:S(2)}) copy-start(bf16[256,384]{1,0:T(8,128)(2,1)S(1)} %collective-permute-done.1.refs_3_) | copy-start | bytes 589828
  36.2 20.5 %collective-permute-start.13 = (bf16[192,1024]{1,0:T(8,128)(2,1)S(1)}, bf16[192,1024]{1,0:T(8,128)(2,1)}, u32[]{:S(2)}, u32[]{:S(2)}) collective-permute-start(bf16[192,1024]{1,0:T(8,128)(2,1)S(1)} %slice.36.refs_2_), channel_id=1, source_target_pairs={{0,128},{64,192},{128,0},{192,64},{1,129},{65,193},{129,1},{193,65... | collective-permute-start | bytes 1179656 | tf_op jit(solution)/shard_map/ppermute | solution.py:21
  37.9 10.7 %copy-start.15 = (bf16[256,384]{1,0:T(8,128)(2,1)}, bf16[256,384]{1,0:T(8,128)(2,1)S(1)}, u32[]{:S(2)}) copy-start(bf16[256,384]{1,0:T(8,128)(2,1)S(1)} %collective-permute-done.2.refs_4_) | copy-start | bytes 589828
  37.9 23.0 %collective-permute-start.14 = (bf16[192,1024]{1,0:T(8,128)(2,1)S(1)}, bf16[192,1024]{1,0:T(8,128)(2,1)S(1)}, u32[]{:S(2)}, u32[]{:S(2)}) collective-permute-start(bf16[192,1024]{1,0:T(8,128)(2,1)S(1)} %slice.36.refs_2_), channel_id=1, source_target_pairs={{0,4},{4,0},{1,5},{5,1},{2,6},{6,2},{3,7},{7,3},{8,12},{12,8},{9,1... | collective-permute-start | bytes 1179656 | tf_op jit(solution)/shard_map/ppermute | solution.py:21
  45.8 3.1 %collective-permute-start.4 = (bf16[8,1536]{1,0:T(8,128)(2,1)S(1)}, bf16[8,1536]{1,0:T(8,128)(2,1)S(1)}, u32[]{:S(2)}, u32[]{:S(2)}) collective-permute-start(bf16[8,1536]{1,0:T(8,128)(2,1)S(1)} %pad_maximum_fusion), channel_id=1, source_target_pairs={{0,4},{4,8},{8,12},{12,16},{16,20},{20,24},{24,28},{28,32},{32,36}... | collective-permute-start | bytes 73736 | tf_op jit(solution)/shard_map/ppermute | solution.py:395
  48.6 30.9 %copy-start = (bf16[192,1664]{1,0:T(8,128)(2,1)}, bf16[192,1664]{1,0:T(8,128)(2,1)S(1)}, u32[]{:S(2)}) copy-start(bf16[192,1664]{1,0:T(8,128)(2,1)S(1)} %slice.40.refs_2_.refs_1_) | copy-start | bytes 1916932
  54.8 10.7 %copy-start.7 = (bf16[192,1024]{1,0:T(8,128)(2,1)}, bf16[192,1024]{1,0:T(8,128)(2,1)S(1)}, u32[]{:S(2)}) copy-start(bf16[192,1024]{1,0:T(8,128)(2,1)S(1)} %collective-permute-done.refs_5_) | copy-start | bytes 1179652
  54.8 8.8 %collective-permute-start.17 = (bf16[192,1024]{1,0:T(8,128)(2,1)S(1)}, bf16[192,1024]{1,0:T(8,128)(2,1)}, u32[]{:S(2)}, u32[]{:S(2)}) collective-permute-start(bf16[192,1024]{1,0:T(8,128)(2,1)S(1)} %collective-permute-done.refs_5_), channel_id=1, source_target_pairs={{0,4},{4,0},{1,5},{5,1},{2,6},{6,2},{3,7},{7,3},{8,12},{12,8},{9,1... | collective-permute-start | bytes 1179656 | tf_op jit(solution)/shard_map/ppermute | solution.py:21
  55.1 10.4 %copy-start.8 = (bf16[192,1024]{1,0:T(8,128)(2,1)}, bf16[192,1024]{1,0:T(8,128)(2,1)S(1)}, u32[]{:S(2)}) copy-start(bf16[192,1024]{1,0:T(8,128)(2,1)S(1)} %collective-permute-done.12.refs_3_) | copy-start | bytes 1179652
  55.1 10.4 %collective-permute-start.15 = (bf16[192,1024]{1,0:T(8,128)(2,1)S(1)}, bf16[192,1024]{1,0:T(8,128)(2,1)}, u32[]{:S(2)}, u32[]{:S(2)}) collective-permute-start(bf16[192,1024]{1,0:T(8,128)(2,1)S(1)} %collective-permute-done.12.refs_3_), channel_id=1, source_target_pairs={{0,4},{4,0},{1,5},{5,1},{2,6},{6,2},{3,7},{7,3},{8,12},{12,8},{9,1... | collective-permute-start | bytes 1179656 | tf_op jit(solution)/shard_map/ppermute | solution.py:21
  56.6 8.9 %collective-permute-start.16 = (bf16[192,1024]{1,0:T(8,128)(2,1)}, bf16[192,1024]{1,0:T(8,128)(2,1)}, u32[]{:S(2)}, u32[]{:S(2)}) collective-permute-start(bf16[192,1024]{1,0:T(8,128)(2,1)} %collective-permute-done.13.refs_4_), channel_id=1, source_target_pairs={{0,4},{4,0},{1,5},{5,1},{2,6},{6,2},{3,7},{7,3},{8,12},{12,8},{9,1... | collective-permute-start | bytes 1179656 | tf_op jit(solution)/shard_map/ppermute | solution.py:21
  56.7 23.4 %collective-permute-start.6 = (bf16[192,1664]{1,0:T(8,128)(2,1)S(1)}, bf16[192,1664]{1,0:T(8,128)(2,1)S(1)}, u32[]{:S(2)}, u32[]{:S(2)}) collective-permute-start(bf16[192,1664]{1,0:T(8,128)(2,1)S(1)} %slice.40.refs_2_.refs_1_), channel_id=1, source_target_pairs={{0,128},{64,192},{128,0},{192,64},{1,129},{65,193},{129,1},{193,65... | collective-permute-start | bytes 1916936 | tf_op jit(solution)/shard_map/ppermute | solution.py:21
  60.9 30.9 %collective-permute-start.7 = (bf16[192,1664]{1,0:T(8,128)(2,1)S(1)}, bf16[192,1664]{1,0:T(8,128)(2,1)S(1)}, u32[]{:S(2)}, u32[]{:S(2)}) collective-permute-start(bf16[192,1664]{1,0:T(8,128)(2,1)S(1)} %slice.40.refs_2_.refs_1_), channel_id=1, source_target_pairs={{0,192},{64,0},{128,64},{192,128},{1,193},{65,1},{129,65},{193,129... | collective-permute-start | bytes 1916936 | tf_op jit(solution)/shard_map/ppermute | solution.py:21
  63.6 29.3 %collective-permute-start.5 = (bf16[192,1664]{1,0:T(8,128)(2,1)S(1)}, bf16[192,1664]{1,0:T(8,128)(2,1)S(1)}, u32[]{:S(2)}, u32[]{:S(2)}) collective-permute-start(bf16[192,1664]{1,0:T(8,128)(2,1)S(1)} %slice.40.refs_2_.refs_1_), channel_id=1, source_target_pairs={{0,64},{64,128},{128,192},{192,0},{1,65},{65,129},{129,193},{193,1... | collective-permute-start | bytes 1916936 | tf_op jit(solution)/shard_map/ppermute | solution.py:21
  72.2 20.8 %all-to-all-start = ((bf16[64,16,128]{2,1,0:T(8,128)(2,1)}), bf16[64,16,128]{2,1,0:T(8,128)(2,1)S(1)}, u32[]{:S(2)}, u32[]{:S(2)}) async-start(bf16[64,16,128]{2,1,0:T(8,128)(2,1)} %bitcast.20), calls=%async_computation | async-start | bytes 524288 | tf_op jit(solution)/shard_map/all_to_all | solution.py:434
  79.6 24.6 %collective-permute-start.8 = (bf16[192,1664]{1,0:T(8,128)(2,1)S(1)}, bf16[192,1664]{1,0:T(8,128)(2,1)S(1)}, u32[]{:S(2)}, u32[]{:S(2)}) collective-permute-start(bf16[192,1664]{1,0:T(8,128)(2,1)S(1)} %slice.40.refs_2_.refs_1_), channel_id=1, source_target_pairs={{0,4},{4,0},{1,5},{5,1},{2,6},{6,2},{3,7},{7,3},{8,12},{12,8},{9,1... | collective-permute-start | bytes 1916936 | tf_op jit(solution)/shard_map/ppermute | solution.py:21
  80.1 24.1 %copy-start.1 = (bf16[192,1664]{1,0:T(8,128)(2,1)}, bf16[192,1664]{1,0:T(8,128)(2,1)S(1)}, u32[]{:S(2)}) copy-start(bf16[192,1664]{1,0:T(8,128)(2,1)S(1)} %collective-permute-done.6.refs_4_.refs_3_) | copy-start | bytes 1916932
  80.1 24.0 %collective-permute-start.10 = (bf16[192,1664]{1,0:T(8,128)(2,1)S(1)}, bf16[192,1664]{1,0:T(8,128)(2,1)}, u32[]{:S(2)}, u32[]{:S(2)}) collective-permute-start(bf16[192,1664]{1,0:T(8,128)(2,1)S(1)} %collective-permute-done.6.refs_4_.refs_3_), channel_id=1, source_target_pairs={{0,4},{4,0},{1,5},{5,1},{2,6},{6,2},{3,7},{7,3},{8,12},{12,8},{9,1... | collective-permute-start | bytes 1916936 | tf_op jit(solution)/shard_map/ppermute | solution.py:21
  91.8 12.4 %copy-start.2 = (bf16[192,1664]{1,0:T(8,128)(2,1)}, bf16[192,1664]{1,0:T(8,128)(2,1)S(1)}, u32[]{:S(2)}) copy-start(bf16[192,1664]{1,0:T(8,128)(2,1)S(1)} %collective-permute-done.7.refs_5_.refs_4_) | copy-start | bytes 1916932
  91.8 12.3 %collective-permute-start.11 = (bf16[192,1664]{1,0:T(8,128)(2,1)S(1)}, bf16[192,1664]{1,0:T(8,128)(2,1)}, u32[]{:S(2)}, u32[]{:S(2)}) collective-permute-start(bf16[192,1664]{1,0:T(8,128)(2,1)S(1)} %collective-permute-done.7.refs_5_.refs_4_), channel_id=1, source_target_pairs={{0,4},{4,0},{1,5},{5,1},{2,6},{6,2},{3,7},{7,3},{8,12},{12,8},{9,1... | collective-permute-start | bytes 1916936 | tf_op jit(solution)/shard_map/ppermute | solution.py:21
  92.9 11.3 %copy-start.3 = (bf16[192,1664]{1,0:T(8,128)(2,1)}, bf16[192,1664]{1,0:T(8,128)(2,1)S(1)}, u32[]{:S(2)}) copy-start(bf16[192,1664]{1,0:T(8,128)(2,1)S(1)} %collective-permute-done.5.refs_3_.refs_2_) | copy-start | bytes 1916932
  92.9 11.3 %collective-permute-start.9 = (bf16[192,1664]{1,0:T(8,128)(2,1)S(1)}, bf16[192,1664]{1,0:T(8,128)(2,1)}, u32[]{:S(2)}, u32[]{:S(2)}) collective-permute-start(bf16[192,1664]{1,0:T(8,128)(2,1)S(1)} %collective-permute-done.5.refs_3_.refs_2_), channel_id=1, source_target_pairs={{0,4},{4,0},{1,5},{5,1},{2,6},{6,2},{3,7},{7,3},{8,12},{12,8},{9,1... | collective-permute-start | bytes 1916936 | tf_op jit(solution)/shard_map/ppermute | solution.py:21
  94.4 19.7 %all-to-all-start.1 = ((bf16[64,16,128]{2,1,0:T(8,128)(2,1)}), bf16[64,16,128]{2,1,0:T(8,128)(2,1)S(1)}, u32[]{:S(2)}, u32[]{:S(2)}) async-start(bf16[64,16,128]{2,1,0:T(8,128)(2,1)} %bitcast.13), calls=%async_computation.1 | async-start | bytes 524288 | tf_op jit(solution)/shard_map/all_to_all | solution.py:443
  120.6 12.0 %collective-permute-start.18 = (bf16[264,384]{1,0:T(8,128)(2,1)}, bf16[264,384]{1,0:T(8,128)(2,1)S(1)}, u32[]{:S(2)}, u32[]{:S(2)}) collective-permute-start(bf16[264,384]{1,0:T(8,128)(2,1)} %get-tuple-element.32), channel_id=1, source_target_pairs={{0,1},{1,2},{2,3},{3,0},{4,5},{5,6},{6,7},{7,4},{8,9},{9,10},{10,1... | collective-permute-start | bytes 608264 | tf_op jit(solution)/shard_map/ppermute | solution.py:21
  121.5 11.1 %collective-permute-start.19 = (bf16[264,384]{1,0:T(8,128)(2,1)}, bf16[264,384]{1,0:T(8,128)(2,1)S(1)}, u32[]{:S(2)}, u32[]{:S(2)}) collective-permute-start(bf16[264,384]{1,0:T(8,128)(2,1)} %get-tuple-element.33), channel_id=1, source_target_pairs={{0,2},{1,3},{2,0},{3,1},{4,6},{5,7},{6,4},{7,5},{8,10},{9,11},{10,... | collective-permute-start | bytes 608264 | tf_op jit(solution)/shard_map/ppermute | solution.py:21
  121.8 11.2 %collective-permute-start.20 = (bf16[264,384]{1,0:T(8,128)(2,1)}, bf16[264,384]{1,0:T(8,128)(2,1)S(1)}, u32[]{:S(2)}, u32[]{:S(2)}) collective-permute-start(bf16[264,384]{1,0:T(8,128)(2,1)} %get-tuple-element.34), channel_id=1, source_target_pairs={{0,3},{1,0},{2,1},{3,2},{4,7},{5,4},{6,5},{7,6},{8,11},{9,8},{10,9... | collective-permute-start | bytes 608264 | tf_op jit(solution)/shard_map/ppermute | solution.py:21
  (10 other events, 11.0 us)

commit v8 on v7

--- a/solution.py
+++ b/solution.py
@@ -121,11 +121,16 @@
     return dot(hi, head_of) + dot((x - hi.astype(F32)).astype(BF16), head_of)
 
 
-def prompt_start(ends_ref, positions):
-    start = jnp.zeros_like(positions)
-    for i in range(ends_ref.shape[0]):
-        start = jnp.maximum(start, jnp.where(positions >= ends_ref[i], ends_ref[i], 0))
+def prompt_start(lengths_ref, positions):
+    start, end = jnp.zeros_like(positions), 0
+    for i in range(lengths_ref.shape[0]):
+        end = end + lengths_ref[i]
+        start = jnp.maximum(start, jnp.where(positions >= end, end, 0))
     return start
+
+
+def lanes(row):
+    return jnp.pad(row, ((0, 0), (0, -row.shape[1] % 128)))
 
 
 def silu(x):
@@ -186,7 +191,7 @@
         h_ref[:, at : at + 256] = total.astype(BF16)
 
 
-def early_body(head_dim, ready, sems, first_ref, ends_ref, *refs):
+def early_body(head_dim, ready, sems, first_ref, lengths_ref, *refs):
     *blocks, h_ref, conv_value, conv_shared, bias, a_log = refs[:-8]
     x_ref, b_ref, dt_ref, cum_ref, sent_ref, held, rows, lines = refs[-8:]
     tokens, inner = x_ref.shape
@@ -200,18 +205,18 @@
         rows[:EDGE, at : at + 256] = part[tokens:]
     first = first_ref[0]
     positions = first + iota((tokens, 128), 0)
-    start = prompt_start(ends_ref, positions)
-    last_start = prompt_start(ends_ref, first + tokens - 1)
+    start = prompt_start(lengths_ref, positions)
+    last_start = prompt_start(lengths_ref, first + tokens - 1)
     for at in range(0, inner, 128):
         x_ref[:, at : at + 128] = convolve(
             rows, at, conv_value[:, at : at + 128], positions, start
         )
     b_half = convolve(rows, inner, conv_shared[:, :128], positions, start)
     b_ref[...] = b_half
-    raw = rows[EDGE:, inner + 128 :] + bias[...]
+    raw = rows[EDGE:, inner + 128 :] + lanes(bias[...])
     dt = jnp.maximum(raw, 0.0) + jnp.log1p(jnp.exp(-jnp.abs(raw)))
     below = (iota((tokens, tokens), 0) >= iota((tokens, tokens), 1)).astype(F32)
-    cum = dot(below, -dt * jnp.exp(a_log[...]), precision=lax.Precision.HIGHEST)
+    cum = dot(below, -dt * jnp.exp(lanes(a_log[...])), precision=lax.Precision.HIGHEST)
     dt_ref[...] = dt
     cum_ref[...] = cum
     last = cum[tokens - 1 :]
@@ -264,7 +269,7 @@
     out_ref[...] = lines[...].astype(BF16)
 
 
-def middle_body(head_dim, ready, sems, first_ref, ends_ref, *refs):
+def middle_body(head_dim, ready, sems, first_ref, lengths_ref, *refs):
     *blocks, h_ref, conv_shared, x_ref, b_ref, dt_ref, cum_ref, skip = refs[:-6]
     direct_ref, carry_ref, c_ref, held, c_rows, gate = refs[-6:]
     tokens, inner = x_ref.shape
@@ -281,7 +286,7 @@
     c_rows[:EDGE] = part[tokens:]
     first = first_ref[0]
     positions = first + iota((tokens, 128), 0)
-    start = prompt_start(ends_ref, positions)
+    start = prompt_start(lengths_ref, positions)
     c_half = convolve(c_rows, 0, conv_shared[:, 128:], positions, start)
     c_ref[...] = c_half
     scores = lax.dot_general(
@@ -295,7 +300,7 @@
     stepped = (spread(dt, head_of) * x_ref[...].astype(F32)).astype(BF16)
     cum_t = cum.T
     carry = jnp.where(start < first, jnp.exp(cum), 0.0)
-    carry_ref[...] = spread(carry, head_of) * gate[...]
+    carry_ref[...] = (spread(carry, head_of) * gate[...]).astype(BF16)
     each = 128 // head_dim
     for at in range(0, inner, 128):
         sums = []
@@ -305,15 +310,22 @@
             sums.append(dot(weights, stepped[:, h * head_dim : (h + 1) * head_dim]))
         cut = slice(at, at + 128)
         direct = jnp.concatenate(sums, axis=1) + skip[:, cut] * x_ref[:, cut].astype(F32)
-        direct_ref[:, cut] = direct * gate[:, cut]
+        direct_ref[:, cut] = (direct * gate[:, cut]).astype(BF16)
 
 
 def last_body(ready, sems, turn_ref, *refs):
     *blocks, carried_ref, direct_ref, carry_ref, c_ref, gain = refs[:-8]
     *outs, held, lines, shares, out_w = refs[-8:]
-    half, wide = len(blocks) // 2, blocks[0].shape[1]
-    order = [i + half * j for i in range(half) for j in (0, 1)]
-    copies = fetch(blocks, out_w, sems, slice(wide - out_w.shape[1], wide), order=order)
+    half, wide, inner = len(blocks) // 2, blocks[0].shape[2], out_w.shape[4]
+    copies = []
+    for i, block in enumerate(blocks):
+        copy = pltpu.make_async_copy(
+            block.at[:, :, wide - inner :],
+            out_w.at[i % half, :, turn_ref[1] ^ (i // half)],
+            sems.at[i],
+        )
+        copy.start()
+        copies.append(copy)
     ready()
     tokens, inner = direct_ref.shape
     lines[...] = carried_ref[...].astype(F32)
@@ -324,14 +336,15 @@
             cut = lines[pl.ds(line, count, stride=LINES), :]
             held[row : row + count, at : at + 128] = cut.astype(BF16)
             line += 1
-    gated = direct_ref[...] + carry_ref[...] * dot(c_ref[...], held[...])
+    direct, carry = direct_ref[...].astype(F32), carry_ref[...].astype(F32)
+    gated = direct + carry * dot(c_ref[...], held[...])
     scaled = (gated * gain[...]).astype(BF16)
     nt = (((1,), (1,)), ((), ()))
     features = shares.shape[2]
     for copy in copies:
         copy.wait()
     for i in range(shares.shape[0]):
-        rows = out_w[i * features : (i + 1) * features]
+        rows = out_w[i].reshape(features, inner)
         shares[i] = lax.dot_general(scaled, rows, nt, preferred_element_type=F32).astype(BF16)
     squares = lax.dot_general(
         jnp.ones((8, inner), F32),
@@ -406,11 +419,7 @@
     other = [ahead(block, "core", 1) for block in own]
     late_own = x_all(late)
 
-    def lanes(row):
-        return jnp.pad(row, (0, -row.shape[0] % 128))[None]
-
     first = jnp.reshape(seq_at * tokens, (1,))
-    doc_ends = jnp.cumsum(prompt_lengths)
     copies = state // seq_count
     x_rows, b_half, steps, cumulative, sent = call(
         functools.partial(early_body, head_dim),
@@ -421,7 +430,7 @@
             ((tokens, 128), F32),
             ((seq_count * LINES, 128), BF16),
         ],
-        [first, doc_ends] + own + other + [h, conv_value, conv_shared, lanes(dt_bias), lanes(a_log)],
+        [first, prompt_lengths] + own + other + [h, conv_value, conv_shared, dt_bias[None], a_log[None]],
         scalars=2,
         blocks=len(own + other),
         scratch=[
@@ -442,21 +451,21 @@
     )
     carried = lax.all_to_all(scanned.reshape(seq_count, LINES, 128), SEQ, 0, 0, tiled=True)
     carried = carried.reshape(seq_count * LINES, 128)
+    late_own, _ = tie((late_own, scanned))
     late_other = [ahead(block, "core", 1) for block in late_own]
     direct, carry, c_half = call(
         functools.partial(middle_body, head_dim),
         [
-            ((tokens, inner), F32),
-            ((tokens, inner), F32),
+            ((tokens, inner), BF16),
+            ((tokens, inner), BF16),
             ((tokens, state), BF16),
         ],
-        [first, doc_ends]
+        [first, prompt_lengths]
         + late_own
         + late_other
         + [h, conv_shared, x_rows, b_half, steps, cumulative, jnp.repeat(skip_gain, head_dim)[None]],
         scalars=2,
         blocks=len(late_own + late_other),
-        near_out=3,
         scratch=[
             ((model_width, inner + state), BF16),
             ((rows, state), F32),
@@ -468,9 +477,8 @@
         last_body,
         [((tokens + 8, features), BF16)] * tp_count,
         [
-            jnp.reshape(x_at - tp_at + tp_count, (1,)),
-            *late_own,
-            *late_other,
+            jnp.stack([x_at - tp_at + tp_count, core_at]),
+            *[block.reshape(z_size, rows_here, -1) for block in late_own + late_other],
             carried,
             direct,
             carry,
@@ -479,12 +487,11 @@
         ],
         scalars=1,
         blocks=len(late_own + late_other),
-        near_in=4,
         scratch=[
             ((state, inner), BF16),
             ((seq_count * LINES, 128), F32),
             ((tp_count, tokens, features), BF16),
-            ((model_width, inner), BF16),
+            ((x_size, z_size, core_size, rows_here, inner), BF16),
         ],
         flops=2 * tokens * inner * model_width,
     )
@@ -492,14 +499,7 @@
     summed = sum(part.astype(F32) for part in parts)
     total = summed[tokens, :tokens] + summed[tokens + 1, :tokens]
     scale = lax.rsqrt(total / (inner * tp_count) + EPSILON)
-    result = (summed[:tokens] * scale[:, None]).astype(BF16)
-
-    lane = jnp.arange(features, dtype=jnp.int32)
-    part, rest = lane // (z_size * rows_here), lane % (z_size * rows_here)
-    core_of = jnp.where(part == 0, core_at, 1 - core_at)
-    target = (rest // rows_here * core_size + core_of) * rows_here + rest % rows_here
-    moves = (target[:, None] == lane[None, :]).astype(BF16)
-    return jnp.dot(result, moves, preferred_element_type=F32).astype(BF16)
+    return (summed[:tokens] * scale[:, None]).astype(BF16)
 
 
 def solution(mesh):

time: 136 us -> 137 us (level)
  blocking collectives: 25.3 us -> 48.2 us
  waiting for transfers between devices: 23.7 us -> 12.8 us
  starting transfers between devices: 49.2 us -> 40.1 us
    all_to_all x0 -> x1, blocking collectives: none -> 22.9 us  [on_device(): lax.all_to_all(sent.reshape(seq_count, LINES, 128), SEQ, 0, 0, tiled=True)]
    ppermute x20, waiting for transfers between devices: 20.7 us -> 10.8 us  [ahead(): lax.ppermute(block, axis, [(i, (i + distance) % count) for i in range(cou...]
    all_to_all x1 -> x0, starting transfers between devices: 7.35 us -> none  [on_device(): lax.all_to_all(sent.reshape(seq_count, LINES, 128), SEQ, 0, 0, tiled=True)]
    ppermute x20, starting transfers between devices: 32 us -> 30 us  [ahead(): lax.ppermute(block, axis, [(i, (i + distance) % count) for i in range(cou...]
    unnamed x38 -> x32, local copies, waits for them, and re-layouts: 3.45 us -> 2.83 us
  transfers between devices with their start and end apart: 23 -> 22, of which waited for: 5 -> 4; matrix products, arithmetic and copies ran while one was open for 3% -> 2% of each run, Pallas kernels for 16% -> 16%
where the time goes in v8:
time: 137 us; the launch traced here: 136 us
  blocking collectives  48.2 us (35%)
  starting transfers between devices  40.1 us (29%)
  Pallas kernels  26.9 us (20%)
  waiting for transfers between devices  12.8 us (9%)
  local copies, waits for them, and re-layouts  4.92 us (4%)
  other arithmetic  3.13 us (2%)
    ppermute x20, starting transfers between devices, ahead(): lax.ppermute(block, axis, [(i, (i + distance) % count) for i in range(cou...  30 us
    all_gather x1, blocking collectives, on_device(): along_z = lax.all_gather(packed, 'z', axis=0, tiled=True)  25.3 us
    pallas_call x5, Pallas kernels, call(): pl.pallas_call(wrapped, out_shape=[jax.ShapeDtypeStruct(shape, kind) for...  25.1 us
    all_to_all x1, blocking collectives, on_device(): lax.all_to_all(sent.reshape(seq_count, LINES, 128), SEQ, 0, 0, tiled=True)  22.9 us
    ppermute x20, waiting for transfers between devices, ahead(): lax.ppermute(block, axis, [(i, (i + distance) % count) for i in range(cou...  10.8 us
    all_to_all x1, starting transfers between devices, on_device(): lax.all_to_all(scanned.reshape(seq_count, LINES, 128), SEQ, 0, 0, tiled=T...  7.95 us
    unnamed x32, local copies, waits for them, and re-layouts  2.83 us
  transfers between devices with their start and end apart: 22, of which 4 were waited for; matrix products, arithmetic and copies ran while one was open for 2% of the time, Pallas kernels for 16%

profile of v8, /device:TPU:1, one launch (start us, length us, event | category | flops | bytes accessed | tf_op | source)
XLA Modules:
  0.0 136.4 jit_solution(15979915911823174756)
XLA Ops:
  0.0 2.1 %collective-permute-start.1 = (bf16[256,384]{1,0:T(8,128)(2,1)}, bf16[256,384]{1,0:T(8,128)(2,1)S(1)}, u32[]{:S(2)}, u32[]{:S(2)}) collective-permute-start(bf16[256,384]{1,0:T(8,128)(2,1)} %refs_2_.1), channel_id=1, source_target_pairs={{0,1},{1,2},{2,3},{3,0},{4,5},{5,6},{6,7},{7,4},{8,9},{9,10},{10,1... | collective-permute-start | bytes 589832 | tf_op jit(solution)/shard_map/ppermute | solution.py:21
  2.1 2.6 %collective-permute-start.2 = (bf16[256,384]{1,0:T(8,128)(2,1)}, bf16[256,384]{1,0:T(8,128)(2,1)S(1)}, u32[]{:S(2)}, u32[]{:S(2)}) collective-permute-start(bf16[256,384]{1,0:T(8,128)(2,1)} %refs_2_.1), channel_id=1, source_target_pairs={{0,2},{1,3},{2,0},{3,1},{4,6},{5,7},{6,4},{7,5},{8,10},{9,11},{10,... | collective-permute-start | bytes 589832 | tf_op jit(solution)/shard_map/ppermute | solution.py:21
  4.7 1.1 collective-permute-start.3
  5.8 1.7 %shard_map.136 = bf16[24,2688]{1,0:T(8,128)(2,1)} custom-call(f32[24,768]{1,0:T(8,128)} %value_ref.1, f32[24,256]{1,0:T(8,128)} %shared_ref.1, f32[12,24]{1,0:T(8,128)} %bitcast.31, f32[24,768]{1,0:T(8,128)} %gate_ref.1, f32[24,768]{1,0:T(8,128)} %bitcast.30), custom_call_target="tpu_custom_call" | custom-call | tf_op jit(solution)/shard_map/pallas_call | solution.py:45
  7.5 25.3 %all_gather.3 = bf16[192,2688]{1,0:T(8,128)(2,1)S(1)} all-gather(bf16[24,2688]{1,0:T(8,128)(2,1)} %shard_map.136), channel_id=1, replica_groups=mesh['x'=4,'z'=8,'core'=2,'tp'=4] {'z'}, dimensions={0}, use_global_device_ids=true | all-gather | bytes 1161216 | tf_op jit(solution)/shard_map/all_gather | solution.py:403
  32.9 1.3 collective-permute-start.8
  34.2 1.5 %collective-permute-start = (bf16[192,1024]{1,0:T(8,128)(2,1)S(1)}, bf16[192,1024]{1,0:T(8,128)(2,1)S(1)}, u32[]{:S(2)}, u32[]{:S(2)}) collective-permute-start(bf16[192,1024]{1,0:T(8,128)(2,1)S(1)} %slice.36.refs_2_), channel_id=1, source_target_pairs={{0,192},{64,0},{128,64},{192,128},{1,193},{65,1},{129,65},{193,129... | collective-permute-start | bytes 1179656 | tf_op jit(solution)/shard_map/ppermute | solution.py:21
  35.7 0.7 slice.28
  36.4 1.5 %collective-permute-start.9 = (bf16[192,1024]{1,0:T(8,128)(2,1)S(1)}, bf16[192,1024]{1,0:T(8,128)(2,1)}, u32[]{:S(2)}, u32[]{:S(2)}) collective-permute-start(bf16[192,1024]{1,0:T(8,128)(2,1)S(1)} %slice.36.refs_2_), channel_id=1, source_target_pairs={{0,128},{64,192},{128,0},{192,64},{1,129},{65,193},{129,1},{193,65... | collective-permute-start | bytes 1179656 | tf_op jit(solution)/shard_map/ppermute | solution.py:21
  37.9 7.9 %collective-permute-start.10 = (bf16[192,1024]{1,0:T(8,128)(2,1)S(1)}, bf16[192,1024]{1,0:T(8,128)(2,1)S(1)}, u32[]{:S(2)}, u32[]{:S(2)}) collective-permute-start(bf16[192,1024]{1,0:T(8,128)(2,1)S(1)} %slice.36.refs_2_), channel_id=1, source_target_pairs={{0,4},{4,0},{1,5},{5,1},{2,6},{6,2},{3,7},{7,3},{8,12},{12,8},{9,1... | collective-permute-start | bytes 1179656 | tf_op jit(solution)/shard_map/ppermute | solution.py:21
  45.8 2.2 %collective-permute-start.4 = (bf16[8,1536]{1,0:T(8,128)(2,1)S(1)}, bf16[8,1536]{1,0:T(8,128)(2,1)S(1)}, u32[]{:S(2)}, u32[]{:S(2)}) collective-permute-start(bf16[8,1536]{1,0:T(8,128)(2,1)S(1)} %pad_maximum_fusion), channel_id=1, source_target_pairs={{0,4},{4,8},{8,12},{12,16},{16,20},{20,24},{24,28},{28,32},{32,36}... | collective-permute-start | bytes 73736 | tf_op jit(solution)/shard_map/ppermute | solution.py:408
  48.0 0.7 pad_add_fusion.1.refs_0_
  48.8 2.1 %collective-permute-start.11 = (bf16[192,1024]{1,0:T(8,128)(2,1)S(1)}, bf16[192,1024]{1,0:T(8,128)(2,1)}, u32[]{:S(2)}, u32[]{:S(2)}) collective-permute-start(bf16[192,1024]{1,0:T(8,128)(2,1)S(1)} %collective-permute-done.8.refs_3_), channel_id=1, source_target_pairs={{0,4},{4,0},{1,5},{5,1},{2,6},{6,2},{3,7},{7,3},{8,12},{12,8},{9,1... | collective-permute-start | bytes 1179656 | tf_op jit(solution)/shard_map/ppermute | solution.py:21
  51.5 5.2 %shard_map.137.refs_10_ = bf16[264,1536]{1,0:T(8,128)(2,1)} custom-call(s32[3]{0:T(128)} %pad_add_fusion.1.refs_0_, s32[64]{0:T(128)} %refs_1_.3, bf16[256,384]{1,0:T(8,128)(2,1)} %refs_2_.1, bf16[256,384]{1,0:T(8,128)(2,1)} %copy-done.12, bf16[256,384]{1,0:T(8,128)(2,1)} %copy-done.13, bf16[256,384]{1,0:T(8,128)(2,1)} %copy-done.14, bf16[8,1536]{1,0:T(8,128)(2,1)} %copy-done.15), custom_call_target="tpu_custom_call" | custom-call | flops 1245708288 | bytes 811276 | tf_op jit(solution)/shard_map/pallas_call | solution.py:93
  57.4 2.2 %collective-permute-start.5 = (bf16[192,1664]{1,0:T(8,128)(2,1)S(1)}, bf16[192,1664]{1,0:T(8,128)(2,1)S(1)}, u32[]{:S(2)}, u32[]{:S(2)}) collective-permute-start(bf16[192,1664]{1,0:T(8,128)(2,1)S(1)} %slice.40.refs_2_), channel_id=1, source_target_pairs={{0,64},{64,128},{128,192},{192,0},{1,65},{65,129},{129,193},{193,1... | collective-permute-start | bytes 1916936 | tf_op jit(solution)/shard_map/ppermute | solution.py:21
  59.6 1.7 %collective-permute-start.6 = (bf16[192,1664]{1,0:T(8,128)(2,1)S(1)}, bf16[192,1664]{1,0:T(8,128)(2,1)S(1)}, u32[]{:S(2)}, u32[]{:S(2)}) collective-permute-start(bf16[192,1664]{1,0:T(8,128)(2,1)S(1)} %slice.40.refs_2_), channel_id=1, source_target_pairs={{0,128},{64,192},{128,0},{192,64},{1,129},{65,193},{129,1},{193,65... | collective-permute-start | bytes 1916936 | tf_op jit(solution)/shard_map/ppermute | solution.py:21
  61.3 1.7 %collective-permute-start.7 = (bf16[192,1664]{1,0:T(8,128)(2,1)S(1)}, bf16[192,1664]{1,0:T(8,128)(2,1)S(1)}, u32[]{:S(2)}, u32[]{:S(2)}) collective-permute-start(bf16[192,1664]{1,0:T(8,128)(2,1)S(1)} %slice.40.refs_2_), channel_id=1, source_target_pairs={{0,192},{64,0},{128,64},{192,128},{1,193},{65,1},{129,65},{193,129... | collective-permute-start | bytes 1916936 | tf_op jit(solution)/shard_map/ppermute | solution.py:21
  63.0 6.7 %shard_map.138 = (bf16[256,768]{1,0:T(8,128)(2,1)}, bf16[256,128]{1,0:T(8,128)(2,1)}, f32[256,128]{1,0:T(8,128)}, f32[256,128]{1,0:T(8,128)}, bf16[1024,128]{1,0:T(8,128)(2,1)}) custom-call(s32[1]{0:T(128)} %bitcast.6.refs_0_, s32[8]{0:T(128)} %refs_1_.5, bf16[192,1024]{1,0:T(8,128)(2,1)} %copy-done.5, bf16[192,1024]{1,0:T(8,128)(2,1)} %copy-done.7, ...), custom_call_target="tpu_custom_call" | custom-call | flops 830472192 | bytes 3973252 | tf_op jit(solution)/shard_map/pallas_call | solution.py:93
  69.7 22.9 %all_to_all.10 = bf16[64,16,128]{2,1,0:T(8,128)(2,1)S(1)} all-to-all(bf16[64,16,128]{2,1,0:T(8,128)(2,1)} %bitcast.29), channel_id=1, replica_groups=mesh['x'=4,'z'=8,'core'=2,'tp'=4] {'x','z','core'}, dimensions={0} | all-to-all | bytes 524288 | tf_op jit(solution)/shard_map/all_to_all | solution.py:443
  92.6 1.4 %shard_map.139 = bf16[1024,128]{1,0:T(8,128)(2,1)} custom-call(bf16[1024,128]{1,0:T(8,128)(2,1)S(1)} %bitcast.22), custom_call_target="tpu_custom_call" | custom-call | bytes 262144 | tf_op jit(solution)/shard_map/pallas_call | solution.py:93
  95.4 8.0 %all-to-all-start.1 = ((bf16[64,16,128]{2,1,0:T(8,128)(2,1)}), bf16[64,16,128]{2,1,0:T(8,128)(2,1)S(1)}, u32[]{:S(2)}, u32[]{:S(2)}) async-start(bf16[64,16,128]{2,1,0:T(8,128)(2,1)} %bitcast.19), calls=%async_computation.1 | async-start | bytes 524288 | tf_op jit(solution)/shard_map/all_to_all | solution.py:452
  106.1 0.8 copy-done.4
  106.9 6.4 %shard_map.140 = (bf16[256,768]{1,0:T(8,128)(2,1)}, bf16[256,768]{1,0:T(8,128)(2,1)}, bf16[256,128]{1,0:T(8,128)(2,1)}) custom-call(s32[1]{0:T(128)} %bitcast.6.refs_0_, s32[8]{0:T(128)} %refs_1_.5, bf16[192,1664]{1,0:T(8,128)(2,1)} %copy-done, bf16[192,1664]{1,0:T(8,128)(2,1)} %copy-done.1, bf16[192,1664]{1,0:T(8,128)(2,1)} %copy-done.2, ...), custom_call_target="tpu_custom_call" | custom-call | flops 726663168 | bytes 6650916 | tf_op jit(solution)/shard_map/pallas_call | solution.py:93
  113.3 2.0 %all-to-all-done.1 = bf16[64,16,128]{2,1,0:T(8,128)(2,1)S(1)} async-done(((bf16[64,16,128]{2,1,0:T(8,128)(2,1)}), bf16[64,16,128]{2,1,0:T(8,128)(2,1)S(1)}, u32[]{:S(2)}, u32[]{:S(2)}) %all-to-all-start.1) | async-done | bytes 262176 | tf_op jit(solution)/shard_map/all_to_all | solution.py:452
  115.4 0.7 copy-done.6
  116.1 5.3 %shard_map.141 = (bf16[264,384]{1,0:T(8,128)(2,1)}, bf16[264,384]{1,0:T(8,128)(2,1)}, bf16[264,384]{1,0:T(8,128)(2,1)}, bf16[264,384]{1,0:T(8,128)(2,1)}) custom-call(s32[2]{0:T(128)} %pad_add_fusion.refs_0_, bf16[8,24,1664]{2,1,0:T(8,128)(2,1)} %bitcast.23, bf16[8,24,1664]{2,1,0:T(8,128)(2,1)} %bitcast.24, bf16[8,24,1664]{2,1,0:T(8,128)(2,1)} %bitcast.25, ...), custom_call_target="tpu_custom_call" | custom-call | flops 603979776 | bytes 6229000 | tf_op jit(solution)/shard_map/pallas_call | solution.py:93
  121.5 2.4 %collective-permute-start.19 = (bf16[264,384]{1,0:T(8,128)(2,1)}, bf16[264,384]{1,0:T(8,128)(2,1)S(1)}, u32[]{:S(2)}, u32[]{:S(2)}) collective-permute-start(bf16[264,384]{1,0:T(8,128)(2,1)} %get-tuple-element.41), channel_id=1, source_target_pairs={{0,2},{1,3},{2,0},{3,1},{4,6},{5,7},{6,4},{7,5},{8,10},{9,11},{10,... | collective-permute-start | bytes 608264 | tf_op jit(solution)/shard_map/ppermute | solution.py:21
  123.8 4.0 %collective-permute-done.20 = bf16[264,384]{1,0:T(8,128)(2,1)S(1)} collective-permute-done((bf16[264,384]{1,0:T(8,128)(2,1)}, bf16[264,384]{1,0:T(8,128)(2,1)S(1)}, u32[]{:S(2)}, u32[]{:S(2)}) %collective-permute-start.20) | collective-permute-done | bytes 202784 | tf_op jit(solution)/shard_map/ppermute | solution.py:21
  127.8 1.6 %collective-permute-done.19 = bf16[264,384]{1,0:T(8,128)(2,1)S(1)} collective-permute-done((bf16[264,384]{1,0:T(8,128)(2,1)}, bf16[264,384]{1,0:T(8,128)(2,1)S(1)}, u32[]{:S(2)}, u32[]{:S(2)}) %collective-permute-start.19) | collective-permute-done | bytes 202784 | tf_op jit(solution)/shard_map/ppermute | solution.py:21
  129.4 5.1 %collective-permute-done.18 = bf16[264,384]{1,0:T(8,128)(2,1)S(1)} collective-permute-done((bf16[264,384]{1,0:T(8,128)(2,1)}, bf16[264,384]{1,0:T(8,128)(2,1)S(1)}, u32[]{:S(2)}, u32[]{:S(2)}) %collective-permute-start.18) | collective-permute-done | bytes 202784 | tf_op jit(solution)/shard_map/ppermute | solution.py:21
  134.6 1.0 convert_add_fusion
  135.6 0.8 fusion
  (67 shorter events, 5.4 us)
Async XLA Ops:
  0.0 45.8 %collective-permute-start.1 = (bf16[256,384]{1,0:T(8,128)(2,1)}, bf16[256,384]{1,0:T(8,128)(2,1)S(1)}, u32[]{:S(2)}, u32[]{:S(2)}) collective-permute-start(bf16[256,384]{1,0:T(8,128)(2,1)} %refs_2_.1), channel_id=1, source_target_pairs={{0,1},{1,2},{2,3},{3,0},{4,5},{5,6},{6,7},{7,4},{8,9},{9,10},{10,1... | collective-permute-start | bytes 589832 | tf_op jit(solution)/shard_map/ppermute | solution.py:21
  2.1 35.8 %collective-permute-start.2 = (bf16[256,384]{1,0:T(8,128)(2,1)}, bf16[256,384]{1,0:T(8,128)(2,1)S(1)}, u32[]{:S(2)}, u32[]{:S(2)}) collective-permute-start(bf16[256,384]{1,0:T(8,128)(2,1)} %refs_2_.1), channel_id=1, source_target_pairs={{0,2},{1,3},{2,0},{3,1},{4,6},{5,7},{6,4},{7,5},{8,10},{9,11},{10,... | collective-permute-start | bytes 589832 | tf_op jit(solution)/shard_map/ppermute | solution.py:21
  4.7 31.6 %collective-permute-start.3 = (bf16[256,384]{1,0:T(8,128)(2,1)}, bf16[256,384]{1,0:T(8,128)(2,1)S(1)}, u32[]{:S(2)}, u32[]{:S(2)}) collective-permute-start(bf16[256,384]{1,0:T(8,128)(2,1)} %refs_2_.1), channel_id=1, source_target_pairs={{0,3},{1,0},{2,1},{3,2},{4,7},{5,4},{6,5},{7,6},{8,11},{9,8},{10,9... | collective-permute-start | bytes 589832 | tf_op jit(solution)/shard_map/ppermute | solution.py:21
  32.9 15.8 %copy-start.5 = (bf16[192,1024]{1,0:T(8,128)(2,1)}, bf16[192,1024]{1,0:T(8,128)(2,1)S(1)}, u32[]{:S(2)}) copy-start(bf16[192,1024]{1,0:T(8,128)(2,1)S(1)} %slice.36.refs_2_) | copy-start | bytes 1179652
  32.9 15.9 %collective-permute-start.8 = (bf16[192,1024]{1,0:T(8,128)(2,1)S(1)}, bf16[192,1024]{1,0:T(8,128)(2,1)S(1)}, u32[]{:S(2)}, u32[]{:S(2)}) collective-permute-start(bf16[192,1024]{1,0:T(8,128)(2,1)S(1)} %slice.36.refs_2_), channel_id=1, source_target_pairs={{0,64},{64,128},{128,192},{192,0},{1,65},{65,129},{129,193},{193,1... | collective-permute-start | bytes 1179656 | tf_op jit(solution)/shard_map/ppermute | solution.py:21
  34.2 22.6 %collective-permute-start = (bf16[192,1024]{1,0:T(8,128)(2,1)S(1)}, bf16[192,1024]{1,0:T(8,128)(2,1)S(1)}, u32[]{:S(2)}, u32[]{:S(2)}) collective-permute-start(bf16[192,1024]{1,0:T(8,128)(2,1)S(1)} %slice.36.refs_2_), channel_id=1, source_target_pairs={{0,192},{64,0},{128,64},{192,128},{1,193},{65,1},{129,65},{193,129... | collective-permute-start | bytes 1179656 | tf_op jit(solution)/shard_map/ppermute | solution.py:21
  36.3 12.4 %copy-start.14 = (bf16[256,384]{1,0:T(8,128)(2,1)}, bf16[256,384]{1,0:T(8,128)(2,1)S(1)}, u32[]{:S(2)}) copy-start(bf16[256,384]{1,0:T(8,128)(2,1)S(1)} %collective-permute-done.3.refs_5_) | copy-start | bytes 589828
  36.4 20.4 %collective-permute-start.9 = (bf16[192,1024]{1,0:T(8,128)(2,1)S(1)}, bf16[192,1024]{1,0:T(8,128)(2,1)}, u32[]{:S(2)}, u32[]{:S(2)}) collective-permute-start(bf16[192,1024]{1,0:T(8,128)(2,1)S(1)} %slice.36.refs_2_), channel_id=1, source_target_pairs={{0,128},{64,192},{128,0},{192,64},{1,129},{65,193},{129,1},{193,65... | collective-permute-start | bytes 1179656 | tf_op jit(solution)/shard_map/ppermute | solution.py:21
  37.9 10.9 %copy-start.13 = (bf16[256,384]{1,0:T(8,128)(2,1)}, bf16[256,384]{1,0:T(8,128)(2,1)S(1)}, u32[]{:S(2)}) copy-start(bf16[256,384]{1,0:T(8,128)(2,1)S(1)} %collective-permute-done.2.refs_4_) | copy-start | bytes 589828
  37.9 21.7 %collective-permute-start.10 = (bf16[192,1024]{1,0:T(8,128)(2,1)S(1)}, bf16[192,1024]{1,0:T(8,128)(2,1)S(1)}, u32[]{:S(2)}, u32[]{:S(2)}) collective-permute-start(bf16[192,1024]{1,0:T(8,128)(2,1)S(1)} %slice.36.refs_2_), channel_id=1, source_target_pairs={{0,4},{4,0},{1,5},{5,1},{2,6},{6,2},{3,7},{7,3},{8,12},{12,8},{9,1... | collective-permute-start | bytes 1179656 | tf_op jit(solution)/shard_map/ppermute | solution.py:21
  45.8 3.0 %copy-start.12 = (bf16[256,384]{1,0:T(8,128)(2,1)}, bf16[256,384]{1,0:T(8,128)(2,1)S(1)}, u32[]{:S(2)}) copy-start(bf16[256,384]{1,0:T(8,128)(2,1)S(1)} %collective-permute-done.1.refs_3_) | copy-start | bytes 589828
  45.8 5.1 %collective-permute-start.4 = (bf16[8,1536]{1,0:T(8,128)(2,1)S(1)}, bf16[8,1536]{1,0:T(8,128)(2,1)S(1)}, u32[]{:S(2)}, u32[]{:S(2)}) collective-permute-start(bf16[8,1536]{1,0:T(8,128)(2,1)S(1)} %pad_maximum_fusion), channel_id=1, source_target_pairs={{0,4},{4,8},{8,12},{12,16},{16,20},{20,24},{24,28},{28,32},{32,36}... | collective-permute-start | bytes 73736 | tf_op jit(solution)/shard_map/ppermute | solution.py:408
  48.8 45.4 %copy-start = (bf16[192,1664]{1,0:T(8,128)(2,1)}, bf16[192,1664]{1,0:T(8,128)(2,1)S(1)}, u32[]{:S(2)}) copy-start(bf16[192,1664]{1,0:T(8,128)(2,1)S(1)} %slice.40.refs_2_) | copy-start | bytes 1916932
  48.8 8.0 %copy-start.7 = (bf16[192,1024]{1,0:T(8,128)(2,1)}, bf16[192,1024]{1,0:T(8,128)(2,1)S(1)}, u32[]{:S(2)}) copy-start(bf16[192,1024]{1,0:T(8,128)(2,1)S(1)} %collective-permute-done.8.refs_3_) | copy-start | bytes 1179652
  48.8 12.5 %collective-permute-start.11 = (bf16[192,1024]{1,0:T(8,128)(2,1)S(1)}, bf16[192,1024]{1,0:T(8,128)(2,1)}, u32[]{:S(2)}, u32[]{:S(2)}) collective-permute-start(bf16[192,1024]{1,0:T(8,128)(2,1)S(1)} %collective-permute-done.8.refs_3_), channel_id=1, source_target_pairs={{0,4},{4,0},{1,5},{5,1},{2,6},{6,2},{3,7},{7,3},{8,12},{12,8},{9,1... | collective-permute-start | bytes 1179656 | tf_op jit(solution)/shard_map/ppermute | solution.py:21
  56.8 6.2 %copy-start.8 = (bf16[192,1024]{1,0:T(8,128)(2,1)}, bf16[192,1024]{1,0:T(8,128)(2,1)S(1)}, u32[]{:S(2)}) copy-start(bf16[192,1024]{1,0:T(8,128)(2,1)S(1)} %collective-permute-done.refs_5_) | copy-start | bytes 1179652
  56.8 6.2 %collective-permute-start.12 = (bf16[192,1024]{1,0:T(8,128)(2,1)}, bf16[192,1024]{1,0:T(8,128)(2,1)}, u32[]{:S(2)}, u32[]{:S(2)}) collective-permute-start(bf16[192,1024]{1,0:T(8,128)(2,1)} %collective-permute-done.9.refs_4_), channel_id=1, source_target_pairs={{0,4},{4,0},{1,5},{5,1},{2,6},{6,2},{3,7},{7,3},{8,12},{12,8},{9,1... | collective-permute-start | bytes 1179656 | tf_op jit(solution)/shard_map/ppermute | solution.py:21
  56.9 6.1 %collective-permute-start.13 = (bf16[192,1024]{1,0:T(8,128)(2,1)S(1)}, bf16[192,1024]{1,0:T(8,128)(2,1)}, u32[]{:S(2)}, u32[]{:S(2)}) collective-permute-start(bf16[192,1024]{1,0:T(8,128)(2,1)S(1)} %collective-permute-done.refs_5_), channel_id=1, source_target_pairs={{0,4},{4,0},{1,5},{5,1},{2,6},{6,2},{3,7},{7,3},{8,12},{12,8},{9,1... | collective-permute-start | bytes 1179656 | tf_op jit(solution)/shard_map/ppermute | solution.py:21
  57.4 36.7 %collective-permute-start.5 = (bf16[192,1664]{1,0:T(8,128)(2,1)S(1)}, bf16[192,1664]{1,0:T(8,128)(2,1)S(1)}, u32[]{:S(2)}, u32[]{:S(2)}) collective-permute-start(bf16[192,1664]{1,0:T(8,128)(2,1)S(1)} %slice.40.refs_2_), channel_id=1, source_target_pairs={{0,64},{64,128},{128,192},{192,0},{1,65},{65,129},{129,193},{193,1... | collective-permute-start | bytes 1916936 | tf_op jit(solution)/shard_map/ppermute | solution.py:21
  59.6 34.5 %collective-permute-start.6 = (bf16[192,1664]{1,0:T(8,128)(2,1)S(1)}, bf16[192,1664]{1,0:T(8,128)(2,1)S(1)}, u32[]{:S(2)}, u32[]{:S(2)}) collective-permute-start(bf16[192,1664]{1,0:T(8,128)(2,1)S(1)} %slice.40.refs_2_), channel_id=1, source_target_pairs={{0,128},{64,192},{128,0},{192,64},{1,129},{65,193},{129,1},{193,65... | collective-permute-start | bytes 1916936 | tf_op jit(solution)/shard_map/ppermute | solution.py:21
  61.3 32.8 %collective-permute-start.7 = (bf16[192,1664]{1,0:T(8,128)(2,1)S(1)}, bf16[192,1664]{1,0:T(8,128)(2,1)S(1)}, u32[]{:S(2)}, u32[]{:S(2)}) collective-permute-start(bf16[192,1664]{1,0:T(8,128)(2,1)S(1)} %slice.40.refs_2_), channel_id=1, source_target_pairs={{0,192},{64,0},{128,64},{192,128},{1,193},{65,1},{129,65},{193,129... | collective-permute-start | bytes 1916936 | tf_op jit(solution)/shard_map/ppermute | solution.py:21
  94.1 12.0 %copy-start.1 = (bf16[192,1664]{1,0:T(8,128)(2,1)}, bf16[192,1664]{1,0:T(8,128)(2,1)S(1)}, u32[]{:S(2)}) copy-start(bf16[192,1664]{1,0:T(8,128)(2,1)S(1)} %collective-permute-done.5.refs_3_) | copy-start | bytes 1916932
  94.1 12.0 %copy-start.2 = (bf16[192,1664]{1,0:T(8,128)(2,1)}, bf16[192,1664]{1,0:T(8,128)(2,1)S(1)}, u32[]{:S(2)}) copy-start(bf16[192,1664]{1,0:T(8,128)(2,1)S(1)} %collective-permute-done.6.refs_4_) | copy-start | bytes 1916932
  94.1 11.9 %copy-start.3 = (bf16[192,1664]{1,0:T(8,128)(2,1)}, bf16[192,1664]{1,0:T(8,128)(2,1)S(1)}, u32[]{:S(2)}) copy-start(bf16[192,1664]{1,0:T(8,128)(2,1)S(1)} %collective-permute-done.7.refs_5_) | copy-start | bytes 1916932
  94.1 11.9 %collective-permute-start.14 = (bf16[192,1664]{1,0:T(8,128)(2,1)S(1)}, bf16[192,1664]{1,0:T(8,128)(2,1)S(1)}, u32[]{:S(2)}, u32[]{:S(2)}) collective-permute-start(bf16[192,1664]{1,0:T(8,128)(2,1)S(1)} %slice.40.refs_2_), channel_id=1, source_target_pairs={{0,4},{4,0},{1,5},{5,1},{2,6},{6,2},{3,7},{7,3},{8,12},{12,8},{9,1... | collective-permute-start | bytes 1916936 | tf_op jit(solution)/shard_map/ppermute | solution.py:21
  94.8 11.2 %collective-permute-start.15 = (bf16[192,1664]{1,0:T(8,128)(2,1)S(1)}, bf16[192,1664]{1,0:T(8,128)(2,1)}, u32[]{:S(2)}, u32[]{:S(2)}) collective-permute-start(bf16[192,1664]{1,0:T(8,128)(2,1)S(1)} %collective-permute-done.5.refs_3_), channel_id=1, source_target_pairs={{0,4},{4,0},{1,5},{5,1},{2,6},{6,2},{3,7},{7,3},{8,12},{12,8},{9,1... | collective-permute-start | bytes 1916936 | tf_op jit(solution)/shard_map/ppermute | solution.py:21
  94.9 11.1 %collective-permute-start.16 = (bf16[192,1664]{1,0:T(8,128)(2,1)S(1)}, bf16[192,1664]{1,0:T(8,128)(2,1)}, u32[]{:S(2)}, u32[]{:S(2)}) collective-permute-start(bf16[192,1664]{1,0:T(8,128)(2,1)S(1)} %collective-permute-done.6.refs_4_), channel_id=1, source_target_pairs={{0,4},{4,0},{1,5},{5,1},{2,6},{6,2},{3,7},{7,3},{8,12},{12,8},{9,1... | collective-permute-start | bytes 1916936 | tf_op jit(solution)/shard_map/ppermute | solution.py:21
  95.3 10.7 %collective-permute-start.17 = (bf16[192,1664]{1,0:T(8,128)(2,1)S(1)}, bf16[192,1664]{1,0:T(8,128)(2,1)}, u32[]{:S(2)}, u32[]{:S(2)}) collective-permute-start(bf16[192,1664]{1,0:T(8,128)(2,1)S(1)} %collective-permute-done.7.refs_5_), channel_id=1, source_target_pairs={{0,4},{4,0},{1,5},{5,1},{2,6},{6,2},{3,7},{7,3},{8,12},{12,8},{9,1... | collective-permute-start | bytes 1916936 | tf_op jit(solution)/shard_map/ppermute | solution.py:21
  95.4 20.0 %all-to-all-start.1 = ((bf16[64,16,128]{2,1,0:T(8,128)(2,1)}), bf16[64,16,128]{2,1,0:T(8,128)(2,1)S(1)}, u32[]{:S(2)}, u32[]{:S(2)}) async-start(bf16[64,16,128]{2,1,0:T(8,128)(2,1)} %bitcast.19), calls=%async_computation.1 | async-start | bytes 524288 | tf_op jit(solution)/shard_map/all_to_all | solution.py:452
  121.4 6.4 %collective-permute-start.20 = (bf16[264,384]{1,0:T(8,128)(2,1)}, bf16[264,384]{1,0:T(8,128)(2,1)S(1)}, u32[]{:S(2)}, u32[]{:S(2)}) collective-permute-start(bf16[264,384]{1,0:T(8,128)(2,1)} %get-tuple-element.42), channel_id=1, source_target_pairs={{0,3},{1,0},{2,1},{3,2},{4,7},{5,4},{6,5},{7,6},{8,11},{9,8},{10,9... | collective-permute-start | bytes 608264 | tf_op jit(solution)/shard_map/ppermute | solution.py:21
  121.5 8.0 %collective-permute-start.19 = (bf16[264,384]{1,0:T(8,128)(2,1)}, bf16[264,384]{1,0:T(8,128)(2,1)S(1)}, u32[]{:S(2)}, u32[]{:S(2)}) collective-permute-start(bf16[264,384]{1,0:T(8,128)(2,1)} %get-tuple-element.41), channel_id=1, source_target_pairs={{0,2},{1,3},{2,0},{3,1},{4,6},{5,7},{6,4},{7,5},{8,10},{9,11},{10,... | collective-permute-start | bytes 608264 | tf_op jit(solution)/shard_map/ppermute | solution.py:21
  123.8 10.7 %collective-permute-start.18 = (bf16[264,384]{1,0:T(8,128)(2,1)}, bf16[264,384]{1,0:T(8,128)(2,1)S(1)}, u32[]{:S(2)}, u32[]{:S(2)}) collective-permute-start(bf16[264,384]{1,0:T(8,128)(2,1)} %get-tuple-element.40), channel_id=1, source_target_pairs={{0,1},{1,2},{2,3},{3,0},{4,5},{5,6},{6,7},{7,4},{8,9},{9,10},{10,1... | collective-permute-start | bytes 608264 | tf_op jit(solution)/shard_map/ppermute | solution.py:21
  (6 other events, 5.2 us)

commit v9 on v8

--- a/solution.py
+++ b/solution.py
@@ -21,40 +21,37 @@
     return lax.ppermute(block, axis, [(i, (i + distance) % count) for i in range(count)])
 
 
-def pack_body(value_ref, shared_ref, step_ref, gate_ref, out_t_ref, out_ref):
+def pack_body(value_ref, shared_ref, step_ref, out_ref):
     inner, half, heads = value_ref.shape[1], shared_ref.shape[1] // 2, step_ref.shape[0]
-    rest = -heads % 128
-    step = jnp.pad(step_ref[...].T, ((0, 0), (0, rest)))
-    at = 0
-    for piece in (
-        value_ref[...],
-        shared_ref[:, :half],
-        step,
-        gate_ref[...],
-        shared_ref[:, half:],
-        out_t_ref[...],
-    ):
-        out_ref[:, at : at + piece.shape[1]] = piece.astype(BF16)
-        at += piece.shape[1]
-
-
-def pack(value, shared, step, gate, out_t):
-    rows, inner = value.shape
-    heads = step.shape[1]
-    width = 3 * inner + shared.shape[1] + heads + -heads % 128
+    out_ref[:, :inner] = value_ref[...].astype(BF16)
+    out_ref[:, inner : inner + half] = shared_ref[:, :half].astype(BF16)
+    step = jnp.pad(step_ref[...].T, ((0, 0), (0, -heads % 128)))
+    out_ref[:, inner + half :] = step.astype(BF16)
+
+
+def pack_late_body(gate_ref, shared_ref, out_t_ref, out_ref):
+    inner, half = gate_ref.shape[1], shared_ref.shape[1] // 2
+    out_ref[:, :inner] = gate_ref[...].astype(BF16)
+    out_ref[:, inner : inner + half] = shared_ref[:, half:].astype(BF16)
+    out_ref[:, inner + half :] = out_t_ref[...].astype(BF16)
+
+
+def pack(body, width, *args):
     return pl.pallas_call(
-        pack_body,
-        out_shape=jax.ShapeDtypeStruct((rows, width), BF16),
-        in_specs=[pl.BlockSpec(memory_space=pltpu.VMEM)] * 5,
+        body,
+        out_shape=jax.ShapeDtypeStruct((args[0].shape[0], width), BF16),
+        in_specs=[pl.BlockSpec(memory_space=pltpu.VMEM)] * 3,
         out_specs=pl.BlockSpec(memory_space=pltpu.VMEM),
-    )(value, shared, step.T, gate, out_t)
+    )(*args)
 
 
 def call(
-    body, shapes, args, scalars=0, blocks=0, near_in=0, near_out=0, scratch=(), flops=0, grant=60
+    body, shapes, args, scalars=0, blocks=0, near_in=0, near_out=0, sent=0, scratch=(), flops=0, grant=60
 ):
     hbm, vmem = pl.BlockSpec(memory_space=pltpu.HBM), pl.BlockSpec(memory_space=pltpu.VMEM)
+    any_space = pl.BlockSpec(memory_space=pl.ANY)
     fixed = scalars + blocks + near_in
+    near_out = near_out + sent
     far_in, far_out = args[fixed:], shapes[near_out:]
     moved = sum(x.size * x.dtype.itemsize for x in args)
 
@@ -89,15 +86,17 @@
     room = [pltpu.VMEM(x.shape, x.dtype) for x in far_in]
     room += [pltpu.VMEM(shape, kind) for shape, kind in far_out]
     room += [pltpu.VMEM(shape, kind) for shape, kind in scratch]
+    if sent:
+        room.append(pltpu.SemaphoreType.DMA((sent,)))
     room.append(pltpu.SemaphoreType.DMA((len(far_in) + len(far_out) + blocks,)))
     return pl.pallas_call(
         wrapped,
         out_shape=[jax.ShapeDtypeStruct(shape, kind) for shape, kind in shapes],
         in_specs=[pl.BlockSpec(memory_space=pltpu.SMEM)] * scalars
-        + [hbm] * blocks
+        + [any_space] * blocks
         + [vmem] * near_in
-        + [hbm] * len(far_in),
-        out_specs=[vmem] * near_out + [hbm] * len(far_out),
+        + [any_space] * len(far_in),
+        out_specs=[vmem] * (near_out - sent) + [hbm] * (len(far_out) + sent),
         scratch_shapes=room,
         compiler_params=pltpu.CompilerParams(vmem_limit_bytes=grant << 20),
         cost_estimate=pl.CostEstimate(flops=flops, bytes_accessed=moved, transcendentals=0),
@@ -159,12 +158,12 @@
     return copies
 
 
-def arrange_body(block_rows, ready, sems, at_ref, order_ref, *refs):
+def arrange_body(block_rows, by_arrival, ready, sems, at_ref, order_ref, *refs):
     *pieces, edge_ref, h_ref, held = refs
-    ready()
     x_at, core_at, tp_at = at_ref[0], at_ref[1], at_ref[2]
     tokens, features = pieces[0].shape
     x_size, z_size, core_size = SIZES
+    ready()
     for d, piece in enumerate(pieces):
         held[:tokens, d * features : (d + 1) * features] = piece[...]
     held[tokens:] = edge_ref[...]
@@ -173,16 +172,20 @@
     lane = iota((8, wide), 1)
     block = lane // block_rows
     source = lane - block * block_rows
-    count = 0
-    for turn in range(core_size):
-        for d in range(x_size):
-            chip = ((x_at + x_size - d) & (x_size - 1)) * z_size
-            for z in range(z_size):
-                model = order_ref[(chip + z) * core_size + (core_at ^ turn)]
-                piece = (tp_at + len(pieces) - model // each) & (len(pieces) - 1)
-                base = (piece * each + (model & (each - 1))) * block_rows
-                source = source + jnp.where(block == count, base, 0)
-                count += 1
+    if by_arrival:
+        chips = [
+            ((x_at + x_size - d) & (x_size - 1)) * z_size + z
+            for d in range(x_size)
+            for z in range(z_size)
+        ]
+        stored = [chip * core_size + (core_at ^ turn) for turn in range(core_size) for chip in chips]
+    else:
+        stored = range(x_size * z_size * core_size)
+    for count, at in enumerate(stored):
+        model = order_ref[at]
+        piece = (tp_at + len(pieces) - model // each) & (len(pieces) - 1)
+        base = (piece * each + (model & (each - 1))) * block_rows
+        source = source + jnp.where(block == count, base, 0)
     for at in range(0, wide, 256):
         total = jnp.zeros((h_ref.shape[0], 256), F32)
         for k in range(0, wide, features):
@@ -197,10 +200,16 @@
     tokens, inner = x_ref.shape
     copies = fetch(blocks, held, sems, slice(0, held.shape[1]))
     ready()
-    for copy in copies:
+    half, middle = len(blocks) // 2, held.shape[0] // 2
+    for copy in copies[:half]:
         copy.wait()
     for at in range(0, held.shape[1], 256):
-        part = dot(h_ref[...], held[:, at : at + 256]).astype(BF16).astype(F32)
+        rows[:, at : at + 256] = dot(h_ref[:, :middle], held[:middle, at : at + 256])
+    for copy in copies[half:]:
+        copy.wait()
+    for at in range(0, held.shape[1], 256):
+        part = rows[:, at : at + 256] + dot(h_ref[:, middle:], held[middle:, at : at + 256])
+        part = part.astype(BF16).astype(F32)
         rows[EDGE:, at : at + 256] = part[:tokens]
         rows[:EDGE, at : at + 256] = part[tokens:]
     first = first_ref[0]
@@ -270,14 +279,13 @@
 
 
 def middle_body(head_dim, ready, sems, first_ref, lengths_ref, *refs):
-    *blocks, h_ref, conv_shared, x_ref, b_ref, dt_ref, cum_ref, skip = refs[:-6]
+    late_ref, h_ref, conv_shared, x_ref, b_ref, dt_ref, cum_ref, skip = refs[:-6]
     direct_ref, carry_ref, c_ref, held, c_rows, gate = refs[-6:]
     tokens, inner = x_ref.shape
-    wide = held.shape[1]
-    copies = fetch(blocks, held, sems, slice(0, wide))
+    copy = pltpu.make_async_copy(late_ref.at[:, : held.shape[1]], held, sems.at[0])
+    copy.start()
     ready()
-    for copy in copies:
-        copy.wait()
+    copy.wait()
     for at in range(0, inner, 256):
         g = dot(h_ref[:tokens], held[:, at : at + 256])
         gate[:, at : at + 256] = silu(g.astype(BF16).astype(F32))
@@ -313,21 +321,14 @@
         direct_ref[:, cut] = (direct * gate[:, cut]).astype(BF16)
 
 
-def last_body(ready, sems, turn_ref, *refs):
-    *blocks, carried_ref, direct_ref, carry_ref, c_ref, gain = refs[:-8]
-    *outs, held, lines, shares, out_w = refs[-8:]
-    half, wide, inner = len(blocks) // 2, blocks[0].shape[2], out_w.shape[4]
-    copies = []
-    for i, block in enumerate(blocks):
-        copy = pltpu.make_async_copy(
-            block.at[:, :, wide - inner :],
-            out_w.at[i % half, :, turn_ref[1] ^ (i // half)],
-            sems.at[i],
-        )
-        copy.start()
-        copies.append(copy)
+def last_body(ready, sems, turn_ref, late_ref, *refs):
+    carried_ref, direct_ref, carry_ref, c_ref, gain = refs[:5]
+    *outs, held, lines, shares, out_w, leaving = refs[5:]
+    tokens, inner = direct_ref.shape
+    wide = late_ref.shape[1]
+    copy = pltpu.make_async_copy(late_ref.at[:, wide - inner :], out_w, sems.at[0])
+    copy.start()
     ready()
-    tokens, inner = direct_ref.shape
     lines[...] = carried_ref[...].astype(F32)
     count = lines.shape[0] // LINES
     line = 0
@@ -341,11 +342,6 @@
     scaled = (gated * gain[...]).astype(BF16)
     nt = (((1,), (1,)), ((), ()))
     features = shares.shape[2]
-    for copy in copies:
-        copy.wait()
-    for i in range(shares.shape[0]):
-        rows = out_w[i].reshape(features, inner)
-        shares[i] = lax.dot_general(scaled, rows, nt, preferred_element_type=F32).astype(BF16)
     squares = lax.dot_general(
         jnp.ones((8, inner), F32),
         gated * gated,
@@ -356,10 +352,19 @@
     hi = squares.astype(BF16).astype(F32)
     row = iota(squares.shape, 0)
     riding = jnp.where(row == 0, hi, jnp.where(row == 1, squares - hi, 0.0)).astype(BF16)
-    for d, out in enumerate(outs):
-        out[:tokens] = shares[(turn_ref[0] + len(outs) - d) % len(outs)]
-        out[tokens:, :tokens] = riding
-        out[tokens:, tokens:] = jnp.zeros((8, features - tokens), BF16)
+    copy.wait()
+    copies = []
+    for d in list(range(1, len(outs))) + [0]:
+        at = pl.multiple_of(((turn_ref[0] + d) & (len(outs) - 1)) * features, features)
+        rows = out_w[pl.ds(at, features), :]
+        product = lax.dot_general(scaled, rows, nt, preferred_element_type=F32)
+        shares[d, :tokens] = product.astype(BF16)
+        shares[d, tokens:, :tokens] = riding
+        shares[d, tokens:, tokens:] = jnp.zeros((8, features - tokens), BF16)
+        copies.append(pltpu.make_async_copy(shares.at[d], outs[d], leaving.at[d]))
+        copies[-1].start()
+    for copy in copies:
+        copy.wait()
 
 
 def on_device(
@@ -399,25 +404,30 @@
     tie = lax.optimization_barrier
 
     pieces = [hidden_in] + [ahead(hidden_in, "tp", d) for d in range(1, tp_count)]
-    packed = pack(w_in_value, w_in_shared, w_in_step, w_in_gate, w_out.T)
-    along_z = lax.all_gather(packed, "z", axis=0, tiled=True)
-    early_width = packed.shape[1] - 2 * inner - state
-    own = x_all(along_z[:, :early_width])
-    late = along_z[:, early_width:]
+    early_width = inner + state + heads + -heads % 128
+    early = pack(pack_body, early_width, w_in_value, w_in_shared, w_in_step.T)
+    late = pack(pack_late_body, 2 * inner + state, w_in_gate, w_in_shared, w_out.T)
+    late = lax.all_gather(late, SEQ, axis=0, tiled=True)
+    own = x_all(lax.all_gather(early, "z", axis=0, tiled=True))
     edge = jnp.concatenate([piece[tokens - EDGE :] for piece in pieces], axis=1)
     edge = lax.ppermute(edge, SEQ, [(i, i + 1) for i in range(seq_count - 1)])
     rows, model_width = tokens + EDGE, features * tp_count
-    (h,) = call(
-        functools.partial(arrange_body, rows_here),
-        [((rows, model_width), BF16)],
-        [jnp.stack([x_at, core_at, tp_at]), row_blocks] + pieces + [edge],
-        scalars=2,
-        scratch=[((rows, model_width), BF16)],
-        flops=2 * rows * model_width * model_width,
-    )
-    own[-1], h, late = tie((own[-1], h, late))
+    places = jnp.stack([x_at, core_at, tp_at])
+
+    def arrange(by_arrival, pieces):
+        return call(
+            functools.partial(arrange_body, rows_here, by_arrival),
+            [((rows, model_width), BF16)],
+            [places, row_blocks] + pieces + [edge],
+            scalars=2,
+            scratch=[((rows, model_width), BF16)],
+            flops=2 * rows * model_width * model_width,
+            grant=40,
+        )[0]
+
+    h = arrange(True, pieces)
+    own[-1], h = tie((own[-1], h))
     other = [ahead(block, "core", 1) for block in own]
-    late_own = x_all(late)
 
     first = jnp.reshape(seq_at * tokens, (1,))
     copies = state // seq_count
@@ -433,6 +443,7 @@
         [first, prompt_lengths] + own + other + [h, conv_value, conv_shared, dt_bias[None], a_log[None]],
         scalars=2,
         blocks=len(own + other),
+        grant=40,
         scratch=[
             ((model_width, early_width), BF16),
             ((rows, early_width), F32),
@@ -451,8 +462,8 @@
     )
     carried = lax.all_to_all(scanned.reshape(seq_count, LINES, 128), SEQ, 0, 0, tiled=True)
     carried = carried.reshape(seq_count * LINES, 128)
-    late_own, _ = tie((late_own, scanned))
-    late_other = [ahead(block, "core", 1) for block in late_own]
+    pieces, _ = tie((pieces, sent))
+    h_late = arrange(False, pieces)
     direct, carry, c_half = call(
         functools.partial(middle_body, head_dim),
         [
@@ -460,12 +471,10 @@
             ((tokens, inner), BF16),
             ((tokens, state), BF16),
         ],
-        [first, prompt_lengths]
-        + late_own
-        + late_other
-        + [h, conv_shared, x_rows, b_half, steps, cumulative, jnp.repeat(skip_gain, head_dim)[None]],
+        [first, prompt_lengths, late]
+        + [h_late, conv_shared, x_rows, b_half, steps, cumulative, jnp.repeat(skip_gain, head_dim)[None]],
         scalars=2,
-        blocks=len(late_own + late_other),
+        blocks=1,
         scratch=[
             ((model_width, inner + state), BF16),
             ((rows, state), F32),
@@ -477,8 +486,8 @@
         last_body,
         [((tokens + 8, features), BF16)] * tp_count,
         [
-            jnp.stack([x_at - tp_at + tp_count, core_at]),
-            *[block.reshape(z_size, rows_here, -1) for block in late_own + late_other],
+            jnp.reshape(tp_at, (1,)),
+            late,
             carried,
             direct,
             carry,
@@ -486,13 +495,14 @@
             norm_gain[None],
         ],
         scalars=1,
-        blocks=len(late_own + late_other),
+        blocks=1,
         scratch=[
             ((state, inner), BF16),
             ((seq_count * LINES, 128), F32),
-            ((tp_count, tokens, features), BF16),
-            ((x_size, z_size, core_size, rows_here, inner), BF16),
+            ((tp_count, tokens + 8, features), BF16),
+            ((model_width, inner), BF16),
         ],
+        sent=tp_count,
         flops=2 * tokens * inner * model_width,
     )
     parts = [shares[0]] + [ahead(shares[d], "tp", d) for d in range(1, tp_count)]

time: 137 us -> 148 us (1.080)
  between operations: 0.33 us -> 13.6 us
  starting transfers between devices: 40.1 us -> 30.8 us
  local copies, waits for them, and re-layouts: 4.92 us -> 10.9 us
  Pallas kernels: 26.9 us -> 30.9 us
  blocking collectives: 48.2 us -> 45.7 us
    ppermute x20 -> x13, starting transfers between devices: 30 us -> 22 us  [ahead(): lax.ppermute(block, axis, [(i, (i + distance) % count) for i in range(cou...]
    unnamed x32 -> x48, local copies, waits for them, and re-layouts: 2.83 us -> 8.88 us
    pallas_call x5 -> x6, Pallas kernels: 25.1 us -> 27.8 us  [call(): pl.pallas_call(wrapped, out_shape=[jax.ShapeDtypeStruct(shape, kind) for...]
    all_to_all x1, waiting for transfers between devices: 2.05 us -> 0.01 us  [on_device(): lax.all_to_all(scanned.reshape(seq_count, LINES, 128), SEQ, 0, 0, tiled=T...]
    all_to_all x1, starting transfers between devices: 7.95 us -> 6.26 us  [on_device(): lax.all_to_all(scanned.reshape(seq_count, LINES, 128), SEQ, 0, 0, tiled=T...]
    pallas_call x1 -> x2, Pallas kernels: 1.71 us -> 3.18 us  [pack(): pl.pallas_call(body, out_shape=jax.ShapeDtypeStruct((args[0].shape[0], wi...]
    ppermute x20 -> x13, waiting for transfers between devices: 10.8 us -> 11.9 us  [ahead(): lax.ppermute(block, axis, [(i, (i + distance) % count) for i in range(cou...]
  transfers between devices with their start and end apart: 22 -> 16, of which waited for: 4 -> 6; matrix products, arithmetic and copies ran while one was open for 2% -> 1% of each run, Pallas kernels for 16% -> 16%
where the time goes in v9:
time: 148 us; the launch traced here: 147 us
  blocking collectives  45.7 us (31%)
  Pallas kernels  30.9 us (21%)
  starting transfers between devices  30.8 us (21%)
  between operations  13.6 us (9%)
  waiting for transfers between devices  12.8 us (9%)
  local copies, waits for them, and re-layouts  10.9 us (7%)
  other arithmetic  1.9 us (1%)
    pallas_call x6, Pallas kernels, call(): pl.pallas_call(wrapped, out_shape=[jax.ShapeDtypeStruct(shape, kind) for...  27.8 us
    all_gather x1, blocking collectives, on_device(): own = x_all(lax.all_gather(early, 'z', axis=0, tiled=True))  24 us
    ppermute x13, starting transfers between devices, ahead(): lax.ppermute(block, axis, [(i, (i + distance) % count) for i in range(cou...  22 us
    all_to_all x1, blocking collectives, on_device(): lax.all_to_all(sent.reshape(seq_count, LINES, 128), SEQ, 0, 0, tiled=True)  21.8 us
    ppermute x13, waiting for transfers between devices, ahead(): lax.ppermute(block, axis, [(i, (i + distance) % count) for i in range(cou...  11.9 us
    unnamed x48, local copies, waits for them, and re-layouts  8.88 us
    all_to_all x1, starting transfers between devices, on_device(): lax.all_to_all(scanned.reshape(seq_count, LINES, 128), SEQ, 0, 0, tiled=T...  6.26 us
    pallas_call x2, Pallas kernels, pack(): pl.pallas_call(body, out_shape=jax.ShapeDtypeStruct((args[0].shape[0], wi...  3.18 us
  transfers between devices with their start and end apart: 16, of which 6 were waited for; matrix products, arithmetic and copies ran while one was open for 1% of the time, Pallas kernels for 16%

profile of v9, /device:TPU:1, one launch (start us, length us, event | category | flops | bytes accessed | tf_op | source)
XLA Modules:
  0.0 146.8 jit_solution(12476142276223323049)
XLA Ops:
  6.6 1.6 %shard_map.136 = bf16[24,1664]{1,0:T(8,128)(2,1)} custom-call(f32[24,768]{1,0:T(8,128)} %gate_ref.1, f32[24,256]{1,0:T(8,128)} %shared_ref.3, f32[24,768]{1,0:T(8,128)} %bitcast.18), custom_call_target="tpu_custom_call" | custom-call | tf_op jit(solution)/shard_map/pallas_call | solution.py:40
  8.2 2.2 %collective-permute-start.3 = (bf16[256,384]{1,0:T(8,128)(2,1)}, bf16[256,384]{1,0:T(8,128)(2,1)S(1)}, u32[]{:S(2)}, u32[]{:S(2)}) collective-permute-start(bf16[256,384]{1,0:T(8,128)(2,1)} %refs_2_.2), channel_id=1, source_target_pairs={{0,1},{1,2},{2,3},{3,0},{4,5},{5,6},{6,7},{7,4},{8,9},{9,10},{10,1... | collective-permute-start | bytes 589832 | tf_op jit(solution)/shard_map/ppermute | solution.py:21
  10.4 2.6 %collective-permute-start.4 = (bf16[256,384]{1,0:T(8,128)(2,1)}, bf16[256,384]{1,0:T(8,128)(2,1)S(1)}, u32[]{:S(2)}, u32[]{:S(2)}) collective-permute-start(bf16[256,384]{1,0:T(8,128)(2,1)} %refs_2_.2), channel_id=1, source_target_pairs={{0,2},{1,3},{2,0},{3,1},{4,6},{5,7},{6,4},{7,5},{8,10},{9,11},{10,... | collective-permute-start | bytes 589832 | tf_op jit(solution)/shard_map/ppermute | solution.py:21
  13.0 1.1 collective-permute-start.5
  14.1 1.6 %shard_map.137 = bf16[24,1024]{1,0:T(8,128)(2,1)} custom-call(f32[24,768]{1,0:T(8,128)} %value_ref.1, f32[24,256]{1,0:T(8,128)} %shared_ref.3, f32[12,24]{1,0:T(8,128)} %bitcast.19), custom_call_target="tpu_custom_call" | custom-call | tf_op jit(solution)/shard_map/pallas_call | solution.py:40
  15.7 24.0 %all_gather.7.refs_2_ = bf16[192,1024]{1,0:T(8,128)(2,1)S(1)} all-gather(bf16[24,1024]{1,0:T(8,128)(2,1)} %shard_map.137), channel_id=1, replica_groups=mesh['x'=4,'z'=8,'core'=2,'tp'=4] {'z'}, dimensions={0}, use_global_device_ids=true | all-gather | bytes 442368 | tf_op jit(solution)/shard_map/all_gather | solution.py:411
  39.6 2.3 %collective-permute-start.2 = (bf16[192,1024]{1,0:T(8,128)(2,1)S(1)}, bf16[192,1024]{1,0:T(8,128)(2,1)S(1)}, u32[]{:S(2)}, u32[]{:S(2)}) collective-permute-start(bf16[192,1024]{1,0:T(8,128)(2,1)S(1)} %all_gather.7.refs_2_), channel_id=1, source_target_pairs={{0,192},{64,0},{128,64},{192,128},{1,193},{65,1},{129,65},{193,129... | collective-permute-start | bytes 1179656 | tf_op jit(solution)/shard_map/ppermute | solution.py:21
  42.6 1.6 %collective-permute-start.1 = (bf16[192,1024]{1,0:T(8,128)(2,1)S(1)}, bf16[192,1024]{1,0:T(8,128)(2,1)S(1)}, u32[]{:S(2)}, u32[]{:S(2)}) collective-permute-start(bf16[192,1024]{1,0:T(8,128)(2,1)S(1)} %all_gather.7.refs_2_), channel_id=1, source_target_pairs={{0,128},{64,192},{128,0},{192,64},{1,129},{65,193},{129,1},{193,65... | collective-permute-start | bytes 1179656 | tf_op jit(solution)/shard_map/ppermute | solution.py:21
  44.3 7.9 %collective-permute-start.7 = (bf16[192,1024]{1,0:T(8,128)(2,1)S(1)}, bf16[192,1024]{1,0:T(8,128)(2,1)S(1)}, u32[]{:S(2)}, u32[]{:S(2)}) collective-permute-start(bf16[192,1024]{1,0:T(8,128)(2,1)S(1)} %all_gather.7.refs_2_), channel_id=1, source_target_pairs={{0,4},{4,0},{1,5},{5,1},{2,6},{6,2},{3,7},{7,3},{8,12},{12,8},{9,1... | collective-permute-start | bytes 1179656 | tf_op jit(solution)/shard_map/ppermute | solution.py:21
  52.9 2.6 %collective-permute-start.6 = (bf16[8,1536]{1,0:T(8,128)(2,1)S(1)}, bf16[8,1536]{1,0:T(8,128)(2,1)S(1)}, u32[]{:S(2)}, u32[]{:S(2)}) collective-permute-start(bf16[8,1536]{1,0:T(8,128)(2,1)S(1)} %pad_maximum_fusion), channel_id=1, source_target_pairs={{0,4},{4,8},{8,12},{12,16},{16,20},{20,24},{24,28},{28,32},{32,36}... | collective-permute-start | bytes 73736 | tf_op jit(solution)/shard_map/ppermute | solution.py:413
  55.6 0.8 collective-permute-done.6.refs_6_
  56.4 0.9 copy-done.10
  57.3 0.9 copy-done.17
  58.9 4.1 %shard_map.138.refs_10_ = bf16[264,1536]{1,0:T(8,128)(2,1)S(1)} custom-call(s32[3]{0:T(128)S(1)} %pad_add_fusion.refs_0_, s32[64]{0:T(128)S(1)} %copy-done.19, bf16[256,384]{1,0:T(8,128)(2,1)S(1)} %copy-done.10, bf16[256,384]{1,0:T(8,128)(2,1)S(1)} %collective-permute-done.3.refs_3_, bf16[256,384]{1,0:T(8,128)(2,1)S(1)} %collective-permute-done.4.refs_4_, ...), custom_call_target="tpu_custom_call" | custom-call | flops 1245708288 | bytes 811276 | tf_op jit(solution)/shard_map/pallas_call | solution.py:92
  64.0 1.4 collective-permute-done.10.refs_9_
  65.4 0.8 collective-permute-done.8.refs_7_
  66.9 6.4 %shard_map.139 = (bf16[256,768]{1,0:T(8,128)(2,1)S(1)}, bf16[256,128]{1,0:T(8,128)(2,1)S(1)}, f32[256,128]{1,0:T(8,128)S(1)}, f32[256,128]{1,0:T(8,128)S(1)}, bf16[1024,128]{1,0:T(8,128)(2,1)S(1)}) custom-call(s32[1]{0:T(128)} %bitcast.2.refs_0_, s32[8]{0:T(128)S(1)} %copy-done.7, bf16[192,1024]{1,0:T(8,128)(2,1)S(1)} %all_gather.7.refs_2_, ...), custom_call_target="tpu_custom_call" | custom-call | flops 830472192 | bytes 3973252 | tf_op jit(solution)/shard_map/pallas_call | solution.py:92
  74.6 21.8 %all_to_all.10 = bf16[64,16,128]{2,1,0:T(8,128)(2,1)S(1)} all-to-all(bf16[64,16,128]{2,1,0:T(8,128)(2,1)S(1)} %bitcast.14), channel_id=1, replica_groups=mesh['x'=4,'z'=8,'core'=2,'tp'=4] {'x','z','core'}, dimensions={0} | all-to-all | bytes 524288 | tf_op jit(solution)/shard_map/all_to_all | solution.py:454
  96.4 1.4 shard_map.140
  97.9 6.3 %all-to-all-start.1 = ((bf16[64,16,128]{2,1,0:T(8,128)(2,1)}), bf16[64,16,128]{2,1,0:T(8,128)(2,1)S(1)}, u32[]{:S(2)}, u32[]{:S(2)}) async-start(bf16[64,16,128]{2,1,0:T(8,128)(2,1)} %bitcast.10), calls=%async_computation.1 | async-start | bytes 524288 | tf_op jit(solution)/shard_map/all_to_all | solution.py:463
  105.5 0.9 copy-done.13
  106.4 0.9 copy-done.15
  107.3 0.9 copy-done.18
  108.3 4.1 %shard_map.141.refs_3_ = bf16[264,1536]{1,0:T(8,128)(2,1)S(1)} custom-call(s32[3]{0:T(128)S(1)} %pad_add_fusion.refs_0_, s32[64]{0:T(128)S(1)} %copy-done.20, bf16[256,384]{1,0:T(8,128)(2,1)S(1)} %copy-done.11, bf16[256,384]{1,0:T(8,128)(2,1)S(1)} %copy-done.13, bf16[256,384]{1,0:T(8,128)(2,1)S(1)} %copy-done.15, bf16[256,384]{1,0:T(8,128)(2,1)S(1)} %copy-done.18, ...), custom_call_target="tpu_custom_call" | custom-call | flops 1245708288 | bytes 811276 | tf_op jit(solution)/shard_map/pallas_call | solution.py:92
  112.4 0.9 copy-done
  113.3 6.5 %shard_map.142 = (bf16[256,768]{1,0:T(8,128)(2,1)}, bf16[256,768]{1,0:T(8,128)(2,1)}, bf16[256,128]{1,0:T(8,128)(2,1)}) custom-call(s32[1]{0:T(128)} %bitcast.2.refs_0_, s32[8]{0:T(128)} %refs_1_.7, bf16[1536,1664]{1,0:T(8,128)(2,1)} %all-gather.2.cloned.1.call-done.refs_2_.refs_1_, bf16[264,1536]{1,0:T(8,128)(2,1)} %copy-done, f32[4,256]{1,0:T(4,128)} %refs_4_.1, ...), custom_call_target="tpu_custom_call" | custom-call | flops 726663168 | bytes 6650916 | tf_op jit(solution)/shard_map/pallas_call | solution.py:92
  120.5 5.2 %shard_map.143 = (bf16[264,384]{1,0:T(8,128)(2,1)}, bf16[264,384]{1,0:T(8,128)(2,1)}, bf16[264,384]{1,0:T(8,128)(2,1)}, bf16[264,384]{1,0:T(8,128)(2,1)}) custom-call(s32[1]{0:T(128)} %bitcast.refs_0_, bf16[1536,1664]{1,0:T(8,128)(2,1)} %all-gather.2.cloned.1.call-done.refs_2_.refs_1_, bf16[1024,128]{1,0:T(8,128)(2,1)} %bitcast.17, ...), custom_call_target="tpu_custom_call" | custom-call | flops 603979776 | bytes 6228996 | tf_op jit(solution)/shard_map/pallas_call | solution.py:92
  125.6 0.9 collective-permute-start.11
  127.2 1.9 %collective-permute-start.13 = (bf16[264,384]{1,0:T(8,128)(2,1)}, bf16[264,384]{1,0:T(8,128)(2,1)S(1)}, u32[]{:S(2)}, u32[]{:S(2)}) collective-permute-start(bf16[264,384]{1,0:T(8,128)(2,1)} %get-tuple-element.40), channel_id=1, source_target_pairs={{0,3},{1,0},{2,1},{3,2},{4,7},{5,4},{6,5},{7,6},{8,11},{9,8},{10,9... | collective-permute-start | bytes 608264 | tf_op jit(solution)/shard_map/ppermute | solution.py:21
  129.0 8.6 %collective-permute-done.11 = bf16[264,384]{1,0:T(8,128)(2,1)S(1)} collective-permute-done((bf16[264,384]{1,0:T(8,128)(2,1)}, bf16[264,384]{1,0:T(8,128)(2,1)S(1)}, u32[]{:S(2)}, u32[]{:S(2)}) %collective-permute-start.11) | collective-permute-done | bytes 202784 | tf_op jit(solution)/shard_map/ppermute | solution.py:21
  138.1 1.0 convert_add_fusion
  139.1 0.8 fusion
  (71 shorter events, 8.2 us)
Async XLA Ops:
  6.5 60.3 %copy-start.8 = (f32[12]{0:T(128)S(1)}, f32[12]{0:T(128)}, u32[]{:S(2)}) copy-start(f32[12]{0:T(128)} %param.21) | copy-start | bytes 148
  6.5 60.3 %copy-start.9 = (f32[12]{0:T(128)S(1)}, f32[12]{0:T(128)}, u32[]{:S(2)}) copy-start(f32[12]{0:T(128)} %param.22) | copy-start | bytes 148
  6.5 60.3 %copy-start.6 = (f32[4,768]{1,0:T(4,128)S(1)}, f32[4,768]{1,0:T(4,128)}, u32[]{:S(2)}) copy-start(f32[4,768]{1,0:T(4,128)} %refs_11_.1) | copy-start | bytes 36868
  6.5 60.3 %copy-start.5 = (f32[4,256]{1,0:T(4,128)S(1)}, f32[4,256]{1,0:T(4,128)}, u32[]{:S(2)}) copy-start(f32[4,256]{1,0:T(4,128)} %refs_4_.1) | copy-start | bytes 12292
  6.5 60.3 %copy-start.7 = (s32[8]{0:T(128)S(1)}, s32[8]{0:T(128)}, u32[]{:S(2)}) copy-start(s32[8]{0:T(128)} %refs_1_.7) | copy-start | bytes 100
  6.6 106.7 %all-gather.2.cloned.1.call-start = ((), (), s32[]{:S(2)}) async-start(), calls=%async_computation.2 | async-start | bytes 5191680 | tf_op jit(solution)/shard_map/all_gather | solution.py:410
  8.2 34.4 %collective-permute-start.3 = (bf16[256,384]{1,0:T(8,128)(2,1)}, bf16[256,384]{1,0:T(8,128)(2,1)S(1)}, u32[]{:S(2)}, u32[]{:S(2)}) collective-permute-start(bf16[256,384]{1,0:T(8,128)(2,1)} %refs_2_.2), channel_id=1, source_target_pairs={{0,1},{1,2},{2,3},{3,0},{4,5},{5,6},{6,7},{7,4},{8,9},{9,10},{10,1... | collective-permute-start | bytes 589832 | tf_op jit(solution)/shard_map/ppermute | solution.py:21
  10.4 33.8 %collective-permute-start.4 = (bf16[256,384]{1,0:T(8,128)(2,1)}, bf16[256,384]{1,0:T(8,128)(2,1)S(1)}, u32[]{:S(2)}, u32[]{:S(2)}) collective-permute-start(bf16[256,384]{1,0:T(8,128)(2,1)} %refs_2_.2), channel_id=1, source_target_pairs={{0,2},{1,3},{2,0},{3,1},{4,6},{5,7},{6,4},{7,5},{8,10},{9,11},{10,... | collective-permute-start | bytes 589832 | tf_op jit(solution)/shard_map/ppermute | solution.py:21
  13.0 39.2 %collective-permute-start.5 = (bf16[256,384]{1,0:T(8,128)(2,1)}, bf16[256,384]{1,0:T(8,128)(2,1)S(1)}, u32[]{:S(2)}, u32[]{:S(2)}) collective-permute-start(bf16[256,384]{1,0:T(8,128)(2,1)} %refs_2_.2), channel_id=1, source_target_pairs={{0,3},{1,0},{2,1},{3,2},{4,7},{5,4},{6,5},{7,6},{8,11},{9,8},{10,9... | collective-permute-start | bytes 589832 | tf_op jit(solution)/shard_map/ppermute | solution.py:21
  39.6 23.4 %collective-permute-start.2 = (bf16[192,1024]{1,0:T(8,128)(2,1)S(1)}, bf16[192,1024]{1,0:T(8,128)(2,1)S(1)}, u32[]{:S(2)}, u32[]{:S(2)}) collective-permute-start(bf16[192,1024]{1,0:T(8,128)(2,1)S(1)} %all_gather.7.refs_2_), channel_id=1, source_target_pairs={{0,192},{64,0},{128,64},{192,128},{1,193},{65,1},{129,65},{193,129... | collective-permute-start | bytes 1179656 | tf_op jit(solution)/shard_map/ppermute | solution.py:21
  41.9 21.3 %collective-permute-start = (bf16[192,1024]{1,0:T(8,128)(2,1)S(1)}, bf16[192,1024]{1,0:T(8,128)(2,1)S(1)}, u32[]{:S(2)}, u32[]{:S(2)}) collective-permute-start(bf16[192,1024]{1,0:T(8,128)(2,1)S(1)} %all_gather.7.refs_2_), channel_id=1, source_target_pairs={{0,64},{64,128},{128,192},{192,0},{1,65},{65,129},{129,193},{193,1... | collective-permute-start | bytes 1179656 | tf_op jit(solution)/shard_map/ppermute | solution.py:21
  42.6 20.5 %copy-start.12 = (bf16[256,384]{1,0:T(8,128)(2,1)}, bf16[256,384]{1,0:T(8,128)(2,1)S(1)}, u32[]{:S(2)}) copy-start(bf16[256,384]{1,0:T(8,128)(2,1)S(1)} %collective-permute-done.3.refs_3_) | copy-start | bytes 589828
  42.6 21.1 %collective-permute-start.1 = (bf16[192,1024]{1,0:T(8,128)(2,1)S(1)}, bf16[192,1024]{1,0:T(8,128)(2,1)S(1)}, u32[]{:S(2)}, u32[]{:S(2)}) collective-permute-start(bf16[192,1024]{1,0:T(8,128)(2,1)S(1)} %all_gather.7.refs_2_), channel_id=1, source_target_pairs={{0,128},{64,192},{128,0},{192,64},{1,129},{65,193},{129,1},{193,65... | collective-permute-start | bytes 1179656 | tf_op jit(solution)/shard_map/ppermute | solution.py:21
  44.2 18.8 %copy-start.14 = (bf16[256,384]{1,0:T(8,128)(2,1)}, bf16[256,384]{1,0:T(8,128)(2,1)S(1)}, u32[]{:S(2)}) copy-start(bf16[256,384]{1,0:T(8,128)(2,1)S(1)} %collective-permute-done.4.refs_4_) | copy-start | bytes 589828
  44.3 19.7 %collective-permute-start.7 = (bf16[192,1024]{1,0:T(8,128)(2,1)S(1)}, bf16[192,1024]{1,0:T(8,128)(2,1)S(1)}, u32[]{:S(2)}, u32[]{:S(2)}) collective-permute-start(bf16[192,1024]{1,0:T(8,128)(2,1)S(1)} %all_gather.7.refs_2_), channel_id=1, source_target_pairs={{0,4},{4,0},{1,5},{5,1},{2,6},{6,2},{3,7},{7,3},{8,12},{12,8},{9,1... | collective-permute-start | bytes 1179656 | tf_op jit(solution)/shard_map/ppermute | solution.py:21
  52.9 51.3 %copy-start.23 = (f32[12]{0:T(128)S(1)}, f32[12]{0:T(128)}, u32[]{:S(2)}) copy-start(f32[12]{0:T(128)} %param.23) | copy-start | bytes 148
  52.9 52.0 %copy-start.22 = (f32[768]{0:T(1024)S(1)}, f32[768]{0:T(1024)}, u32[]{:S(2)}) copy-start(f32[768]{0:T(1024)} %param.24) | copy-start | bytes 9220
  52.9 52.6 %copy-start.20 = (s32[64]{0:T(128)S(1)}, s32[64]{0:T(128)}, u32[]{:S(2)}) copy-start(s32[64]{0:T(128)} %refs_1_.6) | copy-start | bytes 772
  52.9 3.5 %collective-permute-start.6 = (bf16[8,1536]{1,0:T(8,128)(2,1)S(1)}, bf16[8,1536]{1,0:T(8,128)(2,1)S(1)}, u32[]{:S(2)}, u32[]{:S(2)}) collective-permute-start(bf16[8,1536]{1,0:T(8,128)(2,1)S(1)} %pad_maximum_fusion), channel_id=1, source_target_pairs={{0,4},{4,8},{8,12},{12,16},{16,20},{20,24},{24,28},{28,32},{32,36}... | collective-permute-start | bytes 73736 | tf_op jit(solution)/shard_map/ppermute | solution.py:413
  56.4 0.9 copy-start.10
  57.3 0.9 copy-start.17
  58.9 46.6 %copy-start.11 = (bf16[256,384]{1,0:T(8,128)(2,1)S(1)}, bf16[256,384]{1,0:T(8,128)(2,1)}, u32[]{:S(2)}) copy-start(bf16[256,384]{1,0:T(8,128)(2,1)} %refs_2_.2) | copy-start | bytes 589828
  63.1 2.3 %collective-permute-start.10 = (bf16[192,1024]{1,0:T(8,128)(2,1)S(1)}, bf16[192,1024]{1,0:T(8,128)(2,1)S(1)}, u32[]{:S(2)}, u32[]{:S(2)}) collective-permute-start(bf16[192,1024]{1,0:T(8,128)(2,1)S(1)} %collective-permute-done.2.refs_5_), channel_id=1, source_target_pairs={{0,4},{4,0},{1,5},{5,1},{2,6},{6,2},{3,7},{7,3},{8,12},{12,8},{9,1... | collective-permute-start | bytes 1179656 | tf_op jit(solution)/shard_map/ppermute | solution.py:21
  63.2 3.0 %collective-permute-start.8 = (bf16[192,1024]{1,0:T(8,128)(2,1)S(1)}, bf16[192,1024]{1,0:T(8,128)(2,1)}, u32[]{:S(2)}, u32[]{:S(2)}) collective-permute-start(bf16[192,1024]{1,0:T(8,128)(2,1)S(1)} %collective-permute-done.refs_3_), channel_id=1, source_target_pairs={{0,4},{4,0},{1,5},{5,1},{2,6},{6,2},{3,7},{7,3},{8,12},{12,8},{9,1... | collective-permute-start | bytes 1179656 | tf_op jit(solution)/shard_map/ppermute | solution.py:21
  63.7 3.1 %collective-permute-start.9 = (bf16[192,1024]{1,0:T(8,128)(2,1)S(1)}, bf16[192,1024]{1,0:T(8,128)(2,1)}, u32[]{:S(2)}, u32[]{:S(2)}) collective-permute-start(bf16[192,1024]{1,0:T(8,128)(2,1)S(1)} %collective-permute-done.1.refs_4_), channel_id=1, source_target_pairs={{0,4},{4,0},{1,5},{5,1},{2,6},{6,2},{3,7},{7,3},{8,12},{12,8},{9,1... | collective-permute-start | bytes 1179656 | tf_op jit(solution)/shard_map/ppermute | solution.py:21
  74.6 23.2 %copy-start.1 = (bf16[256,768]{1,0:T(8,128)(2,1)}, bf16[256,768]{1,0:T(8,128)(2,1)S(1)}, u32[]{:S(2)}) copy-start(bf16[256,768]{1,0:T(8,128)(2,1)S(1)} %get-tuple-element.30.refs_5_) | copy-start | bytes 1179652
  74.6 23.2 %copy-start.2 = (f32[256,128]{1,0:T(8,128)}, f32[256,128]{1,0:T(8,128)S(1)}, u32[]{:S(2)}) copy-start(f32[256,128]{1,0:T(8,128)S(1)} %get-tuple-element.32.refs_7_) | copy-start | bytes 393220
  97.9 21.9 %all-to-all-start.1 = ((bf16[64,16,128]{2,1,0:T(8,128)(2,1)}), bf16[64,16,128]{2,1,0:T(8,128)(2,1)S(1)}, u32[]{:S(2)}, u32[]{:S(2)}) async-start(bf16[64,16,128]{2,1,0:T(8,128)(2,1)} %bitcast.10), calls=%async_computation.1 | async-start | bytes 524288 | tf_op jit(solution)/shard_map/all_to_all | solution.py:463
  105.5 0.9 copy-start.13
  125.6 12.0 %collective-permute-start.11 = (bf16[264,384]{1,0:T(8,128)(2,1)}, bf16[264,384]{1,0:T(8,128)(2,1)S(1)}, u32[]{:S(2)}, u32[]{:S(2)}) collective-permute-start(bf16[264,384]{1,0:T(8,128)(2,1)} %get-tuple-element.38), channel_id=1, source_target_pairs={{0,1},{1,2},{2,3},{3,0},{4,5},{5,6},{6,7},{7,4},{8,9},{9,10},{10,1... | collective-permute-start | bytes 608264 | tf_op jit(solution)/shard_map/ppermute | solution.py:21
  126.5 11.1 %collective-permute-start.12 = (bf16[264,384]{1,0:T(8,128)(2,1)}, bf16[264,384]{1,0:T(8,128)(2,1)S(1)}, u32[]{:S(2)}, u32[]{:S(2)}) collective-permute-start(bf16[264,384]{1,0:T(8,128)(2,1)} %get-tuple-element.39), channel_id=1, source_target_pairs={{0,2},{1,3},{2,0},{3,1},{4,6},{5,7},{6,4},{7,5},{8,10},{9,11},{10,... | collective-permute-start | bytes 608264 | tf_op jit(solution)/shard_map/ppermute | solution.py:21
  127.2 10.9 %collective-permute-start.13 = (bf16[264,384]{1,0:T(8,128)(2,1)}, bf16[264,384]{1,0:T(8,128)(2,1)S(1)}, u32[]{:S(2)}, u32[]{:S(2)}) collective-permute-start(bf16[264,384]{1,0:T(8,128)(2,1)} %get-tuple-element.40), channel_id=1, source_target_pairs={{0,3},{1,0},{2,1},{3,2},{4,7},{5,4},{6,5},{7,6},{8,11},{9,8},{10,9... | collective-permute-start | bytes 608264 | tf_op jit(solution)/shard_map/ppermute | solution.py:21
  (8 other events, 6.1 us)
Sparse Core Ops, SparseCore 0:
  10.2 86.5 all-gather.1

commit v10 on v8

--- a/solution.py
+++ b/solution.py
@@ -51,10 +51,11 @@
 
 
 def call(
-    body, shapes, args, scalars=0, blocks=0, near_in=0, near_out=0, scratch=(), flops=0, grant=60
+    body, shapes, args, scalars=0, blocks=0, near_in=0, near_out=0, sent=0, scratch=(), flops=0, grant=60
 ):
     hbm, vmem = pl.BlockSpec(memory_space=pltpu.HBM), pl.BlockSpec(memory_space=pltpu.VMEM)
     fixed = scalars + blocks + near_in
+    near_out = near_out + sent
     far_in, far_out = args[fixed:], shapes[near_out:]
     moved = sum(x.size * x.dtype.itemsize for x in args)
 
@@ -89,6 +90,8 @@
     room = [pltpu.VMEM(x.shape, x.dtype) for x in far_in]
     room += [pltpu.VMEM(shape, kind) for shape, kind in far_out]
     room += [pltpu.VMEM(shape, kind) for shape, kind in scratch]
+    if sent:
+        room.append(pltpu.SemaphoreType.DMA((sent,)))
     room.append(pltpu.SemaphoreType.DMA((len(far_in) + len(far_out) + blocks,)))
     return pl.pallas_call(
         wrapped,
@@ -97,7 +100,7 @@
         + [hbm] * blocks
         + [vmem] * near_in
         + [hbm] * len(far_in),
-        out_specs=[vmem] * near_out + [hbm] * len(far_out),
+        out_specs=[vmem] * (near_out - sent) + [hbm] * (len(far_out) + sent),
         scratch_shapes=room,
         compiler_params=pltpu.CompilerParams(vmem_limit_bytes=grant << 20),
         cost_estimate=pl.CostEstimate(flops=flops, bytes_accessed=moved, transcendentals=0),
@@ -197,10 +200,16 @@
     tokens, inner = x_ref.shape
     copies = fetch(blocks, held, sems, slice(0, held.shape[1]))
     ready()
-    for copy in copies:
+    half, middle = len(blocks) // 2, held.shape[0] // 2
+    for copy in copies[:half]:
         copy.wait()
     for at in range(0, held.shape[1], 256):
-        part = dot(h_ref[...], held[:, at : at + 256]).astype(BF16).astype(F32)
+        rows[:, at : at + 256] = dot(h_ref[:, :middle], held[:middle, at : at + 256])
+    for copy in copies[half:]:
+        copy.wait()
+    for at in range(0, held.shape[1], 256):
+        part = rows[:, at : at + 256] + dot(h_ref[:, middle:], held[middle:, at : at + 256])
+        part = part.astype(BF16).astype(F32)
         rows[EDGE:, at : at + 256] = part[:tokens]
         rows[:EDGE, at : at + 256] = part[tokens:]
     first = first_ref[0]
@@ -314,8 +323,8 @@
 
 
 def last_body(ready, sems, turn_ref, *refs):
-    *blocks, carried_ref, direct_ref, carry_ref, c_ref, gain = refs[:-8]
-    *outs, held, lines, shares, out_w = refs[-8:]
+    *blocks, carried_ref, direct_ref, carry_ref, c_ref, gain = refs[:-9]
+    *outs, held, lines, shares, out_w, leaving = refs[-9:]
     half, wide, inner = len(blocks) // 2, blocks[0].shape[2], out_w.shape[4]
     copies = []
     for i, block in enumerate(blocks):
@@ -341,11 +350,6 @@
     scaled = (gated * gain[...]).astype(BF16)
     nt = (((1,), (1,)), ((), ()))
     features = shares.shape[2]
-    for copy in copies:
-        copy.wait()
-    for i in range(shares.shape[0]):
-        rows = out_w[i].reshape(features, inner)
-        shares[i] = lax.dot_general(scaled, rows, nt, preferred_element_type=F32).astype(BF16)
     squares = lax.dot_general(
         jnp.ones((8, inner), F32),
         gated * gated,
@@ -356,10 +360,19 @@
     hi = squares.astype(BF16).astype(F32)
     row = iota(squares.shape, 0)
     riding = jnp.where(row == 0, hi, jnp.where(row == 1, squares - hi, 0.0)).astype(BF16)
-    for d, out in enumerate(outs):
-        out[:tokens] = shares[(turn_ref[0] + len(outs) - d) % len(outs)]
-        out[tokens:, :tokens] = riding
-        out[tokens:, tokens:] = jnp.zeros((8, features - tokens), BF16)
+    for copy in copies:
+        copy.wait()
+    copies = []
+    for d in list(range(1, len(outs))) + [0]:
+        rows = out_w[(turn_ref[0] + len(outs) - d) & (len(outs) - 1)].reshape(features, inner)
+        product = lax.dot_general(scaled, rows, nt, preferred_element_type=F32)
+        shares[d, :tokens] = product.astype(BF16)
+        shares[d, tokens:, :tokens] = riding
+        shares[d, tokens:, tokens:] = jnp.zeros((8, features - tokens), BF16)
+        copies.append(pltpu.make_async_copy(shares.at[d], outs[d], leaving.at[d]))
+        copies[-1].start()
+    for copy in copies:
+        copy.wait()
 
 
 def on_device(
@@ -490,16 +503,17 @@
         scratch=[
             ((state, inner), BF16),
             ((seq_count * LINES, 128), F32),
-            ((tp_count, tokens, features), BF16),
+            ((tp_count, tokens + 8, features), BF16),
             ((x_size, z_size, core_size, rows_here, inner), BF16),
         ],
+        sent=tp_count,
         flops=2 * tokens * inner * model_width,
     )
     parts = [shares[0]] + [ahead(shares[d], "tp", d) for d in range(1, tp_count)]
-    summed = sum(part.astype(F32) for part in parts)
-    total = summed[tokens, :tokens] + summed[tokens + 1, :tokens]
-    scale = lax.rsqrt(total / (inner * tp_count) + EPSILON)
-    return (summed[:tokens] * scale[:, None]).astype(BF16)
+    total = sum(part[tokens : tokens + 2, :tokens].astype(F32) for part in parts)
+    scale = lax.rsqrt((total[0] + total[1]) / (inner * tp_count) + EPSILON)
+    scale = tie(scale)
+    return (sum(part[:tokens].astype(F32) for part in parts) * scale[:, None]).astype(BF16)
 
 
 def solution(mesh):

time: 137 us -> 138 us (level)
  no operation moved by 1% of the time
where the time goes in v10:
time: 138 us
  blocking collectives  48.4 us (35%)
  starting transfers between devices  40.1 us (29%)
  Pallas kernels  27.2 us (20%)
  waiting for transfers between devices  12.8 us (9%)
  local copies, waits for them, and re-layouts  4.92 us (4%)
  other arithmetic  3.74 us (3%)
    ppermute x20, starting transfers between devices, ahead(): lax.ppermute(block, axis, [(i, (i + distance) % count) for i in range(cou...  30 us
    pallas_call x5, Pallas kernels, call(): pl.pallas_call(wrapped, out_shape=[jax.ShapeDtypeStruct(shape, kind) for...  25.5 us
    all_gather x1, blocking collectives, on_device(): along_z = lax.all_gather(packed, 'z', axis=0, tiled=True)  25.3 us
    all_to_all x1, blocking collectives, on_device(): lax.all_to_all(sent.reshape(seq_count, LINES, 128), SEQ, 0, 0, tiled=True)  23.1 us
    ppermute x20, waiting for transfers between devices, ahead(): lax.ppermute(block, axis, [(i, (i + distance) % count) for i in range(cou...  10.8 us
    all_to_all x1, starting transfers between devices, on_device(): lax.all_to_all(scanned.reshape(seq_count, LINES, 128), SEQ, 0, 0, tiled=T...  7.96 us
    unnamed x32, local copies, waits for them, and re-layouts  2.83 us
  transfers between devices with their start and end apart: 22, of which 4 were waited for; matrix products, arithmetic and copies ran while one was open for 2% of the time, Pallas kernels for 16%

profile of v10, /device:TPU:1, one launch (start us, length us, event | category | flops | bytes accessed | tf_op | source)
XLA Modules:
  0.0 137.6 jit_solution(5165990144638903442)
XLA Ops:
  0.0 2.1 %collective-permute-start.1 = (bf16[256,384]{1,0:T(8,128)(2,1)}, bf16[256,384]{1,0:T(8,128)(2,1)S(1)}, u32[]{:S(2)}, u32[]{:S(2)}) collective-permute-start(bf16[256,384]{1,0:T(8,128)(2,1)} %refs_2_.1), channel_id=1, source_target_pairs={{0,1},{1,2},{2,3},{3,0},{4,5},{5,6},{6,7},{7,4},{8,9},{9,10},{10,1... | collective-permute-start | bytes 589832 | tf_op jit(solution)/shard_map/ppermute | solution.py:21
  2.1 2.6 %collective-permute-start.2 = (bf16[256,384]{1,0:T(8,128)(2,1)}, bf16[256,384]{1,0:T(8,128)(2,1)S(1)}, u32[]{:S(2)}, u32[]{:S(2)}) collective-permute-start(bf16[256,384]{1,0:T(8,128)(2,1)} %refs_2_.1), channel_id=1, source_target_pairs={{0,2},{1,3},{2,0},{3,1},{4,6},{5,7},{6,4},{7,5},{8,10},{9,11},{10,... | collective-permute-start | bytes 589832 | tf_op jit(solution)/shard_map/ppermute | solution.py:21
  4.7 1.1 collective-permute-start.3
  5.8 1.7 %shard_map.136 = bf16[24,2688]{1,0:T(8,128)(2,1)} custom-call(f32[24,768]{1,0:T(8,128)} %value_ref.1, f32[24,256]{1,0:T(8,128)} %shared_ref.1, f32[12,24]{1,0:T(8,128)} %bitcast.31, f32[24,768]{1,0:T(8,128)} %gate_ref.1, f32[24,768]{1,0:T(8,128)} %bitcast.30), custom_call_target="tpu_custom_call" | custom-call | tf_op jit(solution)/shard_map/pallas_call | solution.py:45
  7.5 25.3 %all_gather.3 = bf16[192,2688]{1,0:T(8,128)(2,1)S(1)} all-gather(bf16[24,2688]{1,0:T(8,128)(2,1)} %shard_map.136), channel_id=1, replica_groups=mesh['x'=4,'z'=8,'core'=2,'tp'=4] {'z'}, dimensions={0}, use_global_device_ids=true | all-gather | bytes 1161216 | tf_op jit(solution)/shard_map/all_gather | solution.py:416
  32.9 1.3 collective-permute-start.8
  34.2 1.5 %collective-permute-start = (bf16[192,1024]{1,0:T(8,128)(2,1)S(1)}, bf16[192,1024]{1,0:T(8,128)(2,1)S(1)}, u32[]{:S(2)}, u32[]{:S(2)}) collective-permute-start(bf16[192,1024]{1,0:T(8,128)(2,1)S(1)} %slice.64.refs_2_), channel_id=1, source_target_pairs={{0,192},{64,0},{128,64},{192,128},{1,193},{65,1},{129,65},{193,129... | collective-permute-start | bytes 1179656 | tf_op jit(solution)/shard_map/ppermute | solution.py:21
  35.7 0.7 slice.49
  36.4 1.5 %collective-permute-start.9 = (bf16[192,1024]{1,0:T(8,128)(2,1)S(1)}, bf16[192,1024]{1,0:T(8,128)(2,1)}, u32[]{:S(2)}, u32[]{:S(2)}) collective-permute-start(bf16[192,1024]{1,0:T(8,128)(2,1)S(1)} %slice.64.refs_2_), channel_id=1, source_target_pairs={{0,128},{64,192},{128,0},{192,64},{1,129},{65,193},{129,1},{193,65... | collective-permute-start | bytes 1179656 | tf_op jit(solution)/shard_map/ppermute | solution.py:21
  37.9 7.9 %collective-permute-start.10 = (bf16[192,1024]{1,0:T(8,128)(2,1)S(1)}, bf16[192,1024]{1,0:T(8,128)(2,1)S(1)}, u32[]{:S(2)}, u32[]{:S(2)}) collective-permute-start(bf16[192,1024]{1,0:T(8,128)(2,1)S(1)} %slice.64.refs_2_), channel_id=1, source_target_pairs={{0,4},{4,0},{1,5},{5,1},{2,6},{6,2},{3,7},{7,3},{8,12},{12,8},{9,1... | collective-permute-start | bytes 1179656 | tf_op jit(solution)/shard_map/ppermute | solution.py:21
  45.8 2.2 %collective-permute-start.4 = (bf16[8,1536]{1,0:T(8,128)(2,1)S(1)}, bf16[8,1536]{1,0:T(8,128)(2,1)S(1)}, u32[]{:S(2)}, u32[]{:S(2)}) collective-permute-start(bf16[8,1536]{1,0:T(8,128)(2,1)S(1)} %pad_maximum_fusion), channel_id=1, source_target_pairs={{0,4},{4,8},{8,12},{12,16},{16,20},{20,24},{24,28},{28,32},{32,36}... | collective-permute-start | bytes 73736 | tf_op jit(solution)/shard_map/ppermute | solution.py:421
  48.0 0.7 pad_add_fusion.1.refs_0_
  48.8 2.1 %collective-permute-start.11 = (bf16[192,1024]{1,0:T(8,128)(2,1)S(1)}, bf16[192,1024]{1,0:T(8,128)(2,1)}, u32[]{:S(2)}, u32[]{:S(2)}) collective-permute-start(bf16[192,1024]{1,0:T(8,128)(2,1)S(1)} %collective-permute-done.8.refs_3_), channel_id=1, source_target_pairs={{0,4},{4,0},{1,5},{5,1},{2,6},{6,2},{3,7},{7,3},{8,12},{12,8},{9,1... | collective-permute-start | bytes 1179656 | tf_op jit(solution)/shard_map/ppermute | solution.py:21
  51.5 5.2 %shard_map.137.refs_10_ = bf16[264,1536]{1,0:T(8,128)(2,1)} custom-call(s32[3]{0:T(128)} %pad_add_fusion.1.refs_0_, s32[64]{0:T(128)} %refs_1_.3, bf16[256,384]{1,0:T(8,128)(2,1)} %refs_2_.1, bf16[256,384]{1,0:T(8,128)(2,1)} %copy-done.12, bf16[256,384]{1,0:T(8,128)(2,1)} %copy-done.13, bf16[256,384]{1,0:T(8,128)(2,1)} %copy-done.14, bf16[8,1536]{1,0:T(8,128)(2,1)} %copy-done.15), custom_call_target="tpu_custom_call" | custom-call | flops 1245708288 | bytes 811276 | tf_op jit(solution)/shard_map/pallas_call | solution.py:96
  57.4 2.2 %collective-permute-start.5 = (bf16[192,1664]{1,0:T(8,128)(2,1)S(1)}, bf16[192,1664]{1,0:T(8,128)(2,1)S(1)}, u32[]{:S(2)}, u32[]{:S(2)}) collective-permute-start(bf16[192,1664]{1,0:T(8,128)(2,1)S(1)} %slice.68.refs_2_), channel_id=1, source_target_pairs={{0,64},{64,128},{128,192},{192,0},{1,65},{65,129},{129,193},{193,1... | collective-permute-start | bytes 1916936 | tf_op jit(solution)/shard_map/ppermute | solution.py:21
  59.6 1.7 %collective-permute-start.6 = (bf16[192,1664]{1,0:T(8,128)(2,1)S(1)}, bf16[192,1664]{1,0:T(8,128)(2,1)S(1)}, u32[]{:S(2)}, u32[]{:S(2)}) collective-permute-start(bf16[192,1664]{1,0:T(8,128)(2,1)S(1)} %slice.68.refs_2_), channel_id=1, source_target_pairs={{0,128},{64,192},{128,0},{192,64},{1,129},{65,193},{129,1},{193,65... | collective-permute-start | bytes 1916936 | tf_op jit(solution)/shard_map/ppermute | solution.py:21
  61.3 1.7 %collective-permute-start.7 = (bf16[192,1664]{1,0:T(8,128)(2,1)S(1)}, bf16[192,1664]{1,0:T(8,128)(2,1)S(1)}, u32[]{:S(2)}, u32[]{:S(2)}) collective-permute-start(bf16[192,1664]{1,0:T(8,128)(2,1)S(1)} %slice.68.refs_2_), channel_id=1, source_target_pairs={{0,192},{64,0},{128,64},{192,128},{1,193},{65,1},{129,65},{193,129... | collective-permute-start | bytes 1916936 | tf_op jit(solution)/shard_map/ppermute | solution.py:21
  63.0 6.5 %shard_map.138 = (bf16[256,768]{1,0:T(8,128)(2,1)}, bf16[256,128]{1,0:T(8,128)(2,1)}, f32[256,128]{1,0:T(8,128)}, f32[256,128]{1,0:T(8,128)}, bf16[1024,128]{1,0:T(8,128)(2,1)}) custom-call(s32[1]{0:T(128)} %bitcast.6.refs_0_, s32[8]{0:T(128)} %refs_1_.5, bf16[192,1024]{1,0:T(8,128)(2,1)} %copy-done.5, bf16[192,1024]{1,0:T(8,128)(2,1)} %copy-done.7, ...), custom_call_target="tpu_custom_call" | custom-call | flops 830472192 | bytes 3973252 | tf_op jit(solution)/shard_map/pallas_call | solution.py:96
  69.5 23.1 %all_to_all.10 = bf16[64,16,128]{2,1,0:T(8,128)(2,1)S(1)} all-to-all(bf16[64,16,128]{2,1,0:T(8,128)(2,1)} %bitcast.29), channel_id=1, replica_groups=mesh['x'=4,'z'=8,'core'=2,'tp'=4] {'x','z','core'}, dimensions={0} | all-to-all | bytes 524288 | tf_op jit(solution)/shard_map/all_to_all | solution.py:456
  92.6 1.4 %shard_map.139 = bf16[1024,128]{1,0:T(8,128)(2,1)} custom-call(bf16[1024,128]{1,0:T(8,128)(2,1)S(1)} %bitcast.22), custom_call_target="tpu_custom_call" | custom-call | bytes 262144 | tf_op jit(solution)/shard_map/pallas_call | solution.py:96
  95.4 8.0 %all-to-all-start.1 = ((bf16[64,16,128]{2,1,0:T(8,128)(2,1)}), bf16[64,16,128]{2,1,0:T(8,128)(2,1)S(1)}, u32[]{:S(2)}, u32[]{:S(2)}) async-start(bf16[64,16,128]{2,1,0:T(8,128)(2,1)} %bitcast.19), calls=%async_computation.1 | async-start | bytes 524288 | tf_op jit(solution)/shard_map/all_to_all | solution.py:465
  106.1 0.8 copy-done.4
  106.9 6.4 %shard_map.140 = (bf16[256,768]{1,0:T(8,128)(2,1)}, bf16[256,768]{1,0:T(8,128)(2,1)}, bf16[256,128]{1,0:T(8,128)(2,1)}) custom-call(s32[1]{0:T(128)} %bitcast.6.refs_0_, s32[8]{0:T(128)} %refs_1_.5, bf16[192,1664]{1,0:T(8,128)(2,1)} %copy-done, bf16[192,1664]{1,0:T(8,128)(2,1)} %copy-done.1, bf16[192,1664]{1,0:T(8,128)(2,1)} %copy-done.2, ...), custom_call_target="tpu_custom_call" | custom-call | flops 726663168 | bytes 6650916 | tf_op jit(solution)/shard_map/pallas_call | solution.py:96
  113.3 2.0 %all-to-all-done.1 = bf16[64,16,128]{2,1,0:T(8,128)(2,1)S(1)} async-done(((bf16[64,16,128]{2,1,0:T(8,128)(2,1)}), bf16[64,16,128]{2,1,0:T(8,128)(2,1)S(1)}, u32[]{:S(2)}, u32[]{:S(2)}) %all-to-all-start.1) | async-done | bytes 262176 | tf_op jit(solution)/shard_map/all_to_all | solution.py:465
  115.4 0.7 copy-done.6
  116.1 5.9 %shard_map.141 = (bf16[264,384]{1,0:T(8,128)(2,1)}, bf16[264,384]{1,0:T(8,128)(2,1)}, bf16[264,384]{1,0:T(8,128)(2,1)}, bf16[264,384]{1,0:T(8,128)(2,1)}) custom-call(s32[2]{0:T(128)} %pad_add_fusion.refs_0_, bf16[8,24,1664]{2,1,0:T(8,128)(2,1)} %bitcast.23, bf16[8,24,1664]{2,1,0:T(8,128)(2,1)} %bitcast.24, bf16[8,24,1664]{2,1,0:T(8,128)(2,1)} %bitcast.25, ...), custom_call_target="tpu_custom_call" | custom-call | flops 603979776 | bytes 6229000 | tf_op jit(solution)/shard_map/pallas_call | solution.py:96
  122.1 2.4 %collective-permute-start.19 = (bf16[264,384]{1,0:T(8,128)(2,1)}, bf16[264,384]{1,0:T(8,128)(2,1)S(1)}, u32[]{:S(2)}, u32[]{:S(2)}) collective-permute-start(bf16[264,384]{1,0:T(8,128)(2,1)} %get-tuple-element.41), channel_id=1, source_target_pairs={{0,2},{1,3},{2,0},{3,1},{4,6},{5,7},{6,4},{7,5},{8,10},{9,11},{10,... | collective-permute-start | bytes 608264 | tf_op jit(solution)/shard_map/ppermute | solution.py:21
  124.4 4.0 %collective-permute-done.20 = bf16[264,384]{1,0:T(8,128)(2,1)S(1)} collective-permute-done((bf16[264,384]{1,0:T(8,128)(2,1)}, bf16[264,384]{1,0:T(8,128)(2,1)S(1)}, u32[]{:S(2)}, u32[]{:S(2)}) %collective-permute-start.20) | collective-permute-done | bytes 202784 | tf_op jit(solution)/shard_map/ppermute | solution.py:21
  128.4 1.6 %collective-permute-done.19 = bf16[264,384]{1,0:T(8,128)(2,1)S(1)} collective-permute-done((bf16[264,384]{1,0:T(8,128)(2,1)}, bf16[264,384]{1,0:T(8,128)(2,1)S(1)}, u32[]{:S(2)}, u32[]{:S(2)}) %collective-permute-start.19) | collective-permute-done | bytes 202784 | tf_op jit(solution)/shard_map/ppermute | solution.py:21
  130.0 5.1 %collective-permute-done.18 = bf16[264,384]{1,0:T(8,128)(2,1)S(1)} collective-permute-done((bf16[264,384]{1,0:T(8,128)(2,1)}, bf16[264,384]{1,0:T(8,128)(2,1)S(1)}, u32[]{:S(2)}, u32[]{:S(2)}) %collective-permute-start.18) | collective-permute-done | bytes 202784 | tf_op jit(solution)/shard_map/ppermute | solution.py:21
  135.2 0.7 convert_add_fusion
  135.9 1.7 %multiply_convert_fusion = bf16[256,384]{1,0:T(8,128)(2,1)} fusion(bf16[264,384]{1,0:T(8,128)(2,1)S(1)} %collective-permute-done.20, bf16[264,384]{1,0:T(8,128)(2,1)S(1)} %collective-permute-done.19, bf16[264,384]{1,0:T(8,128)(2,1)S(1)} %collective-permute-done.18, f32[256]{0:T(256)S(1)} %bitcast.32, bf16[264,384]{1,0:T(8,128)(2,1)} %get-tuple-element.39), kind=kLoop, calls=%fused_computation | loop fusion | flops 884736 | bytes 984064 | tf_op jit(solution)/shard_map/convert_element_type | solution.py:516
  (67 shorter events, 5.4 us)
Async XLA Ops:
  0.0 45.8 %collective-permute-start.1 = (bf16[256,384]{1,0:T(8,128)(2,1)}, bf16[256,384]{1,0:T(8,128)(2,1)S(1)}, u32[]{:S(2)}, u32[]{:S(2)}) collective-permute-start(bf16[256,384]{1,0:T(8,128)(2,1)} %refs_2_.1), channel_id=1, source_target_pairs={{0,1},{1,2},{2,3},{3,0},{4,5},{5,6},{6,7},{7,4},{8,9},{9,10},{10,1... | collective-permute-start | bytes 589832 | tf_op jit(solution)/shard_map/ppermute | solution.py:21
  2.1 35.8 %collective-permute-start.2 = (bf16[256,384]{1,0:T(8,128)(2,1)}, bf16[256,384]{1,0:T(8,128)(2,1)S(1)}, u32[]{:S(2)}, u32[]{:S(2)}) collective-permute-start(bf16[256,384]{1,0:T(8,128)(2,1)} %refs_2_.1), channel_id=1, source_target_pairs={{0,2},{1,3},{2,0},{3,1},{4,6},{5,7},{6,4},{7,5},{8,10},{9,11},{10,... | collective-permute-start | bytes 589832 | tf_op jit(solution)/shard_map/ppermute | solution.py:21
  4.7 31.6 %collective-permute-start.3 = (bf16[256,384]{1,0:T(8,128)(2,1)}, bf16[256,384]{1,0:T(8,128)(2,1)S(1)}, u32[]{:S(2)}, u32[]{:S(2)}) collective-permute-start(bf16[256,384]{1,0:T(8,128)(2,1)} %refs_2_.1), channel_id=1, source_target_pairs={{0,3},{1,0},{2,1},{3,2},{4,7},{5,4},{6,5},{7,6},{8,11},{9,8},{10,9... | collective-permute-start | bytes 589832 | tf_op jit(solution)/shard_map/ppermute | solution.py:21
  32.9 15.8 %copy-start.5 = (bf16[192,1024]{1,0:T(8,128)(2,1)}, bf16[192,1024]{1,0:T(8,128)(2,1)S(1)}, u32[]{:S(2)}) copy-start(bf16[192,1024]{1,0:T(8,128)(2,1)S(1)} %slice.64.refs_2_) | copy-start | bytes 1179652
  32.9 15.9 %collective-permute-start.8 = (bf16[192,1024]{1,0:T(8,128)(2,1)S(1)}, bf16[192,1024]{1,0:T(8,128)(2,1)S(1)}, u32[]{:S(2)}, u32[]{:S(2)}) collective-permute-start(bf16[192,1024]{1,0:T(8,128)(2,1)S(1)} %slice.64.refs_2_), channel_id=1, source_target_pairs={{0,64},{64,128},{128,192},{192,0},{1,65},{65,129},{129,193},{193,1... | collective-permute-start | bytes 1179656 | tf_op jit(solution)/shard_map/ppermute | solution.py:21
  34.2 22.6 %collective-permute-start = (bf16[192,1024]{1,0:T(8,128)(2,1)S(1)}, bf16[192,1024]{1,0:T(8,128)(2,1)S(1)}, u32[]{:S(2)}, u32[]{:S(2)}) collective-permute-start(bf16[192,1024]{1,0:T(8,128)(2,1)S(1)} %slice.64.refs_2_), channel_id=1, source_target_pairs={{0,192},{64,0},{128,64},{192,128},{1,193},{65,1},{129,65},{193,129... | collective-permute-start | bytes 1179656 | tf_op jit(solution)/shard_map/ppermute | solution.py:21
  36.3 12.4 %copy-start.14 = (bf16[256,384]{1,0:T(8,128)(2,1)}, bf16[256,384]{1,0:T(8,128)(2,1)S(1)}, u32[]{:S(2)}) copy-start(bf16[256,384]{1,0:T(8,128)(2,1)S(1)} %collective-permute-done.3.refs_5_) | copy-start | bytes 589828
  36.4 20.4 %collective-permute-start.9 = (bf16[192,1024]{1,0:T(8,128)(2,1)S(1)}, bf16[192,1024]{1,0:T(8,128)(2,1)}, u32[]{:S(2)}, u32[]{:S(2)}) collective-permute-start(bf16[192,1024]{1,0:T(8,128)(2,1)S(1)} %slice.64.refs_2_), channel_id=1, source_target_pairs={{0,128},{64,192},{128,0},{192,64},{1,129},{65,193},{129,1},{193,65... | collective-permute-start | bytes 1179656 | tf_op jit(solution)/shard_map/ppermute | solution.py:21
  37.9 10.9 %copy-start.13 = (bf16[256,384]{1,0:T(8,128)(2,1)}, bf16[256,384]{1,0:T(8,128)(2,1)S(1)}, u32[]{:S(2)}) copy-start(bf16[256,384]{1,0:T(8,128)(2,1)S(1)} %collective-permute-done.2.refs_4_) | copy-start | bytes 589828
  37.9 21.7 %collective-permute-start.10 = (bf16[192,1024]{1,0:T(8,128)(2,1)S(1)}, bf16[192,1024]{1,0:T(8,128)(2,1)S(1)}, u32[]{:S(2)}, u32[]{:S(2)}) collective-permute-start(bf16[192,1024]{1,0:T(8,128)(2,1)S(1)} %slice.64.refs_2_), channel_id=1, source_target_pairs={{0,4},{4,0},{1,5},{5,1},{2,6},{6,2},{3,7},{7,3},{8,12},{12,8},{9,1... | collective-permute-start | bytes 1179656 | tf_op jit(solution)/shard_map/ppermute | solution.py:21
  45.8 3.0 %copy-start.12 = (bf16[256,384]{1,0:T(8,128)(2,1)}, bf16[256,384]{1,0:T(8,128)(2,1)S(1)}, u32[]{:S(2)}) copy-start(bf16[256,384]{1,0:T(8,128)(2,1)S(1)} %collective-permute-done.1.refs_3_) | copy-start | bytes 589828
  45.8 5.1 %collective-permute-start.4 = (bf16[8,1536]{1,0:T(8,128)(2,1)S(1)}, bf16[8,1536]{1,0:T(8,128)(2,1)S(1)}, u32[]{:S(2)}, u32[]{:S(2)}) collective-permute-start(bf16[8,1536]{1,0:T(8,128)(2,1)S(1)} %pad_maximum_fusion), channel_id=1, source_target_pairs={{0,4},{4,8},{8,12},{12,16},{16,20},{20,24},{24,28},{28,32},{32,36}... | collective-permute-start | bytes 73736 | tf_op jit(solution)/shard_map/ppermute | solution.py:421
  48.8 45.4 %copy-start = (bf16[192,1664]{1,0:T(8,128)(2,1)}, bf16[192,1664]{1,0:T(8,128)(2,1)S(1)}, u32[]{:S(2)}) copy-start(bf16[192,1664]{1,0:T(8,128)(2,1)S(1)} %slice.68.refs_2_) | copy-start | bytes 1916932
  48.8 8.0 %copy-start.7 = (bf16[192,1024]{1,0:T(8,128)(2,1)}, bf16[192,1024]{1,0:T(8,128)(2,1)S(1)}, u32[]{:S(2)}) copy-start(bf16[192,1024]{1,0:T(8,128)(2,1)S(1)} %collective-permute-done.8.refs_3_) | copy-start | bytes 1179652
  48.8 12.5 %collective-permute-start.11 = (bf16[192,1024]{1,0:T(8,128)(2,1)S(1)}, bf16[192,1024]{1,0:T(8,128)(2,1)}, u32[]{:S(2)}, u32[]{:S(2)}) collective-permute-start(bf16[192,1024]{1,0:T(8,128)(2,1)S(1)} %collective-permute-done.8.refs_3_), channel_id=1, source_target_pairs={{0,4},{4,0},{1,5},{5,1},{2,6},{6,2},{3,7},{7,3},{8,12},{12,8},{9,1... | collective-permute-start | bytes 1179656 | tf_op jit(solution)/shard_map/ppermute | solution.py:21
  56.8 6.2 %copy-start.8 = (bf16[192,1024]{1,0:T(8,128)(2,1)}, bf16[192,1024]{1,0:T(8,128)(2,1)S(1)}, u32[]{:S(2)}) copy-start(bf16[192,1024]{1,0:T(8,128)(2,1)S(1)} %collective-permute-done.refs_5_) | copy-start | bytes 1179652
  56.8 6.2 %collective-permute-start.12 = (bf16[192,1024]{1,0:T(8,128)(2,1)}, bf16[192,1024]{1,0:T(8,128)(2,1)}, u32[]{:S(2)}, u32[]{:S(2)}) collective-permute-start(bf16[192,1024]{1,0:T(8,128)(2,1)} %collective-permute-done.9.refs_4_), channel_id=1, source_target_pairs={{0,4},{4,0},{1,5},{5,1},{2,6},{6,2},{3,7},{7,3},{8,12},{12,8},{9,1... | collective-permute-start | bytes 1179656 | tf_op jit(solution)/shard_map/ppermute | solution.py:21
  56.9 6.1 %collective-permute-start.13 = (bf16[192,1024]{1,0:T(8,128)(2,1)S(1)}, bf16[192,1024]{1,0:T(8,128)(2,1)}, u32[]{:S(2)}, u32[]{:S(2)}) collective-permute-start(bf16[192,1024]{1,0:T(8,128)(2,1)S(1)} %collective-permute-done.refs_5_), channel_id=1, source_target_pairs={{0,4},{4,0},{1,5},{5,1},{2,6},{6,2},{3,7},{7,3},{8,12},{12,8},{9,1... | collective-permute-start | bytes 1179656 | tf_op jit(solution)/shard_map/ppermute | solution.py:21
  57.4 36.7 %collective-permute-start.5 = (bf16[192,1664]{1,0:T(8,128)(2,1)S(1)}, bf16[192,1664]{1,0:T(8,128)(2,1)S(1)}, u32[]{:S(2)}, u32[]{:S(2)}) collective-permute-start(bf16[192,1664]{1,0:T(8,128)(2,1)S(1)} %slice.68.refs_2_), channel_id=1, source_target_pairs={{0,64},{64,128},{128,192},{192,0},{1,65},{65,129},{129,193},{193,1... | collective-permute-start | bytes 1916936 | tf_op jit(solution)/shard_map/ppermute | solution.py:21
  59.6 34.5 %collective-permute-start.6 = (bf16[192,1664]{1,0:T(8,128)(2,1)S(1)}, bf16[192,1664]{1,0:T(8,128)(2,1)S(1)}, u32[]{:S(2)}, u32[]{:S(2)}) collective-permute-start(bf16[192,1664]{1,0:T(8,128)(2,1)S(1)} %slice.68.refs_2_), channel_id=1, source_target_pairs={{0,128},{64,192},{128,0},{192,64},{1,129},{65,193},{129,1},{193,65... | collective-permute-start | bytes 1916936 | tf_op jit(solution)/shard_map/ppermute | solution.py:21
  61.3 32.8 %collective-permute-start.7 = (bf16[192,1664]{1,0:T(8,128)(2,1)S(1)}, bf16[192,1664]{1,0:T(8,128)(2,1)S(1)}, u32[]{:S(2)}, u32[]{:S(2)}) collective-permute-start(bf16[192,1664]{1,0:T(8,128)(2,1)S(1)} %slice.68.refs_2_), channel_id=1, source_target_pairs={{0,192},{64,0},{128,64},{192,128},{1,193},{65,1},{129,65},{193,129... | collective-permute-start | bytes 1916936 | tf_op jit(solution)/shard_map/ppermute | solution.py:21
  94.1 12.0 %copy-start.1 = (bf16[192,1664]{1,0:T(8,128)(2,1)}, bf16[192,1664]{1,0:T(8,128)(2,1)S(1)}, u32[]{:S(2)}) copy-start(bf16[192,1664]{1,0:T(8,128)(2,1)S(1)} %collective-permute-done.5.refs_3_) | copy-start | bytes 1916932
  94.1 12.0 %copy-start.2 = (bf16[192,1664]{1,0:T(8,128)(2,1)}, bf16[192,1664]{1,0:T(8,128)(2,1)S(1)}, u32[]{:S(2)}) copy-start(bf16[192,1664]{1,0:T(8,128)(2,1)S(1)} %collective-permute-done.6.refs_4_) | copy-start | bytes 1916932
  94.1 11.9 %copy-start.3 = (bf16[192,1664]{1,0:T(8,128)(2,1)}, bf16[192,1664]{1,0:T(8,128)(2,1)S(1)}, u32[]{:S(2)}) copy-start(bf16[192,1664]{1,0:T(8,128)(2,1)S(1)} %collective-permute-done.7.refs_5_) | copy-start | bytes 1916932
  94.1 11.9 %collective-permute-start.14 = (bf16[192,1664]{1,0:T(8,128)(2,1)S(1)}, bf16[192,1664]{1,0:T(8,128)(2,1)S(1)}, u32[]{:S(2)}, u32[]{:S(2)}) collective-permute-start(bf16[192,1664]{1,0:T(8,128)(2,1)S(1)} %slice.68.refs_2_), channel_id=1, source_target_pairs={{0,4},{4,0},{1,5},{5,1},{2,6},{6,2},{3,7},{7,3},{8,12},{12,8},{9,1... | collective-permute-start | bytes 1916936 | tf_op jit(solution)/shard_map/ppermute | solution.py:21
  94.8 11.2 %collective-permute-start.15 = (bf16[192,1664]{1,0:T(8,128)(2,1)S(1)}, bf16[192,1664]{1,0:T(8,128)(2,1)}, u32[]{:S(2)}, u32[]{:S(2)}) collective-permute-start(bf16[192,1664]{1,0:T(8,128)(2,1)S(1)} %collective-permute-done.5.refs_3_), channel_id=1, source_target_pairs={{0,4},{4,0},{1,5},{5,1},{2,6},{6,2},{3,7},{7,3},{8,12},{12,8},{9,1... | collective-permute-start | bytes 1916936 | tf_op jit(solution)/shard_map/ppermute | solution.py:21
  94.9 11.1 %collective-permute-start.16 = (bf16[192,1664]{1,0:T(8,128)(2,1)S(1)}, bf16[192,1664]{1,0:T(8,128)(2,1)}, u32[]{:S(2)}, u32[]{:S(2)}) collective-permute-start(bf16[192,1664]{1,0:T(8,128)(2,1)S(1)} %collective-permute-done.6.refs_4_), channel_id=1, source_target_pairs={{0,4},{4,0},{1,5},{5,1},{2,6},{6,2},{3,7},{7,3},{8,12},{12,8},{9,1... | collective-permute-start | bytes 1916936 | tf_op jit(solution)/shard_map/ppermute | solution.py:21
  95.3 10.7 %collective-permute-start.17 = (bf16[192,1664]{1,0:T(8,128)(2,1)S(1)}, bf16[192,1664]{1,0:T(8,128)(2,1)}, u32[]{:S(2)}, u32[]{:S(2)}) collective-permute-start(bf16[192,1664]{1,0:T(8,128)(2,1)S(1)} %collective-permute-done.7.refs_5_), channel_id=1, source_target_pairs={{0,4},{4,0},{1,5},{5,1},{2,6},{6,2},{3,7},{7,3},{8,12},{12,8},{9,1... | collective-permute-start | bytes 1916936 | tf_op jit(solution)/shard_map/ppermute | solution.py:21
  95.4 20.0 %all-to-all-start.1 = ((bf16[64,16,128]{2,1,0:T(8,128)(2,1)}), bf16[64,16,128]{2,1,0:T(8,128)(2,1)S(1)}, u32[]{:S(2)}, u32[]{:S(2)}) async-start(bf16[64,16,128]{2,1,0:T(8,128)(2,1)} %bitcast.19), calls=%async_computation.1 | async-start | bytes 524288 | tf_op jit(solution)/shard_map/all_to_all | solution.py:465
  122.0 6.4 %collective-permute-start.20 = (bf16[264,384]{1,0:T(8,128)(2,1)}, bf16[264,384]{1,0:T(8,128)(2,1)S(1)}, u32[]{:S(2)}, u32[]{:S(2)}) collective-permute-start(bf16[264,384]{1,0:T(8,128)(2,1)} %get-tuple-element.42), channel_id=1, source_target_pairs={{0,3},{1,0},{2,1},{3,2},{4,7},{5,4},{6,5},{7,6},{8,11},{9,8},{10,9... | collective-permute-start | bytes 608264 | tf_op jit(solution)/shard_map/ppermute | solution.py:21
  122.1 8.0 %collective-permute-start.19 = (bf16[264,384]{1,0:T(8,128)(2,1)}, bf16[264,384]{1,0:T(8,128)(2,1)S(1)}, u32[]{:S(2)}, u32[]{:S(2)}) collective-permute-start(bf16[264,384]{1,0:T(8,128)(2,1)} %get-tuple-element.41), channel_id=1, source_target_pairs={{0,2},{1,3},{2,0},{3,1},{4,6},{5,7},{6,4},{7,5},{8,10},{9,11},{10,... | collective-permute-start | bytes 608264 | tf_op jit(solution)/shard_map/ppermute | solution.py:21
  124.4 10.7 %collective-permute-start.18 = (bf16[264,384]{1,0:T(8,128)(2,1)}, bf16[264,384]{1,0:T(8,128)(2,1)S(1)}, u32[]{:S(2)}, u32[]{:S(2)}) collective-permute-start(bf16[264,384]{1,0:T(8,128)(2,1)} %get-tuple-element.40), channel_id=1, source_target_pairs={{0,1},{1,2},{2,3},{3,0},{4,5},{5,6},{6,7},{7,4},{8,9},{9,10},{10,1... | collective-permute-start | bytes 608264 | tf_op jit(solution)/shard_map/ppermute | solution.py:21
  (6 other events, 5.2 us)

commit v11 on v8

--- a/solution.py
+++ b/solution.py
@@ -269,13 +269,24 @@
     out_ref[...] = lines[...].astype(BF16)
 
 
-def middle_body(head_dim, ready, sems, first_ref, lengths_ref, *refs):
-    *blocks, h_ref, conv_shared, x_ref, b_ref, dt_ref, cum_ref, skip = refs[:-6]
-    direct_ref, carry_ref, c_ref, held, c_rows, gate = refs[-6:]
+def middle_body(head_dim, ready, sems, first_ref, lengths_ref, core_ref, *refs):
+    *blocks, h_ref, conv_shared, x_ref, b_ref, dt_ref, cum_ref, skip = refs[:-7]
+    direct_ref, carry_ref, c_ref, out_w, held, c_rows, gate = refs[-7:]
+    blocks, deep = blocks[: len(blocks) // 2], blocks[len(blocks) // 2 :]
     tokens, inner = x_ref.shape
     wide = held.shape[1]
     copies = fetch(blocks, held, sems, slice(0, wide))
     ready()
+    half = len(deep) // 2
+    moves = []
+    for i, block in enumerate(deep):
+        move = pltpu.make_async_copy(
+            block.at[:, :, wide:],
+            out_w.at[i % half, :, core_ref[0] ^ (i // half)],
+            sems.at[len(deep) + i],
+        )
+        move.start()
+        moves.append(move)
     for copy in copies:
         copy.wait()
     for at in range(0, inner, 256):
@@ -311,21 +322,15 @@
         cut = slice(at, at + 128)
         direct = jnp.concatenate(sums, axis=1) + skip[:, cut] * x_ref[:, cut].astype(F32)
         direct_ref[:, cut] = (direct * gate[:, cut]).astype(BF16)
+    for move in moves:
+        move.wait()
 
 
 def last_body(ready, sems, turn_ref, *refs):
-    *blocks, carried_ref, direct_ref, carry_ref, c_ref, gain = refs[:-8]
-    *outs, held, lines, shares, out_w = refs[-8:]
-    half, wide, inner = len(blocks) // 2, blocks[0].shape[2], out_w.shape[4]
-    copies = []
-    for i, block in enumerate(blocks):
-        copy = pltpu.make_async_copy(
-            block.at[:, :, wide - inner :],
-            out_w.at[i % half, :, turn_ref[1] ^ (i // half)],
-            sems.at[i],
-        )
-        copy.start()
-        copies.append(copy)
+    weight_ref, carried_ref, direct_ref, carry_ref, c_ref, gain = refs[:6]
+    *outs, held, lines, shares, out_w = refs[6:]
+    weight = pltpu.make_async_copy(weight_ref, out_w, sems.at[0])
+    weight.start()
     ready()
     tokens, inner = direct_ref.shape
     lines[...] = carried_ref[...].astype(F32)
@@ -341,8 +346,7 @@
     scaled = (gated * gain[...]).astype(BF16)
     nt = (((1,), (1,)), ((), ()))
     features = shares.shape[2]
-    for copy in copies:
-        copy.wait()
+    weight.wait()
     for i in range(shares.shape[0]):
         rows = out_w[i].reshape(features, inner)
         shares[i] = lax.dot_general(scaled, rows, nt, preferred_element_type=F32).astype(BF16)
@@ -453,19 +457,23 @@
     carried = carried.reshape(seq_count * LINES, 128)
     late_own, _ = tie((late_own, scanned))
     late_other = [ahead(block, "core", 1) for block in late_own]
-    direct, carry, c_half = call(
+    direct, carry, c_half, out_w = call(
         functools.partial(middle_body, head_dim),
         [
             ((tokens, inner), BF16),
             ((tokens, inner), BF16),
             ((tokens, state), BF16),
+            ((x_size, z_size, core_size, rows_here, inner), BF16),
         ],
-        [first, prompt_lengths]
+        [first, prompt_lengths, jnp.reshape(core_at, (1,))]
         + late_own
         + late_other
+        + [block.reshape(z_size, rows_here, -1) for block in late_own + late_other]
         + [h, conv_shared, x_rows, b_half, steps, cumulative, jnp.repeat(skip_gain, head_dim)[None]],
-        scalars=2,
-        blocks=len(late_own + late_other),
+        scalars=3,
+        blocks=2 * len(late_own + late_other),
+        near_out=4,
+        grant=52,
         scratch=[
             ((model_width, inner + state), BF16),
             ((rows, state), F32),
@@ -477,8 +485,8 @@
         last_body,
         [((tokens + 8, features), BF16)] * tp_count,
         [
-            jnp.stack([x_at - tp_at + tp_count, core_at]),
-            *[block.reshape(z_size, rows_here, -1) for block in late_own + late_other],
+            jnp.reshape(x_at - tp_at + tp_count, (1,)),
+            out_w,
             carried,
             direct,
             carry,
@@ -486,7 +494,9 @@
             norm_gain[None],
         ],
         scalars=1,
-        blocks=len(late_own + late_other),
+        blocks=1,
+        near_in=4,
+        grant=52,
         scratch=[
             ((state, inner), BF16),
             ((seq_count * LINES, 128), F32),

time: 137 us -> 134 us (0.978)
  other arithmetic: 3.13 us -> 1.56 us
    unnamed x32 -> x38, local copies, waits for them, and re-layouts: 2.83 us -> 5.04 us
  transfers between devices with their start and end apart: 22 -> 22, of which waited for: 4 -> 4; matrix products, arithmetic and copies ran while one was open for 2% -> 1% of each run, Pallas kernels for 16% -> 17%
where the time goes in v11:
time: 134 us
  blocking collectives  47.3 us (35%)
  starting transfers between devices  40.2 us (30%)
  Pallas kernels  26.7 us (20%)
  waiting for transfers between devices  11.7 us (9%)
  local copies, waits for them, and re-layouts  5.98 us (4%)
  other arithmetic  1.56 us (1%)
    ppermute x20, starting transfers between devices, ahead(): lax.ppermute(block, axis, [(i, (i + distance) % count) for i in range(cou...  29.9 us
    all_gather x1, blocking collectives, on_device(): along_z = lax.all_gather(packed, 'z', axis=0, tiled=True)  25.3 us
    pallas_call x5, Pallas kernels, call(): pl.pallas_call(wrapped, out_shape=[jax.ShapeDtypeStruct(shape, kind) for...  25 us
    all_to_all x1, blocking collectives, on_device(): lax.all_to_all(sent.reshape(seq_count, LINES, 128), SEQ, 0, 0, tiled=True)  22 us
    ppermute x20, waiting for transfers between devices, ahead(): lax.ppermute(block, axis, [(i, (i + distance) % count) for i in range(cou...  10.7 us
    all_to_all x1, starting transfers between devices, on_device(): lax.all_to_all(scanned.reshape(seq_count, LINES, 128), SEQ, 0, 0, tiled=T...  8.09 us
    unnamed x38, local copies, waits for them, and re-layouts  5.04 us
  transfers between devices with their start and end apart: 22, of which 4 were waited for; matrix products, arithmetic and copies ran while one was open for 1% of the time, Pallas kernels for 17%

profile of v11, /device:TPU:1, one launch (start us, length us, event | category | flops | bytes accessed | tf_op | source)
XLA Modules:
  0.0 133.8 jit_solution(17267733016530507175)
XLA Ops:
  0.0 2.1 %collective-permute-start.1 = (bf16[256,384]{1,0:T(8,128)(2,1)}, bf16[256,384]{1,0:T(8,128)(2,1)S(1)}, u32[]{:S(2)}, u32[]{:S(2)}) collective-permute-start(bf16[256,384]{1,0:T(8,128)(2,1)} %refs_2_.1), channel_id=1, source_target_pairs={{0,1},{1,2},{2,3},{3,0},{4,5},{5,6},{6,7},{7,4},{8,9},{9,10},{10,1... | collective-permute-start | bytes 589832 | tf_op jit(solution)/shard_map/ppermute | solution.py:21
  2.1 2.6 %collective-permute-start.2 = (bf16[256,384]{1,0:T(8,128)(2,1)}, bf16[256,384]{1,0:T(8,128)(2,1)S(1)}, u32[]{:S(2)}, u32[]{:S(2)}) collective-permute-start(bf16[256,384]{1,0:T(8,128)(2,1)} %refs_2_.1), channel_id=1, source_target_pairs={{0,2},{1,3},{2,0},{3,1},{4,6},{5,7},{6,4},{7,5},{8,10},{9,11},{10,... | collective-permute-start | bytes 589832 | tf_op jit(solution)/shard_map/ppermute | solution.py:21
  4.7 1.1 collective-permute-start.3
  5.8 1.7 %shard_map.136 = bf16[24,2688]{1,0:T(8,128)(2,1)} custom-call(f32[24,768]{1,0:T(8,128)} %value_ref.1, f32[24,256]{1,0:T(8,128)} %shared_ref.1, f32[12,24]{1,0:T(8,128)} %bitcast.30, f32[24,768]{1,0:T(8,128)} %gate_ref.1, f32[24,768]{1,0:T(8,128)} %bitcast.29), custom_call_target="tpu_custom_call" | custom-call | tf_op jit(solution)/shard_map/pallas_call | solution.py:45
  7.5 25.3 %all_gather.3 = bf16[192,2688]{1,0:T(8,128)(2,1)S(1)} all-gather(bf16[24,2688]{1,0:T(8,128)(2,1)} %shard_map.136), channel_id=1, replica_groups=mesh['x'=4,'z'=8,'core'=2,'tp'=4] {'z'}, dimensions={0}, use_global_device_ids=true | all-gather | bytes 1161216 | tf_op jit(solution)/shard_map/all_gather | solution.py:407
  32.9 1.3 collective-permute-start.8
  34.2 1.5 %collective-permute-start = (bf16[192,1024]{1,0:T(8,128)(2,1)S(1)}, bf16[192,1024]{1,0:T(8,128)(2,1)}, u32[]{:S(2)}, u32[]{:S(2)}) collective-permute-start(bf16[192,1024]{1,0:T(8,128)(2,1)S(1)} %slice.36.refs_2_), channel_id=1, source_target_pairs={{0,192},{64,0},{128,64},{192,128},{1,193},{65,1},{129,65},{193,129... | collective-permute-start | bytes 1179656 | tf_op jit(solution)/shard_map/ppermute | solution.py:21
  36.4 1.5 %collective-permute-start.9 = (bf16[192,1024]{1,0:T(8,128)(2,1)S(1)}, bf16[192,1024]{1,0:T(8,128)(2,1)}, u32[]{:S(2)}, u32[]{:S(2)}) collective-permute-start(bf16[192,1024]{1,0:T(8,128)(2,1)S(1)} %slice.36.refs_2_), channel_id=1, source_target_pairs={{0,128},{64,192},{128,0},{192,64},{1,129},{65,193},{129,1},{193,65... | collective-permute-start | bytes 1179656 | tf_op jit(solution)/shard_map/ppermute | solution.py:21
  37.9 7.9 %collective-permute-start.10 = (bf16[192,1024]{1,0:T(8,128)(2,1)S(1)}, bf16[192,1024]{1,0:T(8,128)(2,1)S(1)}, u32[]{:S(2)}, u32[]{:S(2)}) collective-permute-start(bf16[192,1024]{1,0:T(8,128)(2,1)S(1)} %slice.36.refs_2_), channel_id=1, source_target_pairs={{0,4},{4,0},{1,5},{5,1},{2,6},{6,2},{3,7},{7,3},{8,12},{12,8},{9,1... | collective-permute-start | bytes 1179656 | tf_op jit(solution)/shard_map/ppermute | solution.py:21
  45.8 2.2 %collective-permute-start.4 = (bf16[8,1536]{1,0:T(8,128)(2,1)S(1)}, bf16[8,1536]{1,0:T(8,128)(2,1)S(1)}, u32[]{:S(2)}, u32[]{:S(2)}) collective-permute-start(bf16[8,1536]{1,0:T(8,128)(2,1)S(1)} %pad_maximum_fusion), channel_id=1, source_target_pairs={{0,4},{4,8},{8,12},{12,16},{16,20},{20,24},{24,28},{28,32},{32,36}... | collective-permute-start | bytes 73736 | tf_op jit(solution)/shard_map/ppermute | solution.py:412
  48.7 2.3 %collective-permute-start.11 = (bf16[192,1024]{1,0:T(8,128)(2,1)}, bf16[192,1024]{1,0:T(8,128)(2,1)S(1)}, u32[]{:S(2)}, u32[]{:S(2)}) collective-permute-start(bf16[192,1024]{1,0:T(8,128)(2,1)} %collective-permute-done.8.refs_3_), channel_id=1, source_target_pairs={{0,4},{4,0},{1,5},{5,1},{2,6},{6,2},{3,7},{7,3},{8,12},{12,8},{9,1... | collective-permute-start | bytes 1179656 | tf_op jit(solution)/shard_map/ppermute | solution.py:21
  51.7 5.2 %shard_map.137.refs_10_.refs_19_ = bf16[264,1536]{1,0:T(8,128)(2,1)} custom-call(s32[3]{0:T(128)} %pad_add_fusion.refs_0_, s32[64]{0:T(128)} %refs_1_.3, bf16[256,384]{1,0:T(8,128)(2,1)} %refs_2_.1, bf16[256,384]{1,0:T(8,128)(2,1)} %copy-done.15, bf16[256,384]{1,0:T(8,128)(2,1)} %copy-done.16, bf16[256,384]{1,0:T(8,128)(2,1)} %copy-done.17, ...), custom_call_target="tpu_custom_call" | custom-call | flops 1245708288 | bytes 811276 | tf_op jit(solution)/shard_map/pallas_call | solution.py:93
  57.5 2.1 %collective-permute-start.5 = (bf16[192,1664]{1,0:T(8,128)(2,1)S(1)}, bf16[192,1664]{1,0:T(8,128)(2,1)S(1)}, u32[]{:S(2)}, u32[]{:S(2)}) collective-permute-start(bf16[192,1664]{1,0:T(8,128)(2,1)S(1)} %slice.40.refs_3_), channel_id=1, source_target_pairs={{0,64},{64,128},{128,192},{192,0},{1,65},{65,129},{129,193},{193,1... | collective-permute-start | bytes 1916936 | tf_op jit(solution)/shard_map/ppermute | solution.py:21
  59.6 1.7 %collective-permute-start.6 = (bf16[192,1664]{1,0:T(8,128)(2,1)S(1)}, bf16[192,1664]{1,0:T(8,128)(2,1)S(1)}, u32[]{:S(2)}, u32[]{:S(2)}) collective-permute-start(bf16[192,1664]{1,0:T(8,128)(2,1)S(1)} %slice.40.refs_3_), channel_id=1, source_target_pairs={{0,128},{64,192},{128,0},{192,64},{1,129},{65,193},{129,1},{193,65... | collective-permute-start | bytes 1916936 | tf_op jit(solution)/shard_map/ppermute | solution.py:21
  61.3 0.7 copy-done.12
  62.1 1.7 %collective-permute-start.7 = (bf16[192,1664]{1,0:T(8,128)(2,1)S(1)}, bf16[192,1664]{1,0:T(8,128)(2,1)S(1)}, u32[]{:S(2)}, u32[]{:S(2)}) collective-permute-start(bf16[192,1664]{1,0:T(8,128)(2,1)S(1)} %slice.40.refs_3_), channel_id=1, source_target_pairs={{0,192},{64,0},{128,64},{192,128},{1,193},{65,1},{129,65},{193,129... | collective-permute-start | bytes 1916936 | tf_op jit(solution)/shard_map/ppermute | solution.py:21
  63.8 6.9 %shard_map.138 = (bf16[256,768]{1,0:T(8,128)(2,1)}, bf16[256,128]{1,0:T(8,128)(2,1)}, f32[256,128]{1,0:T(8,128)}, f32[256,128]{1,0:T(8,128)}, bf16[1024,128]{1,0:T(8,128)(2,1)}) custom-call(s32[1]{0:T(128)} %bitcast.1.refs_0_, s32[8]{0:T(128)} %refs_1_.5, bf16[192,1024]{1,0:T(8,128)(2,1)} %copy-done.10, bf16[192,1024]{1,0:T(8,128)(2,1)} %collective-permute-done.8.refs_3_, ...), custom_call_target="tpu_custom_call" | custom-call | flops 830472192 | bytes 3973252 | tf_op jit(solution)/shard_map/pallas_call | solution.py:93
  70.7 22.0 %all_to_all.10 = bf16[64,16,128]{2,1,0:T(8,128)(2,1)S(1)} all-to-all(bf16[64,16,128]{2,1,0:T(8,128)(2,1)} %bitcast.28), channel_id=1, replica_groups=mesh['x'=4,'z'=8,'core'=2,'tp'=4] {'x','z','core'}, dimensions={0} | all-to-all | bytes 524288 | tf_op jit(solution)/shard_map/all_to_all | solution.py:447
  92.6 1.5 %shard_map.139 = bf16[1024,128]{1,0:T(8,128)(2,1)} custom-call(bf16[1024,128]{1,0:T(8,128)(2,1)S(1)} %bitcast.23), custom_call_target="tpu_custom_call" | custom-call | bytes 262144 | tf_op jit(solution)/shard_map/pallas_call | solution.py:93
  95.4 8.1 %all-to-all-start.1 = ((bf16[64,16,128]{2,1,0:T(8,128)(2,1)}), bf16[64,16,128]{2,1,0:T(8,128)(2,1)S(1)}, u32[]{:S(2)}, u32[]{:S(2)}) async-start(bf16[64,16,128]{2,1,0:T(8,128)(2,1)} %bitcast.19), calls=%async_computation.1 | async-start | bytes 524288 | tf_op jit(solution)/shard_map/all_to_all | solution.py:456
  103.8 1.0 copy-done
  104.8 0.9 copy-done.1
  105.7 0.9 copy-done.2
  106.6 0.8 copy-done.3
  107.4 7.1 %shard_map.140 = (bf16[256,768]{1,0:T(8,128)(2,1)S(1)}, bf16[256,768]{1,0:T(8,128)(2,1)S(1)}, bf16[256,128]{1,0:T(8,128)(2,1)S(1)}, bf16[4,8,2,24,768]{4,3,2,1,0:T(8,128)(2,1)}) custom-call(s32[1]{0:T(128)} %bitcast.1.refs_0_, s32[8]{0:T(128)S(1)} %copy-done.5, s32[1]{0:T(128)} %bitcast.2.refs_2_, bf16[192,1664]{1,0:T(8,128)(2,1)} %copy-done.6, ...), custom_call_target="tpu_custom_call" | custom-call | flops 726663168 | bytes 11762728 | tf_op jit(solution)/shard_map/pallas_call | solution.py:93
  114.5 1.0 all-to-all-done.1
  115.5 4.4 %shard_map.141 = (bf16[264,384]{1,0:T(8,128)(2,1)S(1)}, bf16[264,384]{1,0:T(8,128)(2,1)S(1)}, bf16[264,384]{1,0:T(8,128)(2,1)S(1)}, bf16[264,384]{1,0:T(8,128)(2,1)S(1)}) custom-call(s32[1]{0:T(128)} %bitcast.refs_0_, bf16[4,8,2,24,768]{4,3,2,1,0:T(8,128)(2,1)} %get-tuple-element.37.refs_1_, bf16[1024,128]{1,0:T(8,128)(2,1)S(1)} %bitcast.22, ...), custom_call_target="tpu_custom_call" | custom-call | flops 603979776 | bytes 3476484 | tf_op jit(solution)/shard_map/pallas_call | solution.py:93
  120.0 2.2 %collective-permute-start.19 = (bf16[264,384]{1,0:T(8,128)(2,1)S(1)}, bf16[264,384]{1,0:T(8,128)(2,1)S(1)}, u32[]{:S(2)}, u32[]{:S(2)}) collective-permute-start(bf16[264,384]{1,0:T(8,128)(2,1)S(1)} %get-tuple-element.43), channel_id=1, source_target_pairs={{0,2},{1,3},{2,0},{3,1},{4,6},{5,7},{6,4},{7,5},{8,10},{9,11},{10,... | collective-permute-start | bytes 608264 | tf_op jit(solution)/shard_map/ppermute | solution.py:21
  122.2 3.9 %collective-permute-done.20 = bf16[264,384]{1,0:T(8,128)(2,1)S(1)} collective-permute-done((bf16[264,384]{1,0:T(8,128)(2,1)S(1)}, bf16[264,384]{1,0:T(8,128)(2,1)S(1)}, u32[]{:S(2)}, u32[]{:S(2)}) %collective-permute-start.20) | collective-permute-done | bytes 202784 | tf_op jit(solution)/shard_map/ppermute | solution.py:21
  126.2 1.6 %collective-permute-done.19 = bf16[264,384]{1,0:T(8,128)(2,1)S(1)} collective-permute-done((bf16[264,384]{1,0:T(8,128)(2,1)S(1)}, bf16[264,384]{1,0:T(8,128)(2,1)S(1)}, u32[]{:S(2)}, u32[]{:S(2)}) %collective-permute-start.19) | collective-permute-done | bytes 202784 | tf_op jit(solution)/shard_map/ppermute | solution.py:21
  127.8 5.1 %collective-permute-done.18 = bf16[264,384]{1,0:T(8,128)(2,1)S(1)} collective-permute-done((bf16[264,384]{1,0:T(8,128)(2,1)S(1)}, bf16[264,384]{1,0:T(8,128)(2,1)S(1)}, u32[]{:S(2)}, u32[]{:S(2)}) %collective-permute-start.18) | collective-permute-done | bytes 202784 | tf_op jit(solution)/shard_map/ppermute | solution.py:21
  133.0 0.8 fusion
  (72 shorter events, 4.4 us)
Async XLA Ops:
  0.0 45.8 %collective-permute-start.1 = (bf16[256,384]{1,0:T(8,128)(2,1)}, bf16[256,384]{1,0:T(8,128)(2,1)S(1)}, u32[]{:S(2)}, u32[]{:S(2)}) collective-permute-start(bf16[256,384]{1,0:T(8,128)(2,1)} %refs_2_.1), channel_id=1, source_target_pairs={{0,1},{1,2},{2,3},{3,0},{4,5},{5,6},{6,7},{7,4},{8,9},{9,10},{10,1... | collective-permute-start | bytes 589832 | tf_op jit(solution)/shard_map/ppermute | solution.py:21
  2.1 35.8 %collective-permute-start.2 = (bf16[256,384]{1,0:T(8,128)(2,1)}, bf16[256,384]{1,0:T(8,128)(2,1)S(1)}, u32[]{:S(2)}, u32[]{:S(2)}) collective-permute-start(bf16[256,384]{1,0:T(8,128)(2,1)} %refs_2_.1), channel_id=1, source_target_pairs={{0,2},{1,3},{2,0},{3,1},{4,6},{5,7},{6,4},{7,5},{8,10},{9,11},{10,... | collective-permute-start | bytes 589832 | tf_op jit(solution)/shard_map/ppermute | solution.py:21
  4.7 31.6 %collective-permute-start.3 = (bf16[256,384]{1,0:T(8,128)(2,1)}, bf16[256,384]{1,0:T(8,128)(2,1)S(1)}, u32[]{:S(2)}, u32[]{:S(2)}) collective-permute-start(bf16[256,384]{1,0:T(8,128)(2,1)} %refs_2_.1), channel_id=1, source_target_pairs={{0,3},{1,0},{2,1},{3,2},{4,7},{5,4},{6,5},{7,6},{8,11},{9,8},{10,9... | collective-permute-start | bytes 589832 | tf_op jit(solution)/shard_map/ppermute | solution.py:21
  32.9 24.0 %copy-start.10 = (bf16[192,1024]{1,0:T(8,128)(2,1)}, bf16[192,1024]{1,0:T(8,128)(2,1)S(1)}, u32[]{:S(2)}) copy-start(bf16[192,1024]{1,0:T(8,128)(2,1)S(1)} %slice.36.refs_2_) | copy-start | bytes 1179652
  32.9 15.8 %collective-permute-start.8 = (bf16[192,1024]{1,0:T(8,128)(2,1)S(1)}, bf16[192,1024]{1,0:T(8,128)(2,1)}, u32[]{:S(2)}, u32[]{:S(2)}) collective-permute-start(bf16[192,1024]{1,0:T(8,128)(2,1)S(1)} %slice.36.refs_2_), channel_id=1, source_target_pairs={{0,64},{64,128},{128,192},{192,0},{1,65},{65,129},{129,193},{193,1... | collective-permute-start | bytes 1179656 | tf_op jit(solution)/shard_map/ppermute | solution.py:21
  34.2 22.7 %collective-permute-start = (bf16[192,1024]{1,0:T(8,128)(2,1)S(1)}, bf16[192,1024]{1,0:T(8,128)(2,1)}, u32[]{:S(2)}, u32[]{:S(2)}) collective-permute-start(bf16[192,1024]{1,0:T(8,128)(2,1)S(1)} %slice.36.refs_2_), channel_id=1, source_target_pairs={{0,192},{64,0},{128,64},{192,128},{1,193},{65,1},{129,65},{193,129... | collective-permute-start | bytes 1179656 | tf_op jit(solution)/shard_map/ppermute | solution.py:21
  36.3 14.7 %copy-start.17 = (bf16[256,384]{1,0:T(8,128)(2,1)}, bf16[256,384]{1,0:T(8,128)(2,1)S(1)}, u32[]{:S(2)}) copy-start(bf16[256,384]{1,0:T(8,128)(2,1)S(1)} %collective-permute-done.3.refs_5_) | copy-start | bytes 589828
  36.4 20.6 %collective-permute-start.9 = (bf16[192,1024]{1,0:T(8,128)(2,1)S(1)}, bf16[192,1024]{1,0:T(8,128)(2,1)}, u32[]{:S(2)}, u32[]{:S(2)}) collective-permute-start(bf16[192,1024]{1,0:T(8,128)(2,1)S(1)} %slice.36.refs_2_), channel_id=1, source_target_pairs={{0,128},{64,192},{128,0},{192,64},{1,129},{65,193},{129,1},{193,65... | collective-permute-start | bytes 1179656 | tf_op jit(solution)/shard_map/ppermute | solution.py:21
  37.9 13.1 %copy-start.16 = (bf16[256,384]{1,0:T(8,128)(2,1)}, bf16[256,384]{1,0:T(8,128)(2,1)S(1)}, u32[]{:S(2)}) copy-start(bf16[256,384]{1,0:T(8,128)(2,1)S(1)} %collective-permute-done.2.refs_4_) | copy-start | bytes 589828
  37.9 21.7 %collective-permute-start.10 = (bf16[192,1024]{1,0:T(8,128)(2,1)S(1)}, bf16[192,1024]{1,0:T(8,128)(2,1)S(1)}, u32[]{:S(2)}, u32[]{:S(2)}) collective-permute-start(bf16[192,1024]{1,0:T(8,128)(2,1)S(1)} %slice.36.refs_2_), channel_id=1, source_target_pairs={{0,4},{4,0},{1,5},{5,1},{2,6},{6,2},{3,7},{7,3},{8,12},{12,8},{9,1... | collective-permute-start | bytes 1179656 | tf_op jit(solution)/shard_map/ppermute | solution.py:21
  45.8 5.2 %collective-permute-start.4 = (bf16[8,1536]{1,0:T(8,128)(2,1)S(1)}, bf16[8,1536]{1,0:T(8,128)(2,1)S(1)}, u32[]{:S(2)}, u32[]{:S(2)}) collective-permute-start(bf16[8,1536]{1,0:T(8,128)(2,1)S(1)} %pad_maximum_fusion), channel_id=1, source_target_pairs={{0,4},{4,8},{8,12},{12,16},{16,20},{20,24},{24,28},{28,32},{32,36}... | collective-permute-start | bytes 73736 | tf_op jit(solution)/shard_map/ppermute | solution.py:412
  48.7 45.4 %copy-start.6 = (bf16[192,1664]{1,0:T(8,128)(2,1)}, bf16[192,1664]{1,0:T(8,128)(2,1)S(1)}, u32[]{:S(2)}) copy-start(bf16[192,1664]{1,0:T(8,128)(2,1)S(1)} %slice.40.refs_3_) | copy-start | bytes 1916932
  48.7 12.6 %collective-permute-start.11 = (bf16[192,1024]{1,0:T(8,128)(2,1)}, bf16[192,1024]{1,0:T(8,128)(2,1)S(1)}, u32[]{:S(2)}, u32[]{:S(2)}) collective-permute-start(bf16[192,1024]{1,0:T(8,128)(2,1)} %collective-permute-done.8.refs_3_), channel_id=1, source_target_pairs={{0,4},{4,0},{1,5},{5,1},{2,6},{6,2},{3,7},{7,3},{8,12},{12,8},{9,1... | collective-permute-start | bytes 1179656 | tf_op jit(solution)/shard_map/ppermute | solution.py:21
  56.9 6.8 %collective-permute-start.12 = (bf16[192,1024]{1,0:T(8,128)(2,1)}, bf16[192,1024]{1,0:T(8,128)(2,1)}, u32[]{:S(2)}, u32[]{:S(2)}) collective-permute-start(bf16[192,1024]{1,0:T(8,128)(2,1)} %collective-permute-done.9.refs_4_), channel_id=1, source_target_pairs={{0,4},{4,0},{1,5},{5,1},{2,6},{6,2},{3,7},{7,3},{8,12},{12,8},{9,1... | collective-permute-start | bytes 1179656 | tf_op jit(solution)/shard_map/ppermute | solution.py:21
  57.0 6.7 %collective-permute-start.13 = (bf16[192,1024]{1,0:T(8,128)(2,1)}, bf16[192,1024]{1,0:T(8,128)(2,1)}, u32[]{:S(2)}, u32[]{:S(2)}) collective-permute-start(bf16[192,1024]{1,0:T(8,128)(2,1)} %collective-permute-done.refs_5_), channel_id=1, source_target_pairs={{0,4},{4,0},{1,5},{5,1},{2,6},{6,2},{3,7},{7,3},{8,12},{12,8},{9,1... | collective-permute-start | bytes 1179656 | tf_op jit(solution)/shard_map/ppermute | solution.py:21
  57.5 36.6 %collective-permute-start.5 = (bf16[192,1664]{1,0:T(8,128)(2,1)S(1)}, bf16[192,1664]{1,0:T(8,128)(2,1)S(1)}, u32[]{:S(2)}, u32[]{:S(2)}) collective-permute-start(bf16[192,1664]{1,0:T(8,128)(2,1)S(1)} %slice.40.refs_3_), channel_id=1, source_target_pairs={{0,64},{64,128},{128,192},{192,0},{1,65},{65,129},{129,193},{193,1... | collective-permute-start | bytes 1916936 | tf_op jit(solution)/shard_map/ppermute | solution.py:21
  59.6 34.5 %collective-permute-start.6 = (bf16[192,1664]{1,0:T(8,128)(2,1)S(1)}, bf16[192,1664]{1,0:T(8,128)(2,1)S(1)}, u32[]{:S(2)}, u32[]{:S(2)}) collective-permute-start(bf16[192,1664]{1,0:T(8,128)(2,1)S(1)} %slice.40.refs_3_), channel_id=1, source_target_pairs={{0,128},{64,192},{128,0},{192,64},{1,129},{65,193},{129,1},{193,65... | collective-permute-start | bytes 1916936 | tf_op jit(solution)/shard_map/ppermute | solution.py:21
  62.1 32.1 %collective-permute-start.7 = (bf16[192,1664]{1,0:T(8,128)(2,1)S(1)}, bf16[192,1664]{1,0:T(8,128)(2,1)S(1)}, u32[]{:S(2)}, u32[]{:S(2)}) collective-permute-start(bf16[192,1664]{1,0:T(8,128)(2,1)S(1)} %slice.40.refs_3_), channel_id=1, source_target_pairs={{0,192},{64,0},{128,64},{192,128},{1,193},{65,1},{129,65},{193,129... | collective-permute-start | bytes 1916936 | tf_op jit(solution)/shard_map/ppermute | solution.py:21
  63.7 39.8 %copy-start.14 = (f32[12]{0:T(128)S(1)}, f32[12]{0:T(128)}, u32[]{:S(2)}) copy-start(f32[12]{0:T(128)} %param.23) | copy-start | bytes 148
  63.7 40.0 %copy-start.13 = (f32[768]{0:T(1024)S(1)}, f32[768]{0:T(1024)}, u32[]{:S(2)}) copy-start(f32[768]{0:T(1024)} %param.24) | copy-start | bytes 9220
  63.8 40.0 %copy-start.4 = (f32[4,256]{1,0:T(4,128)S(1)}, f32[4,256]{1,0:T(4,128)}, u32[]{:S(2)}) copy-start(f32[4,256]{1,0:T(4,128)} %refs_20_.1) | copy-start | bytes 12292
  63.8 40.0 %copy-start.5 = (s32[8]{0:T(128)S(1)}, s32[8]{0:T(128)}, u32[]{:S(2)}) copy-start(s32[8]{0:T(128)} %refs_1_.5) | copy-start | bytes 100
  94.1 9.7 %copy-start.7 = (bf16[192,1664]{1,0:T(8,128)(2,1)}, bf16[192,1664]{1,0:T(8,128)(2,1)S(1)}, u32[]{:S(2)}) copy-start(bf16[192,1664]{1,0:T(8,128)(2,1)S(1)} %collective-permute-done.5.refs_4_) | copy-start | bytes 1916932
  94.1 9.6 %copy-start.8 = (bf16[192,1664]{1,0:T(8,128)(2,1)}, bf16[192,1664]{1,0:T(8,128)(2,1)S(1)}, u32[]{:S(2)}) copy-start(bf16[192,1664]{1,0:T(8,128)(2,1)S(1)} %collective-permute-done.6.refs_5_) | copy-start | bytes 1916932
  94.2 9.5 %collective-permute-start.14 = (bf16[192,1664]{1,0:T(8,128)(2,1)S(1)}, bf16[192,1664]{1,0:T(8,128)(2,1)}, u32[]{:S(2)}, u32[]{:S(2)}) collective-permute-start(bf16[192,1664]{1,0:T(8,128)(2,1)S(1)} %slice.40.refs_3_), channel_id=1, source_target_pairs={{0,4},{4,0},{1,5},{5,1},{2,6},{6,2},{3,7},{7,3},{8,12},{12,8},{9,1... | collective-permute-start | bytes 1916936 | tf_op jit(solution)/shard_map/ppermute | solution.py:21
  94.8 8.9 %collective-permute-start.15 = (bf16[192,1664]{1,0:T(8,128)(2,1)S(1)}, bf16[192,1664]{1,0:T(8,128)(2,1)}, u32[]{:S(2)}, u32[]{:S(2)}) collective-permute-start(bf16[192,1664]{1,0:T(8,128)(2,1)S(1)} %collective-permute-done.5.refs_4_), channel_id=1, source_target_pairs={{0,4},{4,0},{1,5},{5,1},{2,6},{6,2},{3,7},{7,3},{8,12},{12,8},{9,1... | collective-permute-start | bytes 1916936 | tf_op jit(solution)/shard_map/ppermute | solution.py:21
  94.9 8.8 %collective-permute-start.16 = (bf16[192,1664]{1,0:T(8,128)(2,1)S(1)}, bf16[192,1664]{1,0:T(8,128)(2,1)}, u32[]{:S(2)}, u32[]{:S(2)}) collective-permute-start(bf16[192,1664]{1,0:T(8,128)(2,1)S(1)} %collective-permute-done.6.refs_5_), channel_id=1, source_target_pairs={{0,4},{4,0},{1,5},{5,1},{2,6},{6,2},{3,7},{7,3},{8,12},{12,8},{9,1... | collective-permute-start | bytes 1916936 | tf_op jit(solution)/shard_map/ppermute | solution.py:21
  95.3 8.4 %collective-permute-start.17 = (bf16[192,1664]{1,0:T(8,128)(2,1)S(1)}, bf16[192,1664]{1,0:T(8,128)(2,1)}, u32[]{:S(2)}, u32[]{:S(2)}) collective-permute-start(bf16[192,1664]{1,0:T(8,128)(2,1)S(1)} %collective-permute-done.7.refs_6_), channel_id=1, source_target_pairs={{0,4},{4,0},{1,5},{5,1},{2,6},{6,2},{3,7},{7,3},{8,12},{12,8},{9,1... | collective-permute-start | bytes 1916936 | tf_op jit(solution)/shard_map/ppermute | solution.py:21
  95.4 20.1 %all-to-all-start.1 = ((bf16[64,16,128]{2,1,0:T(8,128)(2,1)}), bf16[64,16,128]{2,1,0:T(8,128)(2,1)S(1)}, u32[]{:S(2)}, u32[]{:S(2)}) async-start(bf16[64,16,128]{2,1,0:T(8,128)(2,1)} %bitcast.19), calls=%async_computation.1 | async-start | bytes 524288 | tf_op jit(solution)/shard_map/all_to_all | solution.py:456
  119.9 6.2 %collective-permute-start.20 = (bf16[264,384]{1,0:T(8,128)(2,1)S(1)}, bf16[264,384]{1,0:T(8,128)(2,1)S(1)}, u32[]{:S(2)}, u32[]{:S(2)}) collective-permute-start(bf16[264,384]{1,0:T(8,128)(2,1)S(1)} %get-tuple-element.44), channel_id=1, source_target_pairs={{0,3},{1,0},{2,1},{3,2},{4,7},{5,4},{6,5},{7,6},{8,11},{9,8},{10,9... | collective-permute-start | bytes 608264 | tf_op jit(solution)/shard_map/ppermute | solution.py:21
  120.0 7.8 %collective-permute-start.19 = (bf16[264,384]{1,0:T(8,128)(2,1)S(1)}, bf16[264,384]{1,0:T(8,128)(2,1)S(1)}, u32[]{:S(2)}, u32[]{:S(2)}) collective-permute-start(bf16[264,384]{1,0:T(8,128)(2,1)S(1)} %get-tuple-element.43), channel_id=1, source_target_pairs={{0,2},{1,3},{2,0},{3,1},{4,6},{5,7},{6,4},{7,5},{8,10},{9,11},{10,... | collective-permute-start | bytes 608264 | tf_op jit(solution)/shard_map/ppermute | solution.py:21
  122.2 10.7 %collective-permute-start.18 = (bf16[264,384]{1,0:T(8,128)(2,1)S(1)}, bf16[264,384]{1,0:T(8,128)(2,1)S(1)}, u32[]{:S(2)}, u32[]{:S(2)}) collective-permute-start(bf16[264,384]{1,0:T(8,128)(2,1)S(1)} %get-tuple-element.42), channel_id=1, source_target_pairs={{0,1},{1,2},{2,3},{3,0},{4,5},{5,6},{6,7},{7,4},{8,9},{9,10},{10,1... | collective-permute-start | bytes 608264 | tf_op jit(solution)/shard_map/ppermute | solution.py:21
  (9 other events, 21.6 us)
